TPU v7x, 256 devices: a whole 4x4x8 slice. The times are simulated.
256 devices in a mesh: atom: 8 (over x, z_hi), slab: 32 (over y, z_lo, core).
Axes of the slice: x: 4, y: 4, z: 8 (z_hi: 2, z_lo: 4; z = z_hi * 4 + z_lo), core: 2. Of those that a mesh axis runs over, the one named last changes fastest.
Arguments:
- atom_log_density: float32 [8, 512, 64, 512], P('atom', 'slab'), may hold values from -123 to 121
- prior_log_scaling: float32 [8, 512, 64, 512], P('atom', 'slab'), may hold values from -5 to 115
- atom_cotangent_rows: float32 [8, 512, 64, 512], P('atom', 'slab'), may hold values from -6 to 6
- barycenter_cotangent: float32 [512, 64, 512], P('slab'), may hold values from -6 to 6
- weights: float32 [8], replicated, may hold values from 0.2 to 1
- band: int32 [3], replicated, may hold values from 1 to 8, as said below
- slot_atom_index: int32 [8], replicated, may hold values from 0 to 7, each once
Outputs:
- log_atom_gradient: float32 [8, 512, 64, 512], P('atom', 'slab')
- weight_grad: float32 [8], replicated
Inputs may be any that keep to these rules, and one draw needn't show every extreme that they name: `band`: at least one entry equals 8. `slot_atom_index`: each atom is held in exactly one slot.
All inputs are finite; a program needn't handle non-finite values.
Results may differ from a plain program's by a relative error of at most 0.0003.
Values sent between devices are 32-bit elements; how exact they have to be, the bound alone decides.
No kernel may reach another device: no remote copies, remote signals or barrier semaphores. Data moves between devices by JAX's collectives and lax.ppermute only.
A program may use at most 64 MiB of HBM per device.

v0:
```python
import jax
import jax.numpy as jnp
from jax import lax
from jax.sharding import PartitionSpec as P

BAND_MAX = 8


def kernel_table(row_count, col_count, half):
    row_pos = jnp.arange(row_count, dtype=jnp.int32)
    col_pos = jnp.arange(col_count, dtype=jnp.int32)
    offsets = row_pos[:, None] - col_pos[None, :]
    spread = offsets.astype(jnp.float32)
    values = jnp.exp(-2.0 * spread * spread / (BAND_MAX * BAND_MAX))
    return jnp.where(jnp.abs(offsets) <= half, values, jnp.float32(0.0))


def gaussian_blur_slabs(field, kernel_columns, kernel_rows, band):
    high = lax.Precision.HIGHEST
    section = jnp.einsum("azyx,xv->azyv", field, kernel_columns, precision=high)
    section = jnp.einsum("azyx,yv->azvx", section, kernel_rows, precision=high)
    plane_count = field.shape[1]
    all_planes = plane_count * lax.axis_size("slab")
    kern_z = kernel_table(all_planes, all_planes, band[2])
    blurred = jnp.einsum(
        "pq,aqyx->apyx",
        kern_z,
        lax.all_to_all(section, "slab", split_axis=2, concat_axis=1, tiled=True),
        precision=high,
    )
    return lax.all_to_all(blurred, "slab", split_axis=1, concat_axis=2, tiled=True)


def body(
    atom_log_density,
    prior_log_scaling,
    atom_cotangent_rows,
    barycenter_cotangent,
    weights,
    band,
    slot_atom_index,
):
    held = atom_log_density.shape[0]
    plane_count, row_count, col_count = barycenter_cotangent.shape
    all_cells = plane_count * lax.axis_size("slab") * row_count * col_count
    kernel_columns = kernel_table(col_count, col_count, band[0])
    kernel_rows = kernel_table(row_count, row_count, band[1])
    atom_start = lax.axis_index("atom") * held
    slot_ids = lax.dynamic_slice_in_dim(slot_atom_index, atom_start, held)
    onehot = (slot_ids[:, None] == jnp.arange(weights.shape[0], dtype=jnp.int32)[None, :]).astype(
        jnp.float32
    )
    weight_here = jnp.sum(onehot * weights[None, :], axis=1)
    summed = barycenter_cotangent + lax.psum(jnp.sum(atom_cotangent_rows, axis=0), "atom")
    peak_gradient = lax.pmax(jnp.max(prior_log_scaling, axis=(1, 2, 3)), "slab")
    first_entry = gaussian_blur_slabs(
        jnp.exp(prior_log_scaling - peak_gradient[:, None, None, None]),
        kernel_columns,
        kernel_rows,
        band,
    )
    potential = atom_log_density - (jnp.log(first_entry) + peak_gradient[:, None, None, None])
    peak_f = lax.pmax(jnp.max(potential, axis=(1, 2, 3)), "slab")
    shifted = jnp.exp(potential - peak_f[:, None, None, None])
    second = gaussian_blur_slabs(shifted, kernel_columns, kernel_rows, band)
    mixed = jnp.log(second) + peak_f[:, None, None, None]
    adjoint = weight_here[:, None, None, None] * summed[None] - atom_cotangent_rows
    log_atom_gradient = shifted * gaussian_blur_slabs(
        adjoint / second, kernel_columns, kernel_rows, band
    )
    partial_value = jnp.sum(summed[None] * mixed, axis=(1, 2, 3))
    spread_sums = jnp.sum(onehot * partial_value[:, None], axis=0)
    weight_grad = lax.psum(spread_sums, ("atom", "slab")) / all_cells
    return (log_atom_gradient, weight_grad)


def solution(mesh):
    return jax.shard_map(
        body,
        mesh=mesh,
        in_specs=(
            P("atom", "slab", None, None),
            P("atom", "slab", None, None),
            P("atom", "slab", None, None),
            P("slab", None, None),
            P(),
            P(),
            P(),
        ),
        out_specs=(P("atom", "slab", None, None), P()),
        check_vma=False,
    )
```

profile of v0, /device:TPU:10, one launch (start us, length us, event | category | flops | bytes accessed | tf_op | source)
XLA Modules:
  0.0 789.4 jit_solution(9289091748990186530)
XLA Ops:
  7.2 0.0 copy-start.5
  7.2 0.0 copy-start.6
  7.2 2.9 reduce_max.22
  10.1 62.2 %pmax.14 = f32[]{:T(128)} all-reduce(f32[]{:T(128)} %reduce_max.22), channel_id=1, replica_groups=mesh['atom'=8,'slab'=32] {'slab'}, use_global_device_ids=true, to_apply=%region_1.2 | all-reduce | flops 1 | bytes 8 | tf_op jit(solution)/shard_map/pmax | solution.py:55
  72.3 0.6 fusion.112
  72.9 5.4 fusion.3
  78.3 2.6 convolution_bitcast_fusion.5
  80.9 1.2 copy.68
  82.1 63.5 %all_to_all.90 = f32[1,16,64,512]{3,1,0,2:T(8,128)S(1)} all-to-all(f32[1,16,64,512]{3,1,0,2:T(8,128)S(1)} %copy.68), channel_id=1, replica_groups=mesh['atom'=8,'slab'=32] {'slab'}, dimensions={2} | all-to-all | bytes 4194304 | tf_op jit(solution)/shard_map/all_to_all | solution.py:28
  145.6 0.3 copy.69
  145.9 8.7 %convolution_bitcast_fusion.4 = f32[1,512,2,512]{1,3,2,0:T(8,128)} fusion(f32[512,2,512]{2,0,1:T(8,128)S(1)} %bitcast.103, s32[]{:T(128)} %bitcast.10), kind=kOutput, calls=%fused_computation.26 | convolution fusion | flops 3223322624 | bytes 4194308 | tf_op jit(solution)/shard_map/pq,aqyx->apyx/dot_general | solution.py:25
  154.6 4.1 copy.71
  158.7 54.4 %all_to_all.91 = f32[1,512,2,512]{3,2,0,1:T(2,128)S(1)} all-to-all(f32[1,512,2,512]{3,2,0,1:T(2,128)} %copy.71), channel_id=1, replica_groups=mesh['atom'=8,'slab'=32] {'slab'}, dimensions={1} | all-to-all | bytes 4194304 | tf_op jit(solution)/shard_map/all_to_all | solution.py:31
  213.1 1.1 fusion.9
  214.2 0.0 copy-start
  214.2 0.2 copy.73
  214.4 1.4 copy-done
  215.8 1.9 fusion.111
  217.8 61.7 %pmax.15 = f32[]{:T(128)} all-reduce(f32[]{:T(128)} %fusion.111), channel_id=1, replica_groups=mesh['atom'=8,'slab'=32] {'slab'}, use_global_device_ids=true, to_apply=%region_3.4 | all-reduce | flops 1 | bytes 8 | tf_op jit(solution)/shard_map/pmax | solution.py:63
  279.4 3.6 fusion.13
  283.0 5.4 fusion.7
  288.4 2.6 convolution_bitcast_fusion.3
  291.0 1.2 copy.79
  292.2 61.8 %all_to_all.92 = f32[1,16,64,512]{3,1,0,2:T(8,128)S(1)} all-to-all(f32[1,16,64,512]{3,1,0,2:T(8,128)S(1)} %copy.79), channel_id=1, replica_groups=mesh['atom'=8,'slab'=32] {'slab'}, dimensions={2} | all-to-all | bytes 4194304 | tf_op jit(solution)/shard_map/all_to_all | solution.py:28
  354.0 0.3 copy.80
  354.4 8.9 %convolution_bitcast_fusion.2 = f32[1,512,2,512]{1,3,2,0:T(8,128)} fusion(f32[512,2,512]{2,0,1:T(8,128)S(1)} %bitcast.108, s32[]{:T(128)} %bitcast.10), kind=kOutput, calls=%fused_computation.24 | convolution fusion | flops 3223322624 | bytes 4194308 | tf_op jit(solution)/shard_map/pq,aqyx->apyx/dot_general | solution.py:25
  363.3 4.1 copy.82
  367.4 7.2 all-to-all-start.3
  374.7 0.2 all-reduce.2.cloned.1.call-start
  374.9 4.1 copy.118
  379.0 0.0 all-reduce.2.cloned.1.call-update
  379.1 0.6 copy-done.7
  379.7 0.6 dynamic_slice.3
  380.3 1.2 fusion.83
  381.5 119.8 %all-to-all-done.3 = f32[1,512,2,512]{3,2,0,1:T(2,128)} async-done(((f32[1,512,2,512]{3,2,0,1:T(2,128)}), f32[1,512,2,512]{3,2,0,1:T(2,128)}, u32[]{:S(2)}, u32[]{:S(2)}) %all-to-all-start.3) | async-done | bytes 2097184 | tf_op jit(solution)/shard_map/all_to_all | solution.py:31
  501.3 2.0 copy.83
  503.3 1.3 copy-done.2
  504.6 1.6 copy.84
  506.1 86.2 %all-reduce.2.cloned.1.call-done = f32[16,64,512]{2,0,1:T(8,128)} async-done(((f32[16,64,512]{2,0,1:T(8,128)}), f32[16,64,512]{2,0,1:T(8,128)}) %all-reduce.2.cloned.1.call-update) | async-done | bytes 2097168 | tf_op jit(solution)/shard_map/psum | solution.py:54
  592.3 6.8 fusion.2
  599.1 5.4 fusion.5
  604.5 2.6 convolution_bitcast_fusion.1
  607.1 1.4 copy.86
  608.5 55.2 %all_to_all.93 = f32[1,16,64,512]{3,1,0,2:T(8,128)S(1)} all-to-all(f32[1,16,64,512]{3,1,0,2:T(8,128)S(1)} %copy.86), channel_id=1, replica_groups=mesh['atom'=8,'slab'=32] {'slab'}, dimensions={2} | all-to-all | bytes 4194304 | tf_op jit(solution)/shard_map/all_to_all | solution.py:28
  663.7 0.3 copy.87
  664.0 8.9 %convolution_bitcast_fusion = f32[1,512,2,512]{1,3,2,0:T(8,128)} fusion(f32[512,2,512]{2,0,1:T(8,128)S(1)} %bitcast.105, s32[]{:T(128)} %bitcast.10), kind=kOutput, calls=%fused_computation.22 | convolution fusion | flops 3223322624 | bytes 4194308 | tf_op jit(solution)/shard_map/pq,aqyx->apyx/dot_general | solution.py:25
  673.0 4.1 copy.89
  677.1 7.1 all-to-all-start.5
  684.3 2.4 log_add_fusion
  686.7 0.0 copy-start.3
  686.7 0.2 copy.92
  686.9 1.4 copy-done.3
  688.3 0.6 copy-done.4
  688.9 2.2 fusion
  691.2 1.3 compare_select_fusion
  692.5 81.0 %psum.15 = f32[8]{0:T(128)S(1)} all-reduce(f32[8]{0:T(128)S(1)} %compare_select_fusion), channel_id=1, replica_groups=mesh['atom'=8,'slab'=32] {'atom','slab'}, use_global_device_ids=true, to_apply=%region_7.8 | all-reduce | flops 8 | bytes 64 | tf_op jit(solution)/shard_map/psum | solution.py:73
  773.5 0.5 broadcast_multiply_fusion
  774.0 0.0 all-to-all-done.5
  774.0 2.0 copy.90
  776.0 0.0 copy-start.1
  776.0 0.2 copy.91
  776.2 1.4 copy-done.1
  777.6 2.2 fusion.12
  779.8 2.5 copy.93
  (7 shorter events, 0.0 us)
Async XLA Ops:
  7.2 65.8 %copy-start.5 = (f32[1,16,64,512]{3,2,1,0:T(8,128)S(1)}, f32[1,16,64,512]{3,2,1,0:T(8,128)}, u32[]{:S(2)}) copy-start(f32[1,16,64,512]{3,2,1,0:T(8,128)} %param.8) | copy-start | bytes 6291460
  7.2 65.1 %copy-start.6 = (s32[3]{0:T(128)S(1)}, s32[3]{0:T(128)}, u32[]{:S(2)}) copy-start(s32[3]{0:T(128)} %param.12) | copy-start | bytes 40
  214.2 1.6 copy-start
  367.4 133.8 %all-to-all-start.3 = ((f32[1,512,2,512]{3,2,0,1:T(2,128)}), f32[1,512,2,512]{3,2,0,1:T(2,128)}, u32[]{:S(2)}, u32[]{:S(2)}) async-start(f32[1,512,2,512]{3,2,0,1:T(2,128)} %copy.82), calls=%async_computation.3 | async-start | bytes 4194304 | tf_op jit(solution)/shard_map/all_to_all | solution.py:31
  374.7 217.6 %all-reduce.2.cloned.1.call-start = ((), (), s32[]{:S(2)}) async-start(), calls=%async_computation.6 | async-start | bytes 4194304 | tf_op jit(solution)/shard_map/psum | solution.py:54
  379.0 0.7 copy-start.7
  379.0 1.2 copy-start.8
  503.3 1.3 copy-start.2
  677.1 96.9 %all-to-all-start.5 = ((f32[1,512,2,512]{3,2,0,1:T(2,128)}), f32[1,512,2,512]{3,2,0,1:T(2,128)}, u32[]{:S(2)}, u32[]{:S(2)}) async-start(f32[1,512,2,512]{3,2,0,1:T(2,128)} %copy.89), calls=%async_computation.5 | async-start | bytes 4194304 | tf_op jit(solution)/shard_map/all_to_all | solution.py:31
  686.7 1.6 copy-start.3
  686.7 2.2 copy-start.4
  776.0 1.6 copy-start.1
Sparse Core Ops, SparseCore 0:
  379.2 213.0 all-reduce.1
where the time goes:
time: 799 us; the launch traced here: 789 us
  blocking collectives  440 us (55%)
  waiting for transfers between devices  206 us (26%)
  matrix products  50.5 us (6%)
  local copies, waits for them, and re-layouts  37.8 us (5%)
  other arithmetic  26.1 us (3%)
  starting transfers between devices  14.6 us (2%)
  between operations  14.5 us (2%)
    all_to_all x3, blocking collectives, gaussian_blur_slabs(): lax.all_to_all(section, 'slab', split_axis=2, concat_axis=1, tiled=True)  180 us
    all_to_all x2, waiting for transfers between devices, gaussian_blur_slabs(): lax.all_to_all(blurred, 'slab', split_axis=1, concat_axis=2, tiled=True)  120 us
    psum x1, waiting for transfers between devices, body(): lax.psum(jnp.sum(atom_cotangent_rows, axis=0), 'atom')  86.2 us
    psum x1, blocking collectives, body(): weight_grad = lax.psum(spread_sums, ('atom', 'slab')) / all_cells  81 us
    pmax x1, blocking collectives, body(): peak_gradient = lax.pmax(jnp.max(prior_log_scaling, axis=(1, 2, 3)), 'slab')  62.2 us
    pmax x1, blocking collectives, body(): peak_f = lax.pmax(jnp.max(potential, axis=(1, 2, 3)), 'slab')  61.7 us
    all_to_all x1, blocking collectives, gaussian_blur_slabs(): lax.all_to_all(blurred, 'slab', split_axis=1, concat_axis=2, tiled=True)  54.4 us
    dot_general x3, matrix products, gaussian_blur_slabs(): jnp.einsum('pq,aqyx->apyx', kern_z, lax.all_to_all(section, 'slab', split...  26.6 us
  transfers between devices with their start and end apart: 3, of which 2 were waited for; matrix products, arithmetic and copies ran while one was open for 2% of the time, Pallas kernels for 0%

commit v1 on v0

v1 whole, which is shorter than its diff:
```python
import functools

import jax
import jax.numpy as jnp
from jax import lax
from jax.experimental import pallas as pl
from jax.experimental.pallas import tpu as pltpu
from jax.sharding import PartitionSpec as P

BAND_MAX = 8
GROUP = 4
F32 = jnp.float32
BF16 = jnp.bfloat16
VMEM_LIMIT = 40 * 1024 * 1024


def split(value):
    high = value.astype(BF16)
    return high, (value - high.astype(F32)).astype(BF16)


def dot(a, b):
    return jnp.dot(a, b, preferred_element_type=F32)


def dot3(ah, al, bh, bl):
    return dot(ah, bh) + (dot(al, bh) + dot(ah, bl))


def peak(value):
    return jnp.max(jnp.max(value, axis=0, keepdims=True), axis=1, keepdims=True)


def rows_of(values):
    return jnp.concatenate([jnp.broadcast_to(v, (1, 128)) for v in values], axis=0)


def tables_kernel(band, th, tl, kxh, kxl, *, ny):
    shift = ny.bit_length() - 1

    def entries(sq, ok):
        return jnp.where(ok, jnp.exp(sq.astype(F32) * (-2.0 / (BAND_MAX * BAND_MAX))), 0.0)

    shape = th.shape
    row = lax.broadcasted_iota(jnp.int32, shape, 0)
    col = lax.broadcasted_iota(jnp.int32, shape, 1)
    dz = (row >> shift) - (col >> shift) + BAND_MAX
    dy = (row & (ny - 1)) - (col & (ny - 1))
    ok = (jnp.abs(dz) <= band[2]) & (jnp.abs(dy) <= band[1])
    th[...], tl[...] = split(entries(dz * dz + dy * dy, ok))
    shape = kxh.shape
    dx = lax.broadcasted_iota(jnp.int32, shape, 0) - lax.broadcasted_iota(jnp.int32, shape, 1)
    kxh[...], kxl[...] = split(entries(dx * dx, jnp.abs(dx) <= band[0]))


def own_product(th, tl, eh, el, y):
    block = th.shape[0]
    count = y.shape[0] // block
    reach = th.shape[1] // block // 2
    for g in range(count):
        first, last = max(0, g - reach), min(count - 1, g + reach)
        rows = slice(first * block, (last + 1) * block)
        cols = slice((first - g + reach) * block, (last - g + reach + 1) * block)
        y[g * block : (g + 1) * block, :] = dot3(th[:, cols], tl[:, cols], eh[rows, :], el[rows, :])


def own_log_kernel(lo, hi, th, tl, y, stats, eh, el):
    half = lo.shape[0]
    m_lo, m_hi = peak(lo[...]), peak(hi[...])
    m = jnp.maximum(m_lo, m_hi)
    eh[:half, :], el[:half, :] = split(jnp.exp(lo[...] - m))
    eh[half:, :], el[half:, :] = split(jnp.exp(hi[...] - m))
    stats[...] = rows_of([m_lo, m_hi, m, m, m, m, m, m])
    own_product(th, tl, eh, el, y)


def own_linear_kernel(lo, hi, stats, th, tl, y, eh, el):
    half = lo.shape[0]
    c = stats[0:1, 0:1]
    f_lo = jnp.exp((c - stats[1:2, 0:1]) * 0.5)
    f_hi = jnp.exp((c - stats[2:3, 0:1]) * 0.5)
    eh[:half, :], el[:half, :] = split(lo[...] * f_lo * f_lo)
    eh[half:, :], el[half:, :] = split(hi[...] * f_hi * f_hi)
    own_product(th, tl, eh, el, y)


def halo_product(g, count, th, tl, eh, el, acc):
    block = th.shape[0]
    reach = th.shape[1] // block // 2
    for step in range(count):

        @pl.when(g == step)
        def _(step=step):
            parts = []
            left = reach - step
            if left > 0:
                rows = slice((reach - left) * block, reach * block)
                parts.append((slice(0, left * block), rows))
            right = step + reach - count + 1
            if right > 0:
                cols = slice((2 * reach + 1 - right) * block, (2 * reach + 1) * block)
                parts.append((cols, slice(reach * block, (reach + right) * block)))
            total = jnp.zeros(acc.shape, F32)
            for cols, rows in parts:
                total = total + dot3(th[:, cols], tl[:, cols], eh[rows, :], el[rows, :])
            acc[...] = total


def columns_product(value, kxh, kxl):
    vh, vl = split(value)
    return dot3(vh, vl, kxh[...], kxl[...])


def log_halos(where, left, right, stats, eh, el, scale):
    half = left.shape[0]
    has_left, has_right = where[0] > 0, where[1] > 0
    m_own = stats[2:3, 0:1]
    m_left = jnp.where(has_left, peak(left[...]), m_own)
    m_right = jnp.where(has_right, peak(right[...]), m_own)
    c = jnp.maximum(m_own, jnp.maximum(m_left, m_right))
    eh[:half, :], el[:half, :] = split(jnp.where(has_left, jnp.exp(left[...] - c), 0.0))
    eh[half:, :], el[half:, :] = split(jnp.where(has_right, jnp.exp(right[...] - c), 0.0))
    own = jnp.exp(m_own - c)
    scale[...] = rows_of([c, stats[0:1, 0:1], stats[1:2, 0:1], m_left, m_right, own, own, own])


def potential_kernel(
    where, left, right, y, stats, density, th, tl, kxh, kxl, lo, hi, eh, el, scale, acc, *, count
):
    g = pl.program_id(0)

    @pl.when(g == 0)
    def _():
        log_halos(where, left, right, stats, eh, el, scale)

    halo_product(g, count, th, tl, eh, el, acc)
    first = columns_product(y[...] * scale[5:6, 0:1] + acc[...], kxh, kxl)
    potential = density[...] - (jnp.log(first) + scale[0:1, 0:1])

    @pl.when(g < count // 2)
    def _():
        lo[...] = potential

    @pl.when(g >= count // 2)
    def _():
        hi[...] = potential


def ratio_kernel(
    where,
    weight,
    left,
    right,
    y,
    stats,
    bary,
    cot,
    sum0,
    sum1,
    sum2,
    sum3,
    th,
    tl,
    kxh,
    kxl,
    lo,
    hi,
    stats_out,
    total,
    eh,
    el,
    scale,
    acc,
    *,
    count,
):
    g = pl.program_id(0)

    @pl.when(g == 0)
    def _():
        log_halos(where, left, right, stats, eh, el, scale)
        stats_out[...] = scale[...]
        total[...] = jnp.zeros(total.shape, F32)

    halo_product(g, count, th, tl, eh, el, acc)
    c = scale[0:1, 0:1]
    second = columns_product(y[...] * scale[5:6, 0:1] + acc[...], kxh, kxl)
    mixed = jnp.log(second) + c
    away = lax.rem(g - where[2] + count, count)
    over_atoms = jnp.where(
        away == 0,
        sum0[...],
        jnp.where(away == 1, sum1[...], jnp.where(away == 2, sum2[...], sum3[...])),
    )
    summed = bary[...] + over_atoms
    share = summed * mixed
    share = jnp.sum(share.reshape(share.shape[0] // 8, 8, share.shape[1]), axis=0)
    for k in range(share.shape[1] // 128):
        total[...] += share[:, k * 128 : (k + 1) * 128]
    ratio = (weight[0] * summed - cot[...]) / second

    @pl.when(g < count // 2)
    def _():
        f = jnp.exp((scale[1:2, 0:1] - c) * 0.5)
        lo[...] = ratio * f * f

    @pl.when(g >= count // 2)
    def _():
        f = jnp.exp((scale[2:3, 0:1] - c) * 0.5)
        hi[...] = ratio * f * f


def gradient_kernel(where, left, right, y, stats, pot_lo, pot_hi, th, tl, kxh, kxl, out, eh, el, acc, *, count):
    g = pl.program_id(0)
    c = stats[0:1, 0:1]

    @pl.when(g == 0)
    def _():
        half = left.shape[0]
        f = jnp.exp((c - stats[3:4, 0:1]) * 0.5)
        eh[:half, :], el[:half, :] = split(jnp.where(where[0] > 0, left[...] * f * f, 0.0))
        f = jnp.exp((c - stats[4:5, 0:1]) * 0.5)
        eh[half:, :], el[half:, :] = split(jnp.where(where[1] > 0, right[...] * f * f, 0.0))

    halo_product(g, count, th, tl, eh, el, acc)
    blurred = columns_product(y[...] + acc[...], kxh, kxl)
    potential = jnp.where(g < count // 2, pot_lo[...], pot_hi[...])
    out[...] = jnp.exp(potential - c) * blurred


def body(
    atom_log_density,
    prior_log_scaling,
    atom_cotangent_rows,
    barycenter_cotangent,
    weights,
    band,
    slot_atom_index,
):
    planes, ny, nx = barycenter_cotangent.shape
    slabs, atoms = lax.axis_size("slab"), lax.axis_size("atom")
    rows = planes * ny
    half = rows // 2
    block = GROUP * ny
    count = planes // GROUP
    reach = BAND_MAX // GROUP
    slab_at, atom_at = lax.axis_index("slab"), lax.axis_index("atom")
    across = atoms // 2
    x_at = atom_at // 2

    smem = pl.BlockSpec(memory_space=pltpu.SMEM)
    params = pltpu.CompilerParams(vmem_limit_bytes=VMEM_LIMIT)

    def shape(*dims, dtype=F32):
        return jax.ShapeDtypeStruct(dims, dtype)

    def full(*dims):
        return pl.BlockSpec(dims, lambda g: (0,) * len(dims))

    def send(value, axis, pairs):
        return lax.ppermute(value, axis, pairs)

    to_right = [(i, i + 1) for i in range(slabs - 1)]
    to_left = [(i + 1, i) for i in range(slabs - 1)]
    ahead = {
        k: [(2 * x + z, 2 * ((x + k) % across) + z) for x in range(across) for z in range(2)]
        for k in range(1, across)
    }
    swap = [(i, i ^ 1) for i in range(atoms)]

    prior = prior_log_scaling.reshape(rows, nx)
    prior_lo, prior_hi = prior[:half], prior[half:]
    from_left = send(prior_hi, "slab", to_right)
    from_right = send(prior_lo, "slab", to_left)

    cot = atom_cotangent_rows.reshape(rows, nx)

    def block_of(k):
        return lax.dynamic_slice_in_dim(cot, lax.rem(x_at + k, count) * block, block)

    part = block_of(0)
    for k in range(1, across):
        part = part + send(block_of(k), "atom", ahead[k])
    both = part + send(part, "atom", swap)
    sums = [both] + [send(both, "atom", ahead[across - k]) for k in range(1, across)]

    where = jnp.stack([(slab_at > 0), (slab_at < slabs - 1), x_at, x_at]).astype(jnp.int32)
    slot = lax.dynamic_slice_in_dim(slot_atom_index, atom_at, 1)
    onehot = (slot[0] == jnp.arange(weights.shape[0], dtype=jnp.int32)).astype(F32)
    weight = jnp.sum(onehot * weights, keepdims=True)

    t_shape, k_shape = (block, (2 * reach + 1) * block), (nx, nx)
    tables = pl.pallas_call(
        functools.partial(tables_kernel, ny=ny),
        out_shape=[
            shape(*t_shape, dtype=BF16),
            shape(*t_shape, dtype=BF16),
            shape(*k_shape, dtype=BF16),
            shape(*k_shape, dtype=BF16),
        ],
        in_specs=[smem],
        compiler_params=params,
        name="tables",
    )(band)
    pair_scratch = [pltpu.VMEM((rows, nx), BF16), pltpu.VMEM((rows, nx), BF16)]
    own_out = [shape(rows, nx), shape(8, 128)]

    own_log = pl.pallas_call(
        own_log_kernel, out_shape=own_out, scratch_shapes=pair_scratch, compiler_params=params, name="own_log"
    )
    table_specs = [full(*t_shape), full(*t_shape), full(*k_shape), full(*k_shape)]
    halo_specs = [full(half, nx), full(half, nx)]
    one = pl.BlockSpec((block, nx), lambda g: (g, 0))
    lo_spec = pl.BlockSpec((block, nx), lambda g: (jnp.minimum(g, count // 2 - 1), 0))
    hi_spec = pl.BlockSpec((block, nx), lambda g: (jnp.maximum(g - count // 2, 0), 0))
    stat_spec = full(8, 128)
    scale_scratch = [pltpu.VMEM((8, 128), F32)]
    acc_scratch = [pltpu.VMEM((block, nx), F32)]

    y, stats = own_log(prior_lo, prior_hi, *tables[:2])
    pot_lo, pot_hi = pl.pallas_call(
        functools.partial(potential_kernel, count=count),
        grid=(count,),
        in_specs=[smem, *halo_specs, one, stat_spec, one, *table_specs],
        out_specs=[lo_spec, hi_spec],
        out_shape=[shape(half, nx), shape(half, nx)],
        scratch_shapes=pair_scratch + scale_scratch + acc_scratch,
        compiler_params=params,
        name="potential",
    )(where, from_left, from_right, y, stats, atom_log_density.reshape(rows, nx), *tables)

    from_left = send(pot_hi, "slab", to_right)
    from_right = send(pot_lo, "slab", to_left)
    y, stats = own_log(pot_lo, pot_hi, *tables[:2])
    ratio_lo, ratio_hi, stats, total = pl.pallas_call(
        functools.partial(ratio_kernel, count=count),
        grid=(count,),
        in_specs=[smem, smem, *halo_specs, one, stat_spec, one, one]
        + [full(block, nx)] * 4
        + table_specs,
        out_specs=[lo_spec, hi_spec, stat_spec, stat_spec],
        out_shape=[shape(half, nx), shape(half, nx), shape(8, 128), shape(8, 128)],
        scratch_shapes=pair_scratch + scale_scratch + acc_scratch,
        compiler_params=params,
        name="ratio",
    )(
        where,
        weight,
        from_left,
        from_right,
        y,
        stats,
        barycenter_cotangent.reshape(rows, nx),
        cot,
        *sums,
        *tables,
    )

    from_left = send(ratio_hi, "slab", to_right)
    from_right = send(ratio_lo, "slab", to_left)

    value = jnp.broadcast_to(jnp.sum(total), (8, 128))
    hop = 1
    while hop < slabs:
        value = value + send(value, "slab", [(i, i ^ hop) for i in range(slabs)])
        hop *= 2
    lanes = jnp.arange(128, dtype=jnp.int32)[None, :]
    value = jnp.where(lanes == slot[0], value, 0.0)
    hop = 1
    while hop < atoms:
        value = value + send(value, "atom", [(i, i ^ hop) for i in range(atoms)])
        hop *= 2
    weight_grad = value[0, : weights.shape[0]] / (rows * nx * slabs)

    (y,) = pl.pallas_call(
        own_linear_kernel,
        out_shape=[shape(rows, nx)],
        scratch_shapes=pair_scratch,
        compiler_params=params,
        name="own_linear",
    )(ratio_lo, ratio_hi, stats, *tables[:2])
    gradient = pl.pallas_call(
        functools.partial(gradient_kernel, count=count),
        grid=(count,),
        in_specs=[smem, *halo_specs, one, stat_spec, lo_spec, hi_spec, *table_specs],
        out_specs=one,
        out_shape=shape(rows, nx),
        scratch_shapes=pair_scratch + acc_scratch,
        compiler_params=params,
        name="gradient",
    )(where, from_left, from_right, y, stats, pot_lo, pot_hi, *tables)
    return gradient.reshape(atom_log_density.shape), weight_grad


def solution(mesh):
    return jax.shard_map(
        body,
        mesh=mesh,
        in_specs=(
            P("atom", "slab", None, None),
            P("atom", "slab", None, None),
            P("atom", "slab", None, None),
            P("slab", None, None),
            P(),
            P(),
            P(),
        ),
        out_specs=(P("atom", "slab", None, None), P()),
        check_vma=False,
    )
```

time: 799 us -> 178 us (0.22)
  blocking collectives: 440 us -> 0 us
  waiting for transfers between devices: 206 us -> 63 us
  matrix products: 50.5 us -> 0 us
  starting transfers between devices: 14.6 us -> 57 us
  Pallas kernels: 0 us -> 42.2 us
  local copies, waits for them, and re-layouts: 37.8 us -> 5.38 us
  other arithmetic: 26.1 us -> 7.13 us
  between operations: 14.5 us -> 0.91 us
    all_to_all x4 -> x0, blocking collectives: 235 us -> none  [the longest x3 180 us: gaussian_blur_slabs(): lax.all_to_all(section, 'slab', split_axis=2, concat_axis=1, tiled=True)]
    pmax x2 -> x0, blocking collectives: 124 us -> none  [the longest x1 62.2 us: body(): peak_gradient = lax.pmax(jnp.max(prior_log_scaling, axis=(1, 2, 3)), 'slab')]
    all_to_all x2 -> x0, waiting for transfers between devices: 120 us -> none  [gaussian_blur_slabs(): lax.all_to_all(blurred, 'slab', split_axis=1, concat_axis=2, tiled=True)]
    psum x1 -> x0, waiting for transfers between devices: 86.2 us -> none  [body(): lax.psum(jnp.sum(atom_cotangent_rows, axis=0), 'atom')]
    psum x1 -> x0, blocking collectives: 81 us -> none  [body(): weight_grad = lax.psum(spread_sums, ('atom', 'slab')) / all_cells]
    ppermute x0 -> x21, waiting for transfers between devices: none -> 63 us  [send(): return lax.ppermute(value, axis, pairs)]
    ppermute x0 -> x21, starting transfers between devices: none -> 57 us  [send(): return lax.ppermute(value, axis, pairs)]
    dot_general x9 -> x0, matrix products: 50.5 us -> none  [the longest x3 26.6 us: gaussian_blur_slabs(): jnp.einsum('pq,aqyx->apyx', kern_z, lax.all_to_all(section, 'slab', split...]
  transfers between devices with their start and end apart: 3 -> 21, of which waited for: 2 -> 14; matrix products, arithmetic and copies ran while one was open for 2% -> 5% of each run, Pallas kernels for 0% -> 14%
where the time goes in v1:
time: 178 us; the launch traced here: 176 us
  waiting for transfers between devices  63 us (35%)
  starting transfers between devices  57 us (32%)
  Pallas kernels  42.2 us (24%)
  other arithmetic  7.13 us (4%)
  local copies, waits for them, and re-layouts  5.38 us (3%)
    ppermute x21, waiting for transfers between devices, send(): return lax.ppermute(value, axis, pairs)  63 us
    ppermute x21, starting transfers between devices, send(): return lax.ppermute(value, axis, pairs)  57 us
    pallas_call x1, Pallas kernels, body(): pl.pallas_call(functools.partial(ratio_kernel, count=count), grid=(count,...  10.6 us
    pallas_call x1, Pallas kernels, body(): pl.pallas_call(functools.partial(potential_kernel, count=count), grid=(co...  7.96 us
    pallas_call x1, Pallas kernels, body(): pl.pallas_call(functools.partial(gradient_kernel, count=count), grid=(cou...  7.79 us
    pallas_call x1, Pallas kernels, body(): pl.pallas_call(own_linear_kernel, out_shape=[shape(rows, nx)], scratch_sh...  4.74 us
    pallas_call x1, Pallas kernels, body(): y, stats = own_log(prior_lo, prior_hi, *tables[:2])  4.61 us
    pallas_call x1, Pallas kernels, body(): y, stats = own_log(pot_lo, pot_hi, *tables[:2])  4.61 us
  transfers between devices with their start and end apart: 21, of which 14 were waited for; matrix products, arithmetic and copies ran while one was open for 5% of the time, Pallas kernels for 14%

profile of v1, /device:TPU:10, one launch (start us, length us, event | category | flops | bytes accessed | tf_op | source)
XLA Modules:
  0.0 175.7 jit_solution(11063785457752158117)
XLA Ops:
  0.6 0.0 copy-start.3
  0.6 2.9 %fusion.1 = (f32[1,8,64,512]{3,2,1,0:T(8,128)S(1)}, f32[1,8,64,512]{3,2,1,0:T(8,128)}) fusion(f32[1,16,64,512]{3,2,1,0:T(8,128)} %param.8), kind=kLoop, calls=%fused_computation.11 | loop fusion | bytes 4194304 | tf_op jit(solution)/shard_map/slice | solution.py:272
  3.5 2.0 %collective-permute-start = (f32[512,512]{1,0:T(8,128)}, f32[512,512]{1,0:T(8,128)}, u32[]{:S(2)}, u32[]{:S(2)}) collective-permute-start(f32[512,512]{1,0:T(8,128)} %bitcast.5.hi), channel_id=1, source_target_pairs={{0,1},{1,2},{2,3},{3,4},{4,5},{5,6},{6,7},{7,8},{8,9},{9,10},{10,1... | collective-permute-start | bytes 3145736 | tf_op jit(solution)/shard_map/ppermute | solution.py:261
  5.6 6.3 %collective-permute-start.1 = (f32[512,512]{1,0:T(8,128)S(1)}, f32[512,512]{1,0:T(8,128)}, u32[]{:S(2)}, u32[]{:S(2)}) collective-permute-start(f32[512,512]{1,0:T(8,128)S(1)} %bitcast.13), channel_id=1, source_target_pairs={{1,0},{2,1},{3,2},{4,3},{5,4},{6,5},{7,6},{8,7},{9,8},{10,9},{11,1... | collective-permute-start | bytes 3145736 | tf_op jit(solution)/shard_map/ppermute | solution.py:261
  12.0 1.2 constant_dynamic-slice_fusion.2
  13.2 1.5 collective-permute-start.4
  14.7 0.5 collective-permute-start.6
  15.3 2.1 %collective-permute-start.5 = (f32[256,512]{1,0:T(8,128)}, f32[256,512]{1,0:T(8,128)}, u32[]{:S(2)}, u32[]{:S(2)}) collective-permute-start(f32[256,512]{1,0:T(8,128)} %get-tuple-element.32), channel_id=1, source_target_pairs={{0,128},{32,160},{64,192},{96,224},{128,0},{160,32},{192,64},{224,... | collective-permute-start | bytes 1572872 | tf_op jit(solution)/shard_map/ppermute | solution.py:261
  17.4 1.9 %tables.1 = (bf16[256,1280]{1,0:T(8,128)(2,1)S(1)}, bf16[256,1280]{1,0:T(8,128)(2,1)S(1)}, bf16[512,512]{1,0:T(8,128)(2,1)S(1)}, bf16[512,512]{1,0:T(8,128)(2,1)S(1)}) custom-call(s32[3]{0:T(128)S(1)} %copy-done.2), custom_call_target="tpu_custom_call" | custom-call | tf_op jit(solution)/shard_map/tables/pallas_call | solution.py:293
  19.3 4.6 %own_log.2 = (f32[1024,512]{1,0:T(8,128)S(1)}, f32[8,128]{1,0:T(8,128)S(1)}) custom-call(f32[512,512]{1,0:T(8,128)S(1)} %bitcast.14, f32[512,512]{1,0:T(8,128)} %bitcast.5.hi, bf16[256,1280]{1,0:T(8,128)(2,1)S(1)} %get-tuple-element.16.th, bf16[256,1280]{1,0:T(8,128)(2,1)S(1)} %get-tuple-element.17.tl), custom_call_target="tpu_custom_call" | custom-call | tf_op jit(solution)/shard_map/own_log/pallas_call | solution.py:320
  24.0 0.0 copy-start
  24.0 0.1 pad_add_fusion.where
  24.1 4.4 %collective-permute-done.4 = f32[256,512]{1,0:T(8,128)} collective-permute-done((f32[256,512]{1,0:T(8,128)}, f32[256,512]{1,0:T(8,128)}, u32[]{:S(2)}, u32[]{:S(2)}) %collective-permute-start.4) | collective-permute-done | bytes 524320 | tf_op jit(solution)/shard_map/ppermute | solution.py:261
  28.4 0.9 collective-permute-done.6
  29.3 8.8 %collective-permute-done.5 = f32[256,512]{1,0:T(8,128)} collective-permute-done((f32[256,512]{1,0:T(8,128)}, f32[256,512]{1,0:T(8,128)}, u32[]{:S(2)}, u32[]{:S(2)}) %collective-permute-start.5) | collective-permute-done | bytes 524320 | tf_op jit(solution)/shard_map/ppermute | solution.py:261
  38.1 1.7 add_add_fusion
  39.8 6.4 %collective-permute-start.7 = (f32[256,512]{1,0:T(8,128)S(1)}, f32[256,512]{1,0:T(8,128)S(1)}, u32[]{:S(2)}, u32[]{:S(2)}) collective-permute-start(f32[256,512]{1,0:T(8,128)S(1)} %add_add_fusion), channel_id=1, source_target_pairs={{0,32},{32,0},{64,96},{96,64},{128,160},{160,128},{192,224},{224,1... | collective-permute-start | bytes 1572872 | tf_op jit(solution)/shard_map/ppermute | solution.py:261
  46.2 0.0 collective-permute-done.left
  46.2 0.0 collective-permute-done.1.right
  46.2 0.0 copy-start.4
  46.2 0.0 copy-start.5
  46.2 8.0 %potential.1 = (f32[512,512]{1,0:T(8,128)S(1)}, f32[512,512]{1,0:T(8,128)}) custom-call(s32[4]{0:T(128)S(1)} %pad_add_fusion.where, f32[512,512]{1,0:T(8,128)} %collective-permute-done.left, f32[512,512]{1,0:T(8,128)} %collective-permute-done.1.right, f32[1024,512]{1,0:T(8,128)S(1)} %get-tuple-element.18.y, f32[8,128]{1,0:T(8,128)S(1)} %get-tuple-element.19.stats, ...), custom_call_target="tpu_custom_call" | custom-call | tf_op jit(solution)/shard_map/potential/pallas_call | solution.py:321
  54.2 1.9 %collective-permute-start.2 = (f32[512,512]{1,0:T(8,128)}, f32[512,512]{1,0:T(8,128)}, u32[]{:S(2)}, u32[]{:S(2)}) collective-permute-start(f32[512,512]{1,0:T(8,128)} %get-tuple-element.22.hi.pot_hi), channel_id=1, source_target_pairs={{0,1},{1,2},{2,3},{3,4},{4,5},{5,6},{6,7},{7,8},{8,9},{9,10},{10,1... | collective-permute-start | bytes 3145736 | tf_op jit(solution)/shard_map/ppermute | solution.py:261
  56.1 6.3 %collective-permute-start.3 = (f32[512,512]{1,0:T(8,128)S(1)}, f32[512,512]{1,0:T(8,128)}, u32[]{:S(2)}, u32[]{:S(2)}) collective-permute-start(f32[512,512]{1,0:T(8,128)S(1)} %get-tuple-element.23.lo.pot_lo), channel_id=1, source_target_pairs={{1,0},{2,1},{3,2},{4,3},{5,4},{6,5},{7,6},{8,7},{9,8},{10,9},{11,1... | collective-permute-start | bytes 3145736 | tf_op jit(solution)/shard_map/ppermute | solution.py:261
  62.4 0.0 collective-permute-done.7
  62.4 0.9 add.72.sum0
  63.3 0.0 collective-permute-start.10
  63.3 3.0 %collective-permute-start.9 = (f32[256,512]{1,0:T(8,128)}, f32[256,512]{1,0:T(8,128)}, u32[]{:S(2)}, u32[]{:S(2)}) collective-permute-start(f32[256,512]{1,0:T(8,128)} %add.72.sum0), channel_id=1, source_target_pairs={{0,128},{32,160},{64,192},{96,224},{128,0},{160,32},{192,64},{224,... | collective-permute-start | bytes 1572872 | tf_op jit(solution)/shard_map/ppermute | solution.py:261
  66.3 1.4 collective-permute-start.8
  67.7 0.6 dynamic_slice.15
  68.3 1.4 fusion
  69.6 4.6 %own_log.3 = (f32[1024,512]{1,0:T(8,128)S(1)}, f32[8,128]{1,0:T(8,128)S(1)}) custom-call(f32[512,512]{1,0:T(8,128)S(1)} %get-tuple-element.23.lo.pot_lo, f32[512,512]{1,0:T(8,128)} %get-tuple-element.22.hi.pot_hi, bf16[256,1280]{1,0:T(8,128)(2,1)S(1)} %get-tuple-element.16.th, bf16[256,1280]{1,0:T(8,128)(2,1)S(1)} %get-tuple-element.17.tl), custom_call_target="tpu_custom_call" | custom-call | tf_op jit(solution)/shard_map/own_log/pallas_call | solution.py:334
  74.2 4.3 %collective-permute-done.10.sum3 = f32[256,512]{1,0:T(8,128)} collective-permute-done((f32[256,512]{1,0:T(8,128)}, f32[256,512]{1,0:T(8,128)}, u32[]{:S(2)}, u32[]{:S(2)}) %collective-permute-start.10) | collective-permute-done | bytes 524320 | tf_op jit(solution)/shard_map/ppermute | solution.py:261
  78.5 1.5 collective-permute-done.9.sum2
  80.0 6.9 %collective-permute-done.8.sum1 = f32[256,512]{1,0:T(8,128)} collective-permute-done((f32[256,512]{1,0:T(8,128)}, f32[256,512]{1,0:T(8,128)}, u32[]{:S(2)}, u32[]{:S(2)}) %collective-permute-start.8) | collective-permute-done | bytes 524320 | tf_op jit(solution)/shard_map/ppermute | solution.py:261
  86.9 4.7 %collective-permute-done.2.left = f32[512,512]{1,0:T(8,128)} collective-permute-done((f32[512,512]{1,0:T(8,128)}, f32[512,512]{1,0:T(8,128)}, u32[]{:S(2)}, u32[]{:S(2)}) %collective-permute-start.2) | collective-permute-done | bytes 1048608 | tf_op jit(solution)/shard_map/ppermute | solution.py:261
  91.6 0.0 collective-permute-done.3.right
  91.6 10.6 %ratio.1 = (f32[512,512]{1,0:T(8,128)}, f32[512,512]{1,0:T(8,128)}, f32[8,128]{1,0:T(8,128)S(1)}, f32[8,128]{1,0:T(8,128)S(1)}) custom-call(s32[4]{0:T(128)S(1)} %pad_add_fusion.where, f32[1]{0:T(128)} %bitcast.4.weight, f32[512,512]{1,0:T(8,128)} %collective-permute-done.2.left, f32[512,512]{1,0:T(8,128)} %collective-permute-done.3.right, ...), custom_call_target="tpu_custom_call" | custom-call | tf_op jit(solution)/shard_map/ratio/pallas_call | solution.py:335
  102.2 2.2 %collective-permute-start.11 = (f32[512,512]{1,0:T(8,128)}, f32[512,512]{1,0:T(8,128)}, u32[]{:S(2)}, u32[]{:S(2)}) collective-permute-start(f32[512,512]{1,0:T(8,128)} %get-tuple-element.26.hi), channel_id=1, source_target_pairs={{0,1},{1,2},{2,3},{3,4},{4,5},{5,6},{6,7},{7,8},{8,9},{9,10},{10,1... | collective-permute-start | bytes 3145736 | tf_op jit(solution)/shard_map/ppermute | solution.py:261
  104.5 10.3 %collective-permute-start.12 = (f32[512,512]{1,0:T(8,128)}, f32[512,512]{1,0:T(8,128)}, u32[]{:S(2)}, u32[]{:S(2)}) collective-permute-start(f32[512,512]{1,0:T(8,128)} %get-tuple-element.27.lo), channel_id=1, source_target_pairs={{1,0},{2,1},{3,2},{4,3},{5,4},{6,5},{7,6},{8,7},{9,8},{10,9},{11,1... | collective-permute-start | bytes 3145736 | tf_op jit(solution)/shard_map/ppermute | solution.py:261
  114.8 0.6 reduce_sum.19
  115.4 0.6 broadcast_in_dim.21
  116.0 0.1 collective-permute-start.13
  116.1 1.2 collective-permute-done.13
  117.3 0.6 broadcast_add_fusion
  117.9 0.1 collective-permute-start.14
  118.0 14.0 %collective-permute-done.14 = f32[8,128]{1,0:T(8,128)S(1)} collective-permute-done((f32[8,128]{1,0:T(8,128)S(1)}, f32[8,128]{1,0:T(8,128)S(1)}, u32[]{:S(2)}, u32[]{:S(2)}) %collective-permute-start.14) | collective-permute-done | bytes 4128 | tf_op jit(solution)/shard_map/ppermute | solution.py:261
  132.1 0.6 fusion.2
  132.7 5.6 %collective-permute-start.15 = (f32[8,128]{1,0:T(8,128)S(1)}, f32[8,128]{1,0:T(8,128)S(1)}, u32[]{:S(2)}, u32[]{:S(2)}) collective-permute-start(f32[8,128]{1,0:T(8,128)S(1)} %fusion.2), channel_id=1, source_target_pairs={{0,4},{1,5},{2,6},{3,7},{4,0},{5,1},{6,2},{7,3},{8,12},{9,13},{10,... | collective-permute-start | bytes 12296 | tf_op jit(solution)/shard_map/ppermute | solution.py:261
  138.3 1.6 collective-permute-done.15
  139.9 2.8 %collective-permute-start.16 = (f32[8,128]{1,0:T(8,128)S(1)}, f32[8,128]{1,0:T(8,128)S(1)}, u32[]{:S(2)}, u32[]{:S(2)}) collective-permute-start(f32[8,128]{1,0:T(8,128)S(1)} %add.75), channel_id=1, source_target_pairs={{0,8},{1,9},{2,10},{3,11},{4,12},{5,13},{6,14},{7,15},{8,0},{9,1},... | collective-permute-start | bytes 12296 | tf_op jit(solution)/shard_map/ppermute | solution.py:261
  142.6 1.6 collective-permute-done.16
  144.2 0.0 collective-permute-start.17
  144.2 0.7 iota_compare_fusion
  144.9 4.5 %collective-permute-done.17 = f32[8,128]{1,0:T(8,128)S(1)} collective-permute-done((f32[8,128]{1,0:T(8,128)S(1)}, f32[8,128]{1,0:T(8,128)S(1)}, u32[]{:S(2)}, u32[]{:S(2)}) %collective-permute-start.17) | collective-permute-done | bytes 4128 | tf_op jit(solution)/shard_map/ppermute | solution.py:261
  149.3 2.3 %collective-permute-start.18 = (f32[8,128]{1,0:T(8,128)S(1)}, f32[8,128]{1,0:T(8,128)S(1)}, u32[]{:S(2)}, u32[]{:S(2)}) collective-permute-start(f32[8,128]{1,0:T(8,128)S(1)} %add_select_fusion), channel_id=1, source_target_pairs={{0,32},{32,0},{64,96},{96,64},{128,160},{160,128},{192,224},{224,1... | collective-permute-start | bytes 12296 | tf_op jit(solution)/shard_map/ppermute | solution.py:261
  151.6 5.2 %collective-permute-done.18 = f32[8,128]{1,0:T(8,128)S(1)} collective-permute-done((f32[8,128]{1,0:T(8,128)S(1)}, f32[8,128]{1,0:T(8,128)S(1)}, u32[]{:S(2)}, u32[]{:S(2)}) %collective-permute-start.18) | collective-permute-done | bytes 4128 | tf_op jit(solution)/shard_map/ppermute | solution.py:261
  156.8 3.6 %collective-permute-done.19 = f32[8,128]{1,0:T(8,128)S(1)} collective-permute-done((f32[8,128]{1,0:T(8,128)S(1)}, f32[8,128]{1,0:T(8,128)S(1)}, u32[]{:S(2)}, u32[]{:S(2)}) %collective-permute-start.19) | collective-permute-done | bytes 4128 | tf_op jit(solution)/shard_map/ppermute | solution.py:261
  160.5 2.1 %collective-permute-start.20 = (f32[8,128]{1,0:T(8,128)S(1)}, f32[8,128]{1,0:T(8,128)S(1)}, u32[]{:S(2)}, u32[]{:S(2)}) collective-permute-start(f32[8,128]{1,0:T(8,128)S(1)} %add.79), channel_id=1, source_target_pairs={{0,128},{32,160},{64,192},{96,224},{128,0},{160,32},{192,64},{224,... | collective-permute-start | bytes 12296 | tf_op jit(solution)/shard_map/ppermute | solution.py:261
  162.6 4.7 %own_linear.1.y = f32[1024,512]{1,0:T(8,128)S(1)} custom-call(f32[512,512]{1,0:T(8,128)} %get-tuple-element.27.lo, f32[512,512]{1,0:T(8,128)} %get-tuple-element.26.hi, f32[8,128]{1,0:T(8,128)S(1)} %get-tuple-element.28.stats, bf16[256,1280]{1,0:T(8,128)(2,1)S(1)} %get-tuple-element.16.th, bf16[256,1280]{1,0:T(8,128)(2,1)S(1)} %get-tuple-element.17.tl), custom_call_target="tpu_custom_call" | custom-call | tf_op jit(solution)/shard_map/own_linear/pallas_call | solution.py:375
  167.4 0.5 multiply_bitcast_fusion
  167.9 0.0 collective-permute-done.11.left
  167.9 0.0 collective-permute-done.12.right
  167.9 7.8 %gradient.1 = f32[1024,512]{1,0:T(8,128)} custom-call(s32[4]{0:T(128)S(1)} %pad_add_fusion.where, f32[512,512]{1,0:T(8,128)} %collective-permute-done.11.left, f32[512,512]{1,0:T(8,128)} %collective-permute-done.12.right, f32[1024,512]{1,0:T(8,128)S(1)} %own_linear.1.y, f32[8,128]{1,0:T(8,128)S(1)} %get-tuple-element.28.stats, ...), custom_call_target="tpu_custom_call" | custom-call | tf_op jit(solution)/shard_map/gradient/pallas_call | solution.py:382
  (16 shorter events, 0.0 us)
Async XLA Ops:
  0.6 11.4 %copy-start.3 = (f32[1,16,64,512]{3,2,1,0:T(8,128)S(1)}, f32[1,16,64,512]{3,2,1,0:T(8,128)}, u32[]{:S(2)}) copy-start(f32[1,16,64,512]{3,2,1,0:T(8,128)} %param.9) | copy-start | bytes 6291460
  3.5 13.8 %copy-start.2 = (s32[3]{0:T(128)S(1)}, s32[3]{0:T(128)}, u32[]{:S(2)}) copy-start(s32[3]{0:T(128)} %band.1) | copy-start | bytes 40
  3.5 42.6 %collective-permute-start = (f32[512,512]{1,0:T(8,128)}, f32[512,512]{1,0:T(8,128)}, u32[]{:S(2)}, u32[]{:S(2)}) collective-permute-start(f32[512,512]{1,0:T(8,128)} %bitcast.5.hi), channel_id=1, source_target_pairs={{0,1},{1,2},{2,3},{3,4},{4,5},{5,6},{6,7},{7,8},{8,9},{9,10},{10,1... | collective-permute-start | bytes 3145736 | tf_op jit(solution)/shard_map/ppermute | solution.py:261
  5.6 40.6 %collective-permute-start.1 = (f32[512,512]{1,0:T(8,128)S(1)}, f32[512,512]{1,0:T(8,128)}, u32[]{:S(2)}, u32[]{:S(2)}) collective-permute-start(f32[512,512]{1,0:T(8,128)S(1)} %bitcast.13), channel_id=1, source_target_pairs={{1,0},{2,1},{3,2},{4,3},{5,4},{6,5},{7,6},{8,7},{9,8},{10,9},{11,1... | collective-permute-start | bytes 3145736 | tf_op jit(solution)/shard_map/ppermute | solution.py:261
  13.2 15.2 %collective-permute-start.4 = (f32[256,512]{1,0:T(8,128)}, f32[256,512]{1,0:T(8,128)}, u32[]{:S(2)}, u32[]{:S(2)}) collective-permute-start(f32[256,512]{1,0:T(8,128)} %get-tuple-element.30), channel_id=1, source_target_pairs={{0,64},{32,96},{64,128},{96,160},{128,192},{160,224},{192,0},{224,... | collective-permute-start | bytes 1572872 | tf_op jit(solution)/shard_map/ppermute | solution.py:261
  14.7 14.5 %collective-permute-start.6 = (f32[256,512]{1,0:T(8,128)}, f32[256,512]{1,0:T(8,128)}, u32[]{:S(2)}, u32[]{:S(2)}) collective-permute-start(f32[256,512]{1,0:T(8,128)} %get-tuple-element.31), channel_id=1, source_target_pairs={{0,192},{32,224},{64,0},{96,32},{128,64},{160,96},{192,128},{224,1... | collective-permute-start | bytes 1572872 | tf_op jit(solution)/shard_map/ppermute | solution.py:261
  15.3 22.8 %collective-permute-start.5 = (f32[256,512]{1,0:T(8,128)}, f32[256,512]{1,0:T(8,128)}, u32[]{:S(2)}, u32[]{:S(2)}) collective-permute-start(f32[256,512]{1,0:T(8,128)} %get-tuple-element.32), channel_id=1, source_target_pairs={{0,128},{32,160},{64,192},{96,224},{128,0},{160,32},{192,64},{224,... | collective-permute-start | bytes 1572872 | tf_op jit(solution)/shard_map/ppermute | solution.py:261
  24.0 22.2 %copy-start = (f32[1,16,64,512]{3,2,1,0:T(8,128)S(1)}, f32[1,16,64,512]{3,2,1,0:T(8,128)}, u32[]{:S(2)}) copy-start(f32[1,16,64,512]{3,2,1,0:T(8,128)} %param.7) | copy-start | bytes 6291460
  39.8 22.6 %collective-permute-start.7 = (f32[256,512]{1,0:T(8,128)S(1)}, f32[256,512]{1,0:T(8,128)S(1)}, u32[]{:S(2)}, u32[]{:S(2)}) collective-permute-start(f32[256,512]{1,0:T(8,128)S(1)} %add_add_fusion), channel_id=1, source_target_pairs={{0,32},{32,0},{64,96},{96,64},{128,160},{160,128},{192,224},{224,1... | collective-permute-start | bytes 1572872 | tf_op jit(solution)/shard_map/ppermute | solution.py:261
  46.2 21.5 %copy-start.4 = (s32[8]{0:T(128)S(1)}, s32[8]{0:T(128)}, u32[]{:S(2)}) copy-start(s32[8]{0:T(128)} %param.13) | copy-start | bytes 100
  46.2 22.1 %copy-start.5 = (f32[8]{0:T(128)S(1)}, f32[8]{0:T(128)}, u32[]{:S(2)}) copy-start(f32[8]{0:T(128)} %param.11) | copy-start | bytes 100
  54.2 37.4 %collective-permute-start.2 = (f32[512,512]{1,0:T(8,128)}, f32[512,512]{1,0:T(8,128)}, u32[]{:S(2)}, u32[]{:S(2)}) collective-permute-start(f32[512,512]{1,0:T(8,128)} %get-tuple-element.22.hi.pot_hi), channel_id=1, source_target_pairs={{0,1},{1,2},{2,3},{3,4},{4,5},{5,6},{6,7},{7,8},{8,9},{9,10},{10,1... | collective-permute-start | bytes 3145736 | tf_op jit(solution)/shard_map/ppermute | solution.py:261
  56.1 35.5 %collective-permute-start.3 = (f32[512,512]{1,0:T(8,128)S(1)}, f32[512,512]{1,0:T(8,128)}, u32[]{:S(2)}, u32[]{:S(2)}) collective-permute-start(f32[512,512]{1,0:T(8,128)S(1)} %get-tuple-element.23.lo.pot_lo), channel_id=1, source_target_pairs={{1,0},{2,1},{3,2},{4,3},{5,4},{6,5},{7,6},{8,7},{9,8},{10,9},{11,1... | collective-permute-start | bytes 3145736 | tf_op jit(solution)/shard_map/ppermute | solution.py:261
  63.3 15.2 %collective-permute-start.10 = (f32[256,512]{1,0:T(8,128)}, f32[256,512]{1,0:T(8,128)}, u32[]{:S(2)}, u32[]{:S(2)}) collective-permute-start(f32[256,512]{1,0:T(8,128)} %add.72.sum0), channel_id=1, source_target_pairs={{0,64},{32,96},{64,128},{96,160},{128,192},{160,224},{192,0},{224,... | collective-permute-start | bytes 1572872 | tf_op jit(solution)/shard_map/ppermute | solution.py:261
  63.3 16.7 %collective-permute-start.9 = (f32[256,512]{1,0:T(8,128)}, f32[256,512]{1,0:T(8,128)}, u32[]{:S(2)}, u32[]{:S(2)}) collective-permute-start(f32[256,512]{1,0:T(8,128)} %add.72.sum0), channel_id=1, source_target_pairs={{0,128},{32,160},{64,192},{96,224},{128,0},{160,32},{192,64},{224,... | collective-permute-start | bytes 1572872 | tf_op jit(solution)/shard_map/ppermute | solution.py:261
  66.3 20.6 %collective-permute-start.8 = (f32[256,512]{1,0:T(8,128)}, f32[256,512]{1,0:T(8,128)}, u32[]{:S(2)}, u32[]{:S(2)}) collective-permute-start(f32[256,512]{1,0:T(8,128)} %add.72.sum0), channel_id=1, source_target_pairs={{0,192},{32,224},{64,0},{96,32},{128,64},{160,96},{192,128},{224,1... | collective-permute-start | bytes 1572872 | tf_op jit(solution)/shard_map/ppermute | solution.py:261
  67.7 23.9 %copy-start.1 = (f32[16,64,512]{2,1,0:T(8,128)S(1)}, f32[16,64,512]{2,1,0:T(8,128)}, u32[]{:S(2)}) copy-start(f32[16,64,512]{2,1,0:T(8,128)} %param.10) | copy-start | bytes 6291460
  102.2 65.7 %collective-permute-start.11 = (f32[512,512]{1,0:T(8,128)}, f32[512,512]{1,0:T(8,128)}, u32[]{:S(2)}, u32[]{:S(2)}) collective-permute-start(f32[512,512]{1,0:T(8,128)} %get-tuple-element.26.hi), channel_id=1, source_target_pairs={{0,1},{1,2},{2,3},{3,4},{4,5},{5,6},{6,7},{7,8},{8,9},{9,10},{10,1... | collective-permute-start | bytes 3145736 | tf_op jit(solution)/shard_map/ppermute | solution.py:261
  104.5 63.4 %collective-permute-start.12 = (f32[512,512]{1,0:T(8,128)}, f32[512,512]{1,0:T(8,128)}, u32[]{:S(2)}, u32[]{:S(2)}) collective-permute-start(f32[512,512]{1,0:T(8,128)} %get-tuple-element.27.lo), channel_id=1, source_target_pairs={{1,0},{2,1},{3,2},{4,3},{5,4},{6,5},{7,6},{8,7},{9,8},{10,9},{11,1... | collective-permute-start | bytes 3145736 | tf_op jit(solution)/shard_map/ppermute | solution.py:261
  116.0 1.3 collective-permute-start.13
  117.9 14.1 %collective-permute-start.14 = (f32[8,128]{1,0:T(8,128)S(1)}, f32[8,128]{1,0:T(8,128)S(1)}, u32[]{:S(2)}, u32[]{:S(2)}) collective-permute-start(f32[8,128]{1,0:T(8,128)S(1)} %broadcast_add_fusion), channel_id=1, source_target_pairs={{0,2},{1,3},{2,0},{3,1},{4,6},{5,7},{6,4},{7,5},{8,10},{9,11},{10,... | collective-permute-start | bytes 12296 | tf_op jit(solution)/shard_map/ppermute | solution.py:261
  132.7 7.2 %collective-permute-start.15 = (f32[8,128]{1,0:T(8,128)S(1)}, f32[8,128]{1,0:T(8,128)S(1)}, u32[]{:S(2)}, u32[]{:S(2)}) collective-permute-start(f32[8,128]{1,0:T(8,128)S(1)} %fusion.2), channel_id=1, source_target_pairs={{0,4},{1,5},{2,6},{3,7},{4,0},{5,1},{6,2},{7,3},{8,12},{9,13},{10,... | collective-permute-start | bytes 12296 | tf_op jit(solution)/shard_map/ppermute | solution.py:261
  139.9 4.3 %collective-permute-start.16 = (f32[8,128]{1,0:T(8,128)S(1)}, f32[8,128]{1,0:T(8,128)S(1)}, u32[]{:S(2)}, u32[]{:S(2)}) collective-permute-start(f32[8,128]{1,0:T(8,128)S(1)} %add.75), channel_id=1, source_target_pairs={{0,8},{1,9},{2,10},{3,11},{4,12},{5,13},{6,14},{7,15},{8,0},{9,1},... | collective-permute-start | bytes 12296 | tf_op jit(solution)/shard_map/ppermute | solution.py:261
  144.2 5.1 %collective-permute-start.17 = (f32[8,128]{1,0:T(8,128)S(1)}, f32[8,128]{1,0:T(8,128)S(1)}, u32[]{:S(2)}, u32[]{:S(2)}) collective-permute-start(f32[8,128]{1,0:T(8,128)S(1)} %add.76), channel_id=1, source_target_pairs={{0,16},{1,17},{2,18},{3,19},{4,20},{5,21},{6,22},{7,23},{8,24},{9,... | collective-permute-start | bytes 12296 | tf_op jit(solution)/shard_map/ppermute | solution.py:261
  149.3 7.5 %collective-permute-start.18 = (f32[8,128]{1,0:T(8,128)S(1)}, f32[8,128]{1,0:T(8,128)S(1)}, u32[]{:S(2)}, u32[]{:S(2)}) collective-permute-start(f32[8,128]{1,0:T(8,128)S(1)} %add_select_fusion), channel_id=1, source_target_pairs={{0,32},{32,0},{64,96},{96,64},{128,160},{160,128},{192,224},{224,1... | collective-permute-start | bytes 12296 | tf_op jit(solution)/shard_map/ppermute | solution.py:261
  156.8 3.6 %collective-permute-start.19 = (f32[8,128]{1,0:T(8,128)S(1)}, f32[8,128]{1,0:T(8,128)S(1)}, u32[]{:S(2)}, u32[]{:S(2)}) collective-permute-start(f32[8,128]{1,0:T(8,128)S(1)} %add.78), channel_id=1, source_target_pairs={{0,64},{32,96},{64,0},{96,32},{128,192},{160,224},{192,128},{224,1... | collective-permute-start | bytes 12296 | tf_op jit(solution)/shard_map/ppermute | solution.py:261
  160.5 6.9 %collective-permute-start.20 = (f32[8,128]{1,0:T(8,128)S(1)}, f32[8,128]{1,0:T(8,128)S(1)}, u32[]{:S(2)}, u32[]{:S(2)}) collective-permute-start(f32[8,128]{1,0:T(8,128)S(1)} %add.79), channel_id=1, source_target_pairs={{0,128},{32,160},{64,192},{96,224},{128,0},{160,32},{192,64},{224,... | collective-permute-start | bytes 12296 | tf_op jit(solution)/shard_map/ppermute | solution.py:261

commit v2 on v1

--- a/solution.py
+++ b/solution.py
@@ -260,6 +260,7 @@
     def send(value, axis, pairs):
         return lax.ppermute(value, axis, pairs)
 
+    in_order = lax.optimization_barrier
     to_right = [(i, i + 1) for i in range(slabs - 1)]
     to_left = [(i + 1, i) for i in range(slabs - 1)]
     ahead = {
@@ -268,21 +269,23 @@
     }
     swap = [(i, i ^ 1) for i in range(atoms)]
 
+    cot = atom_cotangent_rows.reshape(rows, nx)
+
+    def block_of(k):
+        return lax.dynamic_slice_in_dim(cot, lax.rem(x_at + k, count) * block, block)
+
+    blocks = [block_of(k) for k in range(1, across)]
+    blocks, prior_log_scaling = in_order((blocks, prior_log_scaling))
+    part = block_of(0)
+    for k in range(1, across):
+        part = part + send(blocks[k - 1], "atom", ahead[k])
+
     prior = prior_log_scaling.reshape(rows, nx)
     prior_lo, prior_hi = prior[:half], prior[half:]
     from_left = send(prior_hi, "slab", to_right)
     from_right = send(prior_lo, "slab", to_left)
-
-    cot = atom_cotangent_rows.reshape(rows, nx)
-
-    def block_of(k):
-        return lax.dynamic_slice_in_dim(cot, lax.rem(x_at + k, count) * block, block)
-
-    part = block_of(0)
-    for k in range(1, across):
-        part = part + send(block_of(k), "atom", ahead[k])
-    both = part + send(part, "atom", swap)
-    sums = [both] + [send(both, "atom", ahead[across - k]) for k in range(1, across)]
+    from_left, from_right, part = in_order((from_left, from_right, part))
+    swapped = send(part, "atom", swap)
 
     where = jnp.stack([(slab_at > 0), (slab_at < slabs - 1), x_at, x_at]).astype(jnp.int32)
     slot = lax.dynamic_slice_in_dim(slot_atom_index, atom_at, 1)
@@ -329,6 +332,9 @@
         name="potential",
     )(where, from_left, from_right, y, stats, atom_log_density.reshape(rows, nx), *tables)
 
+    pot_lo, pot_hi, swapped = in_order((pot_lo, pot_hi, swapped))
+    both = part + swapped
+    sums = [both] + [send(both, "atom", ahead[across - k]) for k in range(1, across)]
     from_left = send(pot_hi, "slab", to_right)
     from_right = send(pot_lo, "slab", to_left)
     y, stats = own_log(pot_lo, pot_hi, *tables[:2])
@@ -359,19 +365,6 @@
     from_left = send(ratio_hi, "slab", to_right)
     from_right = send(ratio_lo, "slab", to_left)
 
-    value = jnp.broadcast_to(jnp.sum(total), (8, 128))
-    hop = 1
-    while hop < slabs:
-        value = value + send(value, "slab", [(i, i ^ hop) for i in range(slabs)])
-        hop *= 2
-    lanes = jnp.arange(128, dtype=jnp.int32)[None, :]
-    value = jnp.where(lanes == slot[0], value, 0.0)
-    hop = 1
-    while hop < atoms:
-        value = value + send(value, "atom", [(i, i ^ hop) for i in range(atoms)])
-        hop *= 2
-    weight_grad = value[0, : weights.shape[0]] / (rows * nx * slabs)
-
     (y,) = pl.pallas_call(
         own_linear_kernel,
         out_shape=[shape(rows, nx)],
@@ -379,6 +372,18 @@
         compiler_params=params,
         name="own_linear",
     )(ratio_lo, ratio_hi, stats, *tables[:2])
+    def add(value, axis, pairs):
+        return value + send(value, axis, pairs)
+
+    value = jnp.broadcast_to(jnp.sum(total), (8, 128))
+    lanes = jnp.arange(128, dtype=jnp.int32)[None, :]
+    value = jnp.where(lanes == slot[0], value, 0.0)
+    value = add(value, "slab", [(i, i ^ 1) for i in range(slabs)])
+    for k in (1, 2):
+        value = add(value, "atom", ahead[k])
+    value, y = in_order((value, y))
+    for hop in (8, 16, 2, 4):
+        value = add(value, "slab", [(i, i ^ hop) for i in range(slabs)])
     gradient = pl.pallas_call(
         functools.partial(gradient_kernel, count=count),
         grid=(count,),
@@ -389,6 +394,9 @@
         compiler_params=params,
         name="gradient",
     )(where, from_left, from_right, y, stats, pot_lo, pot_hi, *tables)
+    value, gradient = in_order((value, gradient))
+    value = add(value, "atom", swap)
+    weight_grad = value[0, : weights.shape[0]] / (rows * nx * slabs)
     return gradient.reshape(atom_log_density.shape), weight_grad
 
 

time: 178 us -> 171 us (0.961)
  waiting for transfers between devices: 63 us -> 56.6 us
    ppermute x21, waiting for transfers between devices: 63 us -> 56.6 us  [send(): return lax.ppermute(value, axis, pairs)]
    slice x1, local copies, waits for them, and re-layouts: 2.9 us -> 0.2 us  [body(): prior_lo, prior_hi = (prior[:half], prior[half:])]
    unnamed x12 -> x20, local copies, waits for them, and re-layouts: 0.03 us -> 2.22 us
    add x9 -> x10, other arithmetic: 3.91 us -> 4.66 us  [the longest x1 2.54 us: body(): part = part + send(blocks[k - 1], 'atom', ahead[k])]
  transfers between devices with their start and end apart: 21 -> 21, of which waited for: 14 -> 14; matrix products, arithmetic and copies ran while one was open for 5% -> 5% of each run, Pallas kernels for 14% -> 13%
where the time goes in v2:
time: 171 us; the launch traced here: 168 us
  waiting for transfers between devices  56.6 us (33%)
  starting transfers between devices  56.2 us (33%)
  Pallas kernels  40.6 us (24%)
  other arithmetic  8.49 us (5%)
  local copies, waits for them, and re-layouts  5.69 us (3%)
    ppermute x21, waiting for transfers between devices, send(): return lax.ppermute(value, axis, pairs)  56.6 us
    ppermute x21, starting transfers between devices, send(): return lax.ppermute(value, axis, pairs)  56.2 us
    pallas_call x1, Pallas kernels, body(): pl.pallas_call(functools.partial(ratio_kernel, count=count), grid=(count,...  10.4 us
    pallas_call x1, Pallas kernels, body(): pl.pallas_call(functools.partial(gradient_kernel, count=count), grid=(cou...  7.82 us
    pallas_call x1, Pallas kernels, body(): pl.pallas_call(functools.partial(potential_kernel, count=count), grid=(co...  7.64 us
    pallas_call x1, Pallas kernels, body(): pl.pallas_call(own_linear_kernel, out_shape=[shape(rows, nx)], scratch_sh...  4.74 us
    pallas_call x1, Pallas kernels, body(): y, stats = own_log(pot_lo, pot_hi, *tables[:2])  4.62 us
  transfers between devices with their start and end apart: 21, of which 14 were waited for; matrix products, arithmetic and copies ran while one was open for 5% of the time, Pallas kernels for 13%

profile of v2, /device:TPU:10, one launch (start us, length us, event | category | flops | bytes accessed | tf_op | source)
XLA Modules:
  0.0 168.4 jit_solution(3469345786685117105)
XLA Ops:
  0.7 0.0 copy-start.7
  0.7 2.7 %constant_dynamic-slice_fusion = (f32[256,512]{1,0:T(8,128)}, f32[256,512]{1,0:T(8,128)}, f32[256,512]{1,0:T(8,128)}) fusion(f32[1024,512]{1,0:T(8,128)} %bitcast.19, s32[]{:T(128)S(6)} %select_n.29, s32[]{:T(128)S(6)} %select_n.28, s32[]{:T(128)S(6)} %select_n.27), kind=kLoop, calls=%fused_computation.4 | loop fusion | bytes 3145740 | tf_op jit(solution)/shard_map/dynamic_slice | solution.py:275
  3.4 0.2 fusion.1
  3.6 0.0 copy-start.6
  3.6 2.1 %collective-permute-start = (f32[512,512]{1,0:T(8,128)S(1)}, f32[512,512]{1,0:T(8,128)S(1)}, u32[]{:S(2)}, u32[]{:S(2)}) collective-permute-start(f32[512,512]{1,0:T(8,128)S(1)} %bitcast.15), channel_id=1, source_target_pairs={{0,1},{1,2},{2,3},{3,4},{4,5},{5,6},{6,7},{7,8},{8,9},{9,10},{10,1... | collective-permute-start | bytes 3145736 | tf_op jit(solution)/shard_map/ppermute | solution.py:261
  5.7 6.3 %collective-permute-start.1 = (f32[512,512]{1,0:T(8,128)S(1)}, f32[512,512]{1,0:T(8,128)}, u32[]{:S(2)}, u32[]{:S(2)}) collective-permute-start(f32[512,512]{1,0:T(8,128)S(1)} %bitcast.13), channel_id=1, source_target_pairs={{1,0},{2,1},{3,2},{4,3},{5,4},{6,5},{7,6},{8,7},{9,8},{10,9},{11,1... | collective-permute-start | bytes 3145736 | tf_op jit(solution)/shard_map/ppermute | solution.py:261
  12.0 1.6 collective-permute-start.2
  13.6 1.1 collective-permute-start.3
  14.7 2.2 %collective-permute-start.4 = (f32[256,512]{1,0:T(8,128)}, f32[256,512]{1,0:T(8,128)}, u32[]{:S(2)}, u32[]{:S(2)}) collective-permute-start(f32[256,512]{1,0:T(8,128)} %get-tuple-element.33), channel_id=1, source_target_pairs={{0,192},{32,224},{64,0},{96,32},{128,64},{160,96},{192,128},{224,1... | collective-permute-start | bytes 1572872 | tf_op jit(solution)/shard_map/ppermute | solution.py:261
  16.9 10.4 %collective-permute-done.2 = f32[256,512]{1,0:T(8,128)} collective-permute-done((f32[256,512]{1,0:T(8,128)}, f32[256,512]{1,0:T(8,128)}, u32[]{:S(2)}, u32[]{:S(2)}) %collective-permute-start.2) | collective-permute-done | bytes 524320 | tf_op jit(solution)/shard_map/ppermute | solution.py:261
  27.3 3.0 %collective-permute-done.3 = f32[256,512]{1,0:T(8,128)} collective-permute-done((f32[256,512]{1,0:T(8,128)}, f32[256,512]{1,0:T(8,128)}, u32[]{:S(2)}, u32[]{:S(2)}) %collective-permute-start.3) | collective-permute-done | bytes 524320 | tf_op jit(solution)/shard_map/ppermute | solution.py:261
  30.3 6.9 %collective-permute-done.4 = f32[256,512]{1,0:T(8,128)} collective-permute-done((f32[256,512]{1,0:T(8,128)}, f32[256,512]{1,0:T(8,128)}, u32[]{:S(2)}, u32[]{:S(2)}) %collective-permute-start.4) | collective-permute-done | bytes 524320 | tf_op jit(solution)/shard_map/ppermute | solution.py:261
  37.1 2.5 %add_add_fusion = f32[256,512]{1,0:T(8,128)} fusion(f32[256,512]{1,0:T(8,128)} %collective-permute-done.4, f32[256,512]{1,0:T(8,128)} %collective-permute-done.3, f32[256,512]{1,0:T(8,128)} %collective-permute-done.2, f32[1024,512]{1,0:T(8,128)} %bitcast.20, s32[]{:T(128)S(6)} %select_n.30), kind=kLoop, calls=%fused_computation | loop fusion | flops 393216 | bytes 2621444 | tf_op jit(solution)/shard_map/add | solution.py:281
  39.7 0.0 collective-permute-done.left
  39.7 1.0 copy-done.4
  40.6 0.0 collective-permute-done.1.right
  40.6 6.3 %collective-permute-start.5 = (f32[256,512]{1,0:T(8,128)}, f32[256,512]{1,0:T(8,128)}, u32[]{:S(2)}, u32[]{:S(2)}) collective-permute-start(f32[256,512]{1,0:T(8,128)} %add_add_fusion), channel_id=1, source_target_pairs={{0,32},{32,0},{64,96},{96,64},{128,160},{160,128},{192,224},{224,1... | collective-permute-start | bytes 1572872 | tf_op jit(solution)/shard_map/ppermute | solution.py:261
  46.9 1.9 %tables.1 = (bf16[256,1280]{1,0:T(8,128)(2,1)S(1)}, bf16[256,1280]{1,0:T(8,128)(2,1)S(1)}, bf16[512,512]{1,0:T(8,128)(2,1)S(1)}, bf16[512,512]{1,0:T(8,128)(2,1)S(1)}) custom-call(s32[3]{0:T(128)S(1)} %copy-done.6), custom_call_target="tpu_custom_call" | custom-call | tf_op jit(solution)/shard_map/tables/pallas_call | solution.py:296
  48.9 1.2 copy-done.1
  50.1 3.4 %own_log.2 = (f32[1024,512]{1,0:T(8,128)S(1)}, f32[8,128]{1,0:T(8,128)S(1)}) custom-call(f32[512,512]{1,0:T(8,128)S(1)} %bitcast.14, f32[512,512]{1,0:T(8,128)S(1)} %bitcast.16, bf16[256,1280]{1,0:T(8,128)(2,1)S(1)} %get-tuple-element.36.th, bf16[256,1280]{1,0:T(8,128)(2,1)S(1)} %get-tuple-element.37.tl), custom_call_target="tpu_custom_call" | custom-call | tf_op jit(solution)/shard_map/own_log/pallas_call | solution.py:323
  53.5 0.1 pad_add_fusion.where
  53.6 0.0 copy-start.9
  53.6 7.6 %potential.1 = (f32[512,512]{1,0:T(8,128)S(1)}, f32[512,512]{1,0:T(8,128)}) custom-call(s32[4]{0:T(128)S(1)} %pad_add_fusion.where, f32[512,512]{1,0:T(8,128)S(1)} %copy-done.5, f32[512,512]{1,0:T(8,128)} %collective-permute-done.1.right, f32[1024,512]{1,0:T(8,128)S(1)} %get-tuple-element.38.y, f32[8,128]{1,0:T(8,128)S(1)} %get-tuple-element.39.stats, ...), custom_call_target="tpu_custom_call" | custom-call | tf_op jit(solution)/shard_map/potential/pallas_call | solution.py:324
  61.3 7.9 %collective-permute-done.5 = f32[256,512]{1,0:T(8,128)} collective-permute-done((f32[256,512]{1,0:T(8,128)}, f32[256,512]{1,0:T(8,128)}, u32[]{:S(2)}, u32[]{:S(2)}) %collective-permute-start.5) | collective-permute-done | bytes 524320 | tf_op jit(solution)/shard_map/ppermute | solution.py:261
  69.2 1.9 %collective-permute-start.6 = (f32[512,512]{1,0:T(8,128)}, f32[512,512]{1,0:T(8,128)}, u32[]{:S(2)}, u32[]{:S(2)}) collective-permute-start(f32[512,512]{1,0:T(8,128)} %get-tuple-element.45.hi.pot_hi), channel_id=1, source_target_pairs={{0,1},{1,2},{2,3},{3,4},{4,5},{5,6},{6,7},{7,8},{8,9},{9,10},{10,1... | collective-permute-start | bytes 3145736 | tf_op jit(solution)/shard_map/ppermute | solution.py:261
  71.1 6.3 %collective-permute-start.7 = (f32[512,512]{1,0:T(8,128)S(1)}, f32[512,512]{1,0:T(8,128)}, u32[]{:S(2)}, u32[]{:S(2)}) collective-permute-start(f32[512,512]{1,0:T(8,128)S(1)} %get-tuple-element.46.lo.pot_lo), channel_id=1, source_target_pairs={{1,0},{2,1},{3,2},{4,3},{5,4},{6,5},{7,6},{8,7},{9,8},{10,9},{11,1... | collective-permute-start | bytes 3145736 | tf_op jit(solution)/shard_map/ppermute | solution.py:261
  77.4 2.1 %add.72.sum0 = f32[256,512]{1,0:T(8,128)} add(f32[256,512]{1,0:T(8,128)} %add_add_fusion, f32[256,512]{1,0:T(8,128)} %collective-permute-done.5) | non-fusion elementwise | flops 131072 | bytes 1572864 | tf_op jit(solution)/shard_map/add | solution.py:336
  79.5 1.2 collective-permute-start.10
  80.7 1.3 collective-permute-start.9
  82.1 2.6 %collective-permute-start.8 = (f32[256,512]{1,0:T(8,128)}, f32[256,512]{1,0:T(8,128)}, u32[]{:S(2)}, u32[]{:S(2)}) collective-permute-start(f32[256,512]{1,0:T(8,128)} %add.72.sum0), channel_id=1, source_target_pairs={{0,192},{32,224},{64,0},{96,32},{128,64},{160,96},{192,128},{224,1... | collective-permute-start | bytes 1572872 | tf_op jit(solution)/shard_map/ppermute | solution.py:261
  84.7 0.6 dynamic_slice.15
  85.3 1.3 fusion
  86.6 4.6 %own_log.3 = (f32[1024,512]{1,0:T(8,128)S(1)}, f32[8,128]{1,0:T(8,128)S(1)}) custom-call(f32[512,512]{1,0:T(8,128)S(1)} %get-tuple-element.46.lo.pot_lo, f32[512,512]{1,0:T(8,128)} %get-tuple-element.45.hi.pot_hi, bf16[256,1280]{1,0:T(8,128)(2,1)S(1)} %get-tuple-element.36.th, bf16[256,1280]{1,0:T(8,128)(2,1)S(1)} %get-tuple-element.37.tl), custom_call_target="tpu_custom_call" | custom-call | tf_op jit(solution)/shard_map/own_log/pallas_call | solution.py:340
  91.2 3.5 %collective-permute-done.10.sum3 = f32[256,512]{1,0:T(8,128)} collective-permute-done((f32[256,512]{1,0:T(8,128)}, f32[256,512]{1,0:T(8,128)}, u32[]{:S(2)}, u32[]{:S(2)}) %collective-permute-start.10) | collective-permute-done | bytes 524320 | tf_op jit(solution)/shard_map/ppermute | solution.py:261
  94.7 2.3 %collective-permute-done.9.sum2 = f32[256,512]{1,0:T(8,128)} collective-permute-done((f32[256,512]{1,0:T(8,128)}, f32[256,512]{1,0:T(8,128)}, u32[]{:S(2)}, u32[]{:S(2)}) %collective-permute-start.9) | collective-permute-done | bytes 524320 | tf_op jit(solution)/shard_map/ppermute | solution.py:261
  97.0 5.5 %collective-permute-done.8.sum1 = f32[256,512]{1,0:T(8,128)} collective-permute-done((f32[256,512]{1,0:T(8,128)}, f32[256,512]{1,0:T(8,128)}, u32[]{:S(2)}, u32[]{:S(2)}) %collective-permute-start.8) | collective-permute-done | bytes 524320 | tf_op jit(solution)/shard_map/ppermute | solution.py:261
  102.5 0.0 collective-permute-done.6.left
  102.5 0.0 collective-permute-done.7.right
  102.5 10.4 %ratio.1 = (f32[512,512]{1,0:T(8,128)}, f32[512,512]{1,0:T(8,128)}, f32[8,128]{1,0:T(8,128)S(1)}, f32[8,128]{1,0:T(8,128)S(1)}) custom-call(s32[4]{0:T(128)S(1)} %pad_add_fusion.where, f32[1]{0:T(128)} %bitcast.4.weight, f32[512,512]{1,0:T(8,128)} %collective-permute-done.6.left, f32[512,512]{1,0:T(8,128)} %collective-permute-done.7.right, ...), custom_call_target="tpu_custom_call" | custom-call | tf_op jit(solution)/shard_map/ratio/pallas_call | solution.py:341
  113.0 6.5 %collective-permute-start.19 = (f32[512,512]{1,0:T(8,128)}, f32[512,512]{1,0:T(8,128)}, u32[]{:S(2)}, u32[]{:S(2)}) collective-permute-start(f32[512,512]{1,0:T(8,128)} %get-tuple-element.51.lo), channel_id=1, source_target_pairs={{1,0},{2,1},{3,2},{4,3},{5,4},{6,5},{7,6},{8,7},{9,8},{10,9},{11,1... | collective-permute-start | bytes 3145736 | tf_op jit(solution)/shard_map/ppermute | solution.py:261
  119.5 1.9 %collective-permute-start.18 = (f32[512,512]{1,0:T(8,128)}, f32[512,512]{1,0:T(8,128)}, u32[]{:S(2)}, u32[]{:S(2)}) collective-permute-start(f32[512,512]{1,0:T(8,128)} %get-tuple-element.52.hi), channel_id=1, source_target_pairs={{0,1},{1,2},{2,3},{3,4},{4,5},{5,6},{6,7},{7,8},{8,9},{9,10},{10,1... | collective-permute-start | bytes 3145736 | tf_op jit(solution)/shard_map/ppermute | solution.py:261
  121.4 0.7 reduce_sum.19
  122.0 1.3 compare_select_fusion.1
  123.3 0.1 collective-permute-start.11
  123.5 1.2 collective-permute-done.11
  124.6 0.0 collective-permute-start.12
  124.6 3.6 %collective-permute-done.12 = f32[8,128]{1,0:T(8,128)S(1)} collective-permute-done((f32[8,128]{1,0:T(8,128)S(1)}, f32[8,128]{1,0:T(8,128)S(1)}, u32[]{:S(2)}, u32[]{:S(2)}) %collective-permute-start.12) | collective-permute-done | bytes 4128 | tf_op jit(solution)/shard_map/ppermute | solution.py:261
  128.2 2.4 %collective-permute-start.13 = (f32[8,128]{1,0:T(8,128)S(1)}, f32[8,128]{1,0:T(8,128)S(1)}, u32[]{:S(2)}, u32[]{:S(2)}) collective-permute-start(f32[8,128]{1,0:T(8,128)S(1)} %fusion.2), channel_id=1, source_target_pairs={{0,128},{32,160},{64,192},{96,224},{128,0},{160,32},{192,64},{224,... | collective-permute-start | bytes 12296 | tf_op jit(solution)/shard_map/ppermute | solution.py:261
  130.6 4.7 %own_linear.1.y = f32[1024,512]{1,0:T(8,128)S(1)} custom-call(f32[512,512]{1,0:T(8,128)} %get-tuple-element.51.lo, f32[512,512]{1,0:T(8,128)} %get-tuple-element.52.hi, f32[8,128]{1,0:T(8,128)S(1)} %get-tuple-element.53.stats, bf16[256,1280]{1,0:T(8,128)(2,1)S(1)} %get-tuple-element.36.th, bf16[256,1280]{1,0:T(8,128)(2,1)S(1)} %get-tuple-element.37.tl), custom_call_target="tpu_custom_call" | custom-call | tf_op jit(solution)/shard_map/own_linear/pallas_call | solution.py:368
  135.4 0.0 collective-permute-done.13
  135.4 0.1 collective-permute-start.14
  135.5 3.6 %collective-permute-done.14 = f32[8,128]{1,0:T(8,128)S(1)} collective-permute-done((f32[8,128]{1,0:T(8,128)S(1)}, f32[8,128]{1,0:T(8,128)S(1)}, u32[]{:S(2)}, u32[]{:S(2)}) %collective-permute-start.14) | collective-permute-done | bytes 4128 | tf_op jit(solution)/shard_map/ppermute | solution.py:261
  139.1 2.7 %collective-permute-start.15 = (f32[8,128]{1,0:T(8,128)S(1)}, f32[8,128]{1,0:T(8,128)S(1)}, u32[]{:S(2)}, u32[]{:S(2)}) collective-permute-start(f32[8,128]{1,0:T(8,128)S(1)} %add.76), channel_id=1, source_target_pairs={{0,16},{1,17},{2,18},{3,19},{4,20},{5,21},{6,22},{7,23},{8,24},{9,... | collective-permute-start | bytes 12296 | tf_op jit(solution)/shard_map/ppermute | solution.py:261
  141.8 2.4 %collective-permute-done.15 = f32[8,128]{1,0:T(8,128)S(1)} collective-permute-done((f32[8,128]{1,0:T(8,128)S(1)}, f32[8,128]{1,0:T(8,128)S(1)}, u32[]{:S(2)}, u32[]{:S(2)}) %collective-permute-start.15) | collective-permute-done | bytes 4128 | tf_op jit(solution)/shard_map/ppermute | solution.py:261
  144.2 0.9 collective-permute-start.16
  145.2 2.7 %collective-permute-done.16 = f32[8,128]{1,0:T(8,128)S(1)} collective-permute-done((f32[8,128]{1,0:T(8,128)S(1)}, f32[8,128]{1,0:T(8,128)S(1)}, u32[]{:S(2)}, u32[]{:S(2)}) %collective-permute-start.16) | collective-permute-done | bytes 4128 | tf_op jit(solution)/shard_map/ppermute | solution.py:261
  147.8 3.1 %collective-permute-start.17 = (f32[8,128]{1,0:T(8,128)S(1)}, f32[8,128]{1,0:T(8,128)S(1)}, u32[]{:S(2)}, u32[]{:S(2)}) collective-permute-start(f32[8,128]{1,0:T(8,128)S(1)} %add.78), channel_id=1, source_target_pairs={{0,4},{1,5},{2,6},{3,7},{4,0},{5,1},{6,2},{7,3},{8,12},{9,13},{10,... | collective-permute-start | bytes 12296 | tf_op jit(solution)/shard_map/ppermute | solution.py:261
  151.0 1.6 collective-permute-done.17
  152.6 0.0 collective-permute-done.19.right
  152.6 0.0 collective-permute-done.18.left
  152.6 7.8 %gradient.1 = f32[1024,512]{1,0:T(8,128)} custom-call(s32[4]{0:T(128)S(1)} %pad_add_fusion.where, f32[512,512]{1,0:T(8,128)} %collective-permute-done.18.left, f32[512,512]{1,0:T(8,128)} %collective-permute-done.19.right, f32[1024,512]{1,0:T(8,128)S(1)} %own_linear.1.y, f32[8,128]{1,0:T(8,128)S(1)} %get-tuple-element.53.stats, ...), custom_call_target="tpu_custom_call" | custom-call | tf_op jit(solution)/shard_map/gradient/pallas_call | solution.py:387
  160.4 5.5 %collective-permute-start.20 = (f32[8,128]{1,0:T(8,128)S(1)}, f32[8,128]{1,0:T(8,128)S(1)}, u32[]{:S(2)}, u32[]{:S(2)}) collective-permute-start(f32[8,128]{1,0:T(8,128)S(1)} %add.79), channel_id=1, source_target_pairs={{0,32},{32,0},{64,96},{96,64},{128,160},{160,128},{192,224},{224,1... | collective-permute-start | bytes 12296 | tf_op jit(solution)/shard_map/ppermute | solution.py:261
  165.9 2.0 %collective-permute-done.20 = f32[8,128]{1,0:T(8,128)S(1)} collective-permute-done((f32[8,128]{1,0:T(8,128)S(1)}, f32[8,128]{1,0:T(8,128)S(1)}, u32[]{:S(2)}, u32[]{:S(2)}) %collective-permute-start.20) | collective-permute-done | bytes 4128 | tf_op jit(solution)/shard_map/ppermute | solution.py:261
  167.9 0.5 multiply_bitcast_fusion
  (24 shorter events, 0.1 us)
Async XLA Ops:
  0.7 2.7 %copy-start.7 = (f32[1,16,64,512]{3,2,1,0:T(8,128)S(1)}, f32[1,16,64,512]{3,2,1,0:T(8,128)}, u32[]{:S(2)}) copy-start(f32[1,16,64,512]{3,2,1,0:T(8,128)} %param.8) | copy-start | bytes 6291460
  3.6 43.3 %copy-start = (f32[1,8,64,512]{3,2,1,0:T(8,128)}, f32[1,8,64,512]{3,2,1,0:T(8,128)S(1)}, u32[]{:S(2)}) copy-start(f32[1,8,64,512]{3,2,1,0:T(8,128)S(1)} %get-tuple-element.59) | copy-start | bytes 3145732
  3.6 43.3 %copy-start.6 = (s32[3]{0:T(128)S(1)}, s32[3]{0:T(128)}, u32[]{:S(2)}) copy-start(s32[3]{0:T(128)} %band.1) | copy-start | bytes 40
  3.6 36.1 %collective-permute-start = (f32[512,512]{1,0:T(8,128)S(1)}, f32[512,512]{1,0:T(8,128)S(1)}, u32[]{:S(2)}, u32[]{:S(2)}) collective-permute-start(f32[512,512]{1,0:T(8,128)S(1)} %bitcast.15), channel_id=1, source_target_pairs={{0,1},{1,2},{2,3},{3,4},{4,5},{5,6},{6,7},{7,8},{8,9},{9,10},{10,1... | collective-permute-start | bytes 3145736 | tf_op jit(solution)/shard_map/ppermute | solution.py:261
  5.7 35.0 %collective-permute-start.1 = (f32[512,512]{1,0:T(8,128)S(1)}, f32[512,512]{1,0:T(8,128)}, u32[]{:S(2)}, u32[]{:S(2)}) collective-permute-start(f32[512,512]{1,0:T(8,128)S(1)} %bitcast.13), channel_id=1, source_target_pairs={{1,0},{2,1},{3,2},{4,3},{5,4},{6,5},{7,6},{8,7},{9,8},{10,9},{11,1... | collective-permute-start | bytes 3145736 | tf_op jit(solution)/shard_map/ppermute | solution.py:261
  12.0 15.3 %collective-permute-start.2 = (f32[256,512]{1,0:T(8,128)}, f32[256,512]{1,0:T(8,128)}, u32[]{:S(2)}, u32[]{:S(2)}) collective-permute-start(f32[256,512]{1,0:T(8,128)} %get-tuple-element.31), channel_id=1, source_target_pairs={{0,64},{32,96},{64,128},{96,160},{128,192},{160,224},{192,0},{224,... | collective-permute-start | bytes 1572872 | tf_op jit(solution)/shard_map/ppermute | solution.py:261
  13.6 16.7 %collective-permute-start.3 = (f32[256,512]{1,0:T(8,128)}, f32[256,512]{1,0:T(8,128)}, u32[]{:S(2)}, u32[]{:S(2)}) collective-permute-start(f32[256,512]{1,0:T(8,128)} %get-tuple-element.32), channel_id=1, source_target_pairs={{0,128},{32,160},{64,192},{96,224},{128,0},{160,32},{192,64},{224,... | collective-permute-start | bytes 1572872 | tf_op jit(solution)/shard_map/ppermute | solution.py:261
  14.7 22.4 %collective-permute-start.4 = (f32[256,512]{1,0:T(8,128)}, f32[256,512]{1,0:T(8,128)}, u32[]{:S(2)}, u32[]{:S(2)}) collective-permute-start(f32[256,512]{1,0:T(8,128)} %get-tuple-element.33), channel_id=1, source_target_pairs={{0,192},{32,224},{64,0},{96,32},{128,64},{160,96},{192,128},{224,1... | collective-permute-start | bytes 1572872 | tf_op jit(solution)/shard_map/ppermute | solution.py:261
  39.7 1.0 copy-start.4
  40.6 28.5 %collective-permute-start.5 = (f32[256,512]{1,0:T(8,128)}, f32[256,512]{1,0:T(8,128)}, u32[]{:S(2)}, u32[]{:S(2)}) collective-permute-start(f32[256,512]{1,0:T(8,128)} %add_add_fusion), channel_id=1, source_target_pairs={{0,32},{32,0},{64,96},{96,64},{128,160},{160,128},{192,224},{224,1... | collective-permute-start | bytes 1572872 | tf_op jit(solution)/shard_map/ppermute | solution.py:261
  48.9 1.2 copy-start.1
  50.1 3.5 %copy-start.2 = (f32[1,16,64,512]{3,2,1,0:T(8,128)S(1)}, f32[1,16,64,512]{3,2,1,0:T(8,128)}, u32[]{:S(2)}) copy-start(f32[1,16,64,512]{3,2,1,0:T(8,128)} %param.7) | copy-start | bytes 6291460
  50.1 3.5 %copy-start.5 = (f32[512,512]{1,0:T(8,128)S(1)}, f32[512,512]{1,0:T(8,128)}, u32[]{:S(2)}) copy-start(f32[512,512]{1,0:T(8,128)} %copy-done.4) | copy-start | bytes 3145732
  53.6 31.1 %copy-start.8 = (s32[8]{0:T(128)S(1)}, s32[8]{0:T(128)}, u32[]{:S(2)}) copy-start(s32[8]{0:T(128)} %param.13) | copy-start | bytes 100
  53.6 31.7 %copy-start.9 = (f32[8]{0:T(128)S(1)}, f32[8]{0:T(128)}, u32[]{:S(2)}) copy-start(f32[8]{0:T(128)} %param.11) | copy-start | bytes 100
  69.2 33.3 %collective-permute-start.6 = (f32[512,512]{1,0:T(8,128)}, f32[512,512]{1,0:T(8,128)}, u32[]{:S(2)}, u32[]{:S(2)}) collective-permute-start(f32[512,512]{1,0:T(8,128)} %get-tuple-element.45.hi.pot_hi), channel_id=1, source_target_pairs={{0,1},{1,2},{2,3},{3,4},{4,5},{5,6},{6,7},{7,8},{8,9},{9,10},{10,1... | collective-permute-start | bytes 3145736 | tf_op jit(solution)/shard_map/ppermute | solution.py:261
  71.1 31.4 %collective-permute-start.7 = (f32[512,512]{1,0:T(8,128)S(1)}, f32[512,512]{1,0:T(8,128)}, u32[]{:S(2)}, u32[]{:S(2)}) collective-permute-start(f32[512,512]{1,0:T(8,128)S(1)} %get-tuple-element.46.lo.pot_lo), channel_id=1, source_target_pairs={{1,0},{2,1},{3,2},{4,3},{5,4},{6,5},{7,6},{8,7},{9,8},{10,9},{11,1... | collective-permute-start | bytes 3145736 | tf_op jit(solution)/shard_map/ppermute | solution.py:261
  79.5 15.2 %collective-permute-start.10 = (f32[256,512]{1,0:T(8,128)}, f32[256,512]{1,0:T(8,128)}, u32[]{:S(2)}, u32[]{:S(2)}) collective-permute-start(f32[256,512]{1,0:T(8,128)} %add.72.sum0), channel_id=1, source_target_pairs={{0,64},{32,96},{64,128},{96,160},{128,192},{160,224},{192,0},{224,... | collective-permute-start | bytes 1572872 | tf_op jit(solution)/shard_map/ppermute | solution.py:261
  80.7 16.2 %collective-permute-start.9 = (f32[256,512]{1,0:T(8,128)}, f32[256,512]{1,0:T(8,128)}, u32[]{:S(2)}, u32[]{:S(2)}) collective-permute-start(f32[256,512]{1,0:T(8,128)} %add.72.sum0), channel_id=1, source_target_pairs={{0,128},{32,160},{64,192},{96,224},{128,0},{160,32},{192,64},{224,... | collective-permute-start | bytes 1572872 | tf_op jit(solution)/shard_map/ppermute | solution.py:261
  82.1 20.4 %collective-permute-start.8 = (f32[256,512]{1,0:T(8,128)}, f32[256,512]{1,0:T(8,128)}, u32[]{:S(2)}, u32[]{:S(2)}) collective-permute-start(f32[256,512]{1,0:T(8,128)} %add.72.sum0), channel_id=1, source_target_pairs={{0,192},{32,224},{64,0},{96,32},{128,64},{160,96},{192,128},{224,1... | collective-permute-start | bytes 1572872 | tf_op jit(solution)/shard_map/ppermute | solution.py:261
  84.7 17.8 %copy-start.3 = (f32[16,64,512]{2,1,0:T(8,128)S(1)}, f32[16,64,512]{2,1,0:T(8,128)}, u32[]{:S(2)}) copy-start(f32[16,64,512]{2,1,0:T(8,128)} %param.10) | copy-start | bytes 6291460
  113.0 39.6 %collective-permute-start.19 = (f32[512,512]{1,0:T(8,128)}, f32[512,512]{1,0:T(8,128)}, u32[]{:S(2)}, u32[]{:S(2)}) collective-permute-start(f32[512,512]{1,0:T(8,128)} %get-tuple-element.51.lo), channel_id=1, source_target_pairs={{1,0},{2,1},{3,2},{4,3},{5,4},{6,5},{7,6},{8,7},{9,8},{10,9},{11,1... | collective-permute-start | bytes 3145736 | tf_op jit(solution)/shard_map/ppermute | solution.py:261
  119.5 33.1 %collective-permute-start.18 = (f32[512,512]{1,0:T(8,128)}, f32[512,512]{1,0:T(8,128)}, u32[]{:S(2)}, u32[]{:S(2)}) collective-permute-start(f32[512,512]{1,0:T(8,128)} %get-tuple-element.52.hi), channel_id=1, source_target_pairs={{0,1},{1,2},{2,3},{3,4},{4,5},{5,6},{6,7},{7,8},{8,9},{9,10},{10,1... | collective-permute-start | bytes 3145736 | tf_op jit(solution)/shard_map/ppermute | solution.py:261
  123.3 1.3 collective-permute-start.11
  124.6 3.6 %collective-permute-start.12 = (f32[8,128]{1,0:T(8,128)S(1)}, f32[8,128]{1,0:T(8,128)S(1)}, u32[]{:S(2)}, u32[]{:S(2)}) collective-permute-start(f32[8,128]{1,0:T(8,128)S(1)} %broadcast_add_fusion), channel_id=1, source_target_pairs={{0,64},{32,96},{64,128},{96,160},{128,192},{160,224},{192,0},{224,... | collective-permute-start | bytes 12296 | tf_op jit(solution)/shard_map/ppermute | solution.py:261
  128.2 7.1 %collective-permute-start.13 = (f32[8,128]{1,0:T(8,128)S(1)}, f32[8,128]{1,0:T(8,128)S(1)}, u32[]{:S(2)}, u32[]{:S(2)}) collective-permute-start(f32[8,128]{1,0:T(8,128)S(1)} %fusion.2), channel_id=1, source_target_pairs={{0,128},{32,160},{64,192},{96,224},{128,0},{160,32},{192,64},{224,... | collective-permute-start | bytes 12296 | tf_op jit(solution)/shard_map/ppermute | solution.py:261
  135.4 3.7 %collective-permute-start.14 = (f32[8,128]{1,0:T(8,128)S(1)}, f32[8,128]{1,0:T(8,128)S(1)}, u32[]{:S(2)}, u32[]{:S(2)}) collective-permute-start(f32[8,128]{1,0:T(8,128)S(1)} %add.75), channel_id=1, source_target_pairs={{0,8},{1,9},{2,10},{3,11},{4,12},{5,13},{6,14},{7,15},{8,0},{9,1},... | collective-permute-start | bytes 12296 | tf_op jit(solution)/shard_map/ppermute | solution.py:261
  139.1 5.1 %collective-permute-start.15 = (f32[8,128]{1,0:T(8,128)S(1)}, f32[8,128]{1,0:T(8,128)S(1)}, u32[]{:S(2)}, u32[]{:S(2)}) collective-permute-start(f32[8,128]{1,0:T(8,128)S(1)} %add.76), channel_id=1, source_target_pairs={{0,16},{1,17},{2,18},{3,19},{4,20},{5,21},{6,22},{7,23},{8,24},{9,... | collective-permute-start | bytes 12296 | tf_op jit(solution)/shard_map/ppermute | solution.py:261
  144.2 3.6 %collective-permute-start.16 = (f32[8,128]{1,0:T(8,128)S(1)}, f32[8,128]{1,0:T(8,128)S(1)}, u32[]{:S(2)}, u32[]{:S(2)}) collective-permute-start(f32[8,128]{1,0:T(8,128)S(1)} %add.77), channel_id=1, source_target_pairs={{0,2},{1,3},{2,0},{3,1},{4,6},{5,7},{6,4},{7,5},{8,10},{9,11},{10,... | collective-permute-start | bytes 12296 | tf_op jit(solution)/shard_map/ppermute | solution.py:261
  147.8 4.7 %collective-permute-start.17 = (f32[8,128]{1,0:T(8,128)S(1)}, f32[8,128]{1,0:T(8,128)S(1)}, u32[]{:S(2)}, u32[]{:S(2)}) collective-permute-start(f32[8,128]{1,0:T(8,128)S(1)} %add.78), channel_id=1, source_target_pairs={{0,4},{1,5},{2,6},{3,7},{4,0},{5,1},{6,2},{7,3},{8,12},{9,13},{10,... | collective-permute-start | bytes 12296 | tf_op jit(solution)/shard_map/ppermute | solution.py:261
  160.4 7.5 %collective-permute-start.20 = (f32[8,128]{1,0:T(8,128)S(1)}, f32[8,128]{1,0:T(8,128)S(1)}, u32[]{:S(2)}, u32[]{:S(2)}) collective-permute-start(f32[8,128]{1,0:T(8,128)S(1)} %add.79), channel_id=1, source_target_pairs={{0,32},{32,0},{64,96},{96,64},{128,160},{160,128},{192,224},{224,1... | collective-permute-start | bytes 12296 | tf_op jit(solution)/shard_map/ppermute | solution.py:261

commit v3 on v2

v3 whole, which is shorter than its diff:
```python
import functools

import jax
import jax.numpy as jnp
from jax import lax
from jax.experimental import pallas as pl
from jax.experimental.pallas import tpu as pltpu
from jax.sharding import PartitionSpec as P

BAND_MAX = 8
GROUP = 4
F32 = jnp.float32
BF16 = jnp.bfloat16
VMEM_LIMIT = 40 * 1024 * 1024


def split(value):
    high = value.astype(BF16)
    return high, (value - high.astype(F32)).astype(BF16)


def dot(a, b):
    return jnp.dot(a, b, preferred_element_type=F32)


def dot3(ah, al, bh, bl):
    return dot(ah, bh) + (dot(al, bh) + dot(ah, bl))


def peak(value):
    return jnp.max(jnp.max(value, axis=0, keepdims=True), axis=1, keepdims=True)


def rows_of(values):
    return jnp.concatenate([jnp.broadcast_to(v, (1, 128)) for v in values], axis=0)


def tables_kernel(band, kyh, kyl, kxh, kxl, *, ny):
    def entries(sq, ok):
        return jnp.where(ok, jnp.exp(sq.astype(F32) * (-2.0 / (BAND_MAX * BAND_MAX))), 0.0)

    def offsets(shape):
        return lax.broadcasted_iota(jnp.int32, shape, 0), lax.broadcasted_iota(jnp.int32, shape, 1)

    row, col = offsets(kyh.shape)
    shift = ny.bit_length() - 1
    dy = row - col
    kyh[...], kyl[...] = split(entries(dy * dy, ((row >> shift) == (col >> shift)) & (jnp.abs(dy) <= band[1])))
    row, col = offsets(kxh.shape)
    dx = row - col
    kxh[...], kxl[...] = split(entries(dx * dx, jnp.abs(dx) <= band[0]))


def tile_loop(ny, nx, step):
    across = nx // 128

    def body_of(i, carry):
        row = pl.multiple_of(lax.div(i, across) * 8, 8)
        column = pl.multiple_of(lax.rem(i, across) * 128, 128)
        step(row, pl.ds(column, 128))
        return carry

    lax.fori_loop(0, ny // 8 * across, body_of, 0)


def own_planes(lo, hi, kz, y, ny, entry_lo, entry_hi):
    side = lo.shape[0] // ny
    planes = 2 * side
    taps = [kz[d] for d in range(BAND_MAX + 1)]

    def step(row, columns):
        e = [entry_lo(lo[pl.ds(q * ny + row, 8), columns]) for q in range(side)]
        e += [entry_hi(hi[pl.ds(q * ny + row, 8), columns]) for q in range(side)]
        for p in range(planes):
            total = taps[0] * e[p]
            for d in range(1, BAND_MAX + 1):
                near = [e[q] for q in (p - d, p + d) if 0 <= q < planes]
                total += taps[d] * (near[0] if len(near) == 1 else near[0] + near[1])
            y[pl.ds(p * ny + row, 8), columns] = total

    tile_loop(ny, lo.shape[1], step)


def halo_planes(left, right, kz, y, z, ny, own, entry_left, entry_right):
    side = left.shape[0] // ny
    taps = [kz[d] for d in range(BAND_MAX + 1)]

    def step(row, columns):
        e = [entry_left(left[pl.ds(q * ny + row, 8), columns]) for q in range(side)]
        for p in range(side):
            rows = pl.ds(p * ny + row, 8)
            total = own(y[rows, columns])
            for q in range(max(0, p + side - BAND_MAX), side):
                total += taps[p + side - q] * e[q]
            z[rows, columns] = total
        e = [entry_right(right[pl.ds(q * ny + row, 8), columns]) for q in range(side)]
        for p in range(side):
            rows = pl.ds((side + p) * ny + row, 8)
            total = own(y[rows, columns])
            for q in range(min(side, p + BAND_MAX - side + 1)):
                total += taps[side + q - p] * e[q]
            z[rows, columns] = total

    tile_loop(ny, left.shape[1], step)


def tile(value):
    return jnp.broadcast_to(value, (8, 128))


def own_log_kernel(kz, lo, hi, y, stats, *, ny):
    m_lo, m_hi = peak(lo[...]), peak(hi[...])
    m = jnp.maximum(m_lo, m_hi)
    stats[...] = rows_of([m_lo, m_hi, m, m, m, m, m, m])
    m = tile(m)
    entry = lambda v: jnp.exp(v - m)
    own_planes(lo, hi, kz, y, ny, entry, entry)


def own_linear_kernel(kz, lo, hi, stats, y, *, ny):
    c = stats[0:1, 0:1]
    f_lo = tile(jnp.exp((c - stats[1:2, 0:1]) * 0.5))
    f_hi = tile(jnp.exp((c - stats[2:3, 0:1]) * 0.5))
    own_planes(lo, hi, kz, y, ny, lambda v: v * f_lo * f_lo, lambda v: v * f_hi * f_hi)


def rows_and_columns(z, g, kyh, kyl, kxh, kxl, mid):
    half, block = mid.shape[0], kyh.shape[0]
    for k in range(half // block):
        rows = pl.ds(pl.multiple_of(g * half + k * block, block), block)
        zh, zl = split(z[rows, :])
        mid[k * block : (k + 1) * block, :] = dot3(kyh[...], kyl[...], zh, zl)
    mh, ml = split(mid[...])
    return dot3(mh, ml, kxh[...], kxl[...])


def log_halos(where, kz, left, right, y, stats, z, scale, ny):
    has_left, has_right = where[0] > 0, where[1] > 0
    m_own = stats[2:3, 0:1]
    m_left = jnp.where(has_left, peak(left[...]), m_own)
    m_right = jnp.where(has_right, peak(right[...]), m_own)
    c = jnp.maximum(m_own, jnp.maximum(m_left, m_right))
    scale[...] = rows_of([c, stats[0:1, 0:1], stats[1:2, 0:1], m_left, m_right, c, c, c])
    own = tile(jnp.exp(m_own - c))
    c = tile(c)
    halo_planes(
        left,
        right,
        kz,
        y,
        z,
        ny,
        lambda v: v * own,
        lambda v: jnp.where(has_left, jnp.exp(v - c), 0.0),
        lambda v: jnp.where(has_right, jnp.exp(v - c), 0.0),
    )


def potential_kernel(
    where, kz, left, right, y, stats, density, kyh, kyl, kxh, kxl, lo, hi, z, mid, scale, *, ny
):
    g = pl.program_id(0)

    @pl.when(g == 0)
    def _():
        log_halos(where, kz, left, right, y, stats, z, scale, ny)

    first = rows_and_columns(z, g, kyh, kyl, kxh, kxl, mid)
    potential = density[...] - (jnp.log(first) + scale[0:1, 0:1])

    @pl.when(g == 0)
    def _():
        lo[...] = potential

    @pl.when(g == 1)
    def _():
        hi[...] = potential


def ratio_kernel(
    where,
    weight,
    kz,
    left,
    right,
    y,
    stats,
    bary,
    cot,
    sum0,
    sum1,
    sum2,
    sum3,
    kyh,
    kyl,
    kxh,
    kxl,
    lo,
    hi,
    stats_out,
    total,
    z,
    mid,
    scale,
    *,
    ny,
):
    g = pl.program_id(0)

    @pl.when(g == 0)
    def _():
        log_halos(where, kz, left, right, y, stats, z, scale, ny)
        stats_out[...] = scale[...]
        total[...] = jnp.zeros(total.shape, F32)

    c = scale[0:1, 0:1]
    second = rows_and_columns(z, g, kyh, kyl, kxh, kxl, mid)
    block = sum0.shape[0]
    per_step = mid.shape[0] // block
    count = 2 * per_step
    f = jnp.exp((jnp.where(g == 0, scale[1:2, 0:1], scale[2:3, 0:1]) - c) * 0.5)
    for k in range(per_step):
        rows = slice(k * block, (k + 1) * block)
        away = lax.rem(g * per_step + k - where[2] + count, count)
        over_atoms = jnp.where(
            away == 0,
            sum0[...],
            jnp.where(away == 1, sum1[...], jnp.where(away == 2, sum2[...], sum3[...])),
        )
        summed = bary[rows, :] + over_atoms
        share = summed * (jnp.log(second[rows, :]) + c)
        share = jnp.sum(share.reshape(block // 8, 8, share.shape[1]), axis=0)
        for m in range(share.shape[1] // 128):
            total[...] += share[:, m * 128 : (m + 1) * 128]
        ratio = (weight[0] * summed - cot[rows, :]) / second[rows, :] * f * f

        @pl.when(g == 0)
        def _():
            lo[rows, :] = ratio

        @pl.when(g == 1)
        def _():
            hi[rows, :] = ratio


def gradient_kernel(
    where, kz, left, right, y, stats, pot_lo, pot_hi, kyh, kyl, kxh, kxl, out, z, mid, *, ny
):
    g = pl.program_id(0)
    c = stats[0:1, 0:1]

    @pl.when(g == 0)
    def _():
        f_left = tile(jnp.exp((c - stats[3:4, 0:1]) * 0.5))
        f_right = tile(jnp.exp((c - stats[4:5, 0:1]) * 0.5))
        has_left, has_right = where[0] > 0, where[1] > 0
        halo_planes(
            left,
            right,
            kz,
            y,
            z,
            ny,
            lambda v: v,
            lambda v: jnp.where(has_left, v * f_left * f_left, 0.0),
            lambda v: jnp.where(has_right, v * f_right * f_right, 0.0),
        )

    blurred = rows_and_columns(z, g, kyh, kyl, kxh, kxl, mid)
    potential = jnp.where(g == 0, pot_lo[...], pot_hi[...])
    out[...] = jnp.exp(potential - c) * blurred


def body(
    atom_log_density,
    prior_log_scaling,
    atom_cotangent_rows,
    barycenter_cotangent,
    weights,
    band,
    slot_atom_index,
):
    planes, ny, nx = barycenter_cotangent.shape
    slabs, atoms = lax.axis_size("slab"), lax.axis_size("atom")
    rows = planes * ny
    half = rows // 2
    block = GROUP * ny
    count = planes // GROUP
    slab_at, atom_at = lax.axis_index("slab"), lax.axis_index("atom")
    across = atoms // 2
    x_at = atom_at // 2

    smem = pl.BlockSpec(memory_space=pltpu.SMEM)
    params = pltpu.CompilerParams(vmem_limit_bytes=VMEM_LIMIT)

    def shape(*dims, dtype=F32):
        return jax.ShapeDtypeStruct(dims, dtype)

    def full(*dims):
        return pl.BlockSpec(dims, lambda g: (0,) * len(dims))

    def send(value, axis, pairs):
        return lax.ppermute(value, axis, pairs)

    in_order = lax.optimization_barrier
    to_right = [(i, i + 1) for i in range(slabs - 1)]
    to_left = [(i + 1, i) for i in range(slabs - 1)]
    ahead = {
        k: [(2 * x + z, 2 * ((x + k) % across) + z) for x in range(across) for z in range(2)]
        for k in range(1, across)
    }
    swap = [(i, i ^ 1) for i in range(atoms)]

    cot = atom_cotangent_rows.reshape(rows, nx)

    def block_of(k):
        return lax.dynamic_slice_in_dim(cot, lax.rem(x_at + k, count) * block, block)

    blocks = [block_of(k) for k in range(1, across)]
    part = block_of(0)
    for k in range(1, across):
        part = part + send(blocks[k - 1], "atom", ahead[k])
    swapped = send(part, "atom", swap)

    y_shape, x_shape = (block, block), (nx, nx)
    distance = jnp.arange(BAND_MAX + 1, dtype=jnp.int32)
    kz = jnp.exp((distance * distance).astype(F32) * (-2.0 / (BAND_MAX * BAND_MAX)))
    kz = jnp.where(distance <= band[2], kz, 0.0)
    tables = pl.pallas_call(
        functools.partial(tables_kernel, ny=ny),
        out_shape=[shape(*dims, dtype=BF16) for dims in (y_shape, y_shape, x_shape, x_shape)],
        in_specs=[smem],
        compiler_params=params,
        name="tables",
    )(band)
    prior = prior_log_scaling.reshape(rows, nx)
    prior_lo, prior_hi = prior[:half], prior[half:]
    from_left = send(prior_hi, "slab", to_right)
    from_right = send(prior_lo, "slab", to_left)

    where = jnp.stack([(slab_at > 0), (slab_at < slabs - 1), x_at, x_at]).astype(jnp.int32)
    slot = lax.dynamic_slice_in_dim(slot_atom_index, atom_at, 1)
    onehot = (slot[0] == jnp.arange(weights.shape[0], dtype=jnp.int32)).astype(F32)
    weight = jnp.sum(onehot * weights, keepdims=True)

    vmem = pl.BlockSpec(memory_space=pltpu.VMEM)
    own_out = [shape(rows, nx), shape(8, 128)]
    own_log = pl.pallas_call(
        functools.partial(own_log_kernel, ny=ny),
        in_specs=[smem, vmem, vmem],
        out_shape=own_out,
        compiler_params=params,
        name="own_log",
    )
    halo_specs = [full(half, nx), full(half, nx), full(rows, nx), full(8, 128)]
    table_specs = [full(*y_shape), full(*y_shape), full(*x_shape), full(*x_shape)]
    one = pl.BlockSpec((half, nx), lambda g: (g, 0))
    whole_half = full(half, nx)
    scratch = [pltpu.VMEM((rows, nx), F32), pltpu.VMEM((half, nx), F32)]
    scale = pltpu.VMEM((8, 128), F32)

    y, stats = own_log(kz, prior_lo, prior_hi)
    pot_lo, pot_hi = pl.pallas_call(
        functools.partial(potential_kernel, ny=ny),
        grid=(2,),
        in_specs=[smem, smem, *halo_specs, one, *table_specs],
        out_specs=[whole_half, whole_half],
        out_shape=[shape(half, nx), shape(half, nx)],
        scratch_shapes=[*scratch, scale],
        compiler_params=params,
        name="potential",
    )(where, kz, from_left, from_right, y, stats, atom_log_density.reshape(rows, nx), *tables)

    from_left = send(pot_hi, "slab", to_right)
    from_right = send(pot_lo, "slab", to_left)
    both = part + swapped
    sums = [both] + [send(both, "atom", ahead[across - k]) for k in range(1, across)]
    y, stats = own_log(kz, pot_lo, pot_hi)
    ratio_lo, ratio_hi, stats, total = pl.pallas_call(
        functools.partial(ratio_kernel, ny=ny),
        grid=(2,),
        in_specs=[smem, smem, smem, *halo_specs, one, one] + [full(block, nx)] * 4 + table_specs,
        out_specs=[whole_half, whole_half, full(8, 128), full(8, 128)],
        out_shape=[shape(half, nx), shape(half, nx), shape(8, 128), shape(8, 128)],
        scratch_shapes=[*scratch, scale],
        compiler_params=params,
        name="ratio",
    )(
        where,
        weight,
        kz,
        from_left,
        from_right,
        y,
        stats,
        barycenter_cotangent.reshape(rows, nx),
        cot,
        *sums,
        *tables,
    )

    from_left = send(ratio_hi, "slab", to_right)
    from_right = send(ratio_lo, "slab", to_left)
    (y,) = pl.pallas_call(
        functools.partial(own_linear_kernel, ny=ny),
        in_specs=[smem, vmem, vmem, vmem],
        out_shape=[shape(rows, nx)],
        compiler_params=params,
        name="own_linear",
    )(kz, ratio_lo, ratio_hi, stats)

    total, y = in_order((total, y))
    value = jnp.broadcast_to(jnp.sum(total), (atoms * slabs, 128))
    value = lax.all_to_all(value, ("atom", "slab"), 0, 0, tiled=True)
    by_slot = jnp.sum(value[:, 0].reshape(atoms, slabs), axis=1)
    spread = slot_atom_index[:, None] == jnp.arange(atoms, dtype=jnp.int32)[None, :]
    weight_grad = jnp.sum(jnp.where(spread, by_slot[:, None], 0.0), axis=0) / (rows * nx * slabs)

    gradient = pl.pallas_call(
        functools.partial(gradient_kernel, ny=ny),
        grid=(2,),
        in_specs=[smem, smem, *halo_specs, whole_half, whole_half, *table_specs],
        out_specs=one,
        out_shape=shape(rows, nx),
        scratch_shapes=scratch,
        compiler_params=params,
        name="gradient",
    )(where, kz, from_left, from_right, y, stats, pot_lo, pot_hi, *tables)
    return gradient.reshape(atom_log_density.shape), weight_grad


def solution(mesh):
    return jax.shard_map(
        body,
        mesh=mesh,
        in_specs=(
            P("atom", "slab", None, None),
            P("atom", "slab", None, None),
            P("atom", "slab", None, None),
            P("slab", None, None),
            P(),
            P(),
            P(),
        ),
        out_specs=(P("atom", "slab", None, None), P()),
        check_vma=False,
    )
```

time: 171 us -> 154 us (0.901)
  the two profiles are of different devices: /device:TPU:10 before, /device:TPU:1 now
where the time goes in v3:
time: 154 us
  Pallas kernels  38.2 us (25%)
  waiting for transfers between devices  36.5 us (24%)
  starting transfers between devices  36.1 us (23%)
  blocking collectives  26.9 us (17%)
  local copies, waits for them, and re-layouts  9.42 us (6%)
  other arithmetic  5.92 us (4%)
    ppermute x13, waiting for transfers between devices, send(): return lax.ppermute(value, axis, pairs)  36.5 us
    ppermute x13, starting transfers between devices, send(): return lax.ppermute(value, axis, pairs)  36.1 us
    all_to_all x1, blocking collectives, body(): value = lax.all_to_all(value, ('atom', 'slab'), 0, 0, tiled=True)  26.9 us
    pallas_call x1, Pallas kernels, body(): pl.pallas_call(functools.partial(ratio_kernel, ny=ny), grid=(2,), in_spec...  10.3 us
    pallas_call x1, Pallas kernels, body(): pl.pallas_call(functools.partial(potential_kernel, ny=ny), grid=(2,), in_...  7.76 us
    pallas_call x1, Pallas kernels, body(): pl.pallas_call(functools.partial(gradient_kernel, ny=ny), grid=(2,), in_s...  7.65 us
    pallas_call x1, Pallas kernels, body(): y, stats = own_log(kz, prior_lo, prior_hi)  3.92 us
    pallas_call x1, Pallas kernels, body(): y, stats = own_log(kz, pot_lo, pot_hi)  3.91 us
  transfers between devices with their start and end apart: 13, of which 5 were waited for; matrix products, arithmetic and copies ran while one was open for 6% of the time, Pallas kernels for 13%

profile of v3, /device:TPU:1, one launch (start us, length us, event | category | flops | bytes accessed | tf_op | source)
XLA Modules:
  0.0 153.9 jit_solution(7333506988086497484)
XLA Ops:
  0.6 0.0 copy-start
  0.6 3.2 %fusion.1 = (f32[1,8,64,512]{3,2,1,0:T(8,128)}, f32[1,8,64,512]{3,2,1,0:T(8,128)}) fusion(f32[1,16,64,512]{3,2,1,0:T(8,128)} %param.8), kind=kLoop, calls=%fused_computation.12 | loop fusion | bytes 4194304 | tf_op jit(solution)/shard_map/slice | solution.py:337
  3.9 0.0 copy-start.5
  3.9 5.1 %collective-permute-start = (f32[512,512]{1,0:T(8,128)}, f32[512,512]{1,0:T(8,128)}, u32[]{:S(2)}, u32[]{:S(2)}) collective-permute-start(f32[512,512]{1,0:T(8,128)} %bitcast.6.hi), channel_id=1, source_target_pairs={{0,1},{1,2},{2,3},{3,4},{4,5},{5,6},{6,7},{7,8},{8,9},{9,10},{10,1... | collective-permute-start | bytes 3145736 | tf_op jit(solution)/shard_map/ppermute | solution.py:303
  8.9 2.5 %collective-permute-start.1 = (f32[512,512]{1,0:T(8,128)}, f32[512,512]{1,0:T(8,128)}, u32[]{:S(2)}, u32[]{:S(2)}) collective-permute-start(f32[512,512]{1,0:T(8,128)} %bitcast.7.lo), channel_id=1, source_target_pairs={{1,0},{2,1},{3,2},{4,3},{5,4},{6,5},{7,6},{8,7},{9,8},{10,9},{11,1... | collective-permute-start | bytes 3145736 | tf_op jit(solution)/shard_map/ppermute | solution.py:303
  11.5 0.0 copy-done
  11.5 1.2 constant_dynamic-slice_fusion.2
  12.7 0.7 collective-permute-start.4
  13.3 2.0 %collective-permute-start.6 = (f32[256,512]{1,0:T(8,128)}, f32[256,512]{1,0:T(8,128)}, u32[]{:S(2)}, u32[]{:S(2)}) collective-permute-start(f32[256,512]{1,0:T(8,128)} %get-tuple-element.35), channel_id=1, source_target_pairs={{0,192},{32,224},{64,0},{96,32},{128,64},{160,96},{192,128},{224,1... | collective-permute-start | bytes 1572872 | tf_op jit(solution)/shard_map/ppermute | solution.py:303
  15.4 1.0 collective-permute-start.5
  16.3 0.0 copy-done.5
  16.4 0.6 slice.18
  16.9 1.1 tables.1
  18.0 0.7 compare_select_fusion.1.kz
  18.7 3.9 %own_log.2 = (f32[1024,512]{1,0:T(8,128)S(1)}, f32[8,128]{1,0:T(8,128)S(1)}) custom-call(f32[9]{0:T(128)S(1)} %compare_select_fusion.1.kz, f32[512,512]{1,0:T(8,128)} %bitcast.7.lo, f32[512,512]{1,0:T(8,128)} %bitcast.6.hi), custom_call_target="tpu_custom_call" | custom-call | tf_op jit(solution)/shard_map/own_log/pallas_call | solution.py:362
  22.6 0.0 copy-start.2
  22.6 1.3 copy-done.2
  23.9 0.0 copy-start.1
  23.9 0.1 pad_add_fusion.where
  24.0 15.1 %collective-permute-done.4 = f32[256,512]{1,0:T(8,128)} collective-permute-done((f32[256,512]{1,0:T(8,128)}, f32[256,512]{1,0:T(8,128)}, u32[]{:S(2)}, u32[]{:S(2)}) %collective-permute-start.4) | collective-permute-done | bytes 524320 | tf_op jit(solution)/shard_map/ppermute | solution.py:303
  39.1 0.0 collective-permute-done.6
  39.1 0.0 collective-permute-done.5
  39.1 1.6 %add_add_fusion = f32[256,512]{1,0:T(8,128)S(1)} fusion(f32[256,512]{1,0:T(8,128)} %collective-permute-done.6, f32[256,512]{1,0:T(8,128)} %collective-permute-done.5, f32[256,512]{1,0:T(8,128)} %collective-permute-done.4, f32[1024,512]{1,0:T(8,128)S(1)} %bitcast.14, s32[]{:T(128)S(6)} %select_n.31), kind=kLoop, calls=%fused_computation | loop fusion | flops 393216 | bytes 2621444 | tf_op jit(solution)/shard_map/add | solution.py:322
  40.7 6.7 %collective-permute-start.7 = (f32[256,512]{1,0:T(8,128)S(1)}, f32[256,512]{1,0:T(8,128)S(1)}, u32[]{:S(2)}, u32[]{:S(2)}) collective-permute-start(f32[256,512]{1,0:T(8,128)S(1)} %add_add_fusion), channel_id=1, source_target_pairs={{0,32},{32,0},{64,96},{96,64},{128,160},{160,128},{192,224},{224,1... | collective-permute-start | bytes 1572872 | tf_op jit(solution)/shard_map/ppermute | solution.py:303
  47.3 0.0 collective-permute-done.left
  47.3 0.0 collective-permute-done.1.right
  47.3 0.0 copy-done.1
  47.4 0.0 copy-start.3
  47.4 1.6 %copy-done.3 = f32[1024,512]{1,0:T(8,128)S(1)} copy-done((f32[1024,512]{1,0:T(8,128)S(1)}, f32[1024,512]{1,0:T(8,128)}, u32[]{:S(2)}) %copy-start.3) | copy-done | bytes 2097176
  48.9 0.0 copy-start.7
  48.9 7.8 %potential.1 = (f32[512,512]{1,0:T(8,128)}, f32[512,512]{1,0:T(8,128)}) custom-call(s32[4]{0:T(128)S(1)} %pad_add_fusion.where, f32[9]{0:T(128)S(1)} %compare_select_fusion.1.kz, f32[512,512]{1,0:T(8,128)} %collective-permute-done.left, f32[512,512]{1,0:T(8,128)} %collective-permute-done.1.right, f32[1024,512]{1,0:T(8,128)S(1)} %copy-done.3, ...), custom_call_target="tpu_custom_call" | custom-call | tf_op jit(solution)/shard_map/potential/pallas_call | solution.py:363
  56.7 3.4 %collective-permute-start.2 = (f32[512,512]{1,0:T(8,128)}, f32[512,512]{1,0:T(8,128)}, u32[]{:S(2)}, u32[]{:S(2)}) collective-permute-start(f32[512,512]{1,0:T(8,128)} %get-tuple-element.24.hi.pot_hi), channel_id=1, source_target_pairs={{0,1},{1,2},{2,3},{3,4},{4,5},{5,6},{6,7},{7,8},{8,9},{9,10},{10,1... | collective-permute-start | bytes 3145736 | tf_op jit(solution)/shard_map/ppermute | solution.py:303
  60.1 1.9 %collective-permute-start.3 = (f32[512,512]{1,0:T(8,128)}, f32[512,512]{1,0:T(8,128)}, u32[]{:S(2)}, u32[]{:S(2)}) collective-permute-start(f32[512,512]{1,0:T(8,128)} %get-tuple-element.25.lo.pot_lo), channel_id=1, source_target_pairs={{1,0},{2,1},{3,2},{4,3},{5,4},{6,5},{7,6},{8,7},{9,8},{10,9},{11,1... | collective-permute-start | bytes 3145736 | tf_op jit(solution)/shard_map/ppermute | solution.py:303
  62.0 5.3 %collective-permute-done.7 = f32[256,512]{1,0:T(8,128)S(1)} collective-permute-done((f32[256,512]{1,0:T(8,128)S(1)}, f32[256,512]{1,0:T(8,128)S(1)}, u32[]{:S(2)}, u32[]{:S(2)}) %collective-permute-start.7) | collective-permute-done | bytes 524320 | tf_op jit(solution)/shard_map/ppermute | solution.py:303
  67.3 0.9 add.48.sum0
  68.2 4.2 %collective-permute-start.10 = (f32[256,512]{1,0:T(8,128)}, f32[256,512]{1,0:T(8,128)}, u32[]{:S(2)}, u32[]{:S(2)}) collective-permute-start(f32[256,512]{1,0:T(8,128)} %add.48.sum0), channel_id=1, source_target_pairs={{0,64},{32,96},{64,128},{96,160},{128,192},{160,224},{192,0},{224,... | collective-permute-start | bytes 1572872 | tf_op jit(solution)/shard_map/ppermute | solution.py:303
  72.5 2.1 %collective-permute-start.9 = (f32[256,512]{1,0:T(8,128)}, f32[256,512]{1,0:T(8,128)}, u32[]{:S(2)}, u32[]{:S(2)}) collective-permute-start(f32[256,512]{1,0:T(8,128)} %add.48.sum0), channel_id=1, source_target_pairs={{0,128},{32,160},{64,192},{96,224},{128,0},{160,32},{192,64},{224,... | collective-permute-start | bytes 1572872 | tf_op jit(solution)/shard_map/ppermute | solution.py:303
  74.6 0.2 collective-permute-start.8
  74.9 0.0 copy-done.7
  74.9 0.6 dynamic_slice.15
  75.5 0.0 copy-done.6
  75.5 1.4 fusion
  76.8 3.9 %own_log.3 = (f32[1024,512]{1,0:T(8,128)S(1)}, f32[8,128]{1,0:T(8,128)S(1)}) custom-call(f32[9]{0:T(128)S(1)} %compare_select_fusion.1.kz, f32[512,512]{1,0:T(8,128)} %get-tuple-element.25.lo.pot_lo, f32[512,512]{1,0:T(8,128)} %get-tuple-element.24.hi.pot_hi), custom_call_target="tpu_custom_call" | custom-call | tf_op jit(solution)/shard_map/own_log/pallas_call | solution.py:378
  80.7 3.3 %collective-permute-done.10.sum3 = f32[256,512]{1,0:T(8,128)} collective-permute-done((f32[256,512]{1,0:T(8,128)}, f32[256,512]{1,0:T(8,128)}, u32[]{:S(2)}, u32[]{:S(2)}) %collective-permute-start.10) | collective-permute-done | bytes 524320 | tf_op jit(solution)/shard_map/ppermute | solution.py:303
  84.0 12.3 %collective-permute-done.9.sum2 = f32[256,512]{1,0:T(8,128)} collective-permute-done((f32[256,512]{1,0:T(8,128)}, f32[256,512]{1,0:T(8,128)}, u32[]{:S(2)}, u32[]{:S(2)}) %collective-permute-start.9) | collective-permute-done | bytes 524320 | tf_op jit(solution)/shard_map/ppermute | solution.py:303
  96.3 0.6 collective-permute-done.8.sum1
  96.9 0.0 collective-permute-done.2.left
  96.9 0.0 collective-permute-done.3.right
  96.9 0.0 copy-done.4
  96.9 10.3 %ratio.1 = (f32[512,512]{1,0:T(8,128)}, f32[512,512]{1,0:T(8,128)}, f32[8,128]{1,0:T(8,128)S(1)}, f32[8,128]{1,0:T(8,128)S(1)}) custom-call(s32[4]{0:T(128)S(1)} %pad_add_fusion.where, f32[1]{0:T(128)} %bitcast.5.weight, f32[9]{0:T(128)S(1)} %compare_select_fusion.1.kz, f32[512,512]{1,0:T(8,128)} %collective-permute-done.2.left, ...), custom_call_target="tpu_custom_call" | custom-call | tf_op jit(solution)/shard_map/ratio/pallas_call | solution.py:379
  107.2 1.9 %collective-permute-start.11 = (f32[512,512]{1,0:T(8,128)}, f32[512,512]{1,0:T(8,128)}, u32[]{:S(2)}, u32[]{:S(2)}) collective-permute-start(f32[512,512]{1,0:T(8,128)} %get-tuple-element.28.hi), channel_id=1, source_target_pairs={{0,1},{1,2},{2,3},{3,4},{4,5},{5,6},{6,7},{7,8},{8,9},{9,10},{10,1... | collective-permute-start | bytes 3145736 | tf_op jit(solution)/shard_map/ppermute | solution.py:303
  109.1 4.4 %collective-permute-start.12 = (f32[512,512]{1,0:T(8,128)}, f32[512,512]{1,0:T(8,128)}, u32[]{:S(2)}, u32[]{:S(2)}) collective-permute-start(f32[512,512]{1,0:T(8,128)} %get-tuple-element.29.lo), channel_id=1, source_target_pairs={{1,0},{2,1},{3,2},{4,3},{5,4},{6,5},{7,6},{8,7},{9,8},{10,9},{11,1... | collective-permute-start | bytes 3145736 | tf_op jit(solution)/shard_map/ppermute | solution.py:303
  113.5 3.6 %own_linear.1.y = f32[1024,512]{1,0:T(8,128)S(1)} custom-call(f32[9]{0:T(128)S(1)} %compare_select_fusion.1.kz, f32[512,512]{1,0:T(8,128)} %get-tuple-element.29.lo, f32[512,512]{1,0:T(8,128)} %get-tuple-element.28.hi, f32[8,128]{1,0:T(8,128)S(1)} %get-tuple-element.31.stats), custom_call_target="tpu_custom_call" | custom-call | tf_op jit(solution)/shard_map/own_linear/pallas_call | solution.py:404
  117.2 0.6 reduce_sum.37
  117.8 0.7 broadcast_in_dim.27
  118.5 26.9 %all_to_all.9 = f32[256,1,128]{2,1,0:T(1,128)S(1)} all-to-all(f32[256,1,128]{2,1,0:T(1,128)S(1)} %broadcast_in_dim.27), channel_id=1, replica_groups=mesh['atom'=8,'slab'=32] {'atom','slab'}, dimensions={0} | all-to-all | bytes 262144 | tf_op jit(solution)/shard_map/all_to_all | solution.py:414
  145.4 0.1 slice_reduce_fusion
  145.5 0.1 reshape_squeeze.3
  145.5 0.1 reduce_sum.38
  145.7 0.1 select_reduce_fusion
  145.8 0.5 broadcast_multiply_fusion
  146.3 0.0 collective-permute-done.11.left
  146.3 0.0 collective-permute-done.12.right
  146.3 7.6 %gradient.1 = f32[1024,512]{1,0:T(8,128)} custom-call(s32[4]{0:T(128)S(1)} %pad_add_fusion.where, f32[9]{0:T(128)S(1)} %compare_select_fusion.1.kz, f32[512,512]{1,0:T(8,128)} %collective-permute-done.11.left, f32[512,512]{1,0:T(8,128)} %collective-permute-done.12.right, f32[1024,512]{1,0:T(8,128)S(1)} %own_linear.1.y, ...), custom_call_target="tpu_custom_call" | custom-call | tf_op jit(solution)/shard_map/gradient/pallas_call | solution.py:419
  (2 shorter events, 0.0 us)
Async XLA Ops:
  0.6 10.8 %copy-start = (f32[1,16,64,512]{3,2,1,0:T(8,128)S(1)}, f32[1,16,64,512]{3,2,1,0:T(8,128)}, u32[]{:S(2)}) copy-start(f32[1,16,64,512]{3,2,1,0:T(8,128)} %param.9) | copy-start | bytes 6291460
  3.9 12.5 %copy-start.5 = (s32[3]{0:T(128)S(1)}, s32[3]{0:T(128)}, u32[]{:S(2)}) copy-start(s32[3]{0:T(128)} %band.1) | copy-start | bytes 40
  3.9 43.5 %collective-permute-start = (f32[512,512]{1,0:T(8,128)}, f32[512,512]{1,0:T(8,128)}, u32[]{:S(2)}, u32[]{:S(2)}) collective-permute-start(f32[512,512]{1,0:T(8,128)} %bitcast.6.hi), channel_id=1, source_target_pairs={{0,1},{1,2},{2,3},{3,4},{4,5},{5,6},{6,7},{7,8},{8,9},{9,10},{10,1... | collective-permute-start | bytes 3145736 | tf_op jit(solution)/shard_map/ppermute | solution.py:303
  8.9 38.4 %collective-permute-start.1 = (f32[512,512]{1,0:T(8,128)}, f32[512,512]{1,0:T(8,128)}, u32[]{:S(2)}, u32[]{:S(2)}) collective-permute-start(f32[512,512]{1,0:T(8,128)} %bitcast.7.lo), channel_id=1, source_target_pairs={{1,0},{2,1},{3,2},{4,3},{5,4},{6,5},{7,6},{8,7},{9,8},{10,9},{11,1... | collective-permute-start | bytes 3145736 | tf_op jit(solution)/shard_map/ppermute | solution.py:303
  12.7 26.4 %collective-permute-start.4 = (f32[256,512]{1,0:T(8,128)}, f32[256,512]{1,0:T(8,128)}, u32[]{:S(2)}, u32[]{:S(2)}) collective-permute-start(f32[256,512]{1,0:T(8,128)} %get-tuple-element.34), channel_id=1, source_target_pairs={{0,64},{32,96},{64,128},{96,160},{128,192},{160,224},{192,0},{224,... | collective-permute-start | bytes 1572872 | tf_op jit(solution)/shard_map/ppermute | solution.py:303
  13.3 25.7 %collective-permute-start.6 = (f32[256,512]{1,0:T(8,128)}, f32[256,512]{1,0:T(8,128)}, u32[]{:S(2)}, u32[]{:S(2)}) collective-permute-start(f32[256,512]{1,0:T(8,128)} %get-tuple-element.35), channel_id=1, source_target_pairs={{0,192},{32,224},{64,0},{96,32},{128,64},{160,96},{192,128},{224,1... | collective-permute-start | bytes 1572872 | tf_op jit(solution)/shard_map/ppermute | solution.py:303
  15.4 23.7 %collective-permute-start.5 = (f32[256,512]{1,0:T(8,128)}, f32[256,512]{1,0:T(8,128)}, u32[]{:S(2)}, u32[]{:S(2)}) collective-permute-start(f32[256,512]{1,0:T(8,128)} %get-tuple-element.36), channel_id=1, source_target_pairs={{0,128},{32,160},{64,192},{96,224},{128,0},{160,32},{192,64},{224,... | collective-permute-start | bytes 1572872 | tf_op jit(solution)/shard_map/ppermute | solution.py:303
  22.6 1.3 copy-start.2
  23.9 23.4 %copy-start.1 = (f32[1,16,64,512]{3,2,1,0:T(8,128)S(1)}, f32[1,16,64,512]{3,2,1,0:T(8,128)}, u32[]{:S(2)}) copy-start(f32[1,16,64,512]{3,2,1,0:T(8,128)} %param.7) | copy-start | bytes 6291460
  40.7 26.7 %collective-permute-start.7 = (f32[256,512]{1,0:T(8,128)S(1)}, f32[256,512]{1,0:T(8,128)S(1)}, u32[]{:S(2)}, u32[]{:S(2)}) collective-permute-start(f32[256,512]{1,0:T(8,128)S(1)} %add_add_fusion), channel_id=1, source_target_pairs={{0,32},{32,0},{64,96},{96,64},{128,160},{160,128},{192,224},{224,1... | collective-permute-start | bytes 1572872 | tf_op jit(solution)/shard_map/ppermute | solution.py:303
  47.4 1.6 %copy-start.3 = (f32[1024,512]{1,0:T(8,128)S(1)}, f32[1024,512]{1,0:T(8,128)}, u32[]{:S(2)}) copy-start(f32[1024,512]{1,0:T(8,128)} %copy-done.2) | copy-start | bytes 6291460
  48.9 25.9 %copy-start.7 = (s32[8]{0:T(128)S(1)}, s32[8]{0:T(128)}, u32[]{:S(2)}) copy-start(s32[8]{0:T(128)} %param.13) | copy-start | bytes 100
  48.9 26.5 %copy-start.6 = (f32[8]{0:T(128)S(1)}, f32[8]{0:T(128)}, u32[]{:S(2)}) copy-start(f32[8]{0:T(128)} %param.11) | copy-start | bytes 100
  56.7 40.2 %collective-permute-start.2 = (f32[512,512]{1,0:T(8,128)}, f32[512,512]{1,0:T(8,128)}, u32[]{:S(2)}, u32[]{:S(2)}) collective-permute-start(f32[512,512]{1,0:T(8,128)} %get-tuple-element.24.hi.pot_hi), channel_id=1, source_target_pairs={{0,1},{1,2},{2,3},{3,4},{4,5},{5,6},{6,7},{7,8},{8,9},{9,10},{10,1... | collective-permute-start | bytes 3145736 | tf_op jit(solution)/shard_map/ppermute | solution.py:303
  60.1 36.9 %collective-permute-start.3 = (f32[512,512]{1,0:T(8,128)}, f32[512,512]{1,0:T(8,128)}, u32[]{:S(2)}, u32[]{:S(2)}) collective-permute-start(f32[512,512]{1,0:T(8,128)} %get-tuple-element.25.lo.pot_lo), channel_id=1, source_target_pairs={{1,0},{2,1},{3,2},{4,3},{5,4},{6,5},{7,6},{8,7},{9,8},{10,9},{11,1... | collective-permute-start | bytes 3145736 | tf_op jit(solution)/shard_map/ppermute | solution.py:303
  68.2 15.8 %collective-permute-start.10 = (f32[256,512]{1,0:T(8,128)}, f32[256,512]{1,0:T(8,128)}, u32[]{:S(2)}, u32[]{:S(2)}) collective-permute-start(f32[256,512]{1,0:T(8,128)} %add.48.sum0), channel_id=1, source_target_pairs={{0,64},{32,96},{64,128},{96,160},{128,192},{160,224},{192,0},{224,... | collective-permute-start | bytes 1572872 | tf_op jit(solution)/shard_map/ppermute | solution.py:303
  72.5 23.9 %collective-permute-start.9 = (f32[256,512]{1,0:T(8,128)}, f32[256,512]{1,0:T(8,128)}, u32[]{:S(2)}, u32[]{:S(2)}) collective-permute-start(f32[256,512]{1,0:T(8,128)} %add.48.sum0), channel_id=1, source_target_pairs={{0,128},{32,160},{64,192},{96,224},{128,0},{160,32},{192,64},{224,... | collective-permute-start | bytes 1572872 | tf_op jit(solution)/shard_map/ppermute | solution.py:303
  74.6 22.3 %collective-permute-start.8 = (f32[256,512]{1,0:T(8,128)}, f32[256,512]{1,0:T(8,128)}, u32[]{:S(2)}, u32[]{:S(2)}) collective-permute-start(f32[256,512]{1,0:T(8,128)} %add.48.sum0), channel_id=1, source_target_pairs={{0,192},{32,224},{64,0},{96,32},{128,64},{160,96},{192,128},{224,1... | collective-permute-start | bytes 1572872 | tf_op jit(solution)/shard_map/ppermute | solution.py:303
  74.9 22.1 %copy-start.4 = (f32[16,64,512]{2,1,0:T(8,128)S(1)}, f32[16,64,512]{2,1,0:T(8,128)}, u32[]{:S(2)}) copy-start(f32[16,64,512]{2,1,0:T(8,128)} %param.10) | copy-start | bytes 6291460
  107.2 39.1 %collective-permute-start.11 = (f32[512,512]{1,0:T(8,128)}, f32[512,512]{1,0:T(8,128)}, u32[]{:S(2)}, u32[]{:S(2)}) collective-permute-start(f32[512,512]{1,0:T(8,128)} %get-tuple-element.28.hi), channel_id=1, source_target_pairs={{0,1},{1,2},{2,3},{3,4},{4,5},{5,6},{6,7},{7,8},{8,9},{9,10},{10,1... | collective-permute-start | bytes 3145736 | tf_op jit(solution)/shard_map/ppermute | solution.py:303
  109.1 37.1 %collective-permute-start.12 = (f32[512,512]{1,0:T(8,128)}, f32[512,512]{1,0:T(8,128)}, u32[]{:S(2)}, u32[]{:S(2)}) collective-permute-start(f32[512,512]{1,0:T(8,128)} %get-tuple-element.29.lo), channel_id=1, source_target_pairs={{1,0},{2,1},{3,2},{4,3},{5,4},{6,5},{7,6},{8,7},{9,8},{10,9},{11,1... | collective-permute-start | bytes 3145736 | tf_op jit(solution)/shard_map/ppermute | solution.py:303

commit v4 on v3

--- a/solution.py
+++ b/solution.py
@@ -11,7 +11,7 @@
 GROUP = 4
 F32 = jnp.float32
 BF16 = jnp.bfloat16
-VMEM_LIMIT = 40 * 1024 * 1024
+VMEM_LIMIT = 12 * 1024 * 1024
 
 
 def split(value):
@@ -127,7 +127,7 @@
 def rows_and_columns(z, g, kyh, kyl, kxh, kxl, mid):
     half, block = mid.shape[0], kyh.shape[0]
     for k in range(half // block):
-        rows = pl.ds(pl.multiple_of(g * half + k * block, block), block)
+        rows = pl.ds(g * half + k * block, block)
         zh, zl = split(z[rows, :])
         mid[k * block : (k + 1) * block, :] = dot3(kyh[...], kyl[...], zh, zl)
     mh, ml = split(mid[...])
@@ -159,69 +159,28 @@
 def potential_kernel(
     where, kz, left, right, y, stats, density, kyh, kyl, kxh, kxl, lo, hi, z, mid, scale, *, ny
 ):
-    g = pl.program_id(0)
-
-    @pl.when(g == 0)
-    def _():
-        log_halos(where, kz, left, right, y, stats, z, scale, ny)
-
-    first = rows_and_columns(z, g, kyh, kyl, kxh, kxl, mid)
-    potential = density[...] - (jnp.log(first) + scale[0:1, 0:1])
-
-    @pl.when(g == 0)
-    def _():
-        lo[...] = potential
-
-    @pl.when(g == 1)
-    def _():
-        hi[...] = potential
-
-
-def ratio_kernel(
-    where,
-    weight,
-    kz,
-    left,
-    right,
-    y,
-    stats,
-    bary,
-    cot,
-    sum0,
-    sum1,
-    sum2,
-    sum3,
-    kyh,
-    kyl,
-    kxh,
-    kxl,
-    lo,
-    hi,
-    stats_out,
-    total,
-    z,
-    mid,
-    scale,
-    *,
-    ny,
-):
-    g = pl.program_id(0)
-
-    @pl.when(g == 0)
-    def _():
-        log_halos(where, kz, left, right, y, stats, z, scale, ny)
-        stats_out[...] = scale[...]
-        total[...] = jnp.zeros(total.shape, F32)
-
+    log_halos(where, kz, left, right, y, stats, z, scale, ny)
+    half = mid.shape[0]
+    for g, out in enumerate((lo, hi)):
+        first = rows_and_columns(z, g, kyh, kyl, kxh, kxl, mid)
+        out[...] = density[g * half : (g + 1) * half, :] - (jnp.log(first) + scale[0:1, 0:1])
+
+
+def second_kernel(where, kz, left, right, y, stats, kyh, kyl, kxh, kxl, out, scale, z, mid, *, ny):
+    log_halos(where, kz, left, right, y, stats, z, scale, ny)
+    half = mid.shape[0]
+    for g in range(2):
+        out[g * half : (g + 1) * half, :] = rows_and_columns(z, g, kyh, kyl, kxh, kxl, mid)
+
+
+def ratio_kernel(at, weight, second, scale, bary, cot, sum0, sum1, sum2, sum3, lo, hi, total):
     c = scale[0:1, 0:1]
-    second = rows_and_columns(z, g, kyh, kyl, kxh, kxl, mid)
     block = sum0.shape[0]
-    per_step = mid.shape[0] // block
-    count = 2 * per_step
-    f = jnp.exp((jnp.where(g == 0, scale[1:2, 0:1], scale[2:3, 0:1]) - c) * 0.5)
-    for k in range(per_step):
-        rows = slice(k * block, (k + 1) * block)
-        away = lax.rem(g * per_step + k - where[2] + count, count)
+    count = second.shape[0] // block
+    partial = jnp.zeros(total.shape, F32)
+    for g in range(count):
+        rows = slice(g * block, (g + 1) * block)
+        away = lax.rem(g - at[0] + count, count)
         over_atoms = jnp.where(
             away == 0,
             sum0[...],
@@ -231,16 +190,13 @@
         share = summed * (jnp.log(second[rows, :]) + c)
         share = jnp.sum(share.reshape(block // 8, 8, share.shape[1]), axis=0)
         for m in range(share.shape[1] // 128):
-            total[...] += share[:, m * 128 : (m + 1) * 128]
+            partial += share[:, m * 128 : (m + 1) * 128]
+        low = 2 * g < count
+        f = jnp.exp(((scale[1:2, 0:1] if low else scale[2:3, 0:1]) - c) * 0.5)
         ratio = (weight[0] * summed - cot[rows, :]) / second[rows, :] * f * f
-
-        @pl.when(g == 0)
-        def _():
-            lo[rows, :] = ratio
-
-        @pl.when(g == 1)
-        def _():
-            hi[rows, :] = ratio
+        out, first = (lo, 0) if low else (hi, count // 2)
+        out[(g - first) * block : (g - first + 1) * block, :] = ratio
+    total[...] = partial
 
 
 def gradient_kernel(
@@ -266,9 +222,12 @@
             lambda v: jnp.where(has_right, v * f_right * f_right, 0.0),
         )
 
-    blurred = rows_and_columns(z, g, kyh, kyl, kxh, kxl, mid)
-    potential = jnp.where(g == 0, pot_lo[...], pot_hi[...])
-    out[...] = jnp.exp(potential - c) * blurred
+    for step, pot in enumerate((pot_lo, pot_hi)):
+
+        @pl.when(g == step)
+        def _(step=step, pot=pot):
+            blurred = rows_and_columns(z, step, kyh, kyl, kxh, kxl, mid)
+            out[...] = jnp.exp(pot[...] - c) * blurred
 
 
 def body(
@@ -291,13 +250,11 @@
     x_at = atom_at // 2
 
     smem = pl.BlockSpec(memory_space=pltpu.SMEM)
+    vmem = pl.BlockSpec(memory_space=pltpu.VMEM)
     params = pltpu.CompilerParams(vmem_limit_bytes=VMEM_LIMIT)
 
     def shape(*dims, dtype=F32):
         return jax.ShapeDtypeStruct(dims, dtype)
-
-    def full(*dims):
-        return pl.BlockSpec(dims, lambda g: (0,) * len(dims))
 
     def send(value, axis, pairs):
         return lax.ppermute(value, axis, pairs)
@@ -320,7 +277,6 @@
     part = block_of(0)
     for k in range(1, across):
         part = part + send(blocks[k - 1], "atom", ahead[k])
-    swapped = send(part, "atom", swap)
 
     y_shape, x_shape = (block, block), (nx, nx)
     distance = jnp.arange(BAND_MAX + 1, dtype=jnp.int32)
@@ -330,6 +286,7 @@
         functools.partial(tables_kernel, ny=ny),
         out_shape=[shape(*dims, dtype=BF16) for dims in (y_shape, y_shape, x_shape, x_shape)],
         in_specs=[smem],
+        out_specs=[vmem] * 4,
         compiler_params=params,
         name="tables",
     )(band)
@@ -343,28 +300,26 @@
     onehot = (slot[0] == jnp.arange(weights.shape[0], dtype=jnp.int32)).astype(F32)
     weight = jnp.sum(onehot * weights, keepdims=True)
 
-    vmem = pl.BlockSpec(memory_space=pltpu.VMEM)
     own_out = [shape(rows, nx), shape(8, 128)]
     own_log = pl.pallas_call(
         functools.partial(own_log_kernel, ny=ny),
         in_specs=[smem, vmem, vmem],
+        out_specs=[vmem, vmem],
         out_shape=own_out,
         compiler_params=params,
         name="own_log",
     )
-    halo_specs = [full(half, nx), full(half, nx), full(rows, nx), full(8, 128)]
-    table_specs = [full(*y_shape), full(*y_shape), full(*x_shape), full(*x_shape)]
     one = pl.BlockSpec((half, nx), lambda g: (g, 0))
-    whole_half = full(half, nx)
     scratch = [pltpu.VMEM((rows, nx), F32), pltpu.VMEM((half, nx), F32)]
     scale = pltpu.VMEM((8, 128), F32)
 
     y, stats = own_log(kz, prior_lo, prior_hi)
+    y, part = in_order((y, part))
+    swapped = send(part, "atom", swap)
     pot_lo, pot_hi = pl.pallas_call(
         functools.partial(potential_kernel, ny=ny),
-        grid=(2,),
-        in_specs=[smem, smem, *halo_specs, one, *table_specs],
-        out_specs=[whole_half, whole_half],
+        in_specs=[smem, smem] + [vmem] * 9,
+        out_specs=[vmem, vmem],
         out_shape=[shape(half, nx), shape(half, nx)],
         scratch_shapes=[*scratch, scale],
         compiler_params=params,
@@ -376,27 +331,31 @@
     both = part + swapped
     sums = [both] + [send(both, "atom", ahead[across - k]) for k in range(1, across)]
     y, stats = own_log(kz, pot_lo, pot_hi)
-    ratio_lo, ratio_hi, stats, total = pl.pallas_call(
-        functools.partial(ratio_kernel, ny=ny),
-        grid=(2,),
-        in_specs=[smem, smem, smem, *halo_specs, one, one] + [full(block, nx)] * 4 + table_specs,
-        out_specs=[whole_half, whole_half, full(8, 128), full(8, 128)],
-        out_shape=[shape(half, nx), shape(half, nx), shape(8, 128), shape(8, 128)],
-        scratch_shapes=[*scratch, scale],
+    y, sums[1] = in_order((y, sums[1]))
+    second, stats = pl.pallas_call(
+        functools.partial(second_kernel, ny=ny),
+        in_specs=[smem, smem] + [vmem] * 8,
+        out_specs=[vmem, vmem],
+        out_shape=[shape(rows, nx), shape(8, 128)],
+        scratch_shapes=scratch,
+        compiler_params=params,
+        name="second",
+    )(where, kz, from_left, from_right, y, stats, *tables)
+    ratio_lo, ratio_hi, total = pl.pallas_call(
+        ratio_kernel,
+        in_specs=[smem, smem] + [vmem] * 8,
+        out_specs=[vmem] * 3,
+        out_shape=[shape(half, nx), shape(half, nx), shape(8, 128)],
         compiler_params=params,
         name="ratio",
     )(
-        where,
+        where[2:],
         weight,
-        kz,
-        from_left,
-        from_right,
-        y,
+        second,
         stats,
         barycenter_cotangent.reshape(rows, nx),
         cot,
         *sums,
-        *tables,
     )
 
     from_left = send(ratio_hi, "slab", to_right)
@@ -404,22 +363,35 @@
     (y,) = pl.pallas_call(
         functools.partial(own_linear_kernel, ny=ny),
         in_specs=[smem, vmem, vmem, vmem],
+        out_specs=[vmem],
         out_shape=[shape(rows, nx)],
         compiler_params=params,
         name="own_linear",
     )(kz, ratio_lo, ratio_hi, stats)
 
-    total, y = in_order((total, y))
-    value = jnp.broadcast_to(jnp.sum(total), (atoms * slabs, 128))
-    value = lax.all_to_all(value, ("atom", "slab"), 0, 0, tiled=True)
-    by_slot = jnp.sum(value[:, 0].reshape(atoms, slabs), axis=1)
-    spread = slot_atom_index[:, None] == jnp.arange(atoms, dtype=jnp.int32)[None, :]
-    weight_grad = jnp.sum(jnp.where(spread, by_slot[:, None], 0.0), axis=0) / (rows * nx * slabs)
+    def add(value, axis, patterns):
+        return sum([send(value, axis, pairs) for pairs in patterns], value)
+
+    def flips(hop):
+        return [(i, i ^ hop) for i in range(slabs)]
+
+    value = jnp.broadcast_to(jnp.sum(total), (8, 128))
+    lanes = jnp.arange(128, dtype=jnp.int32)[None, :]
+    value = jnp.where(lanes == slot[0], value, 0.0)
+    value = add(value, "slab", [flips(1)])
+    value = add(value, "atom", [ahead[k] for k in range(1, across)])
+    value, y = in_order((value, y))
+    value = add(value, "slab", [[(i, (i + k) % slabs) for i in range(slabs)] for k in (8, 16, 24)])
+    for hop in (2, 4):
+        value = add(value, "slab", [flips(hop)])
+    value, from_left, from_right = in_order((value, from_left, from_right))
+    value = add(value, "atom", [swap])
+    weight_grad = value[0, : weights.shape[0]] / (rows * nx * slabs)
 
     gradient = pl.pallas_call(
         functools.partial(gradient_kernel, ny=ny),
         grid=(2,),
-        in_specs=[smem, smem, *halo_specs, whole_half, whole_half, *table_specs],
+        in_specs=[smem, smem] + [vmem] * 10,
         out_specs=one,
         out_shape=shape(rows, nx),
         scratch_shapes=scratch,

time: 154 us -> 155 us (level)
  the two profiles are of different devices: /device:TPU:1 before, /device:TPU:10 now
where the time goes in v4:
time: 155 us; the launch traced here: 152 us
  starting transfers between devices  64.1 us (41%)
  Pallas kernels  38.4 us (25%)
  waiting for transfers between devices  33.3 us (21%)
  local copies, waits for them, and re-layouts  8.59 us (6%)
  other arithmetic  6.89 us (4%)
    ppermute x23, starting transfers between devices, send(): return lax.ppermute(value, axis, pairs)  64.1 us
    ppermute x23, waiting for transfers between devices, send(): return lax.ppermute(value, axis, pairs)  33.3 us
    pallas_call x1, Pallas kernels, body(): pl.pallas_call(functools.partial(gradient_kernel, ny=ny), grid=(2,), in_s...  7.13 us
    pallas_call x1, Pallas kernels, body(): pl.pallas_call(functools.partial(potential_kernel, ny=ny), in_specs=[smem...  7.07 us
    pallas_call x1, Pallas kernels, body(): pl.pallas_call(functools.partial(second_kernel, ny=ny), in_specs=[smem, s...  6.19 us
    pallas_call x1, Pallas kernels, body(): pl.pallas_call(ratio_kernel, in_specs=[smem, smem] + [vmem] * 8, out_spec...  5.48 us
    pallas_call x1, Pallas kernels, body(): y, stats = own_log(kz, prior_lo, prior_hi)  3.92 us
    pallas_call x1, Pallas kernels, body(): y, stats = own_log(kz, pot_lo, pot_hi)  3.91 us
  transfers between devices with their start and end apart: 23, of which 10 were waited for; matrix products, arithmetic and copies ran while one was open for 6% of the time, Pallas kernels for 22%

profile of v4, /device:TPU:10, one launch (start us, length us, event | category | flops | bytes accessed | tf_op | source)
XLA Modules:
  0.0 152.2 jit_solution(16822556811540865386)
XLA Ops:
  0.6 3.2 %fusion.1 = (f32[1,8,64,512]{3,2,1,0:T(8,128)}, f32[1,8,64,512]{3,2,1,0:T(8,128)}) fusion(f32[1,16,64,512]{3,2,1,0:T(8,128)} %param.8), kind=kLoop, calls=%fused_computation.14 | loop fusion | bytes 4194304 | tf_op jit(solution)/shard_map/slice | solution.py:294
  3.9 2.0 %collective-permute-start = (f32[512,512]{1,0:T(8,128)}, f32[512,512]{1,0:T(8,128)}, u32[]{:S(2)}, u32[]{:S(2)}) collective-permute-start(f32[512,512]{1,0:T(8,128)} %bitcast.6.hi), channel_id=1, source_target_pairs={{0,1},{1,2},{2,3},{3,4},{4,5},{5,6},{6,7},{7,8},{8,9},{9,10},{10,1... | collective-permute-start | bytes 3145736 | tf_op jit(solution)/shard_map/ppermute | solution.py:260
  5.9 6.3 %collective-permute-start.1 = (f32[512,512]{1,0:T(8,128)}, f32[512,512]{1,0:T(8,128)}, u32[]{:S(2)}, u32[]{:S(2)}) collective-permute-start(f32[512,512]{1,0:T(8,128)} %bitcast.7.lo), channel_id=1, source_target_pairs={{1,0},{2,1},{3,2},{4,3},{5,4},{6,5},{7,6},{8,7},{9,8},{10,9},{11,1... | collective-permute-start | bytes 3145736 | tf_op jit(solution)/shard_map/ppermute | solution.py:260
  12.3 1.2 constant_dynamic-slice_fusion.2
  13.5 1.5 collective-permute-start.2
  15.0 1.1 collective-permute-start.3
  16.1 2.2 %collective-permute-start.4 = (f32[256,512]{1,0:T(8,128)}, f32[256,512]{1,0:T(8,128)}, u32[]{:S(2)}, u32[]{:S(2)}) collective-permute-start(f32[256,512]{1,0:T(8,128)} %get-tuple-element.51), channel_id=1, source_target_pairs={{0,192},{32,224},{64,0},{96,32},{128,64},{160,96},{192,128},{224,1... | collective-permute-start | bytes 1572872 | tf_op jit(solution)/shard_map/ppermute | solution.py:260
  18.3 0.6 slice.20
  18.9 1.1 tables.1
  20.0 0.7 compare_select_fusion.2.kz
  20.6 3.9 %own_log.2 = (f32[1024,512]{1,0:T(8,128)S(1)}, f32[8,128]{1,0:T(8,128)S(1)}) custom-call(f32[9]{0:T(128)S(1)} %compare_select_fusion.2.kz, f32[512,512]{1,0:T(8,128)} %bitcast.7.lo, f32[512,512]{1,0:T(8,128)} %bitcast.6.hi), custom_call_target="tpu_custom_call" | custom-call | tf_op jit(solution)/shard_map/own_log/pallas_call | solution.py:316
  24.6 0.0 copy-start.2
  24.6 1.3 copy-done.2
  25.9 0.1 pad_add_fusion.where
  26.0 2.8 %collective-permute-done.2 = f32[256,512]{1,0:T(8,128)} collective-permute-done((f32[256,512]{1,0:T(8,128)}, f32[256,512]{1,0:T(8,128)}, u32[]{:S(2)}, u32[]{:S(2)}) %collective-permute-start.2) | collective-permute-done | bytes 524320 | tf_op jit(solution)/shard_map/ppermute | solution.py:260
  28.7 3.0 %collective-permute-done.3 = f32[256,512]{1,0:T(8,128)} collective-permute-done((f32[256,512]{1,0:T(8,128)}, f32[256,512]{1,0:T(8,128)}, u32[]{:S(2)}, u32[]{:S(2)}) %collective-permute-start.3) | collective-permute-done | bytes 524320 | tf_op jit(solution)/shard_map/ppermute | solution.py:260
  31.7 6.9 %collective-permute-done.4 = f32[256,512]{1,0:T(8,128)} collective-permute-done((f32[256,512]{1,0:T(8,128)}, f32[256,512]{1,0:T(8,128)}, u32[]{:S(2)}, u32[]{:S(2)}) %collective-permute-start.4) | collective-permute-done | bytes 524320 | tf_op jit(solution)/shard_map/ppermute | solution.py:260
  38.6 1.6 %add_add_fusion = f32[256,512]{1,0:T(8,128)S(1)} fusion(f32[256,512]{1,0:T(8,128)} %collective-permute-done.4, f32[256,512]{1,0:T(8,128)} %collective-permute-done.3, f32[256,512]{1,0:T(8,128)} %collective-permute-done.2, f32[1024,512]{1,0:T(8,128)S(1)} %bitcast.15, s32[]{:T(128)S(6)} %select_n.32), kind=kLoop, calls=%fused_computation | loop fusion | flops 393216 | bytes 2621444 | tf_op jit(solution)/shard_map/add | solution.py:279
  40.1 6.4 %collective-permute-start.7 = (f32[256,512]{1,0:T(8,128)S(1)}, f32[256,512]{1,0:T(8,128)S(1)}, u32[]{:S(2)}, u32[]{:S(2)}) collective-permute-start(f32[256,512]{1,0:T(8,128)S(1)} %add_add_fusion), channel_id=1, source_target_pairs={{0,32},{32,0},{64,96},{96,64},{128,160},{160,128},{192,224},{224,1... | collective-permute-start | bytes 1572872 | tf_op jit(solution)/shard_map/ppermute | solution.py:260
  46.5 0.0 copy-start.3
  46.5 1.6 %copy-done.3 = f32[1024,512]{1,0:T(8,128)S(1)} copy-done((f32[1024,512]{1,0:T(8,128)S(1)}, f32[1024,512]{1,0:T(8,128)}, u32[]{:S(2)}) %copy-start.3) | copy-done | bytes 2097176
  48.1 7.1 %potential.1 = (f32[512,512]{1,0:T(8,128)}, f32[512,512]{1,0:T(8,128)}) custom-call(s32[4]{0:T(128)S(1)} %pad_add_fusion.where, f32[9]{0:T(128)S(1)} %compare_select_fusion.2.kz, f32[512,512]{1,0:T(8,128)} %collective-permute-done.left, f32[512,512]{1,0:T(8,128)} %collective-permute-done.1.right, f32[1024,512]{1,0:T(8,128)S(1)} %copy-done.3, ...), custom_call_target="tpu_custom_call" | custom-call | tf_op jit(solution)/shard_map/potential/pallas_call | solution.py:319
  55.2 1.9 %collective-permute-start.5 = (f32[512,512]{1,0:T(8,128)}, f32[512,512]{1,0:T(8,128)}, u32[]{:S(2)}, u32[]{:S(2)}) collective-permute-start(f32[512,512]{1,0:T(8,128)} %get-tuple-element.33.hi.pot_hi), channel_id=1, source_target_pairs={{0,1},{1,2},{2,3},{3,4},{4,5},{5,6},{6,7},{7,8},{8,9},{9,10},{10,1... | collective-permute-start | bytes 3145736 | tf_op jit(solution)/shard_map/ppermute | solution.py:260
  57.1 6.3 %collective-permute-start.6 = (f32[512,512]{1,0:T(8,128)}, f32[512,512]{1,0:T(8,128)}, u32[]{:S(2)}, u32[]{:S(2)}) collective-permute-start(f32[512,512]{1,0:T(8,128)} %get-tuple-element.34.lo.pot_lo), channel_id=1, source_target_pairs={{1,0},{2,1},{3,2},{4,3},{5,4},{6,5},{7,6},{8,7},{9,8},{10,9},{11,1... | collective-permute-start | bytes 3145736 | tf_op jit(solution)/shard_map/ppermute | solution.py:260
  63.5 5.3 %collective-permute-done.7 = f32[256,512]{1,0:T(8,128)S(1)} collective-permute-done((f32[256,512]{1,0:T(8,128)S(1)}, f32[256,512]{1,0:T(8,128)S(1)}, u32[]{:S(2)}, u32[]{:S(2)}) %collective-permute-start.7) | collective-permute-done | bytes 524320 | tf_op jit(solution)/shard_map/ppermute | solution.py:260
  68.8 0.9 add.78.sum0
  69.7 2.0 %collective-permute-start.10 = (f32[256,512]{1,0:T(8,128)}, f32[256,512]{1,0:T(8,128)}, u32[]{:S(2)}, u32[]{:S(2)}) collective-permute-start(f32[256,512]{1,0:T(8,128)} %add.78.sum0), channel_id=1, source_target_pairs={{0,64},{32,96},{64,128},{96,160},{128,192},{160,224},{192,0},{224,... | collective-permute-start | bytes 1572872 | tf_op jit(solution)/shard_map/ppermute | solution.py:260
  71.7 4.2 %collective-permute-start.9 = (f32[256,512]{1,0:T(8,128)}, f32[256,512]{1,0:T(8,128)}, u32[]{:S(2)}, u32[]{:S(2)}) collective-permute-start(f32[256,512]{1,0:T(8,128)} %add.78.sum0), channel_id=1, source_target_pairs={{0,128},{32,160},{64,192},{96,224},{128,0},{160,32},{192,64},{224,... | collective-permute-start | bytes 1572872 | tf_op jit(solution)/shard_map/ppermute | solution.py:260
  75.9 0.6 dynamic_slice.15
  76.6 0.1 pad_add_fusion.1.at
  76.6 1.2 fusion
  77.9 3.9 %own_log.3 = (f32[1024,512]{1,0:T(8,128)S(1)}, f32[8,128]{1,0:T(8,128)S(1)}) custom-call(f32[9]{0:T(128)S(1)} %compare_select_fusion.2.kz, f32[512,512]{1,0:T(8,128)} %get-tuple-element.34.lo.pot_lo, f32[512,512]{1,0:T(8,128)} %get-tuple-element.33.hi.pot_hi), custom_call_target="tpu_custom_call" | custom-call | tf_op jit(solution)/shard_map/own_log/pallas_call | solution.py:333
  81.8 9.8 %collective-permute-done.5.left = f32[512,512]{1,0:T(8,128)} collective-permute-done((f32[512,512]{1,0:T(8,128)}, f32[512,512]{1,0:T(8,128)}, u32[]{:S(2)}, u32[]{:S(2)}) %collective-permute-start.5) | collective-permute-done | bytes 1048608 | tf_op jit(solution)/shard_map/ppermute | solution.py:260
  91.5 0.0 collective-permute-done.6.right
  91.5 6.2 %second.1 = (f32[1024,512]{1,0:T(8,128)S(1)}, f32[8,128]{1,0:T(8,128)S(1)}) custom-call(s32[4]{0:T(128)S(1)} %pad_add_fusion.where, f32[9]{0:T(128)S(1)} %compare_select_fusion.2.kz, f32[512,512]{1,0:T(8,128)} %collective-permute-done.5.left, f32[512,512]{1,0:T(8,128)} %collective-permute-done.6.right, f32[1024,512]{1,0:T(8,128)S(1)} %get-tuple-element.37.y, ...), custom_call_target="tpu_custom_call" | custom-call | tf_op jit(solution)/shard_map/second/pallas_call | solution.py:335
  97.7 0.0 collective-permute-done.10.sum3
  97.7 0.0 collective-permute-done.9.sum2
  97.8 5.5 %ratio.1 = (f32[512,512]{1,0:T(8,128)}, f32[512,512]{1,0:T(8,128)}, f32[8,128]{1,0:T(8,128)S(1)}) custom-call(s32[2]{0:T(128)S(1)} %pad_add_fusion.1.at, f32[1]{0:T(128)} %bitcast.5.weight, f32[1024,512]{1,0:T(8,128)S(1)} %get-tuple-element.39.second, f32[8,128]{1,0:T(8,128)S(1)} %get-tuple-element.40.scale.stats, f32[1024,512]{1,0:T(8,128)S(1)} %bitcast.18, ...), custom_call_target="tpu_custom_call" | custom-call | tf_op jit(solution)/shard_map/ratio/pallas_call | solution.py:344
  103.3 2.7 %collective-permute-start.20 = (f32[512,512]{1,0:T(8,128)}, f32[512,512]{1,0:T(8,128)S(1)}, u32[]{:S(2)}, u32[]{:S(2)}) collective-permute-start(f32[512,512]{1,0:T(8,128)} %get-tuple-element.44.hi), channel_id=1, source_target_pairs={{0,1},{1,2},{2,3},{3,4},{4,5},{5,6},{6,7},{7,8},{8,9},{9,10},{10,1... | collective-permute-start | bytes 3145736 | tf_op jit(solution)/shard_map/ppermute | solution.py:260
  105.9 5.6 %collective-permute-start.21 = (f32[512,512]{1,0:T(8,128)}, f32[512,512]{1,0:T(8,128)S(1)}, u32[]{:S(2)}, u32[]{:S(2)}) collective-permute-start(f32[512,512]{1,0:T(8,128)} %get-tuple-element.43.lo), channel_id=1, source_target_pairs={{1,0},{2,1},{3,2},{4,3},{5,4},{6,5},{7,6},{8,7},{9,8},{10,9},{11,1... | collective-permute-start | bytes 3145736 | tf_op jit(solution)/shard_map/ppermute | solution.py:260
  111.5 0.6 reduce_sum.19
  112.1 1.3 compare_select_fusion.1
  113.4 0.1 collective-permute-start.11
  113.5 1.2 collective-permute-done.11
  114.7 1.7 %collective-permute-start.12 = (f32[8,128]{1,0:T(8,128)S(1)}, f32[8,128]{1,0:T(8,128)S(1)}, u32[]{:S(2)}, u32[]{:S(2)}) collective-permute-start(f32[8,128]{1,0:T(8,128)S(1)} %broadcast_add_fusion), channel_id=1, source_target_pairs={{0,64},{32,96},{64,128},{96,160},{128,192},{160,224},{192,0},{224,... | collective-permute-start | bytes 12296 | tf_op jit(solution)/shard_map/ppermute | solution.py:260
  116.3 1.6 %collective-permute-start.13 = (f32[8,128]{1,0:T(8,128)S(1)}, f32[8,128]{1,0:T(8,128)S(1)}, u32[]{:S(2)}, u32[]{:S(2)}) collective-permute-start(f32[8,128]{1,0:T(8,128)S(1)} %broadcast_add_fusion), channel_id=1, source_target_pairs={{0,128},{32,160},{64,192},{96,224},{128,0},{160,32},{192,64},{224,... | collective-permute-start | bytes 12296 | tf_op jit(solution)/shard_map/ppermute | solution.py:260
  117.9 2.3 %collective-permute-start.14 = (f32[8,128]{1,0:T(8,128)S(1)}, f32[8,128]{1,0:T(8,128)S(1)}, u32[]{:S(2)}, u32[]{:S(2)}) collective-permute-start(f32[8,128]{1,0:T(8,128)S(1)} %broadcast_add_fusion), channel_id=1, source_target_pairs={{0,192},{32,224},{64,0},{96,32},{128,64},{160,96},{192,128},{224,1... | collective-permute-start | bytes 12296 | tf_op jit(solution)/shard_map/ppermute | solution.py:260
  120.2 3.6 %own_linear.1.y = f32[1024,512]{1,0:T(8,128)S(1)} custom-call(f32[9]{0:T(128)S(1)} %compare_select_fusion.2.kz, f32[512,512]{1,0:T(8,128)} %get-tuple-element.43.lo, f32[512,512]{1,0:T(8,128)} %get-tuple-element.44.hi, f32[8,128]{1,0:T(8,128)S(1)} %get-tuple-element.40.scale.stats), custom_call_target="tpu_custom_call" | custom-call | tf_op jit(solution)/shard_map/own_linear/pallas_call | solution.py:363
  123.8 0.0 collective-permute-done.12
  123.8 0.0 collective-permute-done.14
  123.8 1.7 %collective-permute-start.15 = (f32[8,128]{1,0:T(8,128)S(1)}, f32[8,128]{1,0:T(8,128)S(1)}, u32[]{:S(2)}, u32[]{:S(2)}) collective-permute-start(f32[8,128]{1,0:T(8,128)S(1)} %add_add_fusion.2), channel_id=1, source_target_pairs={{0,8},{1,9},{2,10},{3,11},{4,12},{5,13},{6,14},{7,15},{8,16},{9,17... | collective-permute-start | bytes 12296 | tf_op jit(solution)/shard_map/ppermute | solution.py:260
  125.5 1.3 collective-permute-start.16
  126.8 2.5 %collective-permute-start.17 = (f32[8,128]{1,0:T(8,128)S(1)}, f32[8,128]{1,0:T(8,128)S(1)}, u32[]{:S(2)}, u32[]{:S(2)}) collective-permute-start(f32[8,128]{1,0:T(8,128)S(1)} %add_add_fusion.2), channel_id=1, source_target_pairs={{0,24},{1,25},{2,26},{3,27},{4,28},{5,29},{6,30},{7,31},{8,0},{9,1... | collective-permute-start | bytes 12296 | tf_op jit(solution)/shard_map/ppermute | solution.py:260
  129.4 0.0 collective-permute-done.15
  129.4 1.2 collective-permute-done.16
  130.6 0.1 collective-permute-done.17
  130.7 3.2 %collective-permute-start.18 = (f32[8,128]{1,0:T(8,128)S(1)}, f32[8,128]{1,0:T(8,128)S(1)}, u32[]{:S(2)}, u32[]{:S(2)}) collective-permute-start(f32[8,128]{1,0:T(8,128)S(1)} %add_add_fusion.1), channel_id=1, source_target_pairs={{0,2},{1,3},{2,0},{3,1},{4,6},{5,7},{6,4},{7,5},{8,10},{9,11},{10,... | collective-permute-start | bytes 12296 | tf_op jit(solution)/shard_map/ppermute | solution.py:260
  133.9 1.6 %collective-permute-done.18 = f32[8,128]{1,0:T(8,128)S(1)} collective-permute-done((f32[8,128]{1,0:T(8,128)S(1)}, f32[8,128]{1,0:T(8,128)S(1)}, u32[]{:S(2)}, u32[]{:S(2)}) %collective-permute-start.18) | collective-permute-done | bytes 4128 | tf_op jit(solution)/shard_map/ppermute | solution.py:260
  135.4 3.4 %collective-permute-start.19 = (f32[8,128]{1,0:T(8,128)S(1)}, f32[8,128]{1,0:T(8,128)S(1)}, u32[]{:S(2)}, u32[]{:S(2)}) collective-permute-start(f32[8,128]{1,0:T(8,128)S(1)} %add.86), channel_id=1, source_target_pairs={{0,4},{1,5},{2,6},{3,7},{4,0},{5,1},{6,2},{7,3},{8,12},{9,13},{10,... | collective-permute-start | bytes 12296 | tf_op jit(solution)/shard_map/ppermute | solution.py:260
  138.9 1.6 %collective-permute-done.19 = f32[8,128]{1,0:T(8,128)S(1)} collective-permute-done((f32[8,128]{1,0:T(8,128)S(1)}, f32[8,128]{1,0:T(8,128)S(1)}, u32[]{:S(2)}, u32[]{:S(2)}) %collective-permute-start.19) | collective-permute-done | bytes 4128 | tf_op jit(solution)/shard_map/ppermute | solution.py:260
  140.4 0.0 collective-permute-done.20.left
  140.5 4.1 %collective-permute-start.22 = (f32[8,128]{1,0:T(8,128)S(1)}, f32[8,128]{1,0:T(8,128)S(1)}, u32[]{:S(2)}, u32[]{:S(2)}) collective-permute-start(f32[8,128]{1,0:T(8,128)S(1)} %add.87), channel_id=1, source_target_pairs={{0,32},{32,0},{64,96},{96,64},{128,160},{160,128},{192,224},{224,1... | collective-permute-start | bytes 12296 | tf_op jit(solution)/shard_map/ppermute | solution.py:260
  144.5 7.1 %gradient.1 = f32[1024,512]{1,0:T(8,128)} custom-call(s32[4]{0:T(128)S(1)} %pad_add_fusion.where, f32[9]{0:T(128)S(1)} %compare_select_fusion.2.kz, f32[512,512]{1,0:T(8,128)S(1)} %collective-permute-done.20.left, f32[512,512]{1,0:T(8,128)S(1)} %collective-permute-done.21.right, f32[1024,512]{1,0:T(8,128)S(1)} %own_linear.1.y, ...), custom_call_target="tpu_custom_call" | custom-call | tf_op jit(solution)/shard_map/gradient/pallas_call | solution.py:391
  151.7 0.5 multiply_bitcast_fusion
  (26 shorter events, 0.1 us)
Async XLA Ops:
  0.6 11.7 %copy-start = (f32[1,16,64,512]{3,2,1,0:T(8,128)S(1)}, f32[1,16,64,512]{3,2,1,0:T(8,128)}, u32[]{:S(2)}) copy-start(f32[1,16,64,512]{3,2,1,0:T(8,128)} %param.9) | copy-start | bytes 6291460
  3.9 14.4 %copy-start.5 = (s32[3]{0:T(128)S(1)}, s32[3]{0:T(128)}, u32[]{:S(2)}) copy-start(s32[3]{0:T(128)} %band.1) | copy-start | bytes 40
  3.9 42.6 %collective-permute-start = (f32[512,512]{1,0:T(8,128)}, f32[512,512]{1,0:T(8,128)}, u32[]{:S(2)}, u32[]{:S(2)}) collective-permute-start(f32[512,512]{1,0:T(8,128)} %bitcast.6.hi), channel_id=1, source_target_pairs={{0,1},{1,2},{2,3},{3,4},{4,5},{5,6},{6,7},{7,8},{8,9},{9,10},{10,1... | collective-permute-start | bytes 3145736 | tf_op jit(solution)/shard_map/ppermute | solution.py:260
  5.9 40.6 %collective-permute-start.1 = (f32[512,512]{1,0:T(8,128)}, f32[512,512]{1,0:T(8,128)}, u32[]{:S(2)}, u32[]{:S(2)}) collective-permute-start(f32[512,512]{1,0:T(8,128)} %bitcast.7.lo), channel_id=1, source_target_pairs={{1,0},{2,1},{3,2},{4,3},{5,4},{6,5},{7,6},{8,7},{9,8},{10,9},{11,1... | collective-permute-start | bytes 3145736 | tf_op jit(solution)/shard_map/ppermute | solution.py:260
  13.5 15.2 %collective-permute-start.2 = (f32[256,512]{1,0:T(8,128)}, f32[256,512]{1,0:T(8,128)}, u32[]{:S(2)}, u32[]{:S(2)}) collective-permute-start(f32[256,512]{1,0:T(8,128)} %get-tuple-element.50), channel_id=1, source_target_pairs={{0,64},{32,96},{64,128},{96,160},{128,192},{160,224},{192,0},{224,... | collective-permute-start | bytes 1572872 | tf_op jit(solution)/shard_map/ppermute | solution.py:260
  15.0 16.7 %collective-permute-start.3 = (f32[256,512]{1,0:T(8,128)}, f32[256,512]{1,0:T(8,128)}, u32[]{:S(2)}, u32[]{:S(2)}) collective-permute-start(f32[256,512]{1,0:T(8,128)} %get-tuple-element.52), channel_id=1, source_target_pairs={{0,128},{32,160},{64,192},{96,224},{128,0},{160,32},{192,64},{224,... | collective-permute-start | bytes 1572872 | tf_op jit(solution)/shard_map/ppermute | solution.py:260
  16.1 22.4 %collective-permute-start.4 = (f32[256,512]{1,0:T(8,128)}, f32[256,512]{1,0:T(8,128)}, u32[]{:S(2)}, u32[]{:S(2)}) collective-permute-start(f32[256,512]{1,0:T(8,128)} %get-tuple-element.51), channel_id=1, source_target_pairs={{0,192},{32,224},{64,0},{96,32},{128,64},{160,96},{192,128},{224,1... | collective-permute-start | bytes 1572872 | tf_op jit(solution)/shard_map/ppermute | solution.py:260
  24.6 1.3 copy-start.2
  25.9 20.7 %copy-start.1 = (f32[1,16,64,512]{3,2,1,0:T(8,128)S(1)}, f32[1,16,64,512]{3,2,1,0:T(8,128)}, u32[]{:S(2)}) copy-start(f32[1,16,64,512]{3,2,1,0:T(8,128)} %param.7) | copy-start | bytes 6291460
  40.1 28.6 %collective-permute-start.7 = (f32[256,512]{1,0:T(8,128)S(1)}, f32[256,512]{1,0:T(8,128)S(1)}, u32[]{:S(2)}, u32[]{:S(2)}) collective-permute-start(f32[256,512]{1,0:T(8,128)S(1)} %add_add_fusion), channel_id=1, source_target_pairs={{0,32},{32,0},{64,96},{96,64},{128,160},{160,128},{192,224},{224,1... | collective-permute-start | bytes 1572872 | tf_op jit(solution)/shard_map/ppermute | solution.py:260
  46.5 1.6 %copy-start.3 = (f32[1024,512]{1,0:T(8,128)S(1)}, f32[1024,512]{1,0:T(8,128)}, u32[]{:S(2)}) copy-start(f32[1024,512]{1,0:T(8,128)} %copy-done.2) | copy-start | bytes 6291460
  48.1 27.8 %copy-start.6 = (s32[8]{0:T(128)S(1)}, s32[8]{0:T(128)}, u32[]{:S(2)}) copy-start(s32[8]{0:T(128)} %param.13) | copy-start | bytes 100
  48.1 28.5 %copy-start.7 = (f32[8]{0:T(128)S(1)}, f32[8]{0:T(128)}, u32[]{:S(2)}) copy-start(f32[8]{0:T(128)} %param.11) | copy-start | bytes 100
  55.2 36.3 %collective-permute-start.5 = (f32[512,512]{1,0:T(8,128)}, f32[512,512]{1,0:T(8,128)}, u32[]{:S(2)}, u32[]{:S(2)}) collective-permute-start(f32[512,512]{1,0:T(8,128)} %get-tuple-element.33.hi.pot_hi), channel_id=1, source_target_pairs={{0,1},{1,2},{2,3},{3,4},{4,5},{5,6},{6,7},{7,8},{8,9},{9,10},{10,1... | collective-permute-start | bytes 3145736 | tf_op jit(solution)/shard_map/ppermute | solution.py:260
  57.1 34.4 %collective-permute-start.6 = (f32[512,512]{1,0:T(8,128)}, f32[512,512]{1,0:T(8,128)}, u32[]{:S(2)}, u32[]{:S(2)}) collective-permute-start(f32[512,512]{1,0:T(8,128)} %get-tuple-element.34.lo.pot_lo), channel_id=1, source_target_pairs={{1,0},{2,1},{3,2},{4,3},{5,4},{6,5},{7,6},{8,7},{9,8},{10,9},{11,1... | collective-permute-start | bytes 3145736 | tf_op jit(solution)/shard_map/ppermute | solution.py:260
  69.7 12.1 %collective-permute-start.8 = (f32[256,512]{1,0:T(8,128)}, f32[256,512]{1,0:T(8,128)}, u32[]{:S(2)}, u32[]{:S(2)}) collective-permute-start(f32[256,512]{1,0:T(8,128)} %add.78.sum0), channel_id=1, source_target_pairs={{0,192},{32,224},{64,0},{96,32},{128,64},{160,96},{192,128},{224,1... | collective-permute-start | bytes 1572872 | tf_op jit(solution)/shard_map/ppermute | solution.py:260
  69.7 28.1 %collective-permute-start.10 = (f32[256,512]{1,0:T(8,128)}, f32[256,512]{1,0:T(8,128)}, u32[]{:S(2)}, u32[]{:S(2)}) collective-permute-start(f32[256,512]{1,0:T(8,128)} %add.78.sum0), channel_id=1, source_target_pairs={{0,64},{32,96},{64,128},{96,160},{128,192},{160,224},{192,0},{224,... | collective-permute-start | bytes 1572872 | tf_op jit(solution)/shard_map/ppermute | solution.py:260
  71.7 26.1 %collective-permute-start.9 = (f32[256,512]{1,0:T(8,128)}, f32[256,512]{1,0:T(8,128)}, u32[]{:S(2)}, u32[]{:S(2)}) collective-permute-start(f32[256,512]{1,0:T(8,128)} %add.78.sum0), channel_id=1, source_target_pairs={{0,128},{32,160},{64,192},{96,224},{128,0},{160,32},{192,64},{224,... | collective-permute-start | bytes 1572872 | tf_op jit(solution)/shard_map/ppermute | solution.py:260
  91.5 6.2 %copy-start.4 = (f32[16,64,512]{2,1,0:T(8,128)S(1)}, f32[16,64,512]{2,1,0:T(8,128)}, u32[]{:S(2)}) copy-start(f32[16,64,512]{2,1,0:T(8,128)} %param.10) | copy-start | bytes 6291460
  103.3 37.2 %collective-permute-start.20 = (f32[512,512]{1,0:T(8,128)}, f32[512,512]{1,0:T(8,128)S(1)}, u32[]{:S(2)}, u32[]{:S(2)}) collective-permute-start(f32[512,512]{1,0:T(8,128)} %get-tuple-element.44.hi), channel_id=1, source_target_pairs={{0,1},{1,2},{2,3},{3,4},{4,5},{5,6},{6,7},{7,8},{8,9},{9,10},{10,1... | collective-permute-start | bytes 3145736 | tf_op jit(solution)/shard_map/ppermute | solution.py:260
  105.9 34.5 %collective-permute-start.21 = (f32[512,512]{1,0:T(8,128)}, f32[512,512]{1,0:T(8,128)S(1)}, u32[]{:S(2)}, u32[]{:S(2)}) collective-permute-start(f32[512,512]{1,0:T(8,128)} %get-tuple-element.43.lo), channel_id=1, source_target_pairs={{1,0},{2,1},{3,2},{4,3},{5,4},{6,5},{7,6},{8,7},{9,8},{10,9},{11,1... | collective-permute-start | bytes 3145736 | tf_op jit(solution)/shard_map/ppermute | solution.py:260
  113.4 1.3 collective-permute-start.11
  114.7 9.1 %collective-permute-start.12 = (f32[8,128]{1,0:T(8,128)S(1)}, f32[8,128]{1,0:T(8,128)S(1)}, u32[]{:S(2)}, u32[]{:S(2)}) collective-permute-start(f32[8,128]{1,0:T(8,128)S(1)} %broadcast_add_fusion), channel_id=1, source_target_pairs={{0,64},{32,96},{64,128},{96,160},{128,192},{160,224},{192,0},{224,... | collective-permute-start | bytes 12296 | tf_op jit(solution)/shard_map/ppermute | solution.py:260
  116.3 7.5 %collective-permute-start.13 = (f32[8,128]{1,0:T(8,128)S(1)}, f32[8,128]{1,0:T(8,128)S(1)}, u32[]{:S(2)}, u32[]{:S(2)}) collective-permute-start(f32[8,128]{1,0:T(8,128)S(1)} %broadcast_add_fusion), channel_id=1, source_target_pairs={{0,128},{32,160},{64,192},{96,224},{128,0},{160,32},{192,64},{224,... | collective-permute-start | bytes 12296 | tf_op jit(solution)/shard_map/ppermute | solution.py:260
  117.9 6.0 %collective-permute-start.14 = (f32[8,128]{1,0:T(8,128)S(1)}, f32[8,128]{1,0:T(8,128)S(1)}, u32[]{:S(2)}, u32[]{:S(2)}) collective-permute-start(f32[8,128]{1,0:T(8,128)S(1)} %broadcast_add_fusion), channel_id=1, source_target_pairs={{0,192},{32,224},{64,0},{96,32},{128,64},{160,96},{192,128},{224,1... | collective-permute-start | bytes 12296 | tf_op jit(solution)/shard_map/ppermute | solution.py:260
  123.8 5.5 %collective-permute-start.15 = (f32[8,128]{1,0:T(8,128)S(1)}, f32[8,128]{1,0:T(8,128)S(1)}, u32[]{:S(2)}, u32[]{:S(2)}) collective-permute-start(f32[8,128]{1,0:T(8,128)S(1)} %add_add_fusion.2), channel_id=1, source_target_pairs={{0,8},{1,9},{2,10},{3,11},{4,12},{5,13},{6,14},{7,15},{8,16},{9,17... | collective-permute-start | bytes 12296 | tf_op jit(solution)/shard_map/ppermute | solution.py:260
  125.5 5.1 %collective-permute-start.16 = (f32[8,128]{1,0:T(8,128)S(1)}, f32[8,128]{1,0:T(8,128)S(1)}, u32[]{:S(2)}, u32[]{:S(2)}) collective-permute-start(f32[8,128]{1,0:T(8,128)S(1)} %add_add_fusion.2), channel_id=1, source_target_pairs={{0,16},{1,17},{2,18},{3,19},{4,20},{5,21},{6,22},{7,23},{8,24},{9,... | collective-permute-start | bytes 12296 | tf_op jit(solution)/shard_map/ppermute | solution.py:260
  126.8 3.9 %collective-permute-start.17 = (f32[8,128]{1,0:T(8,128)S(1)}, f32[8,128]{1,0:T(8,128)S(1)}, u32[]{:S(2)}, u32[]{:S(2)}) collective-permute-start(f32[8,128]{1,0:T(8,128)S(1)} %add_add_fusion.2), channel_id=1, source_target_pairs={{0,24},{1,25},{2,26},{3,27},{4,28},{5,29},{6,30},{7,31},{8,0},{9,1... | collective-permute-start | bytes 12296 | tf_op jit(solution)/shard_map/ppermute | solution.py:260
  130.7 4.7 %collective-permute-start.18 = (f32[8,128]{1,0:T(8,128)S(1)}, f32[8,128]{1,0:T(8,128)S(1)}, u32[]{:S(2)}, u32[]{:S(2)}) collective-permute-start(f32[8,128]{1,0:T(8,128)S(1)} %add_add_fusion.1), channel_id=1, source_target_pairs={{0,2},{1,3},{2,0},{3,1},{4,6},{5,7},{6,4},{7,5},{8,10},{9,11},{10,... | collective-permute-start | bytes 12296 | tf_op jit(solution)/shard_map/ppermute | solution.py:260
  135.4 5.0 %collective-permute-start.19 = (f32[8,128]{1,0:T(8,128)S(1)}, f32[8,128]{1,0:T(8,128)S(1)}, u32[]{:S(2)}, u32[]{:S(2)}) collective-permute-start(f32[8,128]{1,0:T(8,128)S(1)} %add.86), channel_id=1, source_target_pairs={{0,4},{1,5},{2,6},{3,7},{4,0},{5,1},{6,2},{7,3},{8,12},{9,13},{10,... | collective-permute-start | bytes 12296 | tf_op jit(solution)/shard_map/ppermute | solution.py:260
  140.5 11.2 %collective-permute-start.22 = (f32[8,128]{1,0:T(8,128)S(1)}, f32[8,128]{1,0:T(8,128)S(1)}, u32[]{:S(2)}, u32[]{:S(2)}) collective-permute-start(f32[8,128]{1,0:T(8,128)S(1)} %add.87), channel_id=1, source_target_pairs={{0,32},{32,0},{64,96},{96,64},{128,160},{160,128},{192,224},{224,1... | collective-permute-start | bytes 12296 | tf_op jit(solution)/shard_map/ppermute | solution.py:260

commit v5 on v4

--- a/solution.py
+++ b/solution.py
@@ -82,18 +82,19 @@
 
 
 def halo_planes(left, right, kz, y, z, ny, own, entry_left, entry_right):
-    side = left.shape[0] // ny
+    per = left[0].shape[0] // ny
+    side = per * len(left)
     taps = [kz[d] for d in range(BAND_MAX + 1)]
 
     def step(row, columns):
-        e = [entry_left(left[pl.ds(q * ny + row, 8), columns]) for q in range(side)]
+        e = [entry_left(left[q // per][pl.ds(q % per * ny + row, 8), columns]) for q in range(side)]
         for p in range(side):
             rows = pl.ds(p * ny + row, 8)
             total = own(y[rows, columns])
             for q in range(max(0, p + side - BAND_MAX), side):
                 total += taps[p + side - q] * e[q]
             z[rows, columns] = total
-        e = [entry_right(right[pl.ds(q * ny + row, 8), columns]) for q in range(side)]
+        e = [entry_right(right[q // per][pl.ds(q % per * ny + row, 8), columns]) for q in range(side)]
         for p in range(side):
             rows = pl.ds((side + p) * ny + row, 8)
             total = own(y[rows, columns])
@@ -101,7 +102,7 @@
                 total += taps[side + q - p] * e[q]
             z[rows, columns] = total
 
-    tile_loop(ny, left.shape[1], step)
+    tile_loop(ny, left[0].shape[1], step)
 
 
 def tile(value):
@@ -117,8 +118,11 @@
     own_planes(lo, hi, kz, y, ny, entry, entry)
 
 
-def own_linear_kernel(kz, lo, hi, stats, y, *, ny):
+def own_linear_kernel(kz, lo, hi, pot_lo, pot_hi, stats, y, shifted, *, ny):
     c = stats[0:1, 0:1]
+    half = lo.shape[0]
+    shifted[:half, :] = jnp.exp(pot_lo[...] - c)
+    shifted[half:, :] = jnp.exp(pot_hi[...] - c)
     f_lo = tile(jnp.exp((c - stats[1:2, 0:1]) * 0.5))
     f_hi = tile(jnp.exp((c - stats[2:3, 0:1]) * 0.5))
     own_planes(lo, hi, kz, y, ny, lambda v: v * f_lo * f_lo, lambda v: v * f_hi * f_hi)
@@ -137,8 +141,8 @@
 def log_halos(where, kz, left, right, y, stats, z, scale, ny):
     has_left, has_right = where[0] > 0, where[1] > 0
     m_own = stats[2:3, 0:1]
-    m_left = jnp.where(has_left, peak(left[...]), m_own)
-    m_right = jnp.where(has_right, peak(right[...]), m_own)
+    m_left = jnp.where(has_left, functools.reduce(jnp.maximum, [peak(ref[...]) for ref in left]), m_own)
+    m_right = jnp.where(has_right, functools.reduce(jnp.maximum, [peak(ref[...]) for ref in right]), m_own)
     c = jnp.maximum(m_own, jnp.maximum(m_left, m_right))
     scale[...] = rows_of([c, stats[0:1, 0:1], stats[1:2, 0:1], m_left, m_right, c, c, c])
     own = tile(jnp.exp(m_own - c))
@@ -157,9 +161,9 @@
 
 
 def potential_kernel(
-    where, kz, left, right, y, stats, density, kyh, kyl, kxh, kxl, lo, hi, z, mid, scale, *, ny
+    where, kz, left0, left1, right0, right1, y, stats, density, kyh, kyl, kxh, kxl, lo, hi, z, mid, scale, *, ny
 ):
-    log_halos(where, kz, left, right, y, stats, z, scale, ny)
+    log_halos(where, kz, (left0, left1), (right0, right1), y, stats, z, scale, ny)
     half = mid.shape[0]
     for g, out in enumerate((lo, hi)):
         first = rows_and_columns(z, g, kyh, kyl, kxh, kxl, mid)
@@ -167,40 +171,54 @@
 
 
 def second_kernel(where, kz, left, right, y, stats, kyh, kyl, kxh, kxl, out, scale, z, mid, *, ny):
-    log_halos(where, kz, left, right, y, stats, z, scale, ny)
+    log_halos(where, kz, (left,), (right,), y, stats, z, scale, ny)
     half = mid.shape[0]
     for g in range(2):
         out[g * half : (g + 1) * half, :] = rows_and_columns(z, g, kyh, kyl, kxh, kxl, mid)
 
 
-def ratio_kernel(at, weight, second, scale, bary, cot, sum0, sum1, sum2, sum3, lo, hi, total):
+def ratio_kernel(
+    at, weight, second, scale, bary, cot, sum0, sum1, sum2, sum3, lo, hi, total, sums, out, sems
+):
     c = scale[0:1, 0:1]
-    block = sum0.shape[0]
-    count = second.shape[0] // block
-    partial = jnp.zeros(total.shape, F32)
-    for g in range(count):
-        rows = slice(g * block, (g + 1) * block)
-        away = lax.rem(g - at[0] + count, count)
-        over_atoms = jnp.where(
-            away == 0,
-            sum0[...],
-            jnp.where(away == 1, sum1[...], jnp.where(away == 2, sum2[...], sum3[...])),
-        )
-        summed = bary[rows, :] + over_atoms
-        share = summed * (jnp.log(second[rows, :]) + c)
-        share = jnp.sum(share.reshape(block // 8, 8, share.shape[1]), axis=0)
-        for m in range(share.shape[1] // 128):
+    block, columns = sums.shape[1:]
+    count = sums.shape[0]
+    half = out.shape[0] // 2
+    arriving = [
+        pltpu.make_async_copy(ref, sums.at[k], sems.at[k]) for k, ref in enumerate((sum0, sum1, sum2, sum3))
+    ]
+    for copy in arriving:
+        copy.start()
+    partial = jnp.zeros((8, 128), F32)
+    f_lo = jnp.exp((scale[1:2, 0:1] - c) * 0.5)
+    f_hi = jnp.exp((scale[2:3, 0:1] - c) * 0.5)
+    for k, copy in enumerate(arriving):
+        copy.wait()
+        g = lax.rem(at[0] + k, count)
+        rows = pl.ds(pl.multiple_of(g * block, block), block)
+        summed = bary[rows, :] + sums[k]
+        denominator = second[rows, :]
+        share = summed * (jnp.log(denominator) + c)
+        share = jnp.sum(share.reshape(block // 8, 8, columns), axis=0)
+        for m in range(columns // 128):
             partial += share[:, m * 128 : (m + 1) * 128]
-        low = 2 * g < count
-        f = jnp.exp(((scale[1:2, 0:1] if low else scale[2:3, 0:1]) - c) * 0.5)
-        ratio = (weight[0] * summed - cot[rows, :]) / second[rows, :] * f * f
-        out, first = (lo, 0) if low else (hi, count // 2)
-        out[(g - first) * block : (g - first + 1) * block, :] = ratio
-    total[...] = partial
+        f = jnp.where(2 * g < count, f_lo, f_hi)
+        out[rows, :] = (weight[0] * summed - cot[rows, :]) / denominator * f * f
+    leaving = [
+        pltpu.make_async_copy(out.at[:half], lo, sems.at[0]),
+        pltpu.make_async_copy(out.at[half:], hi, sems.at[1]),
+    ]
+    for copy in leaving:
+        copy.start()
+    lanes = lax.broadcasted_iota(jnp.int32, total.shape, 1)
+    partial = jnp.sum(jnp.sum(partial, axis=0, keepdims=True), axis=1, keepdims=True)
+    total[...] = jnp.where(lanes == at[1], partial, 0.0)
+    for copy in leaving:
+        copy.wait()
 
 
 def gradient_kernel(
-    where, kz, left, right, y, stats, pot_lo, pot_hi, kyh, kyl, kxh, kxl, out, z, mid, *, ny
+    where, kz, left, right, y, shifted, stats, kyh, kyl, kxh, kxl, out, z, mid, *, ny
 ):
     g = pl.program_id(0)
     c = stats[0:1, 0:1]
@@ -211,8 +229,8 @@
         f_right = tile(jnp.exp((c - stats[4:5, 0:1]) * 0.5))
         has_left, has_right = where[0] > 0, where[1] > 0
         halo_planes(
-            left,
-            right,
+            (left,),
+            (right,),
             kz,
             y,
             z,
@@ -222,12 +240,13 @@
             lambda v: jnp.where(has_right, v * f_right * f_right, 0.0),
         )
 
-    for step, pot in enumerate((pot_lo, pot_hi)):
+    for step in range(2):
 
         @pl.when(g == step)
-        def _(step=step, pot=pot):
+        def _(step=step):
             blurred = rows_and_columns(z, step, kyh, kyl, kxh, kxl, mid)
-            out[...] = jnp.exp(pot[...] - c) * blurred
+            half = out.shape[0]
+            out[...] = shifted[step * half : (step + 1) * half, :] * blurred
 
 
 def body(
@@ -251,6 +270,7 @@
 
     smem = pl.BlockSpec(memory_space=pltpu.SMEM)
     vmem = pl.BlockSpec(memory_space=pltpu.VMEM)
+    anywhere = pl.BlockSpec(memory_space=pl.ANY)
     params = pltpu.CompilerParams(vmem_limit_bytes=VMEM_LIMIT)
 
     def shape(*dims, dtype=F32):
@@ -292,10 +312,11 @@
     )(band)
     prior = prior_log_scaling.reshape(rows, nx)
     prior_lo, prior_hi = prior[:half], prior[half:]
-    from_left = send(prior_hi, "slab", to_right)
-    from_right = send(prior_lo, "slab", to_left)
-
-    where = jnp.stack([(slab_at > 0), (slab_at < slabs - 1), x_at, x_at]).astype(jnp.int32)
+    piece = half // 2
+    from_left = [send(prior_hi[k * piece : (k + 1) * piece], "slab", to_right) for k in range(2)]
+    from_right = [send(prior_lo[k * piece : (k + 1) * piece], "slab", to_left) for k in range(2)]
+
+    where = jnp.stack([slab_at > 0, slab_at < slabs - 1]).astype(jnp.int32)
     slot = lax.dynamic_slice_in_dim(slot_atom_index, atom_at, 1)
     onehot = (slot[0] == jnp.arange(weights.shape[0], dtype=jnp.int32)).astype(F32)
     weight = jnp.sum(onehot * weights, keepdims=True)
@@ -318,13 +339,13 @@
     swapped = send(part, "atom", swap)
     pot_lo, pot_hi = pl.pallas_call(
         functools.partial(potential_kernel, ny=ny),
-        in_specs=[smem, smem] + [vmem] * 9,
+        in_specs=[smem, smem] + [vmem] * 11,
         out_specs=[vmem, vmem],
         out_shape=[shape(half, nx), shape(half, nx)],
         scratch_shapes=[*scratch, scale],
         compiler_params=params,
         name="potential",
-    )(where, kz, from_left, from_right, y, stats, atom_log_density.reshape(rows, nx), *tables)
+    )(where, kz, *from_left, *from_right, y, stats, atom_log_density.reshape(rows, nx), *tables)
 
     from_left = send(pot_hi, "slab", to_right)
     from_right = send(pot_lo, "slab", to_left)
@@ -343,13 +364,18 @@
     )(where, kz, from_left, from_right, y, stats, *tables)
     ratio_lo, ratio_hi, total = pl.pallas_call(
         ratio_kernel,
-        in_specs=[smem, smem] + [vmem] * 8,
-        out_specs=[vmem] * 3,
+        in_specs=[smem, smem] + [vmem] * 4 + [anywhere] * 4,
+        out_specs=[anywhere, anywhere, vmem],
         out_shape=[shape(half, nx), shape(half, nx), shape(8, 128)],
+        scratch_shapes=[
+            pltpu.VMEM((count, block, nx), F32),
+            pltpu.VMEM((rows, nx), F32),
+            pltpu.SemaphoreType.DMA((count,)),
+        ],
         compiler_params=params,
         name="ratio",
     )(
-        where[2:],
+        jnp.stack([x_at, slot[0]]),
         weight,
         second,
         stats,
@@ -360,14 +386,14 @@
 
     from_left = send(ratio_hi, "slab", to_right)
     from_right = send(ratio_lo, "slab", to_left)
-    (y,) = pl.pallas_call(
+    y, shifted = pl.pallas_call(
         functools.partial(own_linear_kernel, ny=ny),
-        in_specs=[smem, vmem, vmem, vmem],
-        out_specs=[vmem],
-        out_shape=[shape(rows, nx)],
+        in_specs=[smem] + [vmem] * 5,
+        out_specs=[vmem, vmem],
+        out_shape=[shape(rows, nx), shape(rows, nx)],
         compiler_params=params,
         name="own_linear",
-    )(kz, ratio_lo, ratio_hi, stats)
+    )(kz, ratio_lo, ratio_hi, pot_lo, pot_hi, stats)
 
     def add(value, axis, patterns):
         return sum([send(value, axis, pairs) for pairs in patterns], value)
@@ -375,10 +401,7 @@
     def flips(hop):
         return [(i, i ^ hop) for i in range(slabs)]
 
-    value = jnp.broadcast_to(jnp.sum(total), (8, 128))
-    lanes = jnp.arange(128, dtype=jnp.int32)[None, :]
-    value = jnp.where(lanes == slot[0], value, 0.0)
-    value = add(value, "slab", [flips(1)])
+    value = add(total, "slab", [flips(1)])
     value = add(value, "atom", [ahead[k] for k in range(1, across)])
     value, y = in_order((value, y))
     value = add(value, "slab", [[(i, (i + k) % slabs) for i in range(slabs)] for k in (8, 16, 24)])
@@ -391,13 +414,13 @@
     gradient = pl.pallas_call(
         functools.partial(gradient_kernel, ny=ny),
         grid=(2,),
-        in_specs=[smem, smem] + [vmem] * 10,
+        in_specs=[smem, smem] + [vmem] * 9,
         out_specs=one,
         out_shape=shape(rows, nx),
         scratch_shapes=scratch,
         compiler_params=params,
         name="gradient",
-    )(where, kz, from_left, from_right, y, stats, pot_lo, pot_hi, *tables)
+    )(where, kz, from_left, from_right, y, shifted, stats, *tables)
     return gradient.reshape(atom_log_density.shape), weight_grad
 
 

time: 155 us -> 159 us (1.026)
  starting transfers between devices: 64.1 us -> 69.9 us
  Pallas kernels: 38.4 us -> 35 us
  waiting for transfers between devices: 33.3 us -> 35.4 us
    ppermute x23 -> x25, starting transfers between devices: 64.1 us -> 69.9 us  [send(): return lax.ppermute(value, axis, pairs)]
    ppermute x23 -> x25, waiting for transfers between devices: 33.3 us -> 35.4 us  [send(): return lax.ppermute(value, axis, pairs)]
    slice x1, local copies, waits for them, and re-layouts: 3.24 us -> 1.6 us  [body(): prior_lo, prior_hi = (prior[:half], prior[half:])]
    unnamed x16 -> x22, local copies, waits for them, and re-layouts: 2.92 us -> 3.27 us
  transfers between devices with their start and end apart: 23 -> 25, of which waited for: 10 -> 8; matrix products, arithmetic and copies ran while one was open for 6% -> 6% of each run, Pallas kernels for 22% -> 20%
where the time goes in v5:
time: 159 us; the launch traced here: 157 us
  starting transfers between devices  69.9 us (44%)
  waiting for transfers between devices  35.4 us (22%)
  Pallas kernels  35 us (22%)
  local copies, waits for them, and re-layouts  9.86 us (6%)
  other arithmetic  5.7 us (4%)
    ppermute x25, starting transfers between devices, send(): return lax.ppermute(value, axis, pairs)  69.9 us
    ppermute x25, waiting for transfers between devices, send(): return lax.ppermute(value, axis, pairs)  35.4 us
    pallas_call x1, Pallas kernels, body(): pl.pallas_call(functools.partial(potential_kernel, ny=ny), in_specs=[smem...  6.93 us
    pallas_call x1, Pallas kernels, body(): pl.pallas_call(functools.partial(second_kernel, ny=ny), in_specs=[smem, s...  6.19 us
    pallas_call x1, Pallas kernels, body(): pl.pallas_call(functools.partial(gradient_kernel, ny=ny), grid=(2,), in_s...  6.12 us
    pallas_call x1, Pallas kernels, body(): pl.pallas_call(functools.partial(own_linear_kernel, ny=ny), in_specs=[sme...  3.96 us
    pallas_call x1, Pallas kernels, body(): pl.pallas_call(ratio_kernel, in_specs=[smem, smem] + [vmem] * 4 + [anywhe...  3.94 us
    pallas_call x1, Pallas kernels, body(): y, stats = own_log(kz, pot_lo, pot_hi)  3.91 us
  transfers between devices with their start and end apart: 25, of which 8 were waited for; matrix products, arithmetic and copies ran while one was open for 6% of the time, Pallas kernels for 20%

profile of v5, /device:TPU:10, one launch (start us, length us, event | category | flops | bytes accessed | tf_op | source)
XLA Modules:
  0.0 156.8 jit_solution(9371881905466296343)
XLA Ops:
  0.7 2.4 %constant_dynamic-slice_fusion.2 = (f32[256,512]{1,0:T(8,128)}, f32[256,512]{1,0:T(8,128)S(1)}, f32[256,512]{1,0:T(8,128)S(1)}) fusion(f32[1024,512]{1,0:T(8,128)} %bitcast.18, s32[]{:T(128)S(6)} %select_n.28, s32[]{:T(128)S(6)} %select_n.30, s32[]{:T(128)S(6)} %select_n.29), kind=kLoop, calls=%fused_computation.8 | loop fusion | bytes 3145740 | tf_op jit(solution)/shard_map/dynamic_slice | solution.py:294
  3.1 0.5 collective-permute-start.6
  3.6 2.4 %collective-permute-start.5 = (f32[256,512]{1,0:T(8,128)S(1)}, f32[256,512]{1,0:T(8,128)S(1)}, u32[]{:S(2)}, u32[]{:S(2)}) collective-permute-start(f32[256,512]{1,0:T(8,128)S(1)} %get-tuple-element.56), channel_id=1, source_target_pairs={{0,128},{32,160},{64,192},{96,224},{128,0},{160,32},{192,64},{224,... | collective-permute-start | bytes 1572872 | tf_op jit(solution)/shard_map/ppermute | solution.py:280
  6.1 1.4 fusion.2
  7.5 1.9 %collective-permute-start = (f32[256,512]{1,0:T(8,128)}, f32[256,512]{1,0:T(8,128)}, u32[]{:S(2)}, u32[]{:S(2)}) collective-permute-start(f32[256,512]{1,0:T(8,128)} %bitcast.6), channel_id=1, source_target_pairs={{0,1},{1,2},{2,3},{3,4},{4,5},{5,6},{6,7},{7,8},{8,9},{9,10},{10,1... | collective-permute-start | bytes 1572872 | tf_op jit(solution)/shard_map/ppermute | solution.py:280
  9.4 3.9 %collective-permute-start.1 = (f32[256,512]{1,0:T(8,128)}, f32[256,512]{1,0:T(8,128)}, u32[]{:S(2)}, u32[]{:S(2)}) collective-permute-start(f32[256,512]{1,0:T(8,128)} %bitcast.7), channel_id=1, source_target_pairs={{0,1},{1,2},{2,3},{3,4},{4,5},{5,6},{6,7},{7,8},{8,9},{9,10},{10,1... | collective-permute-start | bytes 1572872 | tf_op jit(solution)/shard_map/ppermute | solution.py:280
  13.3 4.3 %collective-permute-start.2 = (f32[256,512]{1,0:T(8,128)}, f32[256,512]{1,0:T(8,128)}, u32[]{:S(2)}, u32[]{:S(2)}) collective-permute-start(f32[256,512]{1,0:T(8,128)} %bitcast.8), channel_id=1, source_target_pairs={{1,0},{2,1},{3,2},{4,3},{5,4},{6,5},{7,6},{8,7},{9,8},{10,9},{11,1... | collective-permute-start | bytes 1572872 | tf_op jit(solution)/shard_map/ppermute | solution.py:280
  17.7 4.2 %collective-permute-start.3 = (f32[256,512]{1,0:T(8,128)}, f32[256,512]{1,0:T(8,128)}, u32[]{:S(2)}, u32[]{:S(2)}) collective-permute-start(f32[256,512]{1,0:T(8,128)} %bitcast.9), channel_id=1, source_target_pairs={{1,0},{2,1},{3,2},{4,3},{5,4},{6,5},{7,6},{8,7},{9,8},{10,9},{11,1... | collective-permute-start | bytes 1572872 | tf_op jit(solution)/shard_map/ppermute | solution.py:280
  21.9 7.1 %collective-permute-done.5 = f32[256,512]{1,0:T(8,128)S(1)} collective-permute-done((f32[256,512]{1,0:T(8,128)S(1)}, f32[256,512]{1,0:T(8,128)S(1)}, u32[]{:S(2)}, u32[]{:S(2)}) %collective-permute-start.5) | collective-permute-done | bytes 524320 | tf_op jit(solution)/shard_map/ppermute | solution.py:280
  28.9 0.8 copy-done.8
  29.7 1.6 %fusion.1 = (f32[1,8,64,512]{3,2,1,0:T(8,128)}, f32[1,8,64,512]{3,2,1,0:T(8,128)}) fusion(f32[1,16,64,512]{3,2,1,0:T(8,128)S(1)} %copy-done.6), kind=kLoop, calls=%fused_computation.12 | loop fusion | bytes 4194304 | tf_op jit(solution)/shard_map/slice | solution.py:314
  31.3 0.6 slice.46
  31.9 1.1 tables.1
  33.0 0.6 compare_select_fusion.1.kz
  33.6 0.0 copy-start.1
  33.6 1.2 copy-done.1
  34.8 1.2 copy-done.2
  36.1 2.9 %own_log.2 = (f32[1024,512]{1,0:T(8,128)S(1)}, f32[8,128]{1,0:T(8,128)S(1)}) custom-call(f32[9]{0:T(128)S(1)} %compare_select_fusion.1.kz, f32[512,512]{1,0:T(8,128)S(1)} %bitcast.22, f32[512,512]{1,0:T(8,128)S(1)} %bitcast.21), custom_call_target="tpu_custom_call" | custom-call | tf_op jit(solution)/shard_map/own_log/pallas_call | solution.py:337
  39.0 0.1 add_convert_fusion.where
  39.1 4.7 %collective-permute-done.4 = f32[256,512]{1,0:T(8,128)} collective-permute-done((f32[256,512]{1,0:T(8,128)}, f32[256,512]{1,0:T(8,128)}, u32[]{:S(2)}, u32[]{:S(2)}) %collective-permute-start.4) | collective-permute-done | bytes 524320 | tf_op jit(solution)/shard_map/ppermute | solution.py:280
  43.8 1.6 %add_add_fusion = f32[256,512]{1,0:T(8,128)S(1)} fusion(f32[256,512]{1,0:T(8,128)} %copy-done.7, f32[256,512]{1,0:T(8,128)} %copy-done.8, f32[256,512]{1,0:T(8,128)} %collective-permute-done.4, f32[1024,512]{1,0:T(8,128)S(1)} %bitcast.19, s32[]{:T(128)S(6)} %select_n.27), kind=kLoop, calls=%fused_computation | loop fusion | flops 393216 | bytes 2621444 | tf_op jit(solution)/shard_map/add | solution.py:299
  45.4 7.3 %collective-permute-start.9 = (f32[256,512]{1,0:T(8,128)S(1)}, f32[256,512]{1,0:T(8,128)S(1)}, u32[]{:S(2)}, u32[]{:S(2)}) collective-permute-start(f32[256,512]{1,0:T(8,128)S(1)} %add_add_fusion), channel_id=1, source_target_pairs={{0,32},{32,0},{64,96},{96,64},{128,160},{160,128},{192,224},{224,1... | collective-permute-start | bytes 1572872 | tf_op jit(solution)/shard_map/ppermute | solution.py:280
  52.6 0.0 collective-permute-done.left0
  52.6 0.0 collective-permute-done.1.left1
  52.6 0.0 collective-permute-done.2.right0
  52.7 0.0 copy-start.9
  52.7 0.0 copy-start.10
  52.7 6.9 %potential.1 = (f32[512,512]{1,0:T(8,128)}, f32[512,512]{1,0:T(8,128)}) custom-call(s32[2]{0:T(128)S(1)} %add_convert_fusion.where, f32[9]{0:T(128)S(1)} %compare_select_fusion.1.kz, f32[256,512]{1,0:T(8,128)} %collective-permute-done.left0, f32[256,512]{1,0:T(8,128)} %collective-permute-done.1.left1, f32[256,512]{1,0:T(8,128)} %collective-permute-done.2.right0, ...), custom_call_target="tpu_custom_call" | custom-call | tf_op jit(solution)/shard_map/potential/pallas_call | solution.py:340
  59.6 1.9 %collective-permute-start.7 = (f32[512,512]{1,0:T(8,128)}, f32[512,512]{1,0:T(8,128)}, u32[]{:S(2)}, u32[]{:S(2)}) collective-permute-start(f32[512,512]{1,0:T(8,128)} %get-tuple-element.35.hi.pot_hi), channel_id=1, source_target_pairs={{0,1},{1,2},{2,3},{3,4},{4,5},{5,6},{6,7},{7,8},{8,9},{9,10},{10,1... | collective-permute-start | bytes 3145736 | tf_op jit(solution)/shard_map/ppermute | solution.py:280
  61.5 6.3 %collective-permute-start.8 = (f32[512,512]{1,0:T(8,128)}, f32[512,512]{1,0:T(8,128)}, u32[]{:S(2)}, u32[]{:S(2)}) collective-permute-start(f32[512,512]{1,0:T(8,128)} %get-tuple-element.36.lo.pot_lo), channel_id=1, source_target_pairs={{1,0},{2,1},{3,2},{4,3},{5,4},{6,5},{7,6},{8,7},{9,8},{10,9},{11,1... | collective-permute-start | bytes 3145736 | tf_op jit(solution)/shard_map/ppermute | solution.py:280
  67.9 7.0 %collective-permute-done.9 = f32[256,512]{1,0:T(8,128)S(1)} collective-permute-done((f32[256,512]{1,0:T(8,128)S(1)}, f32[256,512]{1,0:T(8,128)S(1)}, u32[]{:S(2)}, u32[]{:S(2)}) %collective-permute-start.9) | collective-permute-done | bytes 524320 | tf_op jit(solution)/shard_map/ppermute | solution.py:280
  74.8 0.9 add.78.sum0
  75.7 4.5 %collective-permute-start.10 = (f32[256,512]{1,0:T(8,128)}, f32[256,512]{1,0:T(8,128)}, u32[]{:S(2)}, u32[]{:S(2)}) collective-permute-start(f32[256,512]{1,0:T(8,128)} %add.78.sum0), channel_id=1, source_target_pairs={{0,192},{32,224},{64,0},{96,32},{128,64},{160,96},{192,128},{224,1... | collective-permute-start | bytes 1572872 | tf_op jit(solution)/shard_map/ppermute | solution.py:280
  80.2 0.5 collective-permute-start.11
  80.7 2.6 %collective-permute-start.12 = (f32[256,512]{1,0:T(8,128)}, f32[256,512]{1,0:T(8,128)}, u32[]{:S(2)}, u32[]{:S(2)}) collective-permute-start(f32[256,512]{1,0:T(8,128)} %add.78.sum0), channel_id=1, source_target_pairs={{0,64},{32,96},{64,128},{96,160},{128,192},{160,224},{192,0},{224,... | collective-permute-start | bytes 1572872 | tf_op jit(solution)/shard_map/ppermute | solution.py:280
  83.4 0.6 dynamic_slice.15
  83.9 0.7 pad_add_fusion.at
  84.7 1.3 fusion
  86.0 3.9 %own_log.3 = (f32[1024,512]{1,0:T(8,128)S(1)}, f32[8,128]{1,0:T(8,128)S(1)}) custom-call(f32[9]{0:T(128)S(1)} %compare_select_fusion.1.kz, f32[512,512]{1,0:T(8,128)} %get-tuple-element.36.lo.pot_lo, f32[512,512]{1,0:T(8,128)} %get-tuple-element.35.hi.pot_hi), custom_call_target="tpu_custom_call" | custom-call | tf_op jit(solution)/shard_map/own_log/pallas_call | solution.py:354
  89.9 8.8 %collective-permute-done.7.left = f32[512,512]{1,0:T(8,128)} collective-permute-done((f32[512,512]{1,0:T(8,128)}, f32[512,512]{1,0:T(8,128)}, u32[]{:S(2)}, u32[]{:S(2)}) %collective-permute-start.7) | collective-permute-done | bytes 1048608 | tf_op jit(solution)/shard_map/ppermute | solution.py:280
  98.7 6.2 %second.1 = (f32[1024,512]{1,0:T(8,128)S(1)}, f32[8,128]{1,0:T(8,128)S(1)}) custom-call(s32[2]{0:T(128)S(1)} %add_convert_fusion.where, f32[9]{0:T(128)S(1)} %compare_select_fusion.1.kz, f32[512,512]{1,0:T(8,128)} %collective-permute-done.7.left, f32[512,512]{1,0:T(8,128)} %collective-permute-done.8.right, f32[1024,512]{1,0:T(8,128)S(1)} %get-tuple-element.39.y, ...), custom_call_target="tpu_custom_call" | custom-call | tf_op jit(solution)/shard_map/second/pallas_call | solution.py:356
  104.9 0.0 collective-permute-done.11.sum2
  104.9 3.9 %ratio.1 = (f32[512,512]{1,0:T(8,128)S(1)}, f32[512,512]{1,0:T(8,128)S(1)}, f32[8,128]{1,0:T(8,128)S(1)}) custom-call(s32[2]{0:T(128)S(1)} %pad_add_fusion.at, f32[1]{0:T(128)} %bitcast.5.weight, f32[1024,512]{1,0:T(8,128)S(1)} %get-tuple-element.41.second, f32[8,128]{1,0:T(8,128)S(1)} %get-tuple-element.42.scale.stats, f32[1024,512]{1,0:T(8,128)S(1)} %bitcast.24, ...), custom_call_target="tpu_custom_call" | custom-call | tf_op jit(solution)/shard_map/ratio/pallas_call | solution.py:365
  108.9 2.1 %collective-permute-start.22 = (f32[512,512]{1,0:T(8,128)S(1)}, f32[512,512]{1,0:T(8,128)S(1)}, u32[]{:S(2)}, u32[]{:S(2)}) collective-permute-start(f32[512,512]{1,0:T(8,128)S(1)} %get-tuple-element.46.hi), channel_id=1, source_target_pairs={{0,1},{1,2},{2,3},{3,4},{4,5},{5,6},{6,7},{7,8},{8,9},{9,10},{10,1... | collective-permute-start | bytes 3145736 | tf_op jit(solution)/shard_map/ppermute | solution.py:280
  111.0 6.1 %collective-permute-start.23 = (f32[512,512]{1,0:T(8,128)S(1)}, f32[512,512]{1,0:T(8,128)S(1)}, u32[]{:S(2)}, u32[]{:S(2)}) collective-permute-start(f32[512,512]{1,0:T(8,128)S(1)} %get-tuple-element.45.lo), channel_id=1, source_target_pairs={{1,0},{2,1},{3,2},{4,3},{5,4},{6,5},{7,6},{8,7},{9,8},{10,9},{11,1... | collective-permute-start | bytes 3145736 | tf_op jit(solution)/shard_map/ppermute | solution.py:280
  117.2 0.1 collective-permute-start.13
  117.3 1.2 collective-permute-done.13
  118.4 3.8 %collective-permute-start.16 = (f32[8,128]{1,0:T(8,128)S(1)}, f32[8,128]{1,0:T(8,128)S(1)}, u32[]{:S(2)}, u32[]{:S(2)}) collective-permute-start(f32[8,128]{1,0:T(8,128)S(1)} %add.79), channel_id=1, source_target_pairs={{0,192},{32,224},{64,0},{96,32},{128,64},{160,96},{192,128},{224,1... | collective-permute-start | bytes 12296 | tf_op jit(solution)/shard_map/ppermute | solution.py:280
  122.2 0.2 collective-permute-start.15
  122.4 2.6 %collective-permute-start.14 = (f32[8,128]{1,0:T(8,128)S(1)}, f32[8,128]{1,0:T(8,128)S(1)}, u32[]{:S(2)}, u32[]{:S(2)}) collective-permute-start(f32[8,128]{1,0:T(8,128)S(1)} %add.79), channel_id=1, source_target_pairs={{0,64},{32,96},{64,128},{96,160},{128,192},{160,224},{192,0},{224,... | collective-permute-start | bytes 12296 | tf_op jit(solution)/shard_map/ppermute | solution.py:280
  125.0 4.0 %own_linear.1 = (f32[1024,512]{1,0:T(8,128)S(1)}, f32[1024,512]{1,0:T(8,128)S(1)}) custom-call(f32[9]{0:T(128)S(1)} %compare_select_fusion.1.kz, f32[512,512]{1,0:T(8,128)S(1)} %get-tuple-element.45.lo, f32[512,512]{1,0:T(8,128)S(1)} %get-tuple-element.46.hi, f32[512,512]{1,0:T(8,128)} %get-tuple-element.36.lo.pot_lo, ...), custom_call_target="tpu_custom_call" | custom-call | tf_op jit(solution)/shard_map/own_linear/pallas_call | solution.py:389
  129.0 0.0 collective-permute-done.16
  129.0 0.0 collective-permute-done.14
  129.0 0.1 collective-permute-start.19
  129.1 3.0 %collective-permute-start.18 = (f32[8,128]{1,0:T(8,128)S(1)}, f32[8,128]{1,0:T(8,128)S(1)}, u32[]{:S(2)}, u32[]{:S(2)}) collective-permute-start(f32[8,128]{1,0:T(8,128)S(1)} %add_add_fusion.2), channel_id=1, source_target_pairs={{0,16},{1,17},{2,18},{3,19},{4,20},{5,21},{6,22},{7,23},{8,24},{9,... | collective-permute-start | bytes 12296 | tf_op jit(solution)/shard_map/ppermute | solution.py:280
  132.1 2.2 %collective-permute-start.17 = (f32[8,128]{1,0:T(8,128)S(1)}, f32[8,128]{1,0:T(8,128)S(1)}, u32[]{:S(2)}, u32[]{:S(2)}) collective-permute-start(f32[8,128]{1,0:T(8,128)S(1)} %add_add_fusion.2), channel_id=1, source_target_pairs={{0,8},{1,9},{2,10},{3,11},{4,12},{5,13},{6,14},{7,15},{8,16},{9,17... | collective-permute-start | bytes 12296 | tf_op jit(solution)/shard_map/ppermute | solution.py:280
  134.3 1.5 collective-permute-done.17
  135.8 3.6 %collective-permute-done.20 = f32[8,128]{1,0:T(8,128)S(1)} collective-permute-done((f32[8,128]{1,0:T(8,128)S(1)}, f32[8,128]{1,0:T(8,128)S(1)}, u32[]{:S(2)}, u32[]{:S(2)}) %collective-permute-start.20) | collective-permute-done | bytes 4128 | tf_op jit(solution)/shard_map/ppermute | solution.py:280
  139.4 4.2 %collective-permute-start.21 = (f32[8,128]{1,0:T(8,128)S(1)}, f32[8,128]{1,0:T(8,128)S(1)}, u32[]{:S(2)}, u32[]{:S(2)}) collective-permute-start(f32[8,128]{1,0:T(8,128)S(1)} %add.86), channel_id=1, source_target_pairs={{0,4},{1,5},{2,6},{3,7},{4,0},{5,1},{6,2},{7,3},{8,12},{9,13},{10,... | collective-permute-start | bytes 12296 | tf_op jit(solution)/shard_map/ppermute | solution.py:280
  143.6 1.6 %collective-permute-done.21 = f32[8,128]{1,0:T(8,128)S(1)} collective-permute-done((f32[8,128]{1,0:T(8,128)S(1)}, f32[8,128]{1,0:T(8,128)S(1)}, u32[]{:S(2)}, u32[]{:S(2)}) %collective-permute-start.21) | collective-permute-done | bytes 4128 | tf_op jit(solution)/shard_map/ppermute | solution.py:280
  145.2 0.0 collective-permute-done.22.left
  145.2 5.0 %collective-permute-start.24 = (f32[8,128]{1,0:T(8,128)S(1)}, f32[8,128]{1,0:T(8,128)S(1)}, u32[]{:S(2)}, u32[]{:S(2)}) collective-permute-start(f32[8,128]{1,0:T(8,128)S(1)} %add.87), channel_id=1, source_target_pairs={{0,32},{32,0},{64,96},{96,64},{128,160},{160,128},{192,224},{224,1... | collective-permute-start | bytes 12296 | tf_op jit(solution)/shard_map/ppermute | solution.py:280
  150.2 6.1 %gradient.1 = f32[1024,512]{1,0:T(8,128)} custom-call(s32[2]{0:T(128)S(1)} %add_convert_fusion.where, f32[9]{0:T(128)S(1)} %compare_select_fusion.1.kz, f32[512,512]{1,0:T(8,128)S(1)} %collective-permute-done.22.left, f32[512,512]{1,0:T(8,128)S(1)} %collective-permute-done.23.right, f32[1024,512]{1,0:T(8,128)S(1)} %get-tuple-element.51.y, ...), custom_call_target="tpu_custom_call" | custom-call | tf_op jit(solution)/shard_map/gradient/pallas_call | solution.py:414
  156.3 0.5 multiply_bitcast_fusion
  (34 shorter events, 0.1 us)
Async XLA Ops:
  0.6 5.4 %copy-start.6 = (f32[1,16,64,512]{3,2,1,0:T(8,128)S(1)}, f32[1,16,64,512]{3,2,1,0:T(8,128)}, u32[]{:S(2)}) copy-start(f32[1,16,64,512]{3,2,1,0:T(8,128)} %param.8) | copy-start | bytes 6291460
  3.1 14.6 %collective-permute-start.6 = (f32[256,512]{1,0:T(8,128)S(1)}, f32[256,512]{1,0:T(8,128)S(1)}, u32[]{:S(2)}, u32[]{:S(2)}) collective-permute-start(f32[256,512]{1,0:T(8,128)S(1)} %get-tuple-element.55), channel_id=1, source_target_pairs={{0,192},{32,224},{64,0},{96,32},{128,64},{160,96},{192,128},{224,1... | collective-permute-start | bytes 1572872 | tf_op jit(solution)/shard_map/ppermute | solution.py:280
  3.6 25.3 %collective-permute-start.5 = (f32[256,512]{1,0:T(8,128)S(1)}, f32[256,512]{1,0:T(8,128)S(1)}, u32[]{:S(2)}, u32[]{:S(2)}) collective-permute-start(f32[256,512]{1,0:T(8,128)S(1)} %get-tuple-element.56), channel_id=1, source_target_pairs={{0,128},{32,160},{64,192},{96,224},{128,0},{160,32},{192,64},{224,... | collective-permute-start | bytes 1572872 | tf_op jit(solution)/shard_map/ppermute | solution.py:280
  7.5 45.2 %collective-permute-start = (f32[256,512]{1,0:T(8,128)}, f32[256,512]{1,0:T(8,128)}, u32[]{:S(2)}, u32[]{:S(2)}) collective-permute-start(f32[256,512]{1,0:T(8,128)} %bitcast.6), channel_id=1, source_target_pairs={{0,1},{1,2},{2,3},{3,4},{4,5},{5,6},{6,7},{7,8},{8,9},{9,10},{10,1... | collective-permute-start | bytes 1572872 | tf_op jit(solution)/shard_map/ppermute | solution.py:280
  9.4 43.2 %collective-permute-start.1 = (f32[256,512]{1,0:T(8,128)}, f32[256,512]{1,0:T(8,128)}, u32[]{:S(2)}, u32[]{:S(2)}) collective-permute-start(f32[256,512]{1,0:T(8,128)} %bitcast.7), channel_id=1, source_target_pairs={{0,1},{1,2},{2,3},{3,4},{4,5},{5,6},{6,7},{7,8},{8,9},{9,10},{10,1... | collective-permute-start | bytes 1572872 | tf_op jit(solution)/shard_map/ppermute | solution.py:280
  13.3 39.3 %collective-permute-start.2 = (f32[256,512]{1,0:T(8,128)}, f32[256,512]{1,0:T(8,128)}, u32[]{:S(2)}, u32[]{:S(2)}) collective-permute-start(f32[256,512]{1,0:T(8,128)} %bitcast.8), channel_id=1, source_target_pairs={{1,0},{2,1},{3,2},{4,3},{5,4},{6,5},{7,6},{8,7},{9,8},{10,9},{11,1... | collective-permute-start | bytes 1572872 | tf_op jit(solution)/shard_map/ppermute | solution.py:280
  17.7 11.3 %copy-start.7 = (f32[256,512]{1,0:T(8,128)}, f32[256,512]{1,0:T(8,128)S(1)}, u32[]{:S(2)}) copy-start(f32[256,512]{1,0:T(8,128)S(1)} %collective-permute-done.6) | copy-start | bytes 1572868
  17.7 35.0 %collective-permute-start.3 = (f32[256,512]{1,0:T(8,128)}, f32[256,512]{1,0:T(8,128)}, u32[]{:S(2)}, u32[]{:S(2)}) collective-permute-start(f32[256,512]{1,0:T(8,128)} %bitcast.9), channel_id=1, source_target_pairs={{1,0},{2,1},{3,2},{4,3},{5,4},{6,5},{7,6},{8,7},{9,8},{10,9},{11,1... | collective-permute-start | bytes 1572872 | tf_op jit(solution)/shard_map/ppermute | solution.py:280
  28.9 0.8 copy-start.8
  28.9 2.4 %copy-start.5 = (s32[3]{0:T(128)S(1)}, s32[3]{0:T(128)}, u32[]{:S(2)}) copy-start(s32[3]{0:T(128)} %band.1) | copy-start | bytes 40
  28.9 14.8 %collective-permute-start.4 = (f32[256,512]{1,0:T(8,128)}, f32[256,512]{1,0:T(8,128)}, u32[]{:S(2)}, u32[]{:S(2)}) collective-permute-start(f32[256,512]{1,0:T(8,128)} %get-tuple-element.54), channel_id=1, source_target_pairs={{0,64},{32,96},{64,128},{96,160},{128,192},{160,224},{192,0},{224,... | collective-permute-start | bytes 1572872 | tf_op jit(solution)/shard_map/ppermute | solution.py:280
  31.3 12.4 %copy-start = (f32[1,16,64,512]{3,2,1,0:T(8,128)S(1)}, f32[1,16,64,512]{3,2,1,0:T(8,128)}, u32[]{:S(2)}) copy-start(f32[1,16,64,512]{3,2,1,0:T(8,128)} %param.9) | copy-start | bytes 6291460
  33.6 1.2 copy-start.1
  34.8 1.2 copy-start.2
  36.1 16.6 %copy-start.3 = (f32[1,16,64,512]{3,2,1,0:T(8,128)S(1)}, f32[1,16,64,512]{3,2,1,0:T(8,128)}, u32[]{:S(2)}) copy-start(f32[1,16,64,512]{3,2,1,0:T(8,128)} %param.7) | copy-start | bytes 6291460
  45.4 29.5 %collective-permute-start.9 = (f32[256,512]{1,0:T(8,128)S(1)}, f32[256,512]{1,0:T(8,128)S(1)}, u32[]{:S(2)}, u32[]{:S(2)}) collective-permute-start(f32[256,512]{1,0:T(8,128)S(1)} %add_add_fusion), channel_id=1, source_target_pairs={{0,32},{32,0},{64,96},{96,64},{128,160},{160,128},{192,224},{224,1... | collective-permute-start | bytes 1572872 | tf_op jit(solution)/shard_map/ppermute | solution.py:280
  52.7 30.7 %copy-start.9 = (s32[8]{0:T(128)S(1)}, s32[8]{0:T(128)}, u32[]{:S(2)}) copy-start(s32[8]{0:T(128)} %param.13) | copy-start | bytes 100
  52.7 32.0 %copy-start.10 = (f32[8]{0:T(128)S(1)}, f32[8]{0:T(128)}, u32[]{:S(2)}) copy-start(f32[8]{0:T(128)} %param.11) | copy-start | bytes 100
  59.6 39.1 %collective-permute-start.7 = (f32[512,512]{1,0:T(8,128)}, f32[512,512]{1,0:T(8,128)}, u32[]{:S(2)}, u32[]{:S(2)}) collective-permute-start(f32[512,512]{1,0:T(8,128)} %get-tuple-element.35.hi.pot_hi), channel_id=1, source_target_pairs={{0,1},{1,2},{2,3},{3,4},{4,5},{5,6},{6,7},{7,8},{8,9},{9,10},{10,1... | collective-permute-start | bytes 3145736 | tf_op jit(solution)/shard_map/ppermute | solution.py:280
  61.5 37.2 %collective-permute-start.8 = (f32[512,512]{1,0:T(8,128)}, f32[512,512]{1,0:T(8,128)}, u32[]{:S(2)}, u32[]{:S(2)}) collective-permute-start(f32[512,512]{1,0:T(8,128)} %get-tuple-element.36.lo.pot_lo), channel_id=1, source_target_pairs={{1,0},{2,1},{3,2},{4,3},{5,4},{6,5},{7,6},{8,7},{9,8},{10,9},{11,1... | collective-permute-start | bytes 3145736 | tf_op jit(solution)/shard_map/ppermute | solution.py:280
  75.7 14.2 %collective-permute-start.10 = (f32[256,512]{1,0:T(8,128)}, f32[256,512]{1,0:T(8,128)}, u32[]{:S(2)}, u32[]{:S(2)}) collective-permute-start(f32[256,512]{1,0:T(8,128)} %add.78.sum0), channel_id=1, source_target_pairs={{0,192},{32,224},{64,0},{96,32},{128,64},{160,96},{192,128},{224,1... | collective-permute-start | bytes 1572872 | tf_op jit(solution)/shard_map/ppermute | solution.py:280
  80.2 24.7 %collective-permute-start.11 = (f32[256,512]{1,0:T(8,128)}, f32[256,512]{1,0:T(8,128)}, u32[]{:S(2)}, u32[]{:S(2)}) collective-permute-start(f32[256,512]{1,0:T(8,128)} %add.78.sum0), channel_id=1, source_target_pairs={{0,128},{32,160},{64,192},{96,224},{128,0},{160,32},{192,64},{224,... | collective-permute-start | bytes 1572872 | tf_op jit(solution)/shard_map/ppermute | solution.py:280
  80.7 24.2 %collective-permute-start.12 = (f32[256,512]{1,0:T(8,128)}, f32[256,512]{1,0:T(8,128)}, u32[]{:S(2)}, u32[]{:S(2)}) collective-permute-start(f32[256,512]{1,0:T(8,128)} %add.78.sum0), channel_id=1, source_target_pairs={{0,64},{32,96},{64,128},{96,160},{128,192},{160,224},{192,0},{224,... | collective-permute-start | bytes 1572872 | tf_op jit(solution)/shard_map/ppermute | solution.py:280
  98.7 6.2 %copy-start.4 = (f32[16,64,512]{2,1,0:T(8,128)S(1)}, f32[16,64,512]{2,1,0:T(8,128)}, u32[]{:S(2)}) copy-start(f32[16,64,512]{2,1,0:T(8,128)} %param.10) | copy-start | bytes 6291460
  108.9 36.3 %collective-permute-start.22 = (f32[512,512]{1,0:T(8,128)S(1)}, f32[512,512]{1,0:T(8,128)S(1)}, u32[]{:S(2)}, u32[]{:S(2)}) collective-permute-start(f32[512,512]{1,0:T(8,128)S(1)} %get-tuple-element.46.hi), channel_id=1, source_target_pairs={{0,1},{1,2},{2,3},{3,4},{4,5},{5,6},{6,7},{7,8},{8,9},{9,10},{10,1... | collective-permute-start | bytes 3145736 | tf_op jit(solution)/shard_map/ppermute | solution.py:280
  111.0 34.2 %collective-permute-start.23 = (f32[512,512]{1,0:T(8,128)S(1)}, f32[512,512]{1,0:T(8,128)S(1)}, u32[]{:S(2)}, u32[]{:S(2)}) collective-permute-start(f32[512,512]{1,0:T(8,128)S(1)} %get-tuple-element.45.lo), channel_id=1, source_target_pairs={{1,0},{2,1},{3,2},{4,3},{5,4},{6,5},{7,6},{8,7},{9,8},{10,9},{11,1... | collective-permute-start | bytes 3145736 | tf_op jit(solution)/shard_map/ppermute | solution.py:280
  117.2 1.3 collective-permute-start.13
  118.4 10.6 %collective-permute-start.16 = (f32[8,128]{1,0:T(8,128)S(1)}, f32[8,128]{1,0:T(8,128)S(1)}, u32[]{:S(2)}, u32[]{:S(2)}) collective-permute-start(f32[8,128]{1,0:T(8,128)S(1)} %add.79), channel_id=1, source_target_pairs={{0,192},{32,224},{64,0},{96,32},{128,64},{160,96},{192,128},{224,1... | collective-permute-start | bytes 12296 | tf_op jit(solution)/shard_map/ppermute | solution.py:280
  122.2 6.8 %collective-permute-start.15 = (f32[8,128]{1,0:T(8,128)S(1)}, f32[8,128]{1,0:T(8,128)S(1)}, u32[]{:S(2)}, u32[]{:S(2)}) collective-permute-start(f32[8,128]{1,0:T(8,128)S(1)} %add.79), channel_id=1, source_target_pairs={{0,128},{32,160},{64,192},{96,224},{128,0},{160,32},{192,64},{224,... | collective-permute-start | bytes 12296 | tf_op jit(solution)/shard_map/ppermute | solution.py:280
  122.4 6.6 %collective-permute-start.14 = (f32[8,128]{1,0:T(8,128)S(1)}, f32[8,128]{1,0:T(8,128)S(1)}, u32[]{:S(2)}, u32[]{:S(2)}) collective-permute-start(f32[8,128]{1,0:T(8,128)S(1)} %add.79), channel_id=1, source_target_pairs={{0,64},{32,96},{64,128},{96,160},{128,192},{160,224},{192,0},{224,... | collective-permute-start | bytes 12296 | tf_op jit(solution)/shard_map/ppermute | solution.py:280
  129.0 5.3 %collective-permute-start.19 = (f32[8,128]{1,0:T(8,128)S(1)}, f32[8,128]{1,0:T(8,128)S(1)}, u32[]{:S(2)}, u32[]{:S(2)}) collective-permute-start(f32[8,128]{1,0:T(8,128)S(1)} %add_add_fusion.2), channel_id=1, source_target_pairs={{0,24},{1,25},{2,26},{3,27},{4,28},{5,29},{6,30},{7,31},{8,0},{9,1... | collective-permute-start | bytes 12296 | tf_op jit(solution)/shard_map/ppermute | solution.py:280
  129.1 5.2 %collective-permute-start.18 = (f32[8,128]{1,0:T(8,128)S(1)}, f32[8,128]{1,0:T(8,128)S(1)}, u32[]{:S(2)}, u32[]{:S(2)}) collective-permute-start(f32[8,128]{1,0:T(8,128)S(1)} %add_add_fusion.2), channel_id=1, source_target_pairs={{0,16},{1,17},{2,18},{3,19},{4,20},{5,21},{6,22},{7,23},{8,24},{9,... | collective-permute-start | bytes 12296 | tf_op jit(solution)/shard_map/ppermute | solution.py:280
  132.1 3.6 %collective-permute-start.17 = (f32[8,128]{1,0:T(8,128)S(1)}, f32[8,128]{1,0:T(8,128)S(1)}, u32[]{:S(2)}, u32[]{:S(2)}) collective-permute-start(f32[8,128]{1,0:T(8,128)S(1)} %add_add_fusion.2), channel_id=1, source_target_pairs={{0,8},{1,9},{2,10},{3,11},{4,12},{5,13},{6,14},{7,15},{8,16},{9,17... | collective-permute-start | bytes 12296 | tf_op jit(solution)/shard_map/ppermute | solution.py:280
  135.8 3.6 %collective-permute-start.20 = (f32[8,128]{1,0:T(8,128)S(1)}, f32[8,128]{1,0:T(8,128)S(1)}, u32[]{:S(2)}, u32[]{:S(2)}) collective-permute-start(f32[8,128]{1,0:T(8,128)S(1)} %add_add_fusion.1), channel_id=1, source_target_pairs={{0,2},{1,3},{2,0},{3,1},{4,6},{5,7},{6,4},{7,5},{8,10},{9,11},{10,... | collective-permute-start | bytes 12296 | tf_op jit(solution)/shard_map/ppermute | solution.py:280
  139.4 5.8 %collective-permute-start.21 = (f32[8,128]{1,0:T(8,128)S(1)}, f32[8,128]{1,0:T(8,128)S(1)}, u32[]{:S(2)}, u32[]{:S(2)}) collective-permute-start(f32[8,128]{1,0:T(8,128)S(1)} %add.86), channel_id=1, source_target_pairs={{0,4},{1,5},{2,6},{3,7},{4,0},{5,1},{6,2},{7,3},{8,12},{9,13},{10,... | collective-permute-start | bytes 12296 | tf_op jit(solution)/shard_map/ppermute | solution.py:280
  145.2 11.1 %collective-permute-start.24 = (f32[8,128]{1,0:T(8,128)S(1)}, f32[8,128]{1,0:T(8,128)S(1)}, u32[]{:S(2)}, u32[]{:S(2)}) collective-permute-start(f32[8,128]{1,0:T(8,128)S(1)} %add.87), channel_id=1, source_target_pairs={{0,32},{32,0},{64,96},{96,64},{128,160},{160,128},{192,224},{224,1... | collective-permute-start | bytes 12296 | tf_op jit(solution)/shard_map/ppermute | solution.py:280

commit v6 on v5

--- a/solution.py
+++ b/solution.py
@@ -82,19 +82,18 @@
 
 
 def halo_planes(left, right, kz, y, z, ny, own, entry_left, entry_right):
-    per = left[0].shape[0] // ny
-    side = per * len(left)
+    side = left.shape[0] // ny
     taps = [kz[d] for d in range(BAND_MAX + 1)]
 
     def step(row, columns):
-        e = [entry_left(left[q // per][pl.ds(q % per * ny + row, 8), columns]) for q in range(side)]
+        e = [entry_left(left[pl.ds(q * ny + row, 8), columns]) for q in range(side)]
         for p in range(side):
             rows = pl.ds(p * ny + row, 8)
             total = own(y[rows, columns])
             for q in range(max(0, p + side - BAND_MAX), side):
                 total += taps[p + side - q] * e[q]
             z[rows, columns] = total
-        e = [entry_right(right[q // per][pl.ds(q % per * ny + row, 8), columns]) for q in range(side)]
+        e = [entry_right(right[pl.ds(q * ny + row, 8), columns]) for q in range(side)]
         for p in range(side):
             rows = pl.ds((side + p) * ny + row, 8)
             total = own(y[rows, columns])
@@ -102,7 +101,7 @@
                 total += taps[side + q - p] * e[q]
             z[rows, columns] = total
 
-    tile_loop(ny, left[0].shape[1], step)
+    tile_loop(ny, left.shape[1], step)
 
 
 def tile(value):
@@ -141,8 +140,8 @@
 def log_halos(where, kz, left, right, y, stats, z, scale, ny):
     has_left, has_right = where[0] > 0, where[1] > 0
     m_own = stats[2:3, 0:1]
-    m_left = jnp.where(has_left, functools.reduce(jnp.maximum, [peak(ref[...]) for ref in left]), m_own)
-    m_right = jnp.where(has_right, functools.reduce(jnp.maximum, [peak(ref[...]) for ref in right]), m_own)
+    m_left = jnp.where(has_left, peak(left[...]), m_own)
+    m_right = jnp.where(has_right, peak(right[...]), m_own)
     c = jnp.maximum(m_own, jnp.maximum(m_left, m_right))
     scale[...] = rows_of([c, stats[0:1, 0:1], stats[1:2, 0:1], m_left, m_right, c, c, c])
     own = tile(jnp.exp(m_own - c))
@@ -161,9 +160,9 @@
 
 
 def potential_kernel(
-    where, kz, left0, left1, right0, right1, y, stats, density, kyh, kyl, kxh, kxl, lo, hi, z, mid, scale, *, ny
+    where, kz, left, right, y, stats, density, kyh, kyl, kxh, kxl, lo, hi, z, mid, scale, *, ny
 ):
-    log_halos(where, kz, (left0, left1), (right0, right1), y, stats, z, scale, ny)
+    log_halos(where, kz, left, right, y, stats, z, scale, ny)
     half = mid.shape[0]
     for g, out in enumerate((lo, hi)):
         first = rows_and_columns(z, g, kyh, kyl, kxh, kxl, mid)
@@ -171,22 +170,19 @@
 
 
 def second_kernel(where, kz, left, right, y, stats, kyh, kyl, kxh, kxl, out, scale, z, mid, *, ny):
-    log_halos(where, kz, (left,), (right,), y, stats, z, scale, ny)
+    log_halos(where, kz, left, right, y, stats, z, scale, ny)
     half = mid.shape[0]
     for g in range(2):
         out[g * half : (g + 1) * half, :] = rows_and_columns(z, g, kyh, kyl, kxh, kxl, mid)
 
 
-def ratio_kernel(
-    at, weight, second, scale, bary, cot, sum0, sum1, sum2, sum3, lo, hi, total, sums, out, sems
-):
+def ratio_kernel(at, weight, second, scale, bary, cot, *refs):
+    lo, hi, total, sums, out, sems = refs[-6:]
     c = scale[0:1, 0:1]
-    block, columns = sums.shape[1:]
-    count = sums.shape[0]
+    pieces, block, columns = sums.shape
+    count = pieces // 2
     half = out.shape[0] // 2
-    arriving = [
-        pltpu.make_async_copy(ref, sums.at[k], sems.at[k]) for k, ref in enumerate((sum0, sum1, sum2, sum3))
-    ]
+    arriving = [pltpu.make_async_copy(ref, sums.at[k], sems.at[k]) for k, ref in enumerate(refs[:-6])]
     for copy in arriving:
         copy.start()
     partial = jnp.zeros((8, 128), F32)
@@ -195,7 +191,7 @@
     for k, copy in enumerate(arriving):
         copy.wait()
         g = lax.rem(at[0] + k, count)
-        rows = pl.ds(pl.multiple_of(g * block, block), block)
+        rows = pl.ds(pl.multiple_of((2 * g + k // count) * block, block), block)
         summed = bary[rows, :] + sums[k]
         denominator = second[rows, :]
         share = summed * (jnp.log(denominator) + c)
@@ -229,8 +225,8 @@
         f_right = tile(jnp.exp((c - stats[4:5, 0:1]) * 0.5))
         has_left, has_right = where[0] > 0, where[1] > 0
         halo_planes(
-            (left,),
-            (right,),
+            left,
+            right,
             kz,
             y,
             z,
@@ -290,13 +286,14 @@
 
     cot = atom_cotangent_rows.reshape(rows, nx)
 
-    def block_of(k):
-        return lax.dynamic_slice_in_dim(cot, lax.rem(x_at + k, count) * block, block)
-
-    blocks = [block_of(k) for k in range(1, across)]
-    part = block_of(0)
-    for k in range(1, across):
-        part = part + send(blocks[k - 1], "atom", ahead[k])
+    def block_of(k, h):
+        return lax.dynamic_slice_in_dim(cot, lax.rem(x_at + k, count) * block + h * block // 2, block // 2)
+
+    def over_x(h):
+        return sum([send(block_of(k, h), "atom", ahead[k]) for k in range(1, across)], block_of(0, h))
+
+    parts = [over_x(h) for h in range(2)]
+
 
     y_shape, x_shape = (block, block), (nx, nx)
     distance = jnp.arange(BAND_MAX + 1, dtype=jnp.int32)
@@ -312,9 +309,8 @@
     )(band)
     prior = prior_log_scaling.reshape(rows, nx)
     prior_lo, prior_hi = prior[:half], prior[half:]
-    piece = half // 2
-    from_left = [send(prior_hi[k * piece : (k + 1) * piece], "slab", to_right) for k in range(2)]
-    from_right = [send(prior_lo[k * piece : (k + 1) * piece], "slab", to_left) for k in range(2)]
+    from_left = send(prior_hi, "slab", to_right)
+    from_right = send(prior_lo, "slab", to_left)
 
     where = jnp.stack([slab_at > 0, slab_at < slabs - 1]).astype(jnp.int32)
     slot = lax.dynamic_slice_in_dim(slot_atom_index, atom_at, 1)
@@ -335,24 +331,24 @@
     scale = pltpu.VMEM((8, 128), F32)
 
     y, stats = own_log(kz, prior_lo, prior_hi)
-    y, part = in_order((y, part))
-    swapped = send(part, "atom", swap)
+    swapped = [send(part, "atom", swap) for part in parts]
+    y, swapped[0] = in_order((y, swapped[0]))
     pot_lo, pot_hi = pl.pallas_call(
         functools.partial(potential_kernel, ny=ny),
-        in_specs=[smem, smem] + [vmem] * 11,
+        in_specs=[smem, smem] + [vmem] * 9,
         out_specs=[vmem, vmem],
         out_shape=[shape(half, nx), shape(half, nx)],
         scratch_shapes=[*scratch, scale],
         compiler_params=params,
         name="potential",
-    )(where, kz, *from_left, *from_right, y, stats, atom_log_density.reshape(rows, nx), *tables)
+    )(where, kz, from_left, from_right, y, stats, atom_log_density.reshape(rows, nx), *tables)
 
     from_left = send(pot_hi, "slab", to_right)
     from_right = send(pot_lo, "slab", to_left)
-    both = part + swapped
-    sums = [both] + [send(both, "atom", ahead[across - k]) for k in range(1, across)]
+    both = [part + other for part, other in zip(parts, swapped)]
+    sums = [[both[h]] + [send(both[h], "atom", ahead[across - k]) for k in range(1, across)] for h in range(2)]
     y, stats = own_log(kz, pot_lo, pot_hi)
-    y, sums[1] = in_order((y, sums[1]))
+    y, sums[0] = in_order((y, sums[0]))
     second, stats = pl.pallas_call(
         functools.partial(second_kernel, ny=ny),
         in_specs=[smem, smem] + [vmem] * 8,
@@ -364,13 +360,13 @@
     )(where, kz, from_left, from_right, y, stats, *tables)
     ratio_lo, ratio_hi, total = pl.pallas_call(
         ratio_kernel,
-        in_specs=[smem, smem] + [vmem] * 4 + [anywhere] * 4,
+        in_specs=[smem, smem] + [vmem] * 4 + [anywhere] * (2 * count),
         out_specs=[anywhere, anywhere, vmem],
         out_shape=[shape(half, nx), shape(half, nx), shape(8, 128)],
         scratch_shapes=[
-            pltpu.VMEM((count, block, nx), F32),
+            pltpu.VMEM((2 * count, block // 2, nx), F32),
             pltpu.VMEM((rows, nx), F32),
-            pltpu.SemaphoreType.DMA((count,)),
+            pltpu.SemaphoreType.DMA((2 * count,)),
         ],
         compiler_params=params,
         name="ratio",
@@ -381,7 +377,8 @@
         stats,
         barycenter_cotangent.reshape(rows, nx),
         cot,
-        *sums,
+        *sums[0],
+        *sums[1],
     )
 
     from_left = send(ratio_hi, "slab", to_right)
@@ -395,21 +392,10 @@
         name="own_linear",
     )(kz, ratio_lo, ratio_hi, pot_lo, pot_hi, stats)
 
-    def add(value, axis, patterns):
-        return sum([send(value, axis, pairs) for pairs in patterns], value)
-
-    def flips(hop):
-        return [(i, i ^ hop) for i in range(slabs)]
-
-    value = add(total, "slab", [flips(1)])
-    value = add(value, "atom", [ahead[k] for k in range(1, across)])
-    value, y = in_order((value, y))
-    value = add(value, "slab", [[(i, (i + k) % slabs) for i in range(slabs)] for k in (8, 16, 24)])
-    for hop in (2, 4):
-        value = add(value, "slab", [flips(hop)])
-    value, from_left, from_right = in_order((value, from_left, from_right))
-    value = add(value, "atom", [swap])
-    weight_grad = value[0, : weights.shape[0]] / (rows * nx * slabs)
+    total, y = in_order((total, y))
+    value = jnp.broadcast_to(total[:1], (atoms * slabs, 128))
+    value = lax.all_to_all(value, ("atom", "slab"), 0, 0, tiled=True)
+    weight_grad = jnp.sum(value, axis=0)[: weights.shape[0]] / (rows * nx * slabs)
 
     gradient = pl.pallas_call(
         functools.partial(gradient_kernel, ny=ny),

time: 159 us -> 186 us (1.17)
  blocking collectives: 0 us -> 21.5 us
  starting transfers between devices: 69.9 us -> 50.8 us
  waiting for transfers between devices: 35.4 us -> 47.2 us
  local copies, waits for them, and re-layouts: 9.86 us -> 16.5 us
  Pallas kernels: 35 us -> 38.1 us
    all_to_all x0 -> x1, blocking collectives: none -> 21.5 us  [body(): value = lax.all_to_all(value, ('atom', 'slab'), 0, 0, tiled=True)]
    ppermute x25 -> x20, starting transfers between devices: 69.9 us -> 50.8 us  [send(): return lax.ppermute(value, axis, pairs)]
    ppermute x25 -> x20, waiting for transfers between devices: 35.4 us -> 47.2 us  [send(): return lax.ppermute(value, axis, pairs)]
    unnamed x22 -> x38, local copies, waits for them, and re-layouts: 3.27 us -> 10.3 us
  transfers between devices with their start and end apart: 25 -> 20, of which waited for: 8 -> 6; matrix products, arithmetic and copies ran while one was open for 6% -> 6% of each run, Pallas kernels for 20% -> 11%
where the time goes in v6:
time: 186 us; the launch traced here: 182 us
  starting transfers between devices  50.8 us (27%)
  waiting for transfers between devices  47.2 us (25%)
  Pallas kernels  38.1 us (20%)
  blocking collectives  21.5 us (12%)
  local copies, waits for them, and re-layouts  16.5 us (9%)
  other arithmetic  6.94 us (4%)
    ppermute x20, starting transfers between devices, send(): return lax.ppermute(value, axis, pairs)  50.8 us
    ppermute x20, waiting for transfers between devices, send(): return lax.ppermute(value, axis, pairs)  47.2 us
    all_to_all x1, blocking collectives, body(): value = lax.all_to_all(value, ('atom', 'slab'), 0, 0, tiled=True)  21.5 us
    unnamed x38, local copies, waits for them, and re-layouts  10.3 us
    pallas_call x1, Pallas kernels, body(): pl.pallas_call(functools.partial(gradient_kernel, ny=ny), grid=(2,), in_s...  7.12 us
    pallas_call x1, Pallas kernels, body(): pl.pallas_call(functools.partial(potential_kernel, ny=ny), in_specs=[smem...  7.11 us
    pallas_call x1, Pallas kernels, body(): pl.pallas_call(functools.partial(second_kernel, ny=ny), in_specs=[smem, s...  6.19 us
    pallas_call x1, Pallas kernels, body(): pl.pallas_call(functools.partial(own_linear_kernel, ny=ny), in_specs=[sme...  4.53 us
  transfers between devices with their start and end apart: 20, of which 6 were waited for; matrix products, arithmetic and copies ran while one was open for 6% of the time, Pallas kernels for 11%

profile of v6, /device:TPU:10, one launch (start us, length us, event | category | flops | bytes accessed | tf_op | source)
XLA Modules:
  0.0 182.2 jit_solution(10060333682775672169)
XLA Ops:
  0.7 1.9 %constant_dynamic-slice_fusion.2 = (f32[128,512]{1,0:T(8,128)}, f32[128,512]{1,0:T(8,128)S(1)}, f32[128,512]{1,0:T(8,128)S(1)}) fusion(f32[1024,512]{1,0:T(8,128)} %bitcast.15, s32[]{:T(128)S(6)} %select_n.44, s32[]{:T(128)S(6)} %select_n.46, s32[]{:T(128)S(6)} %select_n.45), kind=kLoop, calls=%fused_computation.4 | loop fusion | bytes 1572876 | tf_op jit(solution)/shard_map/dynamic_slice | solution.py:290
  2.6 1.5 collective-permute-start.11
  4.0 1.1 collective-permute-start.12
  5.2 2.2 %collective-permute-start.13 = (f32[128,512]{1,0:T(8,128)S(1)}, f32[128,512]{1,0:T(8,128)S(1)}, u32[]{:S(2)}, u32[]{:S(2)}) collective-permute-start(f32[128,512]{1,0:T(8,128)S(1)} %get-tuple-element.59), channel_id=1, source_target_pairs={{0,192},{32,224},{64,0},{96,32},{128,64},{160,96},{192,128},{224,1... | collective-permute-start | bytes 786440 | tf_op jit(solution)/shard_map/ppermute | solution.py:276
  7.3 3.2 %fusion.1 = (f32[1,8,64,512]{3,2,1,0:T(8,128)}, f32[1,8,64,512]{3,2,1,0:T(8,128)}) fusion(f32[1,16,64,512]{3,2,1,0:T(8,128)} %param.8), kind=kLoop, calls=%fused_computation.15 | loop fusion | bytes 4194304 | tf_op jit(solution)/shard_map/slice | solution.py:311
  10.5 1.9 %collective-permute-start = (f32[512,512]{1,0:T(8,128)}, f32[512,512]{1,0:T(8,128)}, u32[]{:S(2)}, u32[]{:S(2)}) collective-permute-start(f32[512,512]{1,0:T(8,128)} %bitcast.6.hi), channel_id=1, source_target_pairs={{0,1},{1,2},{2,3},{3,4},{4,5},{5,6},{6,7},{7,8},{8,9},{9,10},{10,1... | collective-permute-start | bytes 3145736 | tf_op jit(solution)/shard_map/ppermute | solution.py:276
  12.4 6.3 %collective-permute-start.1 = (f32[512,512]{1,0:T(8,128)}, f32[512,512]{1,0:T(8,128)}, u32[]{:S(2)}, u32[]{:S(2)}) collective-permute-start(f32[512,512]{1,0:T(8,128)} %bitcast.7.lo), channel_id=1, source_target_pairs={{1,0},{2,1},{3,2},{4,3},{5,4},{6,5},{7,6},{8,7},{9,8},{10,9},{11,1... | collective-permute-start | bytes 3145736 | tf_op jit(solution)/shard_map/ppermute | solution.py:276
  18.8 0.0 copy-start.15
  18.8 0.0 collective-permute-done.12
  18.8 0.0 collective-permute-done.13
  18.8 1.0 add_add_fusion
  19.9 0.7 collective-permute-start.2
  20.6 2.8 %collective-permute-start.3 = (f32[128,512]{1,0:T(8,128)S(1)}, f32[128,512]{1,0:T(8,128)S(1)}, u32[]{:S(2)}, u32[]{:S(2)}) collective-permute-start(f32[128,512]{1,0:T(8,128)S(1)} %get-tuple-element.56), channel_id=1, source_target_pairs={{0,128},{32,160},{64,192},{96,224},{128,0},{160,32},{192,64},{224,... | collective-permute-start | bytes 786440 | tf_op jit(solution)/shard_map/ppermute | solution.py:276
  23.4 0.3 collective-permute-start.4
  23.7 5.6 %collective-permute-done.2 = f32[128,512]{1,0:T(8,128)S(1)} collective-permute-done((f32[128,512]{1,0:T(8,128)}, f32[128,512]{1,0:T(8,128)S(1)}, u32[]{:S(2)}, u32[]{:S(2)}) %collective-permute-start.2) | collective-permute-done | bytes 262176 | tf_op jit(solution)/shard_map/ppermute | solution.py:276
  29.3 2.0 %collective-permute-done.3 = f32[128,512]{1,0:T(8,128)S(1)} collective-permute-done((f32[128,512]{1,0:T(8,128)S(1)}, f32[128,512]{1,0:T(8,128)S(1)}, u32[]{:S(2)}, u32[]{:S(2)}) %collective-permute-start.3) | collective-permute-done | bytes 262176 | tf_op jit(solution)/shard_map/ppermute | solution.py:276
  31.3 3.0 %collective-permute-done.4 = f32[128,512]{1,0:T(8,128)S(1)} collective-permute-done((f32[128,512]{1,0:T(8,128)S(1)}, f32[128,512]{1,0:T(8,128)S(1)}, u32[]{:S(2)}, u32[]{:S(2)}) %collective-permute-start.4) | collective-permute-done | bytes 262176 | tf_op jit(solution)/shard_map/ppermute | solution.py:276
  34.3 0.8 add_add_fusion.1
  35.1 7.2 %collective-permute-start.5 = (f32[128,512]{1,0:T(8,128)}, f32[128,512]{1,0:T(8,128)}, u32[]{:S(2)}, u32[]{:S(2)}) collective-permute-start(f32[128,512]{1,0:T(8,128)} %add_add_fusion.1), channel_id=1, source_target_pairs={{0,32},{32,0},{64,96},{96,64},{128,160},{160,128},{192,224},{224,1... | collective-permute-start | bytes 786440 | tf_op jit(solution)/shard_map/ppermute | solution.py:276
  42.3 0.6 slice.23
  42.9 1.1 tables.1
  43.9 0.7 compare_select_fusion.1.kz
  44.6 3.9 %own_log.2 = (f32[1024,512]{1,0:T(8,128)S(1)}, f32[8,128]{1,0:T(8,128)S(1)}) custom-call(f32[9]{0:T(128)S(1)} %compare_select_fusion.1.kz, f32[512,512]{1,0:T(8,128)} %bitcast.7.lo, f32[512,512]{1,0:T(8,128)} %bitcast.6.hi), custom_call_target="tpu_custom_call" | custom-call | tf_op jit(solution)/shard_map/own_log/pallas_call | solution.py:333
  48.5 0.0 copy-start.2
  48.5 1.3 copy-done.2
  49.9 0.1 add_convert_fusion.where
  49.9 0.7 collective-permute-done.5
  50.7 1.6 copy-done.1
  52.3 1.6 copy-done.3
  53.9 7.1 %potential.1 = (f32[512,512]{1,0:T(8,128)}, f32[512,512]{1,0:T(8,128)}) custom-call(s32[2]{0:T(128)S(1)} %add_convert_fusion.where, f32[9]{0:T(128)S(1)} %compare_select_fusion.1.kz, f32[512,512]{1,0:T(8,128)} %collective-permute-done.left, f32[512,512]{1,0:T(8,128)} %collective-permute-done.1.right, f32[1024,512]{1,0:T(8,128)S(1)} %copy-done.3, ...), custom_call_target="tpu_custom_call" | custom-call | tf_op jit(solution)/shard_map/potential/pallas_call | solution.py:336
  61.0 1.9 %collective-permute-start.6 = (f32[512,512]{1,0:T(8,128)}, f32[512,512]{1,0:T(8,128)}, u32[]{:S(2)}, u32[]{:S(2)}) collective-permute-start(f32[512,512]{1,0:T(8,128)} %get-tuple-element.35.hi.pot_hi), channel_id=1, source_target_pairs={{0,1},{1,2},{2,3},{3,4},{4,5},{5,6},{6,7},{7,8},{8,9},{9,10},{10,1... | collective-permute-start | bytes 3145736 | tf_op jit(solution)/shard_map/ppermute | solution.py:276
  62.9 6.3 %collective-permute-start.7 = (f32[512,512]{1,0:T(8,128)}, f32[512,512]{1,0:T(8,128)}, u32[]{:S(2)}, u32[]{:S(2)}) collective-permute-start(f32[512,512]{1,0:T(8,128)} %get-tuple-element.36.lo.pot_lo), channel_id=1, source_target_pairs={{1,0},{2,1},{3,2},{4,3},{5,4},{6,5},{7,6},{8,7},{9,8},{10,9},{11,1... | collective-permute-start | bytes 3145736 | tf_op jit(solution)/shard_map/ppermute | solution.py:276
  69.2 4.7 %collective-permute-start.14 = (f32[128,512]{1,0:T(8,128)S(1)}, f32[128,512]{1,0:T(8,128)S(1)}, u32[]{:S(2)}, u32[]{:S(2)}) collective-permute-start(f32[128,512]{1,0:T(8,128)S(1)} %copy-done.16), channel_id=1, source_target_pairs={{0,32},{32,0},{64,96},{96,64},{128,160},{160,128},{192,224},{224,1... | collective-permute-start | bytes 786440 | tf_op jit(solution)/shard_map/ppermute | solution.py:276
  73.9 1.1 add.95.refs_0_
  75.0 0.1 collective-permute-start.10
  75.1 2.0 %collective-permute-start.8 = (f32[128,512]{1,0:T(8,128)S(1)}, f32[128,512]{1,0:T(8,128)S(1)}, u32[]{:S(2)}, u32[]{:S(2)}) collective-permute-start(f32[128,512]{1,0:T(8,128)S(1)} %add.95.refs_0_), channel_id=1, source_target_pairs={{0,192},{32,224},{64,0},{96,32},{128,64},{160,96},{192,128},{224,1... | collective-permute-start | bytes 786440 | tf_op jit(solution)/shard_map/ppermute | solution.py:276
  77.1 31.5 %collective-permute-done.14 = f32[128,512]{1,0:T(8,128)S(1)} collective-permute-done((f32[128,512]{1,0:T(8,128)S(1)}, f32[128,512]{1,0:T(8,128)S(1)}, u32[]{:S(2)}, u32[]{:S(2)}) %collective-permute-start.14) | collective-permute-done | bytes 262176 | tf_op jit(solution)/shard_map/ppermute | solution.py:276
  108.5 1.9 %collective-permute-start.9 = (f32[128,512]{1,0:T(8,128)S(1)}, f32[128,512]{1,0:T(8,128)S(1)}, u32[]{:S(2)}, u32[]{:S(2)}) collective-permute-start(f32[128,512]{1,0:T(8,128)S(1)} %add.95.refs_0_), channel_id=1, source_target_pairs={{0,128},{32,160},{64,192},{96,224},{128,0},{160,32},{192,64},{224,... | collective-permute-start | bytes 786440 | tf_op jit(solution)/shard_map/ppermute | solution.py:276
  110.5 0.7 copy-done.7
  111.2 0.7 add.107.refs_4_
  111.9 0.0 collective-permute-done.10.refs_3_
  111.9 0.7 copy-done.9
  112.6 0.0 collective-permute-start.15
  112.7 0.7 copy-done.11
  113.4 1.6 collective-permute-start.16
  114.9 4.4 %collective-permute-done.9.refs_2_ = f32[128,512]{1,0:T(8,128)S(1)} collective-permute-done((f32[128,512]{1,0:T(8,128)S(1)}, f32[128,512]{1,0:T(8,128)S(1)}, u32[]{:S(2)}, u32[]{:S(2)}) %collective-permute-start.9) | collective-permute-done | bytes 262176 | tf_op jit(solution)/shard_map/ppermute | solution.py:276
  119.3 0.7 copy-done.13
  120.0 0.6 dynamic_slice.27
  120.6 0.7 pad_add_fusion.at
  121.4 1.3 fusion
  122.7 3.9 %own_log.3 = (f32[1024,512]{1,0:T(8,128)S(1)}, f32[8,128]{1,0:T(8,128)S(1)}) custom-call(f32[9]{0:T(128)S(1)} %compare_select_fusion.1.kz, f32[512,512]{1,0:T(8,128)} %get-tuple-element.36.lo.pot_lo, f32[512,512]{1,0:T(8,128)} %get-tuple-element.35.hi.pot_hi), custom_call_target="tpu_custom_call" | custom-call | tf_op jit(solution)/shard_map/own_log/pallas_call | solution.py:350
  126.6 0.0 copy-start.4
  126.7 6.2 %second.1 = (f32[1024,512]{1,0:T(8,128)S(1)}, f32[8,128]{1,0:T(8,128)S(1)}) custom-call(s32[2]{0:T(128)S(1)} %add_convert_fusion.where, f32[9]{0:T(128)S(1)} %compare_select_fusion.1.kz, f32[512,512]{1,0:T(8,128)} %collective-permute-done.6.left, f32[512,512]{1,0:T(8,128)} %collective-permute-done.7.right, f32[1024,512]{1,0:T(8,128)S(1)} %get-tuple-element.39.y, ...), custom_call_target="tpu_custom_call" | custom-call | tf_op jit(solution)/shard_map/second/pallas_call | solution.py:352
  133.0 4.2 %ratio.1 = (f32[512,512]{1,0:T(8,128)}, f32[512,512]{1,0:T(8,128)}, f32[8,128]{1,0:T(8,128)S(1)}) custom-call(s32[2]{0:T(128)S(1)} %pad_add_fusion.at, f32[1]{0:T(128)} %bitcast.5.weight, f32[1024,512]{1,0:T(8,128)S(1)} %get-tuple-element.41.second, f32[8,128]{1,0:T(8,128)S(1)} %get-tuple-element.42.scale.stats, f32[1024,512]{1,0:T(8,128)S(1)} %bitcast.20, ...), custom_call_target="tpu_custom_call" | custom-call | tf_op jit(solution)/shard_map/ratio/pallas_call | solution.py:361
  137.2 1.9 %collective-permute-start.18 = (f32[512,512]{1,0:T(8,128)}, f32[512,512]{1,0:T(8,128)}, u32[]{:S(2)}, u32[]{:S(2)}) collective-permute-start(f32[512,512]{1,0:T(8,128)} %get-tuple-element.47.hi), channel_id=1, source_target_pairs={{0,1},{1,2},{2,3},{3,4},{4,5},{5,6},{6,7},{7,8},{8,9},{9,10},{10,1... | collective-permute-start | bytes 3145736 | tf_op jit(solution)/shard_map/ppermute | solution.py:276
  139.1 6.3 %collective-permute-start.19 = (f32[512,512]{1,0:T(8,128)}, f32[512,512]{1,0:T(8,128)}, u32[]{:S(2)}, u32[]{:S(2)}) collective-permute-start(f32[512,512]{1,0:T(8,128)} %get-tuple-element.48.lo), channel_id=1, source_target_pairs={{1,0},{2,1},{3,2},{4,3},{5,4},{6,5},{7,6},{8,7},{9,8},{10,9},{11,1... | collective-permute-start | bytes 3145736 | tf_op jit(solution)/shard_map/ppermute | solution.py:276
  145.5 4.5 %own_linear.1 = (f32[1024,512]{1,0:T(8,128)S(1)}, f32[1024,512]{1,0:T(8,128)S(1)}) custom-call(f32[9]{0:T(128)S(1)} %compare_select_fusion.1.kz, f32[512,512]{1,0:T(8,128)} %get-tuple-element.48.lo, f32[512,512]{1,0:T(8,128)} %get-tuple-element.47.hi, f32[512,512]{1,0:T(8,128)} %get-tuple-element.36.lo.pot_lo, f32[512,512]{1,0:T(8,128)} %get-tuple-element.35.hi.pot_hi, ...), custom_call_target="tpu_custom_call" | custom-call | tf_op jit(solution)/shard_map/own_linear/pallas_call | solution.py:386
  150.0 0.0 copy-start.5
  150.0 1.3 copy-done.5
  151.3 0.1 broadcast_in_dim.14
  151.4 21.5 %all_to_all.6 = f32[256,1,128]{2,1,0:T(1,128)S(1)} all-to-all(f32[256,1,128]{2,1,0:T(1,128)S(1)} %broadcast_in_dim.14), channel_id=1, replica_groups=mesh['atom'=8,'slab'=32] {'atom','slab'}, dimensions={0} | all-to-all | bytes 262144 | tf_op jit(solution)/shard_map/all_to_all | solution.py:397
  172.9 0.5 slice_multiply_fusion
  173.5 1.6 copy-done.6
  175.0 7.1 %gradient.1 = f32[1024,512]{1,0:T(8,128)} custom-call(s32[2]{0:T(128)S(1)} %add_convert_fusion.where, f32[9]{0:T(128)S(1)} %compare_select_fusion.1.kz, f32[512,512]{1,0:T(8,128)} %collective-permute-done.18.left, f32[512,512]{1,0:T(8,128)} %collective-permute-done.19.right, f32[1024,512]{1,0:T(8,128)S(1)} %get-tuple-element.51.y, ...), custom_call_target="tpu_custom_call" | custom-call | tf_op jit(solution)/shard_map/gradient/pallas_call | solution.py:400
  (39 shorter events, 0.1 us)
Async XLA Ops:
  2.6 16.2 %collective-permute-start.11 = (f32[128,512]{1,0:T(8,128)}, f32[128,512]{1,0:T(8,128)S(1)}, u32[]{:S(2)}, u32[]{:S(2)}) collective-permute-start(f32[128,512]{1,0:T(8,128)} %get-tuple-element.58), channel_id=1, source_target_pairs={{0,64},{32,96},{64,128},{96,160},{128,192},{160,224},{192,0},{224,... | collective-permute-start | bytes 786440 | tf_op jit(solution)/shard_map/ppermute | solution.py:276
  4.0 14.8 %collective-permute-start.12 = (f32[128,512]{1,0:T(8,128)S(1)}, f32[128,512]{1,0:T(8,128)S(1)}, u32[]{:S(2)}, u32[]{:S(2)}) collective-permute-start(f32[128,512]{1,0:T(8,128)S(1)} %get-tuple-element.60), channel_id=1, source_target_pairs={{0,128},{32,160},{64,192},{96,224},{128,0},{160,32},{192,64},{224,... | collective-permute-start | bytes 786440 | tf_op jit(solution)/shard_map/ppermute | solution.py:276
  5.2 13.7 %copy-start = (f32[1,16,64,512]{3,2,1,0:T(8,128)S(1)}, f32[1,16,64,512]{3,2,1,0:T(8,128)}, u32[]{:S(2)}) copy-start(f32[1,16,64,512]{3,2,1,0:T(8,128)} %param.9) | copy-start | bytes 6291460
  5.2 13.6 %collective-permute-start.13 = (f32[128,512]{1,0:T(8,128)S(1)}, f32[128,512]{1,0:T(8,128)S(1)}, u32[]{:S(2)}, u32[]{:S(2)}) collective-permute-start(f32[128,512]{1,0:T(8,128)S(1)} %get-tuple-element.59), channel_id=1, source_target_pairs={{0,192},{32,224},{64,0},{96,32},{128,64},{160,96},{192,128},{224,1... | collective-permute-start | bytes 786440 | tf_op jit(solution)/shard_map/ppermute | solution.py:276
  10.5 40.2 %collective-permute-start = (f32[512,512]{1,0:T(8,128)}, f32[512,512]{1,0:T(8,128)}, u32[]{:S(2)}, u32[]{:S(2)}) collective-permute-start(f32[512,512]{1,0:T(8,128)} %bitcast.6.hi), channel_id=1, source_target_pairs={{0,1},{1,2},{2,3},{3,4},{4,5},{5,6},{6,7},{7,8},{8,9},{9,10},{10,1... | collective-permute-start | bytes 3145736 | tf_op jit(solution)/shard_map/ppermute | solution.py:276
  12.4 38.3 %collective-permute-start.1 = (f32[512,512]{1,0:T(8,128)}, f32[512,512]{1,0:T(8,128)}, u32[]{:S(2)}, u32[]{:S(2)}) collective-permute-start(f32[512,512]{1,0:T(8,128)} %bitcast.7.lo), channel_id=1, source_target_pairs={{1,0},{2,1},{3,2},{4,3},{5,4},{6,5},{7,6},{8,7},{9,8},{10,9},{11,1... | collective-permute-start | bytes 3145736 | tf_op jit(solution)/shard_map/ppermute | solution.py:276
  18.8 23.5 %copy-start.15 = (s32[3]{0:T(128)S(1)}, s32[3]{0:T(128)}, u32[]{:S(2)}) copy-start(s32[3]{0:T(128)} %band.1) | copy-start | bytes 40
  19.9 9.5 %collective-permute-start.2 = (f32[128,512]{1,0:T(8,128)}, f32[128,512]{1,0:T(8,128)S(1)}, u32[]{:S(2)}, u32[]{:S(2)}) collective-permute-start(f32[128,512]{1,0:T(8,128)} %get-tuple-element.57), channel_id=1, source_target_pairs={{0,64},{32,96},{64,128},{96,160},{128,192},{160,224},{192,0},{224,... | collective-permute-start | bytes 786440 | tf_op jit(solution)/shard_map/ppermute | solution.py:276
  20.6 10.7 %collective-permute-start.3 = (f32[128,512]{1,0:T(8,128)S(1)}, f32[128,512]{1,0:T(8,128)S(1)}, u32[]{:S(2)}, u32[]{:S(2)}) collective-permute-start(f32[128,512]{1,0:T(8,128)S(1)} %get-tuple-element.56), channel_id=1, source_target_pairs={{0,128},{32,160},{64,192},{96,224},{128,0},{160,32},{192,64},{224,... | collective-permute-start | bytes 786440 | tf_op jit(solution)/shard_map/ppermute | solution.py:276
  23.4 11.0 %collective-permute-start.4 = (f32[128,512]{1,0:T(8,128)S(1)}, f32[128,512]{1,0:T(8,128)S(1)}, u32[]{:S(2)}, u32[]{:S(2)}) collective-permute-start(f32[128,512]{1,0:T(8,128)S(1)} %get-tuple-element.55), channel_id=1, source_target_pairs={{0,192},{32,224},{64,0},{96,32},{128,64},{160,96},{192,128},{224,1... | collective-permute-start | bytes 786440 | tf_op jit(solution)/shard_map/ppermute | solution.py:276
  35.1 15.6 %collective-permute-start.5 = (f32[128,512]{1,0:T(8,128)}, f32[128,512]{1,0:T(8,128)}, u32[]{:S(2)}, u32[]{:S(2)}) collective-permute-start(f32[128,512]{1,0:T(8,128)} %add_add_fusion.1), channel_id=1, source_target_pairs={{0,32},{32,0},{64,96},{96,64},{128,160},{160,128},{192,224},{224,1... | collective-permute-start | bytes 786440 | tf_op jit(solution)/shard_map/ppermute | solution.py:276
  48.5 1.3 copy-start.2
  50.7 1.6 copy-start.1
  52.3 1.6 copy-start.3
  53.9 15.4 %copy-start.16 = (f32[128,512]{1,0:T(8,128)S(1)}, f32[128,512]{1,0:T(8,128)}, u32[]{:S(2)}) copy-start(f32[128,512]{1,0:T(8,128)} %get-tuple-element.54) | copy-start | bytes 786436
  53.9 66.2 %copy-start.17 = (s32[8]{0:T(128)S(1)}, s32[8]{0:T(128)}, u32[]{:S(2)}) copy-start(s32[8]{0:T(128)} %param.13) | copy-start | bytes 100
  53.9 67.5 %copy-start.18 = (f32[8]{0:T(128)S(1)}, f32[8]{0:T(128)}, u32[]{:S(2)}) copy-start(f32[8]{0:T(128)} %param.11) | copy-start | bytes 100
  61.0 65.6 %collective-permute-start.6 = (f32[512,512]{1,0:T(8,128)}, f32[512,512]{1,0:T(8,128)}, u32[]{:S(2)}, u32[]{:S(2)}) collective-permute-start(f32[512,512]{1,0:T(8,128)} %get-tuple-element.35.hi.pot_hi), channel_id=1, source_target_pairs={{0,1},{1,2},{2,3},{3,4},{4,5},{5,6},{6,7},{7,8},{8,9},{9,10},{10,1... | collective-permute-start | bytes 3145736 | tf_op jit(solution)/shard_map/ppermute | solution.py:276
  62.9 63.7 %collective-permute-start.7 = (f32[512,512]{1,0:T(8,128)}, f32[512,512]{1,0:T(8,128)}, u32[]{:S(2)}, u32[]{:S(2)}) collective-permute-start(f32[512,512]{1,0:T(8,128)} %get-tuple-element.36.lo.pot_lo), channel_id=1, source_target_pairs={{1,0},{2,1},{3,2},{4,3},{5,4},{6,5},{7,6},{8,7},{9,8},{10,9},{11,1... | collective-permute-start | bytes 3145736 | tf_op jit(solution)/shard_map/ppermute | solution.py:276
  69.2 39.3 %collective-permute-start.14 = (f32[128,512]{1,0:T(8,128)S(1)}, f32[128,512]{1,0:T(8,128)S(1)}, u32[]{:S(2)}, u32[]{:S(2)}) collective-permute-start(f32[128,512]{1,0:T(8,128)S(1)} %copy-done.16), channel_id=1, source_target_pairs={{0,32},{32,0},{64,96},{96,64},{128,160},{160,128},{192,224},{224,1... | collective-permute-start | bytes 786440 | tf_op jit(solution)/shard_map/ppermute | solution.py:276
  75.0 37.0 %collective-permute-start.10 = (f32[128,512]{1,0:T(8,128)S(1)}, f32[128,512]{1,0:T(8,128)S(1)}, u32[]{:S(2)}, u32[]{:S(2)}) collective-permute-start(f32[128,512]{1,0:T(8,128)S(1)} %add.95.refs_0_), channel_id=1, source_target_pairs={{0,64},{32,96},{64,128},{96,160},{128,192},{160,224},{192,0},{224,... | collective-permute-start | bytes 786440 | tf_op jit(solution)/shard_map/ppermute | solution.py:276
  75.1 37.6 %collective-permute-start.8 = (f32[128,512]{1,0:T(8,128)S(1)}, f32[128,512]{1,0:T(8,128)S(1)}, u32[]{:S(2)}, u32[]{:S(2)}) collective-permute-start(f32[128,512]{1,0:T(8,128)S(1)} %add.95.refs_0_), channel_id=1, source_target_pairs={{0,192},{32,224},{64,0},{96,32},{128,64},{160,96},{192,128},{224,1... | collective-permute-start | bytes 786440 | tf_op jit(solution)/shard_map/ppermute | solution.py:276
  108.5 10.8 %collective-permute-start.9 = (f32[128,512]{1,0:T(8,128)S(1)}, f32[128,512]{1,0:T(8,128)S(1)}, u32[]{:S(2)}, u32[]{:S(2)}) collective-permute-start(f32[128,512]{1,0:T(8,128)S(1)} %add.95.refs_0_), channel_id=1, source_target_pairs={{0,128},{32,160},{64,192},{96,224},{128,0},{160,32},{192,64},{224,... | collective-permute-start | bytes 786440 | tf_op jit(solution)/shard_map/ppermute | solution.py:276
  110.5 0.7 copy-start.7
  111.9 0.7 copy-start.9
  112.6 20.2 %collective-permute-start.15 = (f32[128,512]{1,0:T(8,128)}, f32[128,512]{1,0:T(8,128)}, u32[]{:S(2)}, u32[]{:S(2)}) collective-permute-start(f32[128,512]{1,0:T(8,128)} %add.107.refs_4_), channel_id=1, source_target_pairs={{0,192},{32,224},{64,0},{96,32},{128,64},{160,96},{192,128},{224,1... | collective-permute-start | bytes 786440 | tf_op jit(solution)/shard_map/ppermute | solution.py:276
  112.6 0.7 copy-start.11
  113.4 19.5 %collective-permute-start.16 = (f32[128,512]{1,0:T(8,128)}, f32[128,512]{1,0:T(8,128)}, u32[]{:S(2)}, u32[]{:S(2)}) collective-permute-start(f32[128,512]{1,0:T(8,128)} %add.107.refs_4_), channel_id=1, source_target_pairs={{0,128},{32,160},{64,192},{96,224},{128,0},{160,32},{192,64},{224,... | collective-permute-start | bytes 786440 | tf_op jit(solution)/shard_map/ppermute | solution.py:276
  119.3 0.7 copy-start.13
  120.0 12.9 %collective-permute-start.17 = (f32[128,512]{1,0:T(8,128)}, f32[128,512]{1,0:T(8,128)}, u32[]{:S(2)}, u32[]{:S(2)}) collective-permute-start(f32[128,512]{1,0:T(8,128)} %add.107.refs_4_), channel_id=1, source_target_pairs={{0,64},{32,96},{64,128},{96,160},{128,192},{160,224},{192,0},{224,... | collective-permute-start | bytes 786440 | tf_op jit(solution)/shard_map/ppermute | solution.py:276
  126.6 6.3 %copy-start.4 = (f32[16,64,512]{2,1,0:T(8,128)S(1)}, f32[16,64,512]{2,1,0:T(8,128)}, u32[]{:S(2)}) copy-start(f32[16,64,512]{2,1,0:T(8,128)} %param.10) | copy-start | bytes 6291460
  126.6 6.3 %copy-start.8 = (f32[128,512]{1,0:T(8,128)S(1)}, f32[128,512]{1,0:T(8,128)}, u32[]{:S(2)}) copy-start(f32[128,512]{1,0:T(8,128)} %copy-done.7) | copy-start | bytes 786436
  126.6 6.3 %copy-start.10 = (f32[128,512]{1,0:T(8,128)S(1)}, f32[128,512]{1,0:T(8,128)}, u32[]{:S(2)}) copy-start(f32[128,512]{1,0:T(8,128)} %copy-done.9) | copy-start | bytes 786436
  126.7 6.3 %copy-start.12 = (f32[128,512]{1,0:T(8,128)S(1)}, f32[128,512]{1,0:T(8,128)}, u32[]{:S(2)}) copy-start(f32[128,512]{1,0:T(8,128)} %copy-done.11) | copy-start | bytes 786436
  126.7 6.3 %copy-start.14 = (f32[128,512]{1,0:T(8,128)S(1)}, f32[128,512]{1,0:T(8,128)}, u32[]{:S(2)}) copy-start(f32[128,512]{1,0:T(8,128)} %copy-done.13) | copy-start | bytes 786436
  137.2 36.3 %collective-permute-start.18 = (f32[512,512]{1,0:T(8,128)}, f32[512,512]{1,0:T(8,128)}, u32[]{:S(2)}, u32[]{:S(2)}) collective-permute-start(f32[512,512]{1,0:T(8,128)} %get-tuple-element.47.hi), channel_id=1, source_target_pairs={{0,1},{1,2},{2,3},{3,4},{4,5},{5,6},{6,7},{7,8},{8,9},{9,10},{10,1... | collective-permute-start | bytes 3145736 | tf_op jit(solution)/shard_map/ppermute | solution.py:276
  139.1 34.4 %collective-permute-start.19 = (f32[512,512]{1,0:T(8,128)}, f32[512,512]{1,0:T(8,128)}, u32[]{:S(2)}, u32[]{:S(2)}) collective-permute-start(f32[512,512]{1,0:T(8,128)} %get-tuple-element.48.lo), channel_id=1, source_target_pairs={{1,0},{2,1},{3,2},{4,3},{5,4},{6,5},{7,6},{8,7},{9,8},{10,9},{11,1... | collective-permute-start | bytes 3145736 | tf_op jit(solution)/shard_map/ppermute | solution.py:276
  150.0 1.3 copy-start.5
  173.5 1.6 copy-start.6

commit v7 on v5

--- a/solution.py
+++ b/solution.py
@@ -82,19 +82,18 @@
 
 
 def halo_planes(left, right, kz, y, z, ny, own, entry_left, entry_right):
-    per = left[0].shape[0] // ny
-    side = per * len(left)
+    side = left.shape[0] // ny
     taps = [kz[d] for d in range(BAND_MAX + 1)]
 
     def step(row, columns):
-        e = [entry_left(left[q // per][pl.ds(q % per * ny + row, 8), columns]) for q in range(side)]
+        e = [entry_left(left[pl.ds(q * ny + row, 8), columns]) for q in range(side)]
         for p in range(side):
             rows = pl.ds(p * ny + row, 8)
             total = own(y[rows, columns])
             for q in range(max(0, p + side - BAND_MAX), side):
                 total += taps[p + side - q] * e[q]
             z[rows, columns] = total
-        e = [entry_right(right[q // per][pl.ds(q % per * ny + row, 8), columns]) for q in range(side)]
+        e = [entry_right(right[pl.ds(q * ny + row, 8), columns]) for q in range(side)]
         for p in range(side):
             rows = pl.ds((side + p) * ny + row, 8)
             total = own(y[rows, columns])
@@ -102,7 +101,7 @@
                 total += taps[side + q - p] * e[q]
             z[rows, columns] = total
 
-    tile_loop(ny, left[0].shape[1], step)
+    tile_loop(ny, left.shape[1], step)
 
 
 def tile(value):
@@ -141,8 +140,8 @@
 def log_halos(where, kz, left, right, y, stats, z, scale, ny):
     has_left, has_right = where[0] > 0, where[1] > 0
     m_own = stats[2:3, 0:1]
-    m_left = jnp.where(has_left, functools.reduce(jnp.maximum, [peak(ref[...]) for ref in left]), m_own)
-    m_right = jnp.where(has_right, functools.reduce(jnp.maximum, [peak(ref[...]) for ref in right]), m_own)
+    m_left = jnp.where(has_left, peak(left[...]), m_own)
+    m_right = jnp.where(has_right, peak(right[...]), m_own)
     c = jnp.maximum(m_own, jnp.maximum(m_left, m_right))
     scale[...] = rows_of([c, stats[0:1, 0:1], stats[1:2, 0:1], m_left, m_right, c, c, c])
     own = tile(jnp.exp(m_own - c))
@@ -161,9 +160,9 @@
 
 
 def potential_kernel(
-    where, kz, left0, left1, right0, right1, y, stats, density, kyh, kyl, kxh, kxl, lo, hi, z, mid, scale, *, ny
+    where, kz, left, right, y, stats, density, kyh, kyl, kxh, kxl, lo, hi, z, mid, scale, *, ny
 ):
-    log_halos(where, kz, (left0, left1), (right0, right1), y, stats, z, scale, ny)
+    log_halos(where, kz, left, right, y, stats, z, scale, ny)
     half = mid.shape[0]
     for g, out in enumerate((lo, hi)):
         first = rows_and_columns(z, g, kyh, kyl, kxh, kxl, mid)
@@ -171,7 +170,7 @@
 
 
 def second_kernel(where, kz, left, right, y, stats, kyh, kyl, kxh, kxl, out, scale, z, mid, *, ny):
-    log_halos(where, kz, (left,), (right,), y, stats, z, scale, ny)
+    log_halos(where, kz, left, right, y, stats, z, scale, ny)
     half = mid.shape[0]
     for g in range(2):
         out[g * half : (g + 1) * half, :] = rows_and_columns(z, g, kyh, kyl, kxh, kxl, mid)
@@ -229,8 +228,8 @@
         f_right = tile(jnp.exp((c - stats[4:5, 0:1]) * 0.5))
         has_left, has_right = where[0] > 0, where[1] > 0
         halo_planes(
-            (left,),
-            (right,),
+            left,
+            right,
             kz,
             y,
             z,
@@ -312,9 +311,8 @@
     )(band)
     prior = prior_log_scaling.reshape(rows, nx)
     prior_lo, prior_hi = prior[:half], prior[half:]
-    piece = half // 2
-    from_left = [send(prior_hi[k * piece : (k + 1) * piece], "slab", to_right) for k in range(2)]
-    from_right = [send(prior_lo[k * piece : (k + 1) * piece], "slab", to_left) for k in range(2)]
+    from_left = send(prior_hi, "slab", to_right)
+    from_right = send(prior_lo, "slab", to_left)
 
     where = jnp.stack([slab_at > 0, slab_at < slabs - 1]).astype(jnp.int32)
     slot = lax.dynamic_slice_in_dim(slot_atom_index, atom_at, 1)
@@ -339,20 +337,20 @@
     swapped = send(part, "atom", swap)
     pot_lo, pot_hi = pl.pallas_call(
         functools.partial(potential_kernel, ny=ny),
-        in_specs=[smem, smem] + [vmem] * 11,
+        in_specs=[smem, smem] + [vmem] * 9,
         out_specs=[vmem, vmem],
         out_shape=[shape(half, nx), shape(half, nx)],
         scratch_shapes=[*scratch, scale],
         compiler_params=params,
         name="potential",
-    )(where, kz, *from_left, *from_right, y, stats, atom_log_density.reshape(rows, nx), *tables)
+    )(where, kz, from_left, from_right, y, stats, atom_log_density.reshape(rows, nx), *tables)
 
     from_left = send(pot_hi, "slab", to_right)
     from_right = send(pot_lo, "slab", to_left)
     both = part + swapped
+    own_at, both = in_order((pot_lo, both))
     sums = [both] + [send(both, "atom", ahead[across - k]) for k in range(1, across)]
-    y, stats = own_log(kz, pot_lo, pot_hi)
-    y, sums[1] = in_order((y, sums[1]))
+    y, stats = own_log(kz, own_at, pot_hi)
     second, stats = pl.pallas_call(
         functools.partial(second_kernel, ny=ny),
         in_specs=[smem, smem] + [vmem] * 8,

time: 159 us -> 149 us (0.937)
  starting transfers between devices: 69.9 us -> 56.1 us
  waiting for transfers between devices: 35.4 us -> 38.7 us
    ppermute x25 -> x23, starting transfers between devices: 69.9 us -> 56.1 us  [send(): return lax.ppermute(value, axis, pairs)]
    ppermute x25 -> x23, waiting for transfers between devices: 35.4 us -> 38.7 us  [send(): return lax.ppermute(value, axis, pairs)]
    slice x1, local copies, waits for them, and re-layouts: 1.6 us -> 3.26 us  [body(): prior_lo, prior_hi = (prior[:half], prior[half:])]
    unnamed x22 -> x16, local copies, waits for them, and re-layouts: 3.27 us -> 2.92 us
  transfers between devices with their start and end apart: 25 -> 23, of which waited for: 8 -> 10; matrix products, arithmetic and copies ran while one was open for 6% -> 5% of each run, Pallas kernels for 20% -> 22%
where the time goes in v7:
time: 149 us; the launch traced here: 146 us
  starting transfers between devices  56.1 us (38%)
  waiting for transfers between devices  38.7 us (26%)
  Pallas kernels  36 us (24%)
  local copies, waits for them, and re-layouts  8.54 us (6%)
  other arithmetic  5.76 us (4%)
    ppermute x23, starting transfers between devices, send(): return lax.ppermute(value, axis, pairs)  56.1 us
    ppermute x23, waiting for transfers between devices, send(): return lax.ppermute(value, axis, pairs)  38.7 us
    pallas_call x1, Pallas kernels, body(): pl.pallas_call(functools.partial(potential_kernel, ny=ny), in_specs=[smem...  7.1 us
    pallas_call x1, Pallas kernels, body(): pl.pallas_call(functools.partial(second_kernel, ny=ny), in_specs=[smem, s...  6.19 us
    pallas_call x1, Pallas kernels, body(): pl.pallas_call(functools.partial(gradient_kernel, ny=ny), grid=(2,), in_s...  6.12 us
    pallas_call x1, Pallas kernels, body(): pl.pallas_call(functools.partial(own_linear_kernel, ny=ny), in_specs=[sme...  3.96 us
    pallas_call x1, Pallas kernels, body(): y, stats = own_log(kz, prior_lo, prior_hi)  3.92 us
    pallas_call x1, Pallas kernels, body(): y, stats = own_log(kz, own_at, pot_hi)  3.91 us
  transfers between devices with their start and end apart: 23, of which 10 were waited for; matrix products, arithmetic and copies ran while one was open for 5% of the time, Pallas kernels for 22%

profile of v7, /device:TPU:10, one launch (start us, length us, event | category | flops | bytes accessed | tf_op | source)
XLA Modules:
  0.0 146.0 jit_solution(6369735226461245046)
XLA Ops:
  0.6 3.3 %fusion.1 = (f32[1,8,64,512]{3,2,1,0:T(8,128)}, f32[1,8,64,512]{3,2,1,0:T(8,128)}) fusion(f32[1,16,64,512]{3,2,1,0:T(8,128)} %param.8), kind=kLoop, calls=%fused_computation.12 | loop fusion | bytes 4194304 | tf_op jit(solution)/shard_map/slice | solution.py:313
  3.9 2.0 %collective-permute-start = (f32[512,512]{1,0:T(8,128)}, f32[512,512]{1,0:T(8,128)}, u32[]{:S(2)}, u32[]{:S(2)}) collective-permute-start(f32[512,512]{1,0:T(8,128)} %bitcast.6.hi), channel_id=1, source_target_pairs={{0,1},{1,2},{2,3},{3,4},{4,5},{5,6},{6,7},{7,8},{8,9},{9,10},{10,1... | collective-permute-start | bytes 3145736 | tf_op jit(solution)/shard_map/ppermute | solution.py:279
  6.0 6.3 %collective-permute-start.1 = (f32[512,512]{1,0:T(8,128)}, f32[512,512]{1,0:T(8,128)}, u32[]{:S(2)}, u32[]{:S(2)}) collective-permute-start(f32[512,512]{1,0:T(8,128)} %bitcast.7.lo), channel_id=1, source_target_pairs={{1,0},{2,1},{3,2},{4,3},{5,4},{6,5},{7,6},{8,7},{9,8},{10,9},{11,1... | collective-permute-start | bytes 3145736 | tf_op jit(solution)/shard_map/ppermute | solution.py:279
  12.4 1.2 constant_dynamic-slice_fusion.2
  13.6 0.5 collective-permute-start.4
  14.1 2.4 %collective-permute-start.3 = (f32[256,512]{1,0:T(8,128)}, f32[256,512]{1,0:T(8,128)}, u32[]{:S(2)}, u32[]{:S(2)}) collective-permute-start(f32[256,512]{1,0:T(8,128)} %get-tuple-element.56), channel_id=1, source_target_pairs={{0,128},{32,160},{64,192},{96,224},{128,0},{160,32},{192,64},{224,... | collective-permute-start | bytes 1572872 | tf_op jit(solution)/shard_map/ppermute | solution.py:279
  16.5 1.8 %collective-permute-start.2 = (f32[256,512]{1,0:T(8,128)}, f32[256,512]{1,0:T(8,128)}, u32[]{:S(2)}, u32[]{:S(2)}) collective-permute-start(f32[256,512]{1,0:T(8,128)} %get-tuple-element.54), channel_id=1, source_target_pairs={{0,64},{32,96},{64,128},{96,160},{128,192},{160,224},{192,0},{224,... | collective-permute-start | bytes 1572872 | tf_op jit(solution)/shard_map/ppermute | solution.py:279
  18.3 0.6 slice.18
  18.9 1.1 tables.1
  20.0 0.7 compare_select_fusion.1.kz
  20.7 3.9 %own_log.2 = (f32[1024,512]{1,0:T(8,128)S(1)}, f32[8,128]{1,0:T(8,128)S(1)}) custom-call(f32[9]{0:T(128)S(1)} %compare_select_fusion.1.kz, f32[512,512]{1,0:T(8,128)} %bitcast.7.lo, f32[512,512]{1,0:T(8,128)} %bitcast.6.hi), custom_call_target="tpu_custom_call" | custom-call | tf_op jit(solution)/shard_map/own_log/pallas_call | solution.py:335
  24.6 0.0 copy-start.2
  24.6 1.3 copy-done.2
  25.9 0.1 add_convert_fusion.where
  26.0 1.8 %collective-permute-done.4 = f32[256,512]{1,0:T(8,128)} collective-permute-done((f32[256,512]{1,0:T(8,128)}, f32[256,512]{1,0:T(8,128)}, u32[]{:S(2)}, u32[]{:S(2)}) %collective-permute-start.4) | collective-permute-done | bytes 524320 | tf_op jit(solution)/shard_map/ppermute | solution.py:279
  27.8 9.7 %collective-permute-done.3 = f32[256,512]{1,0:T(8,128)} collective-permute-done((f32[256,512]{1,0:T(8,128)}, f32[256,512]{1,0:T(8,128)}, u32[]{:S(2)}, u32[]{:S(2)}) %collective-permute-start.3) | collective-permute-done | bytes 524320 | tf_op jit(solution)/shard_map/ppermute | solution.py:279
  37.5 0.9 collective-permute-done.2
  38.4 1.6 %add_add_fusion = f32[256,512]{1,0:T(8,128)S(1)} fusion(f32[256,512]{1,0:T(8,128)} %collective-permute-done.4, f32[256,512]{1,0:T(8,128)} %collective-permute-done.3, f32[256,512]{1,0:T(8,128)} %collective-permute-done.2, f32[1024,512]{1,0:T(8,128)S(1)} %bitcast.15, s32[]{:T(128)S(6)} %select_n.27), kind=kLoop, calls=%fused_computation | loop fusion | flops 393216 | bytes 2621444 | tf_op jit(solution)/shard_map/add | solution.py:298
  39.9 6.4 %collective-permute-start.7 = (f32[256,512]{1,0:T(8,128)S(1)}, f32[256,512]{1,0:T(8,128)S(1)}, u32[]{:S(2)}, u32[]{:S(2)}) collective-permute-start(f32[256,512]{1,0:T(8,128)S(1)} %add_add_fusion), channel_id=1, source_target_pairs={{0,32},{32,0},{64,96},{96,64},{128,160},{160,128},{192,224},{224,1... | collective-permute-start | bytes 1572872 | tf_op jit(solution)/shard_map/ppermute | solution.py:279
  46.3 0.0 collective-permute-done.left
  46.3 0.0 copy-start.3
  46.4 1.6 %copy-done.3 = f32[1024,512]{1,0:T(8,128)S(1)} copy-done((f32[1024,512]{1,0:T(8,128)S(1)}, f32[1024,512]{1,0:T(8,128)}, u32[]{:S(2)}) %copy-start.3) | copy-done | bytes 2097176
  47.9 7.1 %potential.1 = (f32[512,512]{1,0:T(8,128)}, f32[512,512]{1,0:T(8,128)}) custom-call(s32[2]{0:T(128)S(1)} %add_convert_fusion.where, f32[9]{0:T(128)S(1)} %compare_select_fusion.1.kz, f32[512,512]{1,0:T(8,128)} %collective-permute-done.left, f32[512,512]{1,0:T(8,128)} %collective-permute-done.1.right, f32[1024,512]{1,0:T(8,128)S(1)} %copy-done.3, ...), custom_call_target="tpu_custom_call" | custom-call | tf_op jit(solution)/shard_map/potential/pallas_call | solution.py:338
  55.0 1.9 %collective-permute-start.5 = (f32[512,512]{1,0:T(8,128)}, f32[512,512]{1,0:T(8,128)}, u32[]{:S(2)}, u32[]{:S(2)}) collective-permute-start(f32[512,512]{1,0:T(8,128)} %get-tuple-element.35.hi.pot_hi), channel_id=1, source_target_pairs={{0,1},{1,2},{2,3},{3,4},{4,5},{5,6},{6,7},{7,8},{8,9},{9,10},{10,1... | collective-permute-start | bytes 3145736 | tf_op jit(solution)/shard_map/ppermute | solution.py:279
  57.0 6.3 %collective-permute-start.6 = (f32[512,512]{1,0:T(8,128)}, f32[512,512]{1,0:T(8,128)}, u32[]{:S(2)}, u32[]{:S(2)}) collective-permute-start(f32[512,512]{1,0:T(8,128)} %get-tuple-element.38.lo.pot_lo), channel_id=1, source_target_pairs={{1,0},{2,1},{3,2},{4,3},{5,4},{6,5},{7,6},{8,7},{9,8},{10,9},{11,1... | collective-permute-start | bytes 3145736 | tf_op jit(solution)/shard_map/ppermute | solution.py:279
  63.3 4.7 %collective-permute-done.7 = f32[256,512]{1,0:T(8,128)S(1)} collective-permute-done((f32[256,512]{1,0:T(8,128)S(1)}, f32[256,512]{1,0:T(8,128)S(1)}, u32[]{:S(2)}, u32[]{:S(2)}) %collective-permute-start.7) | collective-permute-done | bytes 524320 | tf_op jit(solution)/shard_map/ppermute | solution.py:279
  68.0 0.9 add.78.sum0
  68.9 4.5 %collective-permute-start.8 = (f32[256,512]{1,0:T(8,128)}, f32[256,512]{1,0:T(8,128)}, u32[]{:S(2)}, u32[]{:S(2)}) collective-permute-start(f32[256,512]{1,0:T(8,128)} %add.78.sum0), channel_id=1, source_target_pairs={{0,192},{32,224},{64,0},{96,32},{128,64},{160,96},{192,128},{224,1... | collective-permute-start | bytes 1572872 | tf_op jit(solution)/shard_map/ppermute | solution.py:279
  73.4 0.2 collective-permute-start.9
  73.6 1.3 collective-permute-start.10
  74.8 0.6 dynamic_slice.15
  75.4 0.7 pad_add_fusion.at
  76.1 1.3 fusion
  77.5 3.9 %own_log.3 = (f32[1024,512]{1,0:T(8,128)S(1)}, f32[8,128]{1,0:T(8,128)S(1)}) custom-call(f32[9]{0:T(128)S(1)} %compare_select_fusion.1.kz, f32[512,512]{1,0:T(8,128)} %get-tuple-element.38.lo.pot_lo, f32[512,512]{1,0:T(8,128)} %get-tuple-element.35.hi.pot_hi), custom_call_target="tpu_custom_call" | custom-call | tf_op jit(solution)/shard_map/own_log/pallas_call | solution.py:353
  81.4 10.1 %collective-permute-done.5.left = f32[512,512]{1,0:T(8,128)} collective-permute-done((f32[512,512]{1,0:T(8,128)}, f32[512,512]{1,0:T(8,128)}, u32[]{:S(2)}, u32[]{:S(2)}) %collective-permute-start.5) | collective-permute-done | bytes 1048608 | tf_op jit(solution)/shard_map/ppermute | solution.py:279
  91.5 0.0 collective-permute-done.6.right
  91.5 6.2 %second.1 = (f32[1024,512]{1,0:T(8,128)S(1)}, f32[8,128]{1,0:T(8,128)S(1)}) custom-call(s32[2]{0:T(128)S(1)} %add_convert_fusion.where, f32[9]{0:T(128)S(1)} %compare_select_fusion.1.kz, f32[512,512]{1,0:T(8,128)} %collective-permute-done.5.left, f32[512,512]{1,0:T(8,128)} %collective-permute-done.6.right, f32[1024,512]{1,0:T(8,128)S(1)} %get-tuple-element.39.y, ...), custom_call_target="tpu_custom_call" | custom-call | tf_op jit(solution)/shard_map/second/pallas_call | solution.py:354
  97.7 0.0 collective-permute-done.8.sum1
  97.7 3.7 %ratio.1 = (f32[512,512]{1,0:T(8,128)S(1)}, f32[512,512]{1,0:T(8,128)S(1)}, f32[8,128]{1,0:T(8,128)S(1)}) custom-call(s32[2]{0:T(128)S(1)} %pad_add_fusion.at, f32[1]{0:T(128)} %bitcast.5.weight, f32[1024,512]{1,0:T(8,128)S(1)} %get-tuple-element.41.second, f32[8,128]{1,0:T(8,128)S(1)} %get-tuple-element.42.scale.stats, f32[1024,512]{1,0:T(8,128)S(1)} %bitcast.18, ...), custom_call_target="tpu_custom_call" | custom-call | tf_op jit(solution)/shard_map/ratio/pallas_call | solution.py:363
  101.5 2.6 %collective-permute-start.20 = (f32[512,512]{1,0:T(8,128)S(1)}, f32[512,512]{1,0:T(8,128)S(1)}, u32[]{:S(2)}, u32[]{:S(2)}) collective-permute-start(f32[512,512]{1,0:T(8,128)S(1)} %get-tuple-element.46.hi), channel_id=1, source_target_pairs={{0,1},{1,2},{2,3},{3,4},{4,5},{5,6},{6,7},{7,8},{8,9},{9,10},{10,1... | collective-permute-start | bytes 3145736 | tf_op jit(solution)/shard_map/ppermute | solution.py:279
  104.1 5.6 %collective-permute-start.21 = (f32[512,512]{1,0:T(8,128)S(1)}, f32[512,512]{1,0:T(8,128)S(1)}, u32[]{:S(2)}, u32[]{:S(2)}) collective-permute-start(f32[512,512]{1,0:T(8,128)S(1)} %get-tuple-element.45.lo), channel_id=1, source_target_pairs={{1,0},{2,1},{3,2},{4,3},{5,4},{6,5},{7,6},{8,7},{9,8},{10,9},{11,1... | collective-permute-start | bytes 3145736 | tf_op jit(solution)/shard_map/ppermute | solution.py:279
  109.7 0.1 collective-permute-start.11
  109.8 1.2 collective-permute-done.11
  111.0 3.7 %collective-permute-start.14 = (f32[8,128]{1,0:T(8,128)S(1)}, f32[8,128]{1,0:T(8,128)S(1)}, u32[]{:S(2)}, u32[]{:S(2)}) collective-permute-start(f32[8,128]{1,0:T(8,128)S(1)} %add.79), channel_id=1, source_target_pairs={{0,192},{32,224},{64,0},{96,32},{128,64},{160,96},{192,128},{224,1... | collective-permute-start | bytes 12296 | tf_op jit(solution)/shard_map/ppermute | solution.py:279
  114.7 0.2 collective-permute-start.13
  114.9 1.3 collective-permute-start.12
  116.1 4.0 %own_linear.1 = (f32[1024,512]{1,0:T(8,128)S(1)}, f32[1024,512]{1,0:T(8,128)S(1)}) custom-call(f32[9]{0:T(128)S(1)} %compare_select_fusion.1.kz, f32[512,512]{1,0:T(8,128)S(1)} %get-tuple-element.45.lo, f32[512,512]{1,0:T(8,128)S(1)} %get-tuple-element.46.hi, f32[512,512]{1,0:T(8,128)} %get-tuple-element.38.lo.pot_lo, ...), custom_call_target="tpu_custom_call" | custom-call | tf_op jit(solution)/shard_map/own_linear/pallas_call | solution.py:387
  120.1 0.0 collective-permute-done.14
  120.1 0.0 collective-permute-done.12
  120.1 0.1 collective-permute-start.17
  120.2 3.0 %collective-permute-start.16 = (f32[8,128]{1,0:T(8,128)S(1)}, f32[8,128]{1,0:T(8,128)S(1)}, u32[]{:S(2)}, u32[]{:S(2)}) collective-permute-start(f32[8,128]{1,0:T(8,128)S(1)} %add_add_fusion.2), channel_id=1, source_target_pairs={{0,16},{1,17},{2,18},{3,19},{4,20},{5,21},{6,22},{7,23},{8,24},{9,... | collective-permute-start | bytes 12296 | tf_op jit(solution)/shard_map/ppermute | solution.py:279
  123.3 2.1 %collective-permute-start.15 = (f32[8,128]{1,0:T(8,128)S(1)}, f32[8,128]{1,0:T(8,128)S(1)}, u32[]{:S(2)}, u32[]{:S(2)}) collective-permute-start(f32[8,128]{1,0:T(8,128)S(1)} %add_add_fusion.2), channel_id=1, source_target_pairs={{0,8},{1,9},{2,10},{3,11},{4,12},{5,13},{6,14},{7,15},{8,16},{9,17... | collective-permute-start | bytes 12296 | tf_op jit(solution)/shard_map/ppermute | solution.py:279
  125.4 0.1 collective-permute-done.16
  125.4 1.5 %collective-permute-done.15 = f32[8,128]{1,0:T(8,128)S(1)} collective-permute-done((f32[8,128]{1,0:T(8,128)S(1)}, f32[8,128]{1,0:T(8,128)S(1)}, u32[]{:S(2)}, u32[]{:S(2)}) %collective-permute-start.15) | collective-permute-done | bytes 4128 | tf_op jit(solution)/shard_map/ppermute | solution.py:279
  126.9 0.0 collective-permute-start.18
  126.9 4.8 %collective-permute-done.18 = f32[8,128]{1,0:T(8,128)S(1)} collective-permute-done((f32[8,128]{1,0:T(8,128)S(1)}, f32[8,128]{1,0:T(8,128)S(1)}, u32[]{:S(2)}, u32[]{:S(2)}) %collective-permute-start.18) | collective-permute-done | bytes 4128 | tf_op jit(solution)/shard_map/ppermute | solution.py:279
  131.7 0.6 collective-permute-start.19
  132.3 4.0 %collective-permute-done.19 = f32[8,128]{1,0:T(8,128)S(1)} collective-permute-done((f32[8,128]{1,0:T(8,128)S(1)}, f32[8,128]{1,0:T(8,128)S(1)}, u32[]{:S(2)}, u32[]{:S(2)}) %collective-permute-start.19) | collective-permute-done | bytes 4128 | tf_op jit(solution)/shard_map/ppermute | solution.py:279
  136.2 0.0 collective-permute-done.20.left
  136.2 0.0 collective-permute-done.21.right
  136.3 3.1 %collective-permute-start.22 = (f32[8,128]{1,0:T(8,128)S(1)}, f32[8,128]{1,0:T(8,128)S(1)}, u32[]{:S(2)}, u32[]{:S(2)}) collective-permute-start(f32[8,128]{1,0:T(8,128)S(1)} %add.87), channel_id=1, source_target_pairs={{0,32},{32,0},{64,96},{96,64},{128,160},{160,128},{192,224},{224,1... | collective-permute-start | bytes 12296 | tf_op jit(solution)/shard_map/ppermute | solution.py:279
  139.4 6.1 %gradient.1 = f32[1024,512]{1,0:T(8,128)} custom-call(s32[2]{0:T(128)S(1)} %add_convert_fusion.where, f32[9]{0:T(128)S(1)} %compare_select_fusion.1.kz, f32[512,512]{1,0:T(8,128)S(1)} %collective-permute-done.20.left, f32[512,512]{1,0:T(8,128)S(1)} %collective-permute-done.21.right, f32[1024,512]{1,0:T(8,128)S(1)} %get-tuple-element.51.y, ...), custom_call_target="tpu_custom_call" | custom-call | tf_op jit(solution)/shard_map/gradient/pallas_call | solution.py:412
  145.5 0.0 collective-permute-done.22
  145.5 0.5 multiply_bitcast_fusion
  (23 shorter events, 0.1 us)
Async XLA Ops:
  0.6 11.7 %copy-start = (f32[1,16,64,512]{3,2,1,0:T(8,128)S(1)}, f32[1,16,64,512]{3,2,1,0:T(8,128)}, u32[]{:S(2)}) copy-start(f32[1,16,64,512]{3,2,1,0:T(8,128)} %param.9) | copy-start | bytes 6291460
  3.9 14.4 %copy-start.5 = (s32[3]{0:T(128)S(1)}, s32[3]{0:T(128)}, u32[]{:S(2)}) copy-start(s32[3]{0:T(128)} %band.1) | copy-start | bytes 40
  3.9 42.4 %collective-permute-start = (f32[512,512]{1,0:T(8,128)}, f32[512,512]{1,0:T(8,128)}, u32[]{:S(2)}, u32[]{:S(2)}) collective-permute-start(f32[512,512]{1,0:T(8,128)} %bitcast.6.hi), channel_id=1, source_target_pairs={{0,1},{1,2},{2,3},{3,4},{4,5},{5,6},{6,7},{7,8},{8,9},{9,10},{10,1... | collective-permute-start | bytes 3145736 | tf_op jit(solution)/shard_map/ppermute | solution.py:279
  6.0 40.4 %collective-permute-start.1 = (f32[512,512]{1,0:T(8,128)}, f32[512,512]{1,0:T(8,128)}, u32[]{:S(2)}, u32[]{:S(2)}) collective-permute-start(f32[512,512]{1,0:T(8,128)} %bitcast.7.lo), channel_id=1, source_target_pairs={{1,0},{2,1},{3,2},{4,3},{5,4},{6,5},{7,6},{8,7},{9,8},{10,9},{11,1... | collective-permute-start | bytes 3145736 | tf_op jit(solution)/shard_map/ppermute | solution.py:279
  13.6 14.2 %collective-permute-start.4 = (f32[256,512]{1,0:T(8,128)}, f32[256,512]{1,0:T(8,128)}, u32[]{:S(2)}, u32[]{:S(2)}) collective-permute-start(f32[256,512]{1,0:T(8,128)} %get-tuple-element.55), channel_id=1, source_target_pairs={{0,192},{32,224},{64,0},{96,32},{128,64},{160,96},{192,128},{224,1... | collective-permute-start | bytes 1572872 | tf_op jit(solution)/shard_map/ppermute | solution.py:279
  14.1 23.4 %collective-permute-start.3 = (f32[256,512]{1,0:T(8,128)}, f32[256,512]{1,0:T(8,128)}, u32[]{:S(2)}, u32[]{:S(2)}) collective-permute-start(f32[256,512]{1,0:T(8,128)} %get-tuple-element.56), channel_id=1, source_target_pairs={{0,128},{32,160},{64,192},{96,224},{128,0},{160,32},{192,64},{224,... | collective-permute-start | bytes 1572872 | tf_op jit(solution)/shard_map/ppermute | solution.py:279
  16.5 21.9 %collective-permute-start.2 = (f32[256,512]{1,0:T(8,128)}, f32[256,512]{1,0:T(8,128)}, u32[]{:S(2)}, u32[]{:S(2)}) collective-permute-start(f32[256,512]{1,0:T(8,128)} %get-tuple-element.54), channel_id=1, source_target_pairs={{0,64},{32,96},{64,128},{96,160},{128,192},{160,224},{192,0},{224,... | collective-permute-start | bytes 1572872 | tf_op jit(solution)/shard_map/ppermute | solution.py:279
  24.6 1.3 copy-start.2
  25.9 20.4 %copy-start.1 = (f32[1,16,64,512]{3,2,1,0:T(8,128)S(1)}, f32[1,16,64,512]{3,2,1,0:T(8,128)}, u32[]{:S(2)}) copy-start(f32[1,16,64,512]{3,2,1,0:T(8,128)} %param.7) | copy-start | bytes 6291460
  39.9 28.1 %collective-permute-start.7 = (f32[256,512]{1,0:T(8,128)S(1)}, f32[256,512]{1,0:T(8,128)S(1)}, u32[]{:S(2)}, u32[]{:S(2)}) collective-permute-start(f32[256,512]{1,0:T(8,128)S(1)} %add_add_fusion), channel_id=1, source_target_pairs={{0,32},{32,0},{64,96},{96,64},{128,160},{160,128},{192,224},{224,1... | collective-permute-start | bytes 1572872 | tf_op jit(solution)/shard_map/ppermute | solution.py:279
  46.3 1.6 %copy-start.3 = (f32[1024,512]{1,0:T(8,128)S(1)}, f32[1024,512]{1,0:T(8,128)}, u32[]{:S(2)}) copy-start(f32[1024,512]{1,0:T(8,128)} %copy-done.2) | copy-start | bytes 6291460
  47.9 26.9 %copy-start.6 = (s32[8]{0:T(128)S(1)}, s32[8]{0:T(128)}, u32[]{:S(2)}) copy-start(s32[8]{0:T(128)} %param.13) | copy-start | bytes 100
  47.9 28.2 %copy-start.7 = (f32[8]{0:T(128)S(1)}, f32[8]{0:T(128)}, u32[]{:S(2)}) copy-start(f32[8]{0:T(128)} %param.11) | copy-start | bytes 100
  55.0 36.4 %collective-permute-start.5 = (f32[512,512]{1,0:T(8,128)}, f32[512,512]{1,0:T(8,128)}, u32[]{:S(2)}, u32[]{:S(2)}) collective-permute-start(f32[512,512]{1,0:T(8,128)} %get-tuple-element.35.hi.pot_hi), channel_id=1, source_target_pairs={{0,1},{1,2},{2,3},{3,4},{4,5},{5,6},{6,7},{7,8},{8,9},{9,10},{10,1... | collective-permute-start | bytes 3145736 | tf_op jit(solution)/shard_map/ppermute | solution.py:279
  57.0 34.5 %collective-permute-start.6 = (f32[512,512]{1,0:T(8,128)}, f32[512,512]{1,0:T(8,128)}, u32[]{:S(2)}, u32[]{:S(2)}) collective-permute-start(f32[512,512]{1,0:T(8,128)} %get-tuple-element.38.lo.pot_lo), channel_id=1, source_target_pairs={{1,0},{2,1},{3,2},{4,3},{5,4},{6,5},{7,6},{8,7},{9,8},{10,9},{11,1... | collective-permute-start | bytes 3145736 | tf_op jit(solution)/shard_map/ppermute | solution.py:279
  68.9 28.8 %collective-permute-start.8 = (f32[256,512]{1,0:T(8,128)}, f32[256,512]{1,0:T(8,128)}, u32[]{:S(2)}, u32[]{:S(2)}) collective-permute-start(f32[256,512]{1,0:T(8,128)} %add.78.sum0), channel_id=1, source_target_pairs={{0,192},{32,224},{64,0},{96,32},{128,64},{160,96},{192,128},{224,1... | collective-permute-start | bytes 1572872 | tf_op jit(solution)/shard_map/ppermute | solution.py:279
  73.4 24.3 %collective-permute-start.9 = (f32[256,512]{1,0:T(8,128)}, f32[256,512]{1,0:T(8,128)}, u32[]{:S(2)}, u32[]{:S(2)}) collective-permute-start(f32[256,512]{1,0:T(8,128)} %add.78.sum0), channel_id=1, source_target_pairs={{0,128},{32,160},{64,192},{96,224},{128,0},{160,32},{192,64},{224,... | collective-permute-start | bytes 1572872 | tf_op jit(solution)/shard_map/ppermute | solution.py:279
  73.6 24.1 %collective-permute-start.10 = (f32[256,512]{1,0:T(8,128)}, f32[256,512]{1,0:T(8,128)}, u32[]{:S(2)}, u32[]{:S(2)}) collective-permute-start(f32[256,512]{1,0:T(8,128)} %add.78.sum0), channel_id=1, source_target_pairs={{0,64},{32,96},{64,128},{96,160},{128,192},{160,224},{192,0},{224,... | collective-permute-start | bytes 1572872 | tf_op jit(solution)/shard_map/ppermute | solution.py:279
  91.5 6.2 %copy-start.4 = (f32[16,64,512]{2,1,0:T(8,128)S(1)}, f32[16,64,512]{2,1,0:T(8,128)}, u32[]{:S(2)}) copy-start(f32[16,64,512]{2,1,0:T(8,128)} %param.10) | copy-start | bytes 6291460
  101.5 34.8 %collective-permute-start.20 = (f32[512,512]{1,0:T(8,128)S(1)}, f32[512,512]{1,0:T(8,128)S(1)}, u32[]{:S(2)}, u32[]{:S(2)}) collective-permute-start(f32[512,512]{1,0:T(8,128)S(1)} %get-tuple-element.46.hi), channel_id=1, source_target_pairs={{0,1},{1,2},{2,3},{3,4},{4,5},{5,6},{6,7},{7,8},{8,9},{9,10},{10,1... | collective-permute-start | bytes 3145736 | tf_op jit(solution)/shard_map/ppermute | solution.py:279
  104.1 32.1 %collective-permute-start.21 = (f32[512,512]{1,0:T(8,128)S(1)}, f32[512,512]{1,0:T(8,128)S(1)}, u32[]{:S(2)}, u32[]{:S(2)}) collective-permute-start(f32[512,512]{1,0:T(8,128)S(1)} %get-tuple-element.45.lo), channel_id=1, source_target_pairs={{1,0},{2,1},{3,2},{4,3},{5,4},{6,5},{7,6},{8,7},{9,8},{10,9},{11,1... | collective-permute-start | bytes 3145736 | tf_op jit(solution)/shard_map/ppermute | solution.py:279
  109.7 1.3 collective-permute-start.11
  111.0 9.1 %collective-permute-start.14 = (f32[8,128]{1,0:T(8,128)S(1)}, f32[8,128]{1,0:T(8,128)S(1)}, u32[]{:S(2)}, u32[]{:S(2)}) collective-permute-start(f32[8,128]{1,0:T(8,128)S(1)} %add.79), channel_id=1, source_target_pairs={{0,192},{32,224},{64,0},{96,32},{128,64},{160,96},{192,128},{224,1... | collective-permute-start | bytes 12296 | tf_op jit(solution)/shard_map/ppermute | solution.py:279
  114.7 5.4 %collective-permute-start.13 = (f32[8,128]{1,0:T(8,128)S(1)}, f32[8,128]{1,0:T(8,128)S(1)}, u32[]{:S(2)}, u32[]{:S(2)}) collective-permute-start(f32[8,128]{1,0:T(8,128)S(1)} %add.79), channel_id=1, source_target_pairs={{0,128},{32,160},{64,192},{96,224},{128,0},{160,32},{192,64},{224,... | collective-permute-start | bytes 12296 | tf_op jit(solution)/shard_map/ppermute | solution.py:279
  114.9 5.3 %collective-permute-start.12 = (f32[8,128]{1,0:T(8,128)S(1)}, f32[8,128]{1,0:T(8,128)S(1)}, u32[]{:S(2)}, u32[]{:S(2)}) collective-permute-start(f32[8,128]{1,0:T(8,128)S(1)} %add.79), channel_id=1, source_target_pairs={{0,64},{32,96},{64,128},{96,160},{128,192},{160,224},{192,0},{224,... | collective-permute-start | bytes 12296 | tf_op jit(solution)/shard_map/ppermute | solution.py:279
  120.1 5.2 %collective-permute-start.17 = (f32[8,128]{1,0:T(8,128)S(1)}, f32[8,128]{1,0:T(8,128)S(1)}, u32[]{:S(2)}, u32[]{:S(2)}) collective-permute-start(f32[8,128]{1,0:T(8,128)S(1)} %add_add_fusion.2), channel_id=1, source_target_pairs={{0,24},{1,25},{2,26},{3,27},{4,28},{5,29},{6,30},{7,31},{8,0},{9,1... | collective-permute-start | bytes 12296 | tf_op jit(solution)/shard_map/ppermute | solution.py:279
  120.2 5.2 %collective-permute-start.16 = (f32[8,128]{1,0:T(8,128)S(1)}, f32[8,128]{1,0:T(8,128)S(1)}, u32[]{:S(2)}, u32[]{:S(2)}) collective-permute-start(f32[8,128]{1,0:T(8,128)S(1)} %add_add_fusion.2), channel_id=1, source_target_pairs={{0,16},{1,17},{2,18},{3,19},{4,20},{5,21},{6,22},{7,23},{8,24},{9,... | collective-permute-start | bytes 12296 | tf_op jit(solution)/shard_map/ppermute | solution.py:279
  123.3 3.6 %collective-permute-start.15 = (f32[8,128]{1,0:T(8,128)S(1)}, f32[8,128]{1,0:T(8,128)S(1)}, u32[]{:S(2)}, u32[]{:S(2)}) collective-permute-start(f32[8,128]{1,0:T(8,128)S(1)} %add_add_fusion.2), channel_id=1, source_target_pairs={{0,8},{1,9},{2,10},{3,11},{4,12},{5,13},{6,14},{7,15},{8,16},{9,17... | collective-permute-start | bytes 12296 | tf_op jit(solution)/shard_map/ppermute | solution.py:279
  126.9 4.8 %collective-permute-start.18 = (f32[8,128]{1,0:T(8,128)S(1)}, f32[8,128]{1,0:T(8,128)S(1)}, u32[]{:S(2)}, u32[]{:S(2)}) collective-permute-start(f32[8,128]{1,0:T(8,128)S(1)} %add_add_fusion.1), channel_id=1, source_target_pairs={{0,2},{1,3},{2,0},{3,1},{4,6},{5,7},{6,4},{7,5},{8,10},{9,11},{10,... | collective-permute-start | bytes 12296 | tf_op jit(solution)/shard_map/ppermute | solution.py:279
  131.7 4.5 %collective-permute-start.19 = (f32[8,128]{1,0:T(8,128)S(1)}, f32[8,128]{1,0:T(8,128)S(1)}, u32[]{:S(2)}, u32[]{:S(2)}) collective-permute-start(f32[8,128]{1,0:T(8,128)S(1)} %add.86), channel_id=1, source_target_pairs={{0,4},{1,5},{2,6},{3,7},{4,0},{5,1},{6,2},{7,3},{8,12},{9,13},{10,... | collective-permute-start | bytes 12296 | tf_op jit(solution)/shard_map/ppermute | solution.py:279
  136.3 9.2 %collective-permute-start.22 = (f32[8,128]{1,0:T(8,128)S(1)}, f32[8,128]{1,0:T(8,128)S(1)}, u32[]{:S(2)}, u32[]{:S(2)}) collective-permute-start(f32[8,128]{1,0:T(8,128)S(1)} %add.87), channel_id=1, source_target_pairs={{0,32},{32,0},{64,96},{96,64},{128,160},{160,128},{192,224},{224,1... | collective-permute-start | bytes 12296 | tf_op jit(solution)/shard_map/ppermute | solution.py:279

commit v8 on v7

v8 whole, which is shorter than its diff:
```python
import functools

import jax
import jax.numpy as jnp
from jax import lax
from jax.experimental import pallas as pl
from jax.experimental.pallas import tpu as pltpu
from jax.sharding import PartitionSpec as P

BAND_MAX = 8
GROUP = 4
F32 = jnp.float32
BF16 = jnp.bfloat16
VMEM_LIMIT = 16 * 1024 * 1024


def split(value):
    high = value.astype(BF16)
    return high, (value - high.astype(F32)).astype(BF16)


def dot(a, b):
    return jnp.dot(a, b, preferred_element_type=F32)


def dot3(ah, al, bh, bl):
    return dot(ah, bh) + (dot(al, bh) + dot(ah, bl))


def peak(value):
    return jnp.max(jnp.max(value, axis=0, keepdims=True), axis=1, keepdims=True)


def rows_of(values):
    return jnp.concatenate([jnp.broadcast_to(v, (1, 128)) for v in values], axis=0)


def tables_kernel(band, kyh, kyl, kxh, kxl, *, ny):
    def entries(sq, ok):
        return jnp.where(ok, jnp.exp(sq.astype(F32) * (-2.0 / (BAND_MAX * BAND_MAX))), 0.0)

    def offsets(shape):
        return lax.broadcasted_iota(jnp.int32, shape, 0), lax.broadcasted_iota(jnp.int32, shape, 1)

    row, col = offsets(kyh.shape)
    shift = ny.bit_length() - 1
    dy = row - col
    kyh[...], kyl[...] = split(entries(dy * dy, ((row >> shift) == (col >> shift)) & (jnp.abs(dy) <= band[1])))
    row, col = offsets(kxh.shape)
    dx = row - col
    kxh[...], kxl[...] = split(entries(dx * dx, jnp.abs(dx) <= band[0]))


def tile_loop(ny, nx, step):
    across = nx // 128

    def body_of(i, carry):
        row = pl.multiple_of(lax.div(i, across) * 8, 8)
        column = pl.multiple_of(lax.rem(i, across) * 128, 128)
        step(row, pl.ds(column, 128))
        return carry

    lax.fori_loop(0, ny // 8 * across, body_of, 0)


def own_planes(field, kz, y, ny, entry_lo, entry_hi):
    planes = field.shape[0] // ny
    taps = [kz[d] for d in range(BAND_MAX + 1)]

    def step(row, columns):
        e = [
            (entry_lo if 2 * q < planes else entry_hi)(field[pl.ds(q * ny + row, 8), columns])
            for q in range(planes)
        ]
        for p in range(planes):
            total = taps[0] * e[p]
            for d in range(1, BAND_MAX + 1):
                near = [e[q] for q in (p - d, p + d) if 0 <= q < planes]
                total += taps[d] * (near[0] if len(near) == 1 else near[0] + near[1])
            y[pl.ds(p * ny + row, 8), columns] = total

    tile_loop(ny, field.shape[1], step)


def halo_copies(near, far, halo, sems, core):
    return [
        pltpu.make_async_copy(near, halo.at[1 - core], sems.at[0]),
        pltpu.make_async_copy(far, halo.at[core], sems.at[1]),
    ]


def edge_copies(field, near, far, sems, core):
    half = near.shape[0]

    def rows(k):
        return pl.ds(pl.multiple_of(k * half, half), half)

    return [
        pltpu.make_async_copy(field.at[rows(1 - core)], near, sems.at[0]),
        pltpu.make_async_copy(field.at[rows(core)], far, sems.at[1]),
    ]


def halo_planes(halo, kz, y, z, ny, own, entry_left, entry_right):
    side = halo.shape[1] // ny
    taps = [kz[d] for d in range(BAND_MAX + 1)]

    def step(row, columns):
        e = [entry_left(halo[0, pl.ds(q * ny + row, 8), columns]) for q in range(side)]
        for p in range(side):
            rows = pl.ds(p * ny + row, 8)
            total = own(y[rows, columns])
            for q in range(max(0, p + side - BAND_MAX), side):
                total += taps[p + side - q] * e[q]
            z[rows, columns] = total
        e = [entry_right(halo[1, pl.ds(q * ny + row, 8), columns]) for q in range(side)]
        for p in range(side):
            rows = pl.ds((side + p) * ny + row, 8)
            total = own(y[rows, columns])
            for q in range(min(side, p + BAND_MAX - side + 1)):
                total += taps[side + q - p] * e[q]
            z[rows, columns] = total

    tile_loop(ny, halo.shape[2], step)


def tile(value):
    return jnp.broadcast_to(value, (8, 128))


def own_log_kernel(kz, field, y, stats, *, ny):
    half = field.shape[0] // 2
    m_lo, m_hi = peak(field[:half, :]), peak(field[half:, :])
    m = jnp.maximum(m_lo, m_hi)
    stats[...] = rows_of([m_lo, m_hi, m, m, m, m, m, m])
    m = tile(m)
    entry = lambda v: jnp.exp(v - m)
    own_planes(field, kz, y, ny, entry, entry)


def own_linear_kernel(kz, field, potential, stats, y, shifted, *, ny):
    c = stats[0:1, 0:1]
    shifted[...] = jnp.exp(potential[...] - c)
    f_lo = tile(jnp.exp((c - stats[1:2, 0:1]) * 0.5))
    f_hi = tile(jnp.exp((c - stats[2:3, 0:1]) * 0.5))
    own_planes(field, kz, y, ny, lambda v: v * f_lo * f_lo, lambda v: v * f_hi * f_hi)


def rows_and_columns(z, g, kyh, kyl, kxh, kxl, mid):
    half, block = mid.shape[0], kyh.shape[0]
    for k in range(half // block):
        rows = pl.ds(g * half + k * block, block)
        zh, zl = split(z[rows, :])
        mid[k * block : (k + 1) * block, :] = dot3(kyh[...], kyl[...], zh, zl)
    mh, ml = split(mid[...])
    return dot3(mh, ml, kxh[...], kxl[...])


def log_halos(where, kz, halo, y, stats, z, scale, ny):
    has_left, has_right = where[0] > 0, where[1] > 0
    m_own = stats[2:3, 0:1]
    m_left = jnp.where(has_left, peak(halo[0]), m_own)
    m_right = jnp.where(has_right, peak(halo[1]), m_own)
    c = jnp.maximum(m_own, jnp.maximum(m_left, m_right))
    scale[...] = rows_of([c, stats[0:1, 0:1], stats[1:2, 0:1], m_left, m_right, c, c, c])
    own = tile(jnp.exp(m_own - c))
    c = tile(c)
    halo_planes(
        halo,
        kz,
        y,
        z,
        ny,
        lambda v: v * own,
        lambda v: jnp.where(has_left, jnp.exp(v - c), 0.0),
        lambda v: jnp.where(has_right, jnp.exp(v - c), 0.0),
    )


def potential_kernel(
    where, kz, near, far, y_in, stats, density_in, kyh, kyl, kxh, kxl, potential, to_near, to_far,
    halo, y, density, z, mid, scale, sems, *, ny
):
    core = where[2]
    arriving = halo_copies(near, far, halo, sems, core)
    late = [pltpu.make_async_copy(y_in, y, sems.at[2]), pltpu.make_async_copy(density_in, density, sems.at[3])]
    for copy in arriving + late:
        copy.start()
    for copy in arriving + late[:1]:
        copy.wait()
    log_halos(where, kz, halo, y, stats, z, scale, ny)
    half = mid.shape[0]
    late[1].wait()
    for g in range(2):
        rows = slice(g * half, (g + 1) * half)
        first = rows_and_columns(z, g, kyh, kyl, kxh, kxl, mid)
        potential[rows, :] = density[rows, :] - (jnp.log(first) + scale[0:1, 0:1])
    leaving = edge_copies(potential, to_near, to_far, sems, core)
    for copy in leaving:
        copy.start()
    for copy in leaving:
        copy.wait()


def second_kernel(
    where, kz, near, far, y, stats, kyh, kyl, kxh, kxl, out, scale, halo, z, mid, sems, *, ny
):
    arriving = halo_copies(near, far, halo, sems, where[2])
    for copy in arriving:
        copy.start()
    for copy in arriving:
        copy.wait()
    log_halos(where, kz, halo, y, stats, z, scale, ny)
    half = mid.shape[0]
    for g in range(2):
        out[g * half : (g + 1) * half, :] = rows_and_columns(z, g, kyh, kyl, kxh, kxl, mid)


def ratio_kernel(
    at, weight, second, scale, bary, cot, sum0, sum1, sum2, sum3, out, to_near, to_far, total, sums, sems
):
    c = scale[0:1, 0:1]
    block, columns = sums.shape[1:]
    count = sums.shape[0]
    arriving = [
        pltpu.make_async_copy(ref, sums.at[k], sems.at[k]) for k, ref in enumerate((sum0, sum1, sum2, sum3))
    ]
    for copy in arriving:
        copy.start()
    partial = jnp.zeros((8, 128), F32)
    f_lo = jnp.exp((scale[1:2, 0:1] - c) * 0.5)
    f_hi = jnp.exp((scale[2:3, 0:1] - c) * 0.5)
    for k, copy in enumerate(arriving):
        copy.wait()
        g = lax.rem(at[0] + k, count)
        rows = pl.ds(pl.multiple_of(g * block, block), block)
        summed = bary[rows, :] + sums[k]
        denominator = second[rows, :]
        share = summed * (jnp.log(denominator) + c)
        share = jnp.sum(share.reshape(block // 8, 8, columns), axis=0)
        for m in range(columns // 128):
            partial += share[:, m * 128 : (m + 1) * 128]
        f = jnp.where(2 * g < count, f_lo, f_hi)
        out[rows, :] = (weight[0] * summed - cot[rows, :]) / denominator * f * f
    leaving = edge_copies(out, to_near, to_far, sems, at[2])
    for copy in leaving:
        copy.start()
    lanes = lax.broadcasted_iota(jnp.int32, total.shape, 1)
    partial = jnp.sum(jnp.sum(partial, axis=0, keepdims=True), axis=1, keepdims=True)
    total[...] = jnp.where(lanes == at[1], partial, 0.0)
    for copy in leaving:
        copy.wait()


def gradient_kernel(
    where, kz, near, far, y, shifted, stats, kyh, kyl, kxh, kxl, out, halo, z, mid, result, sems, *, ny
):
    arriving = halo_copies(near, far, halo, sems, where[2])
    for copy in arriving:
        copy.start()
    c = stats[0:1, 0:1]
    f_left = tile(jnp.exp((c - stats[3:4, 0:1]) * 0.5))
    f_right = tile(jnp.exp((c - stats[4:5, 0:1]) * 0.5))
    has_left, has_right = where[0] > 0, where[1] > 0
    for copy in arriving:
        copy.wait()
    halo_planes(
        halo,
        kz,
        y,
        z,
        ny,
        lambda v: v,
        lambda v: jnp.where(has_left, v * f_left * f_left, 0.0),
        lambda v: jnp.where(has_right, v * f_right * f_right, 0.0),
    )
    half = mid.shape[0]
    leaving = []
    for g in range(2):
        rows = slice(g * half, (g + 1) * half)
        result[rows, :] = shifted[rows, :] * rows_and_columns(z, g, kyh, kyl, kxh, kxl, mid)
        leaving.append(pltpu.make_async_copy(result.at[rows], out.at[rows], sems.at[g]))
        leaving[-1].start()
    for copy in leaving:
        copy.wait()


def body(
    atom_log_density,
    prior_log_scaling,
    atom_cotangent_rows,
    barycenter_cotangent,
    weights,
    band,
    slot_atom_index,
):
    planes, ny, nx = barycenter_cotangent.shape
    slabs, atoms = lax.axis_size("slab"), lax.axis_size("atom")
    rows = planes * ny
    half = rows // 2
    block = GROUP * ny
    count = planes // GROUP
    slab_at, atom_at = lax.axis_index("slab"), lax.axis_index("atom")
    across = atoms // 2
    x_at = atom_at // 2

    smem = pl.BlockSpec(memory_space=pltpu.SMEM)
    vmem = pl.BlockSpec(memory_space=pltpu.VMEM)
    anywhere = pl.BlockSpec(memory_space=pl.ANY)
    hbm = pl.BlockSpec(memory_space=pltpu.HBM)
    params = pltpu.CompilerParams(vmem_limit_bytes=VMEM_LIMIT)

    def shape(*dims, dtype=F32):
        return jax.ShapeDtypeStruct(dims, dtype)

    def send(value, axis, pairs):
        return lax.ppermute(value, axis, pairs)

    in_order = lax.optimization_barrier
    cores = [(i, i ^ 1) for i in range(slabs)]
    chips = [(i, i + 1) for i in range(1, slabs - 1, 2)] + [(i + 1, i) for i in range(1, slabs - 1, 2)]
    core = slab_at % 2
    ahead = {
        k: [(2 * x + z, 2 * ((x + k) % across) + z) for x in range(across) for z in range(2)]
        for k in range(1, across)
    }
    swap = [(i, i ^ 1) for i in range(atoms)]

    cot = atom_cotangent_rows.reshape(rows, nx)

    def block_of(k):
        return lax.dynamic_slice_in_dim(cot, lax.rem(x_at + k, count) * block, block)

    blocks = [block_of(k) for k in range(1, across)]
    part = block_of(0)
    for k in range(1, across):
        part = part + send(blocks[k - 1], "atom", ahead[k])

    y_shape, x_shape = (block, block), (nx, nx)
    distance = jnp.arange(BAND_MAX + 1, dtype=jnp.int32)
    kz = jnp.exp((distance * distance).astype(F32) * (-2.0 / (BAND_MAX * BAND_MAX)))
    kz = jnp.where(distance <= band[2], kz, 0.0)
    tables = pl.pallas_call(
        functools.partial(tables_kernel, ny=ny),
        out_shape=[shape(*dims, dtype=BF16) for dims in (y_shape, y_shape, x_shape, x_shape)],
        in_specs=[smem],
        out_specs=[vmem] * 4,
        compiler_params=params,
        name="tables",
    )(band)
    prior = prior_log_scaling.reshape(rows, nx)
    to_near = lax.dynamic_slice_in_dim(prior, (1 - core) * half, half)
    to_far = lax.dynamic_slice_in_dim(prior, core * half, half)
    far = send(to_far, "slab", chips)
    near = send(to_near, "slab", cores)

    where = jnp.stack([slab_at > 0, slab_at < slabs - 1, core > 0]).astype(jnp.int32)
    slot = lax.dynamic_slice_in_dim(slot_atom_index, atom_at, 1)
    onehot = (slot[0] == jnp.arange(weights.shape[0], dtype=jnp.int32)).astype(F32)
    weight = jnp.sum(onehot * weights, keepdims=True)

    own_out = [shape(rows, nx), shape(8, 128)]
    own_log = pl.pallas_call(
        functools.partial(own_log_kernel, ny=ny),
        in_specs=[smem, vmem],
        out_specs=[vmem, vmem],
        out_shape=own_out,
        compiler_params=params,
        name="own_log",
    )
    whole, halo = pltpu.VMEM((rows, nx), F32), pltpu.VMEM((2, half, nx), F32)
    scratch = [pltpu.VMEM((rows, nx), F32), pltpu.VMEM((half, nx), F32)]
    scale = pltpu.VMEM((8, 128), F32)

    y, stats = own_log(kz, prior)
    y, part = in_order((y, part))
    swapped = send(part, "atom", swap)
    potential, to_near, to_far = pl.pallas_call(
        functools.partial(potential_kernel, ny=ny),
        in_specs=[smem, smem, hbm, hbm, hbm, vmem, hbm] + [vmem] * 4,
        out_specs=[vmem, anywhere, anywhere],
        out_shape=[shape(rows, nx), shape(half, nx), shape(half, nx)],
        scratch_shapes=[halo, whole, whole, *scratch, scale, pltpu.SemaphoreType.DMA((4,))],
        compiler_params=params,
        name="potential",
    )(where, kz, near, far, y, stats, atom_log_density.reshape(rows, nx), *tables)

    far = send(to_far, "slab", chips)
    near = send(to_near, "slab", cores)
    both = part + swapped
    own_at, both = in_order((potential, both))
    sums = [both] + [send(both, "atom", ahead[across - k]) for k in range(1, across)]
    y, stats = own_log(kz, own_at)
    second, stats = pl.pallas_call(
        functools.partial(second_kernel, ny=ny),
        in_specs=[smem, smem, anywhere, anywhere] + [vmem] * 6,
        out_specs=[vmem, vmem],
        out_shape=[shape(rows, nx), shape(8, 128)],
        scratch_shapes=[halo, *scratch, pltpu.SemaphoreType.DMA((2,))],
        compiler_params=params,
        name="second",
    )(where, kz, near, far, y, stats, *tables)
    ratio, to_near, to_far, total = pl.pallas_call(
        ratio_kernel,
        in_specs=[smem, smem] + [vmem] * 4 + [anywhere] * 4,
        out_specs=[vmem, anywhere, anywhere, vmem],
        out_shape=[shape(rows, nx), shape(half, nx), shape(half, nx), shape(8, 128)],
        scratch_shapes=[
            pltpu.VMEM((count, block, nx), F32),
            pltpu.SemaphoreType.DMA((count,)),
        ],
        compiler_params=params,
        name="ratio",
    )(
        jnp.stack([x_at, slot[0], core]),
        weight,
        second,
        stats,
        barycenter_cotangent.reshape(rows, nx),
        cot,
        *sums,
    )

    far = send(to_far, "slab", chips)
    near = send(to_near, "slab", cores)
    y, shifted = pl.pallas_call(
        functools.partial(own_linear_kernel, ny=ny),
        in_specs=[smem] + [vmem] * 3,
        out_specs=[vmem, vmem],
        out_shape=[shape(rows, nx), shape(rows, nx)],
        compiler_params=params,
        name="own_linear",
    )(kz, ratio, potential, stats)

    def add(value, axis, patterns):
        return sum([send(value, axis, pairs) for pairs in patterns], value)

    def flips(hop):
        return [(i, i ^ hop) for i in range(slabs)]

    value = add(total, "slab", [cores])
    value = add(value, "atom", [ahead[k] for k in range(1, across)])
    value, y = in_order((value, y))
    value = add(value, "slab", [[(i, (i + k) % slabs) for i in range(slabs)] for k in (8, 16, 24)])
    for hop in (2, 4):
        value = add(value, "slab", [flips(hop)])
    value, near, far = in_order((value, near, far))
    value = add(value, "atom", [swap])
    weight_grad = value[0, : weights.shape[0]] / (rows * nx * slabs)

    gradient = pl.pallas_call(
        functools.partial(gradient_kernel, ny=ny),
        in_specs=[smem, smem, anywhere, anywhere] + [vmem] * 7,
        out_specs=anywhere,
        out_shape=shape(rows, nx),
        scratch_shapes=[halo, *scratch, whole, pltpu.SemaphoreType.DMA((2,))],
        compiler_params=params,
        name="gradient",
    )(where, kz, near, far, y, shifted, stats, *tables)
    return gradient.reshape(atom_log_density.shape), weight_grad


def solution(mesh):
    return jax.shard_map(
        body,
        mesh=mesh,
        in_specs=(
            P("atom", "slab", None, None),
            P("atom", "slab", None, None),
            P("atom", "slab", None, None),
            P("slab", None, None),
            P(),
            P(),
            P(),
        ),
        out_specs=(P("atom", "slab", None, None), P()),
        check_vma=False,
    )
```

time: 149 us -> 144 us (0.966)
  starting transfers between devices: 56.1 us -> 46.9 us
  waiting for transfers between devices: 38.7 us -> 44.9 us
  Pallas kernels: 36 us -> 34.3 us
    ppermute x23, starting transfers between devices: 56.1 us -> 46.9 us  [send(): return lax.ppermute(value, axis, pairs)]
    ppermute x23, waiting for transfers between devices: 38.7 us -> 44.9 us  [send(): return lax.ppermute(value, axis, pairs)]
    slice x1 -> x0, local copies, waits for them, and re-layouts: 3.26 us -> none  [body(): prior_lo, prior_hi = (prior[:half], prior[half:])]
    dynamic_slice x0 -> x1, local copies, waits for them, and re-layouts: none -> 3.05 us  [body(): to_far = lax.dynamic_slice_in_dim(prior, core * half, half)]
    pallas_call x3, Pallas kernels: 13.9 us -> 11.9 us  [the longest x1 5.88 us: body(): pl.pallas_call(functools.partial(gradient_kernel, ny=ny), in_specs=[smem,...]
  transfers between devices with their start and end apart: 23 -> 23, of which waited for: 10 -> 10; matrix products, arithmetic and copies ran while one was open for 5% -> 6% of each run, Pallas kernels for 22% -> 21%
where the time goes in v8:
time: 144 us; the launch traced here: 142 us
  starting transfers between devices  46.9 us (33%)
  waiting for transfers between devices  44.9 us (31%)
  Pallas kernels  34.3 us (24%)
  local copies, waits for them, and re-layouts  9.68 us (7%)
  other arithmetic  5.68 us (4%)
    ppermute x23, starting transfers between devices, send(): return lax.ppermute(value, axis, pairs)  46.9 us
    ppermute x23, waiting for transfers between devices, send(): return lax.ppermute(value, axis, pairs)  44.9 us
    pallas_call x1, Pallas kernels, body(): pl.pallas_call(functools.partial(potential_kernel, ny=ny), in_specs=[smem...  7.86 us
    pallas_call x1, Pallas kernels, body(): pl.pallas_call(functools.partial(second_kernel, ny=ny), in_specs=[smem, s...  6.76 us
    pallas_call x1, Pallas kernels, body(): pl.pallas_call(functools.partial(gradient_kernel, ny=ny), in_specs=[smem,...  5.88 us
    pallas_call x1, Pallas kernels, body(): pl.pallas_call(ratio_kernel, in_specs=[smem, smem] + [vmem] * 4 + [anywhe...  3.7 us
    dynamic_slice x1, local copies, waits for them, and re-layouts, body(): to_far = lax.dynamic_slice_in_dim(prior, core * half, half)  3.05 us
    pallas_call x1, Pallas kernels, body(): y, stats = own_log(kz, prior)  3.01 us
  transfers between devices with their start and end apart: 23, of which 10 were waited for; matrix products, arithmetic and copies ran while one was open for 6% of the time, Pallas kernels for 21%

profile of v8, /device:TPU:10, one launch (start us, length us, event | category | flops | bytes accessed | tf_op | source)
XLA Modules:
  0.0 142.4 jit_solution(17015658339221764454)
XLA Ops:
  0.7 3.0 %constant_dynamic-slice_fusion.3 = (f32[512,512]{1,0:T(8,128)}, f32[512,512]{1,0:T(8,128)}) fusion(f32[1024,512]{1,0:T(8,128)} %bitcast.15, s32[]{:T(128)S(6)} %select_n.41, s32[]{:T(128)S(6)} %select_n.40), kind=kLoop, calls=%fused_computation.9 | loop fusion | bytes 4194312 | tf_op jit(solution)/shard_map/dynamic_slice | solution.py:353
  3.7 6.0 %collective-permute-start.1 = (f32[512,512]{1,0:T(8,128)}, f32[512,512]{1,0:T(8,128)}, u32[]{:S(2)}, u32[]{:S(2)}) collective-permute-start(f32[512,512]{1,0:T(8,128)} %get-tuple-element.61), channel_id=1, source_target_pairs={{1,2},{3,4},{5,6},{7,8},{9,10},{11,12},{13,14},{15,16},{17,18},{19... | collective-permute-start | bytes 3145736 | tf_op jit(solution)/shard_map/ppermute | solution.py:317
  9.7 0.1 collective-permute-start
  9.8 2.6 %constant_dynamic-slice_fusion.2 = (f32[256,512]{1,0:T(8,128)}, f32[256,512]{1,0:T(8,128)}, f32[256,512]{1,0:T(8,128)}) fusion(f32[1024,512]{1,0:T(8,128)} %bitcast.17, s32[]{:T(128)S(6)} %select_n.43, s32[]{:T(128)S(6)} %select_n.45, s32[]{:T(128)S(6)} %select_n.44), kind=kLoop, calls=%fused_computation.8 | loop fusion | bytes 3145740 | tf_op jit(solution)/shard_map/dynamic_slice | solution.py:332
  12.4 1.5 %collective-permute-start.2 = (f32[256,512]{1,0:T(8,128)}, f32[256,512]{1,0:T(8,128)}, u32[]{:S(2)}, u32[]{:S(2)}) collective-permute-start(f32[256,512]{1,0:T(8,128)} %get-tuple-element.58), channel_id=1, source_target_pairs={{0,64},{32,96},{64,128},{96,160},{128,192},{160,224},{192,0},{224,... | collective-permute-start | bytes 1572872 | tf_op jit(solution)/shard_map/ppermute | solution.py:317
  13.9 0.5 collective-permute-start.4
  14.4 2.1 %collective-permute-start.3 = (f32[256,512]{1,0:T(8,128)}, f32[256,512]{1,0:T(8,128)}, u32[]{:S(2)}, u32[]{:S(2)}) collective-permute-start(f32[256,512]{1,0:T(8,128)} %get-tuple-element.60), channel_id=1, source_target_pairs={{0,128},{32,160},{64,192},{96,224},{128,0},{160,32},{192,64},{224,... | collective-permute-start | bytes 1572872 | tf_op jit(solution)/shard_map/ppermute | solution.py:317
  16.6 0.6 slice.6
  17.1 1.1 tables.1
  18.2 0.7 compare_select_fusion.1.kz
  18.9 3.0 %own_log.2 = (f32[1024,512]{1,0:T(8,128)S(1)}, f32[8,128]{1,0:T(8,128)S(1)}) custom-call(f32[9]{0:T(128)S(1)} %compare_select_fusion.1.kz, f32[1024,512]{1,0:T(8,128)S(1)} %bitcast.16), custom_call_target="tpu_custom_call" | custom-call | tf_op jit(solution)/shard_map/own_log/pallas_call | solution.py:375
  21.9 0.0 copy-start.3
  21.9 1.3 copy-done.3
  23.2 0.1 add_convert_fusion.where
  23.3 4.1 %collective-permute-done.2 = f32[256,512]{1,0:T(8,128)} collective-permute-done((f32[256,512]{1,0:T(8,128)}, f32[256,512]{1,0:T(8,128)}, u32[]{:S(2)}, u32[]{:S(2)}) %collective-permute-start.2) | collective-permute-done | bytes 524320 | tf_op jit(solution)/shard_map/ppermute | solution.py:317
  27.4 0.9 collective-permute-done.4
  28.3 11.7 %collective-permute-done.3 = f32[256,512]{1,0:T(8,128)} collective-permute-done((f32[256,512]{1,0:T(8,128)}, f32[256,512]{1,0:T(8,128)}, u32[]{:S(2)}, u32[]{:S(2)}) %collective-permute-start.3) | collective-permute-done | bytes 524320 | tf_op jit(solution)/shard_map/ppermute | solution.py:317
  40.1 1.7 %add_add_fusion = f32[256,512]{1,0:T(8,128)S(1)} fusion(f32[256,512]{1,0:T(8,128)} %collective-permute-done.4, f32[256,512]{1,0:T(8,128)} %collective-permute-done.3, f32[256,512]{1,0:T(8,128)} %collective-permute-done.2, f32[1024,512]{1,0:T(8,128)} %bitcast.18, s32[]{:T(128)S(6)} %select_n.42), kind=kLoop, calls=%fused_computation | loop fusion | flops 393216 | bytes 2621444 | tf_op jit(solution)/shard_map/add | solution.py:337
  41.8 4.6 %collective-permute-start.7 = (f32[256,512]{1,0:T(8,128)S(1)}, f32[256,512]{1,0:T(8,128)S(1)}, u32[]{:S(2)}, u32[]{:S(2)}) collective-permute-start(f32[256,512]{1,0:T(8,128)S(1)} %add_add_fusion), channel_id=1, source_target_pairs={{0,32},{32,0},{64,96},{96,64},{128,160},{160,128},{192,224},{224,1... | collective-permute-start | bytes 1572872 | tf_op jit(solution)/shard_map/ppermute | solution.py:317
  46.4 0.0 collective-permute-done.1.far
  46.4 0.0 collective-permute-done.near
  46.4 0.0 copy-start.2
  46.4 1.6 %copy-done.2 = f32[1,16,64,512]{3,2,1,0:T(8,128)S(1)} copy-done((f32[1,16,64,512]{3,2,1,0:T(8,128)S(1)}, f32[1,16,64,512]{3,2,1,0:T(8,128)}, u32[]{:S(2)}) %copy-start.2) | copy-done | bytes 2097176
  48.0 7.9 %potential.1 = (f32[1024,512]{1,0:T(8,128)S(1)}, f32[512,512]{1,0:T(8,128)}, f32[512,512]{1,0:T(8,128)}) custom-call(s32[3]{0:T(128)S(1)} %add_convert_fusion.where, f32[9]{0:T(128)S(1)} %compare_select_fusion.1.kz, f32[512,512]{1,0:T(8,128)} %collective-permute-done.near, f32[512,512]{1,0:T(8,128)} %collective-permute-done.1.far, ...), custom_call_target="tpu_custom_call" | custom-call | tf_op jit(solution)/shard_map/potential/pallas_call | solution.py:378
  55.9 0.1 collective-permute-start.5
  56.0 5.1 %collective-permute-start.6 = (f32[512,512]{1,0:T(8,128)}, f32[512,512]{1,0:T(8,128)}, u32[]{:S(2)}, u32[]{:S(2)}) collective-permute-start(f32[512,512]{1,0:T(8,128)} %get-tuple-element.38), channel_id=1, source_target_pairs={{1,2},{3,4},{5,6},{7,8},{9,10},{11,12},{13,14},{15,16},{17,18},{19... | collective-permute-start | bytes 3145736 | tf_op jit(solution)/shard_map/ppermute | solution.py:317
  61.1 10.3 %collective-permute-done.7 = f32[256,512]{1,0:T(8,128)S(1)} collective-permute-done((f32[256,512]{1,0:T(8,128)S(1)}, f32[256,512]{1,0:T(8,128)S(1)}, u32[]{:S(2)}, u32[]{:S(2)}) %collective-permute-start.7) | collective-permute-done | bytes 524320 | tf_op jit(solution)/shard_map/ppermute | solution.py:317
  71.4 0.9 add.91.sum0
  72.3 2.9 %collective-permute-start.9 = (f32[256,512]{1,0:T(8,128)}, f32[256,512]{1,0:T(8,128)}, u32[]{:S(2)}, u32[]{:S(2)}) collective-permute-start(f32[256,512]{1,0:T(8,128)} %add.91.sum0), channel_id=1, source_target_pairs={{0,128},{32,160},{64,192},{96,224},{128,0},{160,32},{192,64},{224,... | collective-permute-start | bytes 1572872 | tf_op jit(solution)/shard_map/ppermute | solution.py:317
  75.2 1.6 %collective-permute-start.8 = (f32[256,512]{1,0:T(8,128)}, f32[256,512]{1,0:T(8,128)}, u32[]{:S(2)}, u32[]{:S(2)}) collective-permute-start(f32[256,512]{1,0:T(8,128)} %add.91.sum0), channel_id=1, source_target_pairs={{0,192},{32,224},{64,0},{96,32},{128,64},{160,96},{192,128},{224,1... | collective-permute-start | bytes 1572872 | tf_op jit(solution)/shard_map/ppermute | solution.py:317
  76.8 0.6 dynamic_slice.21
  77.4 0.6 pad_add_fusion.at
  78.0 1.2 fusion
  79.2 3.0 %own_log.3 = (f32[1024,512]{1,0:T(8,128)S(1)}, f32[8,128]{1,0:T(8,128)S(1)}) custom-call(f32[9]{0:T(128)S(1)} %compare_select_fusion.1.kz, f32[1024,512]{1,0:T(8,128)S(1)} %get-tuple-element.41.field.potential), custom_call_target="tpu_custom_call" | custom-call | tf_op jit(solution)/shard_map/own_log/pallas_call | solution.py:393
  82.2 0.0 collective-permute-done.5.near
  82.2 7.9 %collective-permute-done.6.far = f32[512,512]{1,0:T(8,128)} collective-permute-done((f32[512,512]{1,0:T(8,128)}, f32[512,512]{1,0:T(8,128)}, u32[]{:S(2)}, u32[]{:S(2)}) %collective-permute-start.6) | collective-permute-done | bytes 1048608 | tf_op jit(solution)/shard_map/ppermute | solution.py:317
  90.1 6.8 %second.1 = (f32[1024,512]{1,0:T(8,128)S(1)}, f32[8,128]{1,0:T(8,128)S(1)}) custom-call(s32[3]{0:T(128)S(1)} %add_convert_fusion.where, f32[9]{0:T(128)S(1)} %compare_select_fusion.1.kz, f32[512,512]{1,0:T(8,128)} %collective-permute-done.5.near, f32[512,512]{1,0:T(8,128)} %collective-permute-done.6.far, f32[1024,512]{1,0:T(8,128)S(1)} %get-tuple-element.42.y, ...), custom_call_target="tpu_custom_call" | custom-call | tf_op jit(solution)/shard_map/second/pallas_call | solution.py:394
  96.9 0.0 collective-permute-done.10.sum3
  96.9 0.0 collective-permute-done.8.sum1
  96.9 3.7 %ratio.1 = (f32[1024,512]{1,0:T(8,128)S(1)}, f32[512,512]{1,0:T(8,128)S(1)}, f32[512,512]{1,0:T(8,128)S(1)}, f32[8,128]{1,0:T(8,128)S(1)}) custom-call(s32[3]{0:T(128)S(1)} %pad_add_fusion.at, f32[1]{0:T(128)} %bitcast.7.weight, f32[1024,512]{1,0:T(8,128)S(1)} %get-tuple-element.44.second, f32[8,128]{1,0:T(8,128)S(1)} %get-tuple-element.45.scale.stats, ...), custom_call_target="tpu_custom_call" | custom-call | tf_op jit(solution)/shard_map/ratio/pallas_call | solution.py:403
  100.6 1.7 %collective-permute-start.20 = (f32[512,512]{1,0:T(8,128)S(1)}, f32[512,512]{1,0:T(8,128)S(1)}, u32[]{:S(2)}, u32[]{:S(2)}) collective-permute-start(f32[512,512]{1,0:T(8,128)S(1)} %get-tuple-element.51), channel_id=1, source_target_pairs={{0,1},{1,0},{2,3},{3,2},{4,5},{5,4},{6,7},{7,6},{8,9},{9,8},{10,11... | collective-permute-start | bytes 3145736 | tf_op jit(solution)/shard_map/ppermute | solution.py:317
  102.3 4.9 %collective-permute-start.21 = (f32[512,512]{1,0:T(8,128)S(1)}, f32[512,512]{1,0:T(8,128)S(1)}, u32[]{:S(2)}, u32[]{:S(2)}) collective-permute-start(f32[512,512]{1,0:T(8,128)S(1)} %get-tuple-element.52), channel_id=1, source_target_pairs={{1,2},{3,4},{5,6},{7,8},{9,10},{11,12},{13,14},{15,16},{17,18},{19... | collective-permute-start | bytes 3145736 | tf_op jit(solution)/shard_map/ppermute | solution.py:317
  107.3 0.1 collective-permute-start.11
  107.4 1.2 collective-permute-done.11
  108.5 1.1 collective-permute-start.14
  109.6 0.3 collective-permute-start.13
  110.0 2.6 %collective-permute-start.12 = (f32[8,128]{1,0:T(8,128)S(1)}, f32[8,128]{1,0:T(8,128)S(1)}, u32[]{:S(2)}, u32[]{:S(2)}) collective-permute-start(f32[8,128]{1,0:T(8,128)S(1)} %add.92), channel_id=1, source_target_pairs={{0,64},{32,96},{64,128},{96,160},{128,192},{160,224},{192,0},{224,... | collective-permute-start | bytes 12296 | tf_op jit(solution)/shard_map/ppermute | solution.py:317
  112.6 3.0 %own_linear.1 = (f32[1024,512]{1,0:T(8,128)S(1)}, f32[1024,512]{1,0:T(8,128)S(1)}) custom-call(f32[9]{0:T(128)S(1)} %compare_select_fusion.1.kz, f32[1024,512]{1,0:T(8,128)S(1)} %get-tuple-element.48.field, f32[1024,512]{1,0:T(8,128)S(1)} %get-tuple-element.41.field.potential, f32[8,128]{1,0:T(8,128)S(1)} %get-tuple-element.45.scale.stats), custom_call_target="tpu_custom_call" | custom-call | tf_op jit(solution)/shard_map/own_linear/pallas_call | solution.py:426
  115.6 0.0 collective-permute-done.14
  115.6 0.0 collective-permute-done.12
  115.6 0.1 collective-permute-start.17
  115.7 3.0 %collective-permute-start.16 = (f32[8,128]{1,0:T(8,128)S(1)}, f32[8,128]{1,0:T(8,128)S(1)}, u32[]{:S(2)}, u32[]{:S(2)}) collective-permute-start(f32[8,128]{1,0:T(8,128)S(1)} %add_add_fusion.2), channel_id=1, source_target_pairs={{0,16},{1,17},{2,18},{3,19},{4,20},{5,21},{6,22},{7,23},{8,24},{9,... | collective-permute-start | bytes 12296 | tf_op jit(solution)/shard_map/ppermute | solution.py:317
  118.7 1.8 %collective-permute-start.15 = (f32[8,128]{1,0:T(8,128)S(1)}, f32[8,128]{1,0:T(8,128)S(1)}, u32[]{:S(2)}, u32[]{:S(2)}) collective-permute-start(f32[8,128]{1,0:T(8,128)S(1)} %add_add_fusion.2), channel_id=1, source_target_pairs={{0,8},{1,9},{2,10},{3,11},{4,12},{5,13},{6,14},{7,15},{8,16},{9,17... | collective-permute-start | bytes 12296 | tf_op jit(solution)/shard_map/ppermute | solution.py:317
  120.5 0.0 collective-permute-done.17
  120.5 0.4 collective-permute-done.16
  120.9 1.5 %collective-permute-done.15 = f32[8,128]{1,0:T(8,128)S(1)} collective-permute-done((f32[8,128]{1,0:T(8,128)S(1)}, f32[8,128]{1,0:T(8,128)S(1)}, u32[]{:S(2)}, u32[]{:S(2)}) %collective-permute-start.15) | collective-permute-done | bytes 4128 | tf_op jit(solution)/shard_map/ppermute | solution.py:317
  122.4 0.0 collective-permute-start.18
  122.4 5.3 %collective-permute-done.18 = f32[8,128]{1,0:T(8,128)S(1)} collective-permute-done((f32[8,128]{1,0:T(8,128)S(1)}, f32[8,128]{1,0:T(8,128)S(1)}, u32[]{:S(2)}, u32[]{:S(2)}) %collective-permute-start.18) | collective-permute-done | bytes 4128 | tf_op jit(solution)/shard_map/ppermute | solution.py:317
  127.7 4.1 %collective-permute-start.19 = (f32[8,128]{1,0:T(8,128)S(1)}, f32[8,128]{1,0:T(8,128)S(1)}, u32[]{:S(2)}, u32[]{:S(2)}) collective-permute-start(f32[8,128]{1,0:T(8,128)S(1)} %add.99), channel_id=1, source_target_pairs={{0,4},{1,5},{2,6},{3,7},{4,0},{5,1},{6,2},{7,3},{8,12},{9,13},{10,... | collective-permute-start | bytes 12296 | tf_op jit(solution)/shard_map/ppermute | solution.py:317
  131.8 1.6 %collective-permute-done.19 = f32[8,128]{1,0:T(8,128)S(1)} collective-permute-done((f32[8,128]{1,0:T(8,128)S(1)}, f32[8,128]{1,0:T(8,128)S(1)}, u32[]{:S(2)}, u32[]{:S(2)}) %collective-permute-start.19) | collective-permute-done | bytes 4128 | tf_op jit(solution)/shard_map/ppermute | solution.py:317
  133.4 0.0 collective-permute-done.20.near
  133.4 2.6 %collective-permute-start.22 = (f32[8,128]{1,0:T(8,128)S(1)}, f32[8,128]{1,0:T(8,128)S(1)}, u32[]{:S(2)}, u32[]{:S(2)}) collective-permute-start(f32[8,128]{1,0:T(8,128)S(1)} %add.100), channel_id=1, source_target_pairs={{0,32},{32,0},{64,96},{96,64},{128,160},{160,128},{192,224},{224,1... | collective-permute-start | bytes 12296 | tf_op jit(solution)/shard_map/ppermute | solution.py:317
  136.0 5.9 %gradient.1 = f32[1024,512]{1,0:T(8,128)} custom-call(s32[3]{0:T(128)S(1)} %add_convert_fusion.where, f32[9]{0:T(128)S(1)} %compare_select_fusion.1.kz, f32[512,512]{1,0:T(8,128)S(1)} %collective-permute-done.20.near, f32[512,512]{1,0:T(8,128)S(1)} %collective-permute-done.21.far, f32[1024,512]{1,0:T(8,128)S(1)} %get-tuple-element.55.y, ...), custom_call_target="tpu_custom_call" | custom-call | tf_op jit(solution)/shard_map/gradient/pallas_call | solution.py:451
  141.9 0.5 multiply_bitcast_fusion
  (25 shorter events, 0.1 us)
Async XLA Ops:
  3.7 12.9 %copy-start.6 = (s32[3]{0:T(128)S(1)}, s32[3]{0:T(128)}, u32[]{:S(2)}) copy-start(s32[3]{0:T(128)} %band.1) | copy-start | bytes 40
  3.7 15.2 %copy-start = (f32[1,16,64,512]{3,2,1,0:T(8,128)S(1)}, f32[1,16,64,512]{3,2,1,0:T(8,128)}, u32[]{:S(2)}) copy-start(f32[1,16,64,512]{3,2,1,0:T(8,128)} %param.8) | copy-start | bytes 6291460
  3.7 42.7 %collective-permute-start.1 = (f32[512,512]{1,0:T(8,128)}, f32[512,512]{1,0:T(8,128)}, u32[]{:S(2)}, u32[]{:S(2)}) collective-permute-start(f32[512,512]{1,0:T(8,128)} %get-tuple-element.61), channel_id=1, source_target_pairs={{1,2},{3,4},{5,6},{7,8},{9,10},{11,12},{13,14},{15,16},{17,18},{19... | collective-permute-start | bytes 3145736 | tf_op jit(solution)/shard_map/ppermute | solution.py:317
  9.7 36.7 %collective-permute-start = (f32[512,512]{1,0:T(8,128)}, f32[512,512]{1,0:T(8,128)}, u32[]{:S(2)}, u32[]{:S(2)}) collective-permute-start(f32[512,512]{1,0:T(8,128)} %get-tuple-element.62), channel_id=1, source_target_pairs={{0,1},{1,0},{2,3},{3,2},{4,5},{5,4},{6,7},{7,6},{8,9},{9,8},{10,11... | collective-permute-start | bytes 3145736 | tf_op jit(solution)/shard_map/ppermute | solution.py:317
  12.4 15.0 %collective-permute-start.2 = (f32[256,512]{1,0:T(8,128)}, f32[256,512]{1,0:T(8,128)}, u32[]{:S(2)}, u32[]{:S(2)}) collective-permute-start(f32[256,512]{1,0:T(8,128)} %get-tuple-element.58), channel_id=1, source_target_pairs={{0,64},{32,96},{64,128},{96,160},{128,192},{160,224},{192,0},{224,... | collective-permute-start | bytes 1572872 | tf_op jit(solution)/shard_map/ppermute | solution.py:317
  13.9 14.4 %collective-permute-start.4 = (f32[256,512]{1,0:T(8,128)}, f32[256,512]{1,0:T(8,128)}, u32[]{:S(2)}, u32[]{:S(2)}) collective-permute-start(f32[256,512]{1,0:T(8,128)} %get-tuple-element.59), channel_id=1, source_target_pairs={{0,192},{32,224},{64,0},{96,32},{128,64},{160,96},{192,128},{224,1... | collective-permute-start | bytes 1572872 | tf_op jit(solution)/shard_map/ppermute | solution.py:317
  14.4 25.6 %collective-permute-start.3 = (f32[256,512]{1,0:T(8,128)}, f32[256,512]{1,0:T(8,128)}, u32[]{:S(2)}, u32[]{:S(2)}) collective-permute-start(f32[256,512]{1,0:T(8,128)} %get-tuple-element.60), channel_id=1, source_target_pairs={{0,128},{32,160},{64,192},{96,224},{128,0},{160,32},{192,64},{224,... | collective-permute-start | bytes 1572872 | tf_op jit(solution)/shard_map/ppermute | solution.py:317
  21.9 1.3 copy-start.3
  23.2 23.2 %copy-start.4 = (f32[1024,512]{1,0:T(8,128)S(1)}, f32[1024,512]{1,0:T(8,128)}, u32[]{:S(2)}) copy-start(f32[1024,512]{1,0:T(8,128)} %copy-done.3) | copy-start | bytes 6291460
  41.8 29.6 %collective-permute-start.7 = (f32[256,512]{1,0:T(8,128)S(1)}, f32[256,512]{1,0:T(8,128)S(1)}, u32[]{:S(2)}, u32[]{:S(2)}) collective-permute-start(f32[256,512]{1,0:T(8,128)S(1)} %add_add_fusion), channel_id=1, source_target_pairs={{0,32},{32,0},{64,96},{96,64},{128,160},{160,128},{192,224},{224,1... | collective-permute-start | bytes 1572872 | tf_op jit(solution)/shard_map/ppermute | solution.py:317
  46.4 1.6 %copy-start.2 = (f32[1,16,64,512]{3,2,1,0:T(8,128)S(1)}, f32[1,16,64,512]{3,2,1,0:T(8,128)}, u32[]{:S(2)}) copy-start(f32[1,16,64,512]{3,2,1,0:T(8,128)} %param.7) | copy-start | bytes 6291460
  48.0 28.8 %copy-start.7 = (s32[8]{0:T(128)S(1)}, s32[8]{0:T(128)}, u32[]{:S(2)}) copy-start(s32[8]{0:T(128)} %param.13) | copy-start | bytes 100
  48.0 30.0 %copy-start.8 = (f32[8]{0:T(128)S(1)}, f32[8]{0:T(128)}, u32[]{:S(2)}) copy-start(f32[8]{0:T(128)} %param.11) | copy-start | bytes 100
  55.9 26.3 %collective-permute-start.5 = (f32[512,512]{1,0:T(8,128)}, f32[512,512]{1,0:T(8,128)}, u32[]{:S(2)}, u32[]{:S(2)}) collective-permute-start(f32[512,512]{1,0:T(8,128)} %get-tuple-element.37), channel_id=1, source_target_pairs={{0,1},{1,0},{2,3},{3,2},{4,5},{5,4},{6,7},{7,6},{8,9},{9,8},{10,11... | collective-permute-start | bytes 3145736 | tf_op jit(solution)/shard_map/ppermute | solution.py:317
  56.0 34.1 %collective-permute-start.6 = (f32[512,512]{1,0:T(8,128)}, f32[512,512]{1,0:T(8,128)}, u32[]{:S(2)}, u32[]{:S(2)}) collective-permute-start(f32[512,512]{1,0:T(8,128)} %get-tuple-element.38), channel_id=1, source_target_pairs={{1,2},{3,4},{5,6},{7,8},{9,10},{11,12},{13,14},{15,16},{17,18},{19... | collective-permute-start | bytes 3145736 | tf_op jit(solution)/shard_map/ppermute | solution.py:317
  72.3 24.6 %collective-permute-start.10 = (f32[256,512]{1,0:T(8,128)}, f32[256,512]{1,0:T(8,128)}, u32[]{:S(2)}, u32[]{:S(2)}) collective-permute-start(f32[256,512]{1,0:T(8,128)} %add.91.sum0), channel_id=1, source_target_pairs={{0,64},{32,96},{64,128},{96,160},{128,192},{160,224},{192,0},{224,... | collective-permute-start | bytes 1572872 | tf_op jit(solution)/shard_map/ppermute | solution.py:317
  72.3 24.6 %collective-permute-start.9 = (f32[256,512]{1,0:T(8,128)}, f32[256,512]{1,0:T(8,128)}, u32[]{:S(2)}, u32[]{:S(2)}) collective-permute-start(f32[256,512]{1,0:T(8,128)} %add.91.sum0), channel_id=1, source_target_pairs={{0,128},{32,160},{64,192},{96,224},{128,0},{160,32},{192,64},{224,... | collective-permute-start | bytes 1572872 | tf_op jit(solution)/shard_map/ppermute | solution.py:317
  75.2 21.7 %collective-permute-start.8 = (f32[256,512]{1,0:T(8,128)}, f32[256,512]{1,0:T(8,128)}, u32[]{:S(2)}, u32[]{:S(2)}) collective-permute-start(f32[256,512]{1,0:T(8,128)} %add.91.sum0), channel_id=1, source_target_pairs={{0,192},{32,224},{64,0},{96,32},{128,64},{160,96},{192,128},{224,1... | collective-permute-start | bytes 1572872 | tf_op jit(solution)/shard_map/ppermute | solution.py:317
  90.1 6.8 %copy-start.1 = (f32[1,16,64,512]{3,2,1,0:T(8,128)S(1)}, f32[1,16,64,512]{3,2,1,0:T(8,128)}, u32[]{:S(2)}) copy-start(f32[1,16,64,512]{3,2,1,0:T(8,128)} %param.9) | copy-start | bytes 6291460
  90.1 6.8 %copy-start.5 = (f32[16,64,512]{2,1,0:T(8,128)S(1)}, f32[16,64,512]{2,1,0:T(8,128)}, u32[]{:S(2)}) copy-start(f32[16,64,512]{2,1,0:T(8,128)} %param.10) | copy-start | bytes 6291460
  100.6 32.8 %collective-permute-start.20 = (f32[512,512]{1,0:T(8,128)S(1)}, f32[512,512]{1,0:T(8,128)S(1)}, u32[]{:S(2)}, u32[]{:S(2)}) collective-permute-start(f32[512,512]{1,0:T(8,128)S(1)} %get-tuple-element.51), channel_id=1, source_target_pairs={{0,1},{1,0},{2,3},{3,2},{4,5},{5,4},{6,7},{7,6},{8,9},{9,8},{10,11... | collective-permute-start | bytes 3145736 | tf_op jit(solution)/shard_map/ppermute | solution.py:317
  102.3 31.1 %collective-permute-start.21 = (f32[512,512]{1,0:T(8,128)S(1)}, f32[512,512]{1,0:T(8,128)S(1)}, u32[]{:S(2)}, u32[]{:S(2)}) collective-permute-start(f32[512,512]{1,0:T(8,128)S(1)} %get-tuple-element.52), channel_id=1, source_target_pairs={{1,2},{3,4},{5,6},{7,8},{9,10},{11,12},{13,14},{15,16},{17,18},{19... | collective-permute-start | bytes 3145736 | tf_op jit(solution)/shard_map/ppermute | solution.py:317
  107.3 1.3 collective-permute-start.11
  108.5 7.1 %collective-permute-start.14 = (f32[8,128]{1,0:T(8,128)S(1)}, f32[8,128]{1,0:T(8,128)S(1)}, u32[]{:S(2)}, u32[]{:S(2)}) collective-permute-start(f32[8,128]{1,0:T(8,128)S(1)} %add.92), channel_id=1, source_target_pairs={{0,192},{32,224},{64,0},{96,32},{128,64},{160,96},{192,128},{224,1... | collective-permute-start | bytes 12296 | tf_op jit(solution)/shard_map/ppermute | solution.py:317
  109.6 5.9 %collective-permute-start.13 = (f32[8,128]{1,0:T(8,128)S(1)}, f32[8,128]{1,0:T(8,128)S(1)}, u32[]{:S(2)}, u32[]{:S(2)}) collective-permute-start(f32[8,128]{1,0:T(8,128)S(1)} %add.92), channel_id=1, source_target_pairs={{0,128},{32,160},{64,192},{96,224},{128,0},{160,32},{192,64},{224,... | collective-permute-start | bytes 12296 | tf_op jit(solution)/shard_map/ppermute | solution.py:317
  110.0 5.6 %collective-permute-start.12 = (f32[8,128]{1,0:T(8,128)S(1)}, f32[8,128]{1,0:T(8,128)S(1)}, u32[]{:S(2)}, u32[]{:S(2)}) collective-permute-start(f32[8,128]{1,0:T(8,128)S(1)} %add.92), channel_id=1, source_target_pairs={{0,64},{32,96},{64,128},{96,160},{128,192},{160,224},{192,0},{224,... | collective-permute-start | bytes 12296 | tf_op jit(solution)/shard_map/ppermute | solution.py:317
  115.6 4.9 %collective-permute-start.17 = (f32[8,128]{1,0:T(8,128)S(1)}, f32[8,128]{1,0:T(8,128)S(1)}, u32[]{:S(2)}, u32[]{:S(2)}) collective-permute-start(f32[8,128]{1,0:T(8,128)S(1)} %add_add_fusion.2), channel_id=1, source_target_pairs={{0,24},{1,25},{2,26},{3,27},{4,28},{5,29},{6,30},{7,31},{8,0},{9,1... | collective-permute-start | bytes 12296 | tf_op jit(solution)/shard_map/ppermute | solution.py:317
  115.7 5.2 %collective-permute-start.16 = (f32[8,128]{1,0:T(8,128)S(1)}, f32[8,128]{1,0:T(8,128)S(1)}, u32[]{:S(2)}, u32[]{:S(2)}) collective-permute-start(f32[8,128]{1,0:T(8,128)S(1)} %add_add_fusion.2), channel_id=1, source_target_pairs={{0,16},{1,17},{2,18},{3,19},{4,20},{5,21},{6,22},{7,23},{8,24},{9,... | collective-permute-start | bytes 12296 | tf_op jit(solution)/shard_map/ppermute | solution.py:317
  118.7 3.6 %collective-permute-start.15 = (f32[8,128]{1,0:T(8,128)S(1)}, f32[8,128]{1,0:T(8,128)S(1)}, u32[]{:S(2)}, u32[]{:S(2)}) collective-permute-start(f32[8,128]{1,0:T(8,128)S(1)} %add_add_fusion.2), channel_id=1, source_target_pairs={{0,8},{1,9},{2,10},{3,11},{4,12},{5,13},{6,14},{7,15},{8,16},{9,17... | collective-permute-start | bytes 12296 | tf_op jit(solution)/shard_map/ppermute | solution.py:317
  122.4 5.3 %collective-permute-start.18 = (f32[8,128]{1,0:T(8,128)S(1)}, f32[8,128]{1,0:T(8,128)S(1)}, u32[]{:S(2)}, u32[]{:S(2)}) collective-permute-start(f32[8,128]{1,0:T(8,128)S(1)} %add_add_fusion.1), channel_id=1, source_target_pairs={{0,2},{1,3},{2,0},{3,1},{4,6},{5,7},{6,4},{7,5},{8,10},{9,11},{10,... | collective-permute-start | bytes 12296 | tf_op jit(solution)/shard_map/ppermute | solution.py:317
  127.7 5.7 %collective-permute-start.19 = (f32[8,128]{1,0:T(8,128)S(1)}, f32[8,128]{1,0:T(8,128)S(1)}, u32[]{:S(2)}, u32[]{:S(2)}) collective-permute-start(f32[8,128]{1,0:T(8,128)S(1)} %add.99), channel_id=1, source_target_pairs={{0,4},{1,5},{2,6},{3,7},{4,0},{5,1},{6,2},{7,3},{8,12},{9,13},{10,... | collective-permute-start | bytes 12296 | tf_op jit(solution)/shard_map/ppermute | solution.py:317
  133.4 8.4 %collective-permute-start.22 = (f32[8,128]{1,0:T(8,128)S(1)}, f32[8,128]{1,0:T(8,128)S(1)}, u32[]{:S(2)}, u32[]{:S(2)}) collective-permute-start(f32[8,128]{1,0:T(8,128)S(1)} %add.100), channel_id=1, source_target_pairs={{0,32},{32,0},{64,96},{96,64},{128,160},{160,128},{192,224},{224,1... | collective-permute-start | bytes 12296 | tf_op jit(solution)/shard_map/ppermute | solution.py:317

commit v9 on v8

--- a/solution.py
+++ b/solution.py
@@ -373,8 +373,12 @@
     scale = pltpu.VMEM((8, 128), F32)
 
     y, stats = own_log(kz, prior)
-    y, part = in_order((y, part))
-    swapped = send(part, "atom", swap)
+    one, two = block * 32 // 256, block * 96 // 256
+    swapped = [send(part[:one], "atom", swap)]
+    following, swapped[0] = in_order((part[one:two], swapped[0]))
+    swapped += [send(following, "atom", swap), send(part[two:], "atom", swap)]
+    y, swapped[1] = in_order((y, swapped[1]))
+    swapped = jnp.concatenate(swapped)
     potential, to_near, to_far = pl.pallas_call(
         functools.partial(potential_kernel, ny=ny),
         in_specs=[smem, smem, hbm, hbm, hbm, vmem, hbm] + [vmem] * 4,

time: 144 us -> 148 us (1.028)
  waiting for transfers between devices: 44.9 us -> 50.5 us
  local copies, waits for them, and re-layouts: 9.68 us -> 6.01 us
    ppermute x23 -> x25, waiting for transfers between devices: 44.9 us -> 50.5 us  [send(): return lax.ppermute(value, axis, pairs)]
    unnamed x18 -> x22, local copies, waits for them, and re-layouts: 2.93 us -> 0.05 us
    dynamic_slice x1, local copies, waits for them, and re-layouts: 3.05 us -> 1.55 us  [body(): to_far = lax.dynamic_slice_in_dim(prior, core * half, half)]
    ppermute x23 -> x25, starting transfers between devices: 46.9 us -> 47.7 us  [send(): return lax.ppermute(value, axis, pairs)]
  transfers between devices with their start and end apart: 23 -> 25, of which waited for: 10 -> 11; matrix products, arithmetic and copies ran while one was open for 6% -> 6% of each run, Pallas kernels for 21% -> 21%
where the time goes in v9:
time: 148 us; the launch traced here: 146 us
  waiting for transfers between devices  50.5 us (34%)
  starting transfers between devices  47.7 us (32%)
  Pallas kernels  34.3 us (23%)
  local copies, waits for them, and re-layouts  6.01 us (4%)
  other arithmetic  5.96 us (4%)
    ppermute x25, waiting for transfers between devices, send(): return lax.ppermute(value, axis, pairs)  50.5 us
    ppermute x25, starting transfers between devices, send(): return lax.ppermute(value, axis, pairs)  47.7 us
    pallas_call x1, Pallas kernels, body(): pl.pallas_call(functools.partial(potential_kernel, ny=ny), in_specs=[smem...  7.89 us
    pallas_call x1, Pallas kernels, body(): pl.pallas_call(functools.partial(second_kernel, ny=ny), in_specs=[smem, s...  6.76 us
    pallas_call x1, Pallas kernels, body(): pl.pallas_call(functools.partial(gradient_kernel, ny=ny), in_specs=[smem,...  5.88 us
    pallas_call x1, Pallas kernels, body(): pl.pallas_call(ratio_kernel, in_specs=[smem, smem] + [vmem] * 4 + [anywhe...  3.7 us
    pallas_call x1, Pallas kernels, body(): y, stats = own_log(kz, prior)  3.01 us
    pallas_call x1, Pallas kernels, body(): y, stats = own_log(kz, own_at)  3.01 us
  transfers between devices with their start and end apart: 25, of which 11 were waited for; matrix products, arithmetic and copies ran while one was open for 6% of the time, Pallas kernels for 21%

profile of v9, /device:TPU:10, one launch (start us, length us, event | category | flops | bytes accessed | tf_op | source)
XLA Modules:
  0.0 145.6 jit_solution(12450659679041748249)
XLA Ops:
  0.7 2.4 %constant_dynamic-slice_fusion.2 = (f32[256,512]{1,0:T(8,128)}, f32[256,512]{1,0:T(8,128)S(1)}, f32[256,512]{1,0:T(8,128)S(1)}) fusion(f32[1024,512]{1,0:T(8,128)} %bitcast.17, s32[]{:T(128)S(6)} %select_n.43, s32[]{:T(128)S(6)} %select_n.45, s32[]{:T(128)S(6)} %select_n.44), kind=kLoop, calls=%fused_computation.9 | loop fusion | bytes 3145740 | tf_op jit(solution)/shard_map/dynamic_slice | solution.py:332
  3.1 1.5 %collective-permute-start.2 = (f32[256,512]{1,0:T(8,128)}, f32[256,512]{1,0:T(8,128)}, u32[]{:S(2)}, u32[]{:S(2)}) collective-permute-start(f32[256,512]{1,0:T(8,128)} %get-tuple-element.62), channel_id=1, source_target_pairs={{0,64},{32,96},{64,128},{96,160},{128,192},{160,224},{192,0},{224,... | collective-permute-start | bytes 1572872 | tf_op jit(solution)/shard_map/ppermute | solution.py:317
  4.6 0.5 collective-permute-start.4
  5.1 2.1 %collective-permute-start.3 = (f32[256,512]{1,0:T(8,128)S(1)}, f32[256,512]{1,0:T(8,128)}, u32[]{:S(2)}, u32[]{:S(2)}) collective-permute-start(f32[256,512]{1,0:T(8,128)S(1)} %get-tuple-element.64), channel_id=1, source_target_pairs={{0,128},{32,160},{64,192},{96,224},{128,0},{160,32},{192,64},{224,... | collective-permute-start | bytes 1572872 | tf_op jit(solution)/shard_map/ppermute | solution.py:317
  7.3 1.5 %constant_dynamic-slice_fusion.3 = (f32[512,512]{1,0:T(8,128)}, f32[512,512]{1,0:T(8,128)}) fusion(f32[1024,512]{1,0:T(8,128)S(1)} %bitcast.15, s32[]{:T(128)S(6)} %select_n.41, s32[]{:T(128)S(6)} %select_n.40), kind=kLoop, calls=%fused_computation.10 | loop fusion | bytes 4194312 | tf_op jit(solution)/shard_map/dynamic_slice | solution.py:353
  8.8 5.1 %collective-permute-start.1 = (f32[512,512]{1,0:T(8,128)}, f32[512,512]{1,0:T(8,128)}, u32[]{:S(2)}, u32[]{:S(2)}) collective-permute-start(f32[512,512]{1,0:T(8,128)} %get-tuple-element.65), channel_id=1, source_target_pairs={{1,2},{3,4},{5,6},{7,8},{9,10},{11,12},{13,14},{15,16},{17,18},{19... | collective-permute-start | bytes 3145736 | tf_op jit(solution)/shard_map/ppermute | solution.py:317
  14.0 0.1 collective-permute-start
  14.1 4.2 %collective-permute-done.2 = f32[256,512]{1,0:T(8,128)} collective-permute-done((f32[256,512]{1,0:T(8,128)}, f32[256,512]{1,0:T(8,128)}, u32[]{:S(2)}, u32[]{:S(2)}) %collective-permute-start.2) | collective-permute-done | bytes 524320 | tf_op jit(solution)/shard_map/ppermute | solution.py:317
  18.2 0.7 collective-permute-done.4
  18.9 11.0 %collective-permute-done.3 = f32[256,512]{1,0:T(8,128)} collective-permute-done((f32[256,512]{1,0:T(8,128)S(1)}, f32[256,512]{1,0:T(8,128)}, u32[]{:S(2)}, u32[]{:S(2)}) %collective-permute-start.3) | collective-permute-done | bytes 524320 | tf_op jit(solution)/shard_map/ppermute | solution.py:317
  29.9 1.7 %add_add_fusion = f32[256,512]{1,0:T(8,128)S(1)} fusion(f32[256,512]{1,0:T(8,128)} %collective-permute-done.4, f32[256,512]{1,0:T(8,128)} %collective-permute-done.3, f32[256,512]{1,0:T(8,128)} %collective-permute-done.2, f32[1024,512]{1,0:T(8,128)} %bitcast.18, s32[]{:T(128)S(6)} %select_n.42), kind=kLoop, calls=%fused_computation.1 | loop fusion | flops 393216 | bytes 2621444 | tf_op jit(solution)/shard_map/add | solution.py:337
  31.7 7.3 %collective-permute-start.5 = (f32[32,512]{1,0:T(8,128)S(1)}, f32[32,512]{1,0:T(8,128)S(1)}, u32[]{:S(2)}, u32[]{:S(2)}) collective-permute-start(f32[32,512]{1,0:T(8,128)S(1)} %slice.21), channel_id=1, source_target_pairs={{0,32},{32,0},{64,96},{96,64},{128,160},{160,128},{192,224},{224,1... | collective-permute-start | bytes 196616 | tf_op jit(solution)/shard_map/ppermute | solution.py:317
  39.0 0.7 slice.15
  39.7 0.6 slice.20
  40.3 4.4 %collective-permute-done.5 = f32[32,512]{1,0:T(8,128)S(1)} collective-permute-done((f32[32,512]{1,0:T(8,128)S(1)}, f32[32,512]{1,0:T(8,128)S(1)}, u32[]{:S(2)}, u32[]{:S(2)}) %collective-permute-start.5) | collective-permute-done | bytes 65568 | tf_op jit(solution)/shard_map/ppermute | solution.py:317
  44.7 2.9 %collective-permute-start.6 = (f32[64,512]{1,0:T(8,128)}, f32[64,512]{1,0:T(8,128)S(1)}, u32[]{:S(2)}, u32[]{:S(2)}) collective-permute-start(f32[64,512]{1,0:T(8,128)} %slice.20), channel_id=1, source_target_pairs={{0,32},{32,0},{64,96},{96,64},{128,160},{160,128},{192,224},{224,1... | collective-permute-start | bytes 393224 | tf_op jit(solution)/shard_map/ppermute | solution.py:317
  47.6 0.7 compare_select_fusion.1.kz
  48.3 0.0 copy-start.2
  48.4 3.1 %collective-permute-start.9 = (f32[160,512]{1,0:T(8,128)S(1)}, f32[160,512]{1,0:T(8,128)S(1)}, u32[]{:S(2)}, u32[]{:S(2)}) collective-permute-start(f32[160,512]{1,0:T(8,128)S(1)} %slice.22), channel_id=1, source_target_pairs={{0,32},{32,0},{64,96},{96,64},{128,160},{160,128},{192,224},{224,1... | collective-permute-start | bytes 983048 | tf_op jit(solution)/shard_map/ppermute | solution.py:317
  51.5 0.1 add_convert_fusion.where
  51.6 1.1 tables.1
  52.7 3.0 %own_log.2 = (f32[1024,512]{1,0:T(8,128)S(1)}, f32[8,128]{1,0:T(8,128)S(1)}) custom-call(f32[9]{0:T(128)S(1)} %compare_select_fusion.1.kz, f32[1024,512]{1,0:T(8,128)S(1)} %bitcast.16), custom_call_target="tpu_custom_call" | custom-call | tf_op jit(solution)/shard_map/own_log/pallas_call | solution.py:375
  55.7 2.2 %collective-permute-done.6 = f32[64,512]{1,0:T(8,128)S(1)} collective-permute-done((f32[64,512]{1,0:T(8,128)}, f32[64,512]{1,0:T(8,128)S(1)}, u32[]{:S(2)}, u32[]{:S(2)}) %collective-permute-start.6) | collective-permute-done | bytes 131104 | tf_op jit(solution)/shard_map/ppermute | solution.py:317
  57.8 0.0 collective-permute-done.1.far
  57.8 0.0 collective-permute-done.near
  57.9 0.0 copy-start.9
  57.9 0.0 copy-start.10
  57.9 7.9 %potential.1 = (f32[1024,512]{1,0:T(8,128)S(1)}, f32[512,512]{1,0:T(8,128)}, f32[512,512]{1,0:T(8,128)}) custom-call(s32[3]{0:T(128)S(1)} %add_convert_fusion.where, f32[9]{0:T(128)S(1)} %compare_select_fusion.1.kz, f32[512,512]{1,0:T(8,128)} %collective-permute-done.near, f32[512,512]{1,0:T(8,128)} %collective-permute-done.1.far, ...), custom_call_target="tpu_custom_call" | custom-call | tf_op jit(solution)/shard_map/potential/pallas_call | solution.py:382
  65.8 0.1 collective-permute-start.7
  65.9 1.9 %collective-permute-start.8 = (f32[512,512]{1,0:T(8,128)}, f32[512,512]{1,0:T(8,128)}, u32[]{:S(2)}, u32[]{:S(2)}) collective-permute-start(f32[512,512]{1,0:T(8,128)} %get-tuple-element.41), channel_id=1, source_target_pairs={{1,2},{3,4},{5,6},{7,8},{9,10},{11,12},{13,14},{15,16},{17,18},{19... | collective-permute-start | bytes 3145736 | tf_op jit(solution)/shard_map/ppermute | solution.py:317
  67.8 2.3 %collective-permute-done.9 = f32[160,512]{1,0:T(8,128)S(1)} collective-permute-done((f32[160,512]{1,0:T(8,128)S(1)}, f32[160,512]{1,0:T(8,128)S(1)}, u32[]{:S(2)}, u32[]{:S(2)}) %collective-permute-start.9) | collective-permute-done | bytes 327712 | tf_op jit(solution)/shard_map/ppermute | solution.py:317
  70.1 0.9 maximum_add_fusion.sum0
  71.0 2.1 %collective-permute-start.12 = (f32[256,512]{1,0:T(8,128)}, f32[256,512]{1,0:T(8,128)}, u32[]{:S(2)}, u32[]{:S(2)}) collective-permute-start(f32[256,512]{1,0:T(8,128)} %maximum_add_fusion.sum0), channel_id=1, source_target_pairs={{0,64},{32,96},{64,128},{96,160},{128,192},{160,224},{192,0},{224,... | collective-permute-start | bytes 1572872 | tf_op jit(solution)/shard_map/ppermute | solution.py:317
  73.1 1.3 collective-permute-start.11
  74.4 0.8 collective-permute-start.10
  75.2 0.7 dynamic_slice.21
  75.8 0.8 pad_add_fusion.at
  76.6 1.3 fusion
  77.9 3.0 %own_log.3 = (f32[1024,512]{1,0:T(8,128)S(1)}, f32[8,128]{1,0:T(8,128)S(1)}) custom-call(f32[9]{0:T(128)S(1)} %compare_select_fusion.1.kz, f32[1024,512]{1,0:T(8,128)S(1)} %get-tuple-element.45.field.potential), custom_call_target="tpu_custom_call" | custom-call | tf_op jit(solution)/shard_map/own_log/pallas_call | solution.py:397
  80.9 0.0 collective-permute-done.7.near
  80.9 12.6 %collective-permute-done.8.far = f32[512,512]{1,0:T(8,128)} collective-permute-done((f32[512,512]{1,0:T(8,128)}, f32[512,512]{1,0:T(8,128)}, u32[]{:S(2)}, u32[]{:S(2)}) %collective-permute-start.8) | collective-permute-done | bytes 1048608 | tf_op jit(solution)/shard_map/ppermute | solution.py:317
  93.6 6.8 %second.1 = (f32[1024,512]{1,0:T(8,128)S(1)}, f32[8,128]{1,0:T(8,128)S(1)}) custom-call(s32[3]{0:T(128)S(1)} %add_convert_fusion.where, f32[9]{0:T(128)S(1)} %compare_select_fusion.1.kz, f32[512,512]{1,0:T(8,128)} %collective-permute-done.7.near, f32[512,512]{1,0:T(8,128)} %collective-permute-done.8.far, f32[1024,512]{1,0:T(8,128)S(1)} %get-tuple-element.46.y, ...), custom_call_target="tpu_custom_call" | custom-call | tf_op jit(solution)/shard_map/second/pallas_call | solution.py:398
  100.3 0.0 collective-permute-done.12.sum3
  100.3 0.0 collective-permute-done.10.sum1
  100.4 3.7 %ratio.1 = (f32[1024,512]{1,0:T(8,128)S(1)}, f32[512,512]{1,0:T(8,128)S(1)}, f32[512,512]{1,0:T(8,128)S(1)}, f32[8,128]{1,0:T(8,128)S(1)}) custom-call(s32[3]{0:T(128)S(1)} %pad_add_fusion.at, f32[1]{0:T(128)} %bitcast.7.weight, f32[1024,512]{1,0:T(8,128)S(1)} %get-tuple-element.48.second, f32[8,128]{1,0:T(8,128)S(1)} %get-tuple-element.49.scale.stats, ...), custom_call_target="tpu_custom_call" | custom-call | tf_op jit(solution)/shard_map/ratio/pallas_call | solution.py:407
  104.1 0.1 collective-permute-start.22
  104.2 4.1 %collective-permute-start.23 = (f32[512,512]{1,0:T(8,128)S(1)}, f32[512,512]{1,0:T(8,128)S(1)}, u32[]{:S(2)}, u32[]{:S(2)}) collective-permute-start(f32[512,512]{1,0:T(8,128)S(1)} %get-tuple-element.56), channel_id=1, source_target_pairs={{1,2},{3,4},{5,6},{7,8},{9,10},{11,12},{13,14},{15,16},{17,18},{19... | collective-permute-start | bytes 3145736 | tf_op jit(solution)/shard_map/ppermute | solution.py:317
  108.3 0.1 collective-permute-start.13
  108.4 1.2 collective-permute-done.13
  109.6 1.4 collective-permute-start.16
  111.0 2.7 %collective-permute-start.15 = (f32[8,128]{1,0:T(8,128)S(1)}, f32[8,128]{1,0:T(8,128)S(1)}, u32[]{:S(2)}, u32[]{:S(2)}) collective-permute-start(f32[8,128]{1,0:T(8,128)S(1)} %add.92), channel_id=1, source_target_pairs={{0,128},{32,160},{64,192},{96,224},{128,0},{160,32},{192,64},{224,... | collective-permute-start | bytes 12296 | tf_op jit(solution)/shard_map/ppermute | solution.py:317
  113.7 1.0 collective-permute-start.14
  114.7 3.0 %own_linear.1 = (f32[1024,512]{1,0:T(8,128)S(1)}, f32[1024,512]{1,0:T(8,128)S(1)}) custom-call(f32[9]{0:T(128)S(1)} %compare_select_fusion.1.kz, f32[1024,512]{1,0:T(8,128)S(1)} %get-tuple-element.52.field, f32[1024,512]{1,0:T(8,128)S(1)} %get-tuple-element.45.field.potential, f32[8,128]{1,0:T(8,128)S(1)} %get-tuple-element.49.scale.stats), custom_call_target="tpu_custom_call" | custom-call | tf_op jit(solution)/shard_map/own_linear/pallas_call | solution.py:430
  117.7 0.0 collective-permute-done.16
  117.7 0.0 collective-permute-done.15
  117.7 0.1 collective-permute-start.19
  117.8 3.4 %collective-permute-start.18 = (f32[8,128]{1,0:T(8,128)S(1)}, f32[8,128]{1,0:T(8,128)S(1)}, u32[]{:S(2)}, u32[]{:S(2)}) collective-permute-start(f32[8,128]{1,0:T(8,128)S(1)} %add_add_fusion.2), channel_id=1, source_target_pairs={{0,16},{1,17},{2,18},{3,19},{4,20},{5,21},{6,22},{7,23},{8,24},{9,... | collective-permute-start | bytes 12296 | tf_op jit(solution)/shard_map/ppermute | solution.py:317
  121.2 2.3 %collective-permute-start.17 = (f32[8,128]{1,0:T(8,128)S(1)}, f32[8,128]{1,0:T(8,128)S(1)}, u32[]{:S(2)}, u32[]{:S(2)}) collective-permute-start(f32[8,128]{1,0:T(8,128)S(1)} %add_add_fusion.2), channel_id=1, source_target_pairs={{0,8},{1,9},{2,10},{3,11},{4,12},{5,13},{6,14},{7,15},{8,16},{9,17... | collective-permute-start | bytes 12296 | tf_op jit(solution)/shard_map/ppermute | solution.py:317
  123.6 1.3 collective-permute-done.17
  124.9 6.2 %collective-permute-done.20 = f32[8,128]{1,0:T(8,128)S(1)} collective-permute-done((f32[8,128]{1,0:T(8,128)S(1)}, f32[8,128]{1,0:T(8,128)S(1)}, u32[]{:S(2)}, u32[]{:S(2)}) %collective-permute-start.20) | collective-permute-done | bytes 4128 | tf_op jit(solution)/shard_map/ppermute | solution.py:317
  131.1 4.5 %collective-permute-done.21 = f32[8,128]{1,0:T(8,128)S(1)} collective-permute-done((f32[8,128]{1,0:T(8,128)S(1)}, f32[8,128]{1,0:T(8,128)S(1)}, u32[]{:S(2)}, u32[]{:S(2)}) %collective-permute-start.21) | collective-permute-done | bytes 4128 | tf_op jit(solution)/shard_map/ppermute | solution.py:317
  135.6 3.6 %collective-permute-start.24 = (f32[8,128]{1,0:T(8,128)S(1)}, f32[8,128]{1,0:T(8,128)S(1)}, u32[]{:S(2)}, u32[]{:S(2)}) collective-permute-start(f32[8,128]{1,0:T(8,128)S(1)} %add.100), channel_id=1, source_target_pairs={{0,32},{32,0},{64,96},{96,64},{128,160},{160,128},{192,224},{224,1... | collective-permute-start | bytes 12296 | tf_op jit(solution)/shard_map/ppermute | solution.py:317
  139.1 5.9 %gradient.1 = f32[1024,512]{1,0:T(8,128)} custom-call(s32[3]{0:T(128)S(1)} %add_convert_fusion.where, f32[9]{0:T(128)S(1)} %compare_select_fusion.1.kz, f32[512,512]{1,0:T(8,128)S(1)} %collective-permute-done.22.near, f32[512,512]{1,0:T(8,128)S(1)} %collective-permute-done.23.far, f32[1024,512]{1,0:T(8,128)S(1)} %get-tuple-element.59.y, ...), custom_call_target="tpu_custom_call" | custom-call | tf_op jit(solution)/shard_map/gradient/pallas_call | solution.py:455
  145.0 0.5 multiply_bitcast_fusion
  (36 shorter events, 0.1 us)
Async XLA Ops:
  0.6 6.6 %copy-start = (f32[1,16,64,512]{3,2,1,0:T(8,128)S(1)}, f32[1,16,64,512]{3,2,1,0:T(8,128)}, u32[]{:S(2)}) copy-start(f32[1,16,64,512]{3,2,1,0:T(8,128)} %param.8) | copy-start | bytes 6291460
  3.1 15.1 %collective-permute-start.2 = (f32[256,512]{1,0:T(8,128)}, f32[256,512]{1,0:T(8,128)}, u32[]{:S(2)}, u32[]{:S(2)}) collective-permute-start(f32[256,512]{1,0:T(8,128)} %get-tuple-element.62), channel_id=1, source_target_pairs={{0,64},{32,96},{64,128},{96,160},{128,192},{160,224},{192,0},{224,... | collective-permute-start | bytes 1572872 | tf_op jit(solution)/shard_map/ppermute | solution.py:317
  4.6 14.3 %collective-permute-start.4 = (f32[256,512]{1,0:T(8,128)S(1)}, f32[256,512]{1,0:T(8,128)}, u32[]{:S(2)}, u32[]{:S(2)}) collective-permute-start(f32[256,512]{1,0:T(8,128)S(1)} %get-tuple-element.63), channel_id=1, source_target_pairs={{0,192},{32,224},{64,0},{96,32},{128,64},{160,96},{192,128},{224,1... | collective-permute-start | bytes 1572872 | tf_op jit(solution)/shard_map/ppermute | solution.py:317
  5.1 24.8 %collective-permute-start.3 = (f32[256,512]{1,0:T(8,128)S(1)}, f32[256,512]{1,0:T(8,128)}, u32[]{:S(2)}, u32[]{:S(2)}) collective-permute-start(f32[256,512]{1,0:T(8,128)S(1)} %get-tuple-element.64), channel_id=1, source_target_pairs={{0,128},{32,160},{64,192},{96,224},{128,0},{160,32},{192,64},{224,... | collective-permute-start | bytes 1572872 | tf_op jit(solution)/shard_map/ppermute | solution.py:317
  8.8 30.2 %copy-start.4 = (s32[3]{0:T(128)S(1)}, s32[3]{0:T(128)}, u32[]{:S(2)}) copy-start(s32[3]{0:T(128)} %band.1) | copy-start | bytes 40
  8.8 49.0 %collective-permute-start.1 = (f32[512,512]{1,0:T(8,128)}, f32[512,512]{1,0:T(8,128)}, u32[]{:S(2)}, u32[]{:S(2)}) collective-permute-start(f32[512,512]{1,0:T(8,128)} %get-tuple-element.65), channel_id=1, source_target_pairs={{1,2},{3,4},{5,6},{7,8},{9,10},{11,12},{13,14},{15,16},{17,18},{19... | collective-permute-start | bytes 3145736 | tf_op jit(solution)/shard_map/ppermute | solution.py:317
  14.0 43.9 %collective-permute-start = (f32[512,512]{1,0:T(8,128)}, f32[512,512]{1,0:T(8,128)}, u32[]{:S(2)}, u32[]{:S(2)}) collective-permute-start(f32[512,512]{1,0:T(8,128)} %get-tuple-element.66), channel_id=1, source_target_pairs={{0,1},{1,0},{2,3},{3,2},{4,5},{5,4},{6,7},{7,6},{8,9},{9,8},{10,11... | collective-permute-start | bytes 3145736 | tf_op jit(solution)/shard_map/ppermute | solution.py:317
  31.7 19.8 %copy-start.5 = (f32[256,512]{1,0:T(8,128)}, f32[256,512]{1,0:T(8,128)S(1)}, u32[]{:S(2)}) copy-start(f32[256,512]{1,0:T(8,128)S(1)} %add_add_fusion) | copy-start | bytes 1572868
  31.7 13.0 %collective-permute-start.5 = (f32[32,512]{1,0:T(8,128)S(1)}, f32[32,512]{1,0:T(8,128)S(1)}, u32[]{:S(2)}, u32[]{:S(2)}) collective-permute-start(f32[32,512]{1,0:T(8,128)S(1)} %slice.21), channel_id=1, source_target_pairs={{0,32},{32,0},{64,96},{96,64},{128,160},{160,128},{192,224},{224,1... | collective-permute-start | bytes 196616 | tf_op jit(solution)/shard_map/ppermute | solution.py:317
  44.7 6.8 %copy-start.7 = (f32[32,512]{1,0:T(8,128)}, f32[32,512]{1,0:T(8,128)S(1)}, u32[]{:S(2)}) copy-start(f32[32,512]{1,0:T(8,128)S(1)} %collective-permute-done.5) | copy-start | bytes 196612
  44.7 13.1 %collective-permute-start.6 = (f32[64,512]{1,0:T(8,128)}, f32[64,512]{1,0:T(8,128)S(1)}, u32[]{:S(2)}, u32[]{:S(2)}) collective-permute-start(f32[64,512]{1,0:T(8,128)} %slice.20), channel_id=1, source_target_pairs={{0,32},{32,0},{64,96},{96,64},{128,160},{160,128},{192,224},{224,1... | collective-permute-start | bytes 393224 | tf_op jit(solution)/shard_map/ppermute | solution.py:317
  48.3 9.5 %copy-start.2 = (f32[1,16,64,512]{3,2,1,0:T(8,128)S(1)}, f32[1,16,64,512]{3,2,1,0:T(8,128)}, u32[]{:S(2)}) copy-start(f32[1,16,64,512]{3,2,1,0:T(8,128)} %param.7) | copy-start | bytes 6291460
  48.4 21.7 %collective-permute-start.9 = (f32[160,512]{1,0:T(8,128)S(1)}, f32[160,512]{1,0:T(8,128)S(1)}, u32[]{:S(2)}, u32[]{:S(2)}) collective-permute-start(f32[160,512]{1,0:T(8,128)S(1)} %slice.22), channel_id=1, source_target_pairs={{0,32},{32,0},{64,96},{96,64},{128,160},{160,128},{192,224},{224,1... | collective-permute-start | bytes 983048 | tf_op jit(solution)/shard_map/ppermute | solution.py:317
  57.9 12.2 %copy-start.6 = (f32[256,512]{1,0:T(8,128)S(1)}, f32[256,512]{1,0:T(8,128)}, u32[]{:S(2)}) copy-start(f32[256,512]{1,0:T(8,128)} %copy-done.5) | copy-start | bytes 1572868
  57.9 12.2 %copy-start.8 = (f32[32,512]{1,0:T(8,128)S(1)}, f32[32,512]{1,0:T(8,128)}, u32[]{:S(2)}) copy-start(f32[32,512]{1,0:T(8,128)} %copy-done.7) | copy-start | bytes 196612
  57.9 17.3 %copy-start.9 = (s32[8]{0:T(128)S(1)}, s32[8]{0:T(128)}, u32[]{:S(2)}) copy-start(s32[8]{0:T(128)} %param.13) | copy-start | bytes 100
  57.9 18.7 %copy-start.10 = (f32[8]{0:T(128)S(1)}, f32[8]{0:T(128)}, u32[]{:S(2)}) copy-start(f32[8]{0:T(128)} %param.11) | copy-start | bytes 100
  65.8 15.1 %collective-permute-start.7 = (f32[512,512]{1,0:T(8,128)}, f32[512,512]{1,0:T(8,128)}, u32[]{:S(2)}, u32[]{:S(2)}) collective-permute-start(f32[512,512]{1,0:T(8,128)} %get-tuple-element.40), channel_id=1, source_target_pairs={{0,1},{1,0},{2,3},{3,2},{4,5},{5,4},{6,7},{7,6},{8,9},{9,8},{10,11... | collective-permute-start | bytes 3145736 | tf_op jit(solution)/shard_map/ppermute | solution.py:317
  65.9 27.7 %collective-permute-start.8 = (f32[512,512]{1,0:T(8,128)}, f32[512,512]{1,0:T(8,128)}, u32[]{:S(2)}, u32[]{:S(2)}) collective-permute-start(f32[512,512]{1,0:T(8,128)} %get-tuple-element.41), channel_id=1, source_target_pairs={{1,2},{3,4},{5,6},{7,8},{9,10},{11,12},{13,14},{15,16},{17,18},{19... | collective-permute-start | bytes 3145736 | tf_op jit(solution)/shard_map/ppermute | solution.py:317
  71.0 29.4 %collective-permute-start.12 = (f32[256,512]{1,0:T(8,128)}, f32[256,512]{1,0:T(8,128)}, u32[]{:S(2)}, u32[]{:S(2)}) collective-permute-start(f32[256,512]{1,0:T(8,128)} %maximum_add_fusion.sum0), channel_id=1, source_target_pairs={{0,64},{32,96},{64,128},{96,160},{128,192},{160,224},{192,0},{224,... | collective-permute-start | bytes 1572872 | tf_op jit(solution)/shard_map/ppermute | solution.py:317
  73.1 27.2 %collective-permute-start.11 = (f32[256,512]{1,0:T(8,128)}, f32[256,512]{1,0:T(8,128)}, u32[]{:S(2)}, u32[]{:S(2)}) collective-permute-start(f32[256,512]{1,0:T(8,128)} %maximum_add_fusion.sum0), channel_id=1, source_target_pairs={{0,128},{32,160},{64,192},{96,224},{128,0},{160,32},{192,64},{224,... | collective-permute-start | bytes 1572872 | tf_op jit(solution)/shard_map/ppermute | solution.py:317
  74.4 26.0 %collective-permute-start.10 = (f32[256,512]{1,0:T(8,128)}, f32[256,512]{1,0:T(8,128)}, u32[]{:S(2)}, u32[]{:S(2)}) collective-permute-start(f32[256,512]{1,0:T(8,128)} %maximum_add_fusion.sum0), channel_id=1, source_target_pairs={{0,192},{32,224},{64,0},{96,32},{128,64},{160,96},{192,128},{224,1... | collective-permute-start | bytes 1572872 | tf_op jit(solution)/shard_map/ppermute | solution.py:317
  93.5 6.8 %copy-start.1 = (f32[1,16,64,512]{3,2,1,0:T(8,128)S(1)}, f32[1,16,64,512]{3,2,1,0:T(8,128)}, u32[]{:S(2)}) copy-start(f32[1,16,64,512]{3,2,1,0:T(8,128)} %param.9) | copy-start | bytes 6291460
  93.6 6.8 %copy-start.3 = (f32[16,64,512]{2,1,0:T(8,128)S(1)}, f32[16,64,512]{2,1,0:T(8,128)}, u32[]{:S(2)}) copy-start(f32[16,64,512]{2,1,0:T(8,128)} %param.10) | copy-start | bytes 6291460
  104.1 31.5 %collective-permute-start.22 = (f32[512,512]{1,0:T(8,128)S(1)}, f32[512,512]{1,0:T(8,128)S(1)}, u32[]{:S(2)}, u32[]{:S(2)}) collective-permute-start(f32[512,512]{1,0:T(8,128)S(1)} %get-tuple-element.55), channel_id=1, source_target_pairs={{0,1},{1,0},{2,3},{3,2},{4,5},{5,4},{6,7},{7,6},{8,9},{9,8},{10,11... | collective-permute-start | bytes 3145736 | tf_op jit(solution)/shard_map/ppermute | solution.py:317
  104.2 31.4 %collective-permute-start.23 = (f32[512,512]{1,0:T(8,128)S(1)}, f32[512,512]{1,0:T(8,128)S(1)}, u32[]{:S(2)}, u32[]{:S(2)}) collective-permute-start(f32[512,512]{1,0:T(8,128)S(1)} %get-tuple-element.56), channel_id=1, source_target_pairs={{1,2},{3,4},{5,6},{7,8},{9,10},{11,12},{13,14},{15,16},{17,18},{19... | collective-permute-start | bytes 3145736 | tf_op jit(solution)/shard_map/ppermute | solution.py:317
  108.3 1.3 collective-permute-start.13
  109.6 8.1 %collective-permute-start.16 = (f32[8,128]{1,0:T(8,128)S(1)}, f32[8,128]{1,0:T(8,128)S(1)}, u32[]{:S(2)}, u32[]{:S(2)}) collective-permute-start(f32[8,128]{1,0:T(8,128)S(1)} %add.92), channel_id=1, source_target_pairs={{0,192},{32,224},{64,0},{96,32},{128,64},{160,96},{192,128},{224,1... | collective-permute-start | bytes 12296 | tf_op jit(solution)/shard_map/ppermute | solution.py:317
  111.0 6.7 %collective-permute-start.15 = (f32[8,128]{1,0:T(8,128)S(1)}, f32[8,128]{1,0:T(8,128)S(1)}, u32[]{:S(2)}, u32[]{:S(2)}) collective-permute-start(f32[8,128]{1,0:T(8,128)S(1)} %add.92), channel_id=1, source_target_pairs={{0,128},{32,160},{64,192},{96,224},{128,0},{160,32},{192,64},{224,... | collective-permute-start | bytes 12296 | tf_op jit(solution)/shard_map/ppermute | solution.py:317
  113.7 4.0 %collective-permute-start.14 = (f32[8,128]{1,0:T(8,128)S(1)}, f32[8,128]{1,0:T(8,128)S(1)}, u32[]{:S(2)}, u32[]{:S(2)}) collective-permute-start(f32[8,128]{1,0:T(8,128)S(1)} %add.92), channel_id=1, source_target_pairs={{0,64},{32,96},{64,128},{96,160},{128,192},{160,224},{192,0},{224,... | collective-permute-start | bytes 12296 | tf_op jit(solution)/shard_map/ppermute | solution.py:317
  117.7 5.8 %collective-permute-start.19 = (f32[8,128]{1,0:T(8,128)S(1)}, f32[8,128]{1,0:T(8,128)S(1)}, u32[]{:S(2)}, u32[]{:S(2)}) collective-permute-start(f32[8,128]{1,0:T(8,128)S(1)} %add_add_fusion.2), channel_id=1, source_target_pairs={{0,24},{1,25},{2,26},{3,27},{4,28},{5,29},{6,30},{7,31},{8,0},{9,1... | collective-permute-start | bytes 12296 | tf_op jit(solution)/shard_map/ppermute | solution.py:317
  117.8 5.7 %collective-permute-start.18 = (f32[8,128]{1,0:T(8,128)S(1)}, f32[8,128]{1,0:T(8,128)S(1)}, u32[]{:S(2)}, u32[]{:S(2)}) collective-permute-start(f32[8,128]{1,0:T(8,128)S(1)} %add_add_fusion.2), channel_id=1, source_target_pairs={{0,16},{1,17},{2,18},{3,19},{4,20},{5,21},{6,22},{7,23},{8,24},{9,... | collective-permute-start | bytes 12296 | tf_op jit(solution)/shard_map/ppermute | solution.py:317
  121.2 3.7 %collective-permute-start.17 = (f32[8,128]{1,0:T(8,128)S(1)}, f32[8,128]{1,0:T(8,128)S(1)}, u32[]{:S(2)}, u32[]{:S(2)}) collective-permute-start(f32[8,128]{1,0:T(8,128)S(1)} %add_add_fusion.2), channel_id=1, source_target_pairs={{0,8},{1,9},{2,10},{3,11},{4,12},{5,13},{6,14},{7,15},{8,16},{9,17... | collective-permute-start | bytes 12296 | tf_op jit(solution)/shard_map/ppermute | solution.py:317
  124.9 6.2 %collective-permute-start.20 = (f32[8,128]{1,0:T(8,128)S(1)}, f32[8,128]{1,0:T(8,128)S(1)}, u32[]{:S(2)}, u32[]{:S(2)}) collective-permute-start(f32[8,128]{1,0:T(8,128)S(1)} %add_add_fusion.1), channel_id=1, source_target_pairs={{0,2},{1,3},{2,0},{3,1},{4,6},{5,7},{6,4},{7,5},{8,10},{9,11},{10,... | collective-permute-start | bytes 12296 | tf_op jit(solution)/shard_map/ppermute | solution.py:317
  131.1 4.5 %collective-permute-start.21 = (f32[8,128]{1,0:T(8,128)S(1)}, f32[8,128]{1,0:T(8,128)S(1)}, u32[]{:S(2)}, u32[]{:S(2)}) collective-permute-start(f32[8,128]{1,0:T(8,128)S(1)} %add.99), channel_id=1, source_target_pairs={{0,4},{1,5},{2,6},{3,7},{4,0},{5,1},{6,2},{7,3},{8,12},{9,13},{10,... | collective-permute-start | bytes 12296 | tf_op jit(solution)/shard_map/ppermute | solution.py:317
  135.6 9.4 %collective-permute-start.24 = (f32[8,128]{1,0:T(8,128)S(1)}, f32[8,128]{1,0:T(8,128)S(1)}, u32[]{:S(2)}, u32[]{:S(2)}) collective-permute-start(f32[8,128]{1,0:T(8,128)S(1)} %add.100), channel_id=1, source_target_pairs={{0,32},{32,0},{64,96},{96,64},{128,160},{160,128},{192,224},{224,1... | collective-permute-start | bytes 12296 | tf_op jit(solution)/shard_map/ppermute | solution.py:317

commit v10 on v8

--- a/solution.py
+++ b/solution.py
@@ -178,11 +178,16 @@
 
 
 def potential_kernel(
-    where, kz, near, far, y_in, stats, density_in, kyh, kyl, kxh, kxl, potential, to_near, to_far,
+    where, kz, near, far, more, y_in, stats, density_in, kyh, kyl, kxh, kxl, potential, to_near, to_far,
     halo, y, density, z, mid, scale, sems, *, ny
 ):
     core = where[2]
-    arriving = halo_copies(near, far, halo, sems, core)
+    piece = far.shape[0]
+    arriving = [
+        pltpu.make_async_copy(near, halo.at[1 - core], sems.at[0]),
+        pltpu.make_async_copy(far, halo.at[core, pl.ds(0, piece)], sems.at[1]),
+        pltpu.make_async_copy(more, halo.at[core, pl.ds(piece, piece)], sems.at[4]),
+    ]
     late = [pltpu.make_async_copy(y_in, y, sems.at[2]), pltpu.make_async_copy(density_in, density, sems.at[3])]
     for copy in arriving + late:
         copy.start()
@@ -332,9 +337,7 @@
         return lax.dynamic_slice_in_dim(cot, lax.rem(x_at + k, count) * block, block)
 
     blocks = [block_of(k) for k in range(1, across)]
-    part = block_of(0)
-    for k in range(1, across):
-        part = part + send(blocks[k - 1], "atom", ahead[k])
+    arrived = [send(blocks[k - 1], "atom", ahead[k]) for k in range(1, across)]
 
     y_shape, x_shape = (block, block), (nx, nx)
     distance = jnp.arange(BAND_MAX + 1, dtype=jnp.int32)
@@ -351,7 +354,7 @@
     prior = prior_log_scaling.reshape(rows, nx)
     to_near = lax.dynamic_slice_in_dim(prior, (1 - core) * half, half)
     to_far = lax.dynamic_slice_in_dim(prior, core * half, half)
-    far = send(to_far, "slab", chips)
+    far = [send(to_far[k : k + half // 2], "slab", chips) for k in (0, half // 2)]
     near = send(to_near, "slab", cores)
 
     where = jnp.stack([slab_at > 0, slab_at < slabs - 1, core > 0]).astype(jnp.int32)
@@ -373,17 +376,18 @@
     scale = pltpu.VMEM((8, 128), F32)
 
     y, stats = own_log(kz, prior)
+    part = sum(arrived, block_of(0))
     y, part = in_order((y, part))
     swapped = send(part, "atom", swap)
     potential, to_near, to_far = pl.pallas_call(
         functools.partial(potential_kernel, ny=ny),
-        in_specs=[smem, smem, hbm, hbm, hbm, vmem, hbm] + [vmem] * 4,
+        in_specs=[smem, smem, hbm, hbm, hbm, hbm, vmem, hbm] + [vmem] * 4,
         out_specs=[vmem, anywhere, anywhere],
         out_shape=[shape(rows, nx), shape(half, nx), shape(half, nx)],
-        scratch_shapes=[halo, whole, whole, *scratch, scale, pltpu.SemaphoreType.DMA((4,))],
+        scratch_shapes=[halo, whole, whole, *scratch, scale, pltpu.SemaphoreType.DMA((5,))],
         compiler_params=params,
         name="potential",
-    )(where, kz, near, far, y, stats, atom_log_density.reshape(rows, nx), *tables)
+    )(where, kz, near, *far, y, stats, atom_log_density.reshape(rows, nx), *tables)
 
     far = send(to_far, "slab", chips)
     near = send(to_near, "slab", cores)

time: 144 us -> 143 us (level)
  starting transfers between devices: 46.9 us -> 50.8 us
  waiting for transfers between devices: 44.9 us -> 41.4 us
    ppermute x23 -> x24, starting transfers between devices: 46.9 us -> 50.8 us  [send(): return lax.ppermute(value, axis, pairs)]
    ppermute x23 -> x24, waiting for transfers between devices: 44.9 us -> 41.4 us  [send(): return lax.ppermute(value, axis, pairs)]
    dynamic_slice x1, local copies, waits for them, and re-layouts: 3.05 us -> 1.04 us  [body(): to_near = lax.dynamic_slice_in_dim(prior, (1 - core) * half, half)]
  transfers between devices with their start and end apart: 23 -> 24, of which waited for: 10 -> 9; matrix products, arithmetic and copies ran while one was open for 6% -> 6% of each run, Pallas kernels for 21% -> 21%
where the time goes in v10:
time: 143 us; the launch traced here: 142 us
  starting transfers between devices  50.8 us (36%)
  waiting for transfers between devices  41.4 us (29%)
  Pallas kernels  34.2 us (24%)
  local copies, waits for them, and re-layouts  8.91 us (6%)
  other arithmetic  5.91 us (4%)
    ppermute x24, starting transfers between devices, send(): return lax.ppermute(value, axis, pairs)  50.8 us
    ppermute x24, waiting for transfers between devices, send(): return lax.ppermute(value, axis, pairs)  41.4 us
    pallas_call x1, Pallas kernels, body(): pl.pallas_call(functools.partial(potential_kernel, ny=ny), in_specs=[smem...  7.84 us
    pallas_call x1, Pallas kernels, body(): pl.pallas_call(functools.partial(second_kernel, ny=ny), in_specs=[smem, s...  6.76 us
    pallas_call x1, Pallas kernels, body(): pl.pallas_call(functools.partial(gradient_kernel, ny=ny), in_specs=[smem,...  5.88 us
    pallas_call x1, Pallas kernels, body(): pl.pallas_call(ratio_kernel, in_specs=[smem, smem] + [vmem] * 4 + [anywhe...  3.7 us
    pallas_call x1, Pallas kernels, body(): y, stats = own_log(kz, prior)  3.01 us
    pallas_call x1, Pallas kernels, body(): y, stats = own_log(kz, own_at)  3.01 us
  transfers between devices with their start and end apart: 24, of which 9 were waited for; matrix products, arithmetic and copies ran while one was open for 6% of the time, Pallas kernels for 21%

profile of v10, /device:TPU:10, one launch (start us, length us, event | category | flops | bytes accessed | tf_op | source)
XLA Modules:
  0.0 142.4 jit_solution(14518521958143349727)
XLA Ops:
  0.7 2.6 %constant_dynamic-slice_fusion.3 = (f32[256,512]{1,0:T(8,128)S(1)}, f32[256,512]{1,0:T(8,128)}, f32[256,512]{1,0:T(8,128)}) fusion(f32[1024,512]{1,0:T(8,128)} %bitcast.18, s32[]{:T(128)S(6)} %select_n.43, s32[]{:T(128)S(6)} %select_n.45, s32[]{:T(128)S(6)} %select_n.44), kind=kLoop, calls=%fused_computation.9 | loop fusion | bytes 3145740 | tf_op jit(solution)/shard_map/dynamic_slice | solution.py:337
  3.3 1.5 %collective-permute-start.3 = (f32[256,512]{1,0:T(8,128)S(1)}, f32[256,512]{1,0:T(8,128)}, u32[]{:S(2)}, u32[]{:S(2)}) collective-permute-start(f32[256,512]{1,0:T(8,128)S(1)} %get-tuple-element.58), channel_id=1, source_target_pairs={{0,64},{32,96},{64,128},{96,160},{128,192},{160,224},{192,0},{224,... | collective-permute-start | bytes 1572872 | tf_op jit(solution)/shard_map/ppermute | solution.py:322
  4.8 1.0 constant_dynamic-slice_fusion.5
  5.9 0.5 collective-permute-start.5
  6.4 2.1 %collective-permute-start.4 = (f32[256,512]{1,0:T(8,128)}, f32[256,512]{1,0:T(8,128)}, u32[]{:S(2)}, u32[]{:S(2)}) collective-permute-start(f32[256,512]{1,0:T(8,128)} %get-tuple-element.60), channel_id=1, source_target_pairs={{0,128},{32,160},{64,192},{96,224},{128,0},{160,32},{192,64},{224,... | collective-permute-start | bytes 1572872 | tf_op jit(solution)/shard_map/ppermute | solution.py:322
  8.5 1.1 constant_dynamic-slice_fusion.4
  9.6 6.0 %collective-permute-start.2 = (f32[256,512]{1,0:T(8,128)}, f32[256,512]{1,0:T(8,128)}, u32[]{:S(2)}, u32[]{:S(2)}) collective-permute-start(f32[256,512]{1,0:T(8,128)} %get-tuple-element.61), channel_id=1, source_target_pairs={{1,2},{3,4},{5,6},{7,8},{9,10},{11,12},{13,14},{15,16},{17,18},{19... | collective-permute-start | bytes 1572872 | tf_op jit(solution)/shard_map/ppermute | solution.py:322
  15.6 2.7 %collective-permute-done.3 = f32[256,512]{1,0:T(8,128)} collective-permute-done((f32[256,512]{1,0:T(8,128)S(1)}, f32[256,512]{1,0:T(8,128)}, u32[]{:S(2)}, u32[]{:S(2)}) %collective-permute-start.3) | collective-permute-done | bytes 524320 | tf_op jit(solution)/shard_map/ppermute | solution.py:322
  18.2 3.8 %collective-permute-start.1 = (f32[256,512]{1,0:T(8,128)}, f32[256,512]{1,0:T(8,128)}, u32[]{:S(2)}, u32[]{:S(2)}) collective-permute-start(f32[256,512]{1,0:T(8,128)} %get-tuple-element.62), channel_id=1, source_target_pairs={{1,2},{3,4},{5,6},{7,8},{9,10},{11,12},{13,14},{15,16},{17,18},{19... | collective-permute-start | bytes 1572872 | tf_op jit(solution)/shard_map/ppermute | solution.py:322
  22.1 0.6 slice.12
  22.7 1.1 tables.1
  23.8 0.7 compare_select_fusion.1.kz
  24.4 3.0 %own_log.2 = (f32[1024,512]{1,0:T(8,128)S(1)}, f32[8,128]{1,0:T(8,128)S(1)}) custom-call(f32[9]{0:T(128)S(1)} %compare_select_fusion.1.kz, f32[1024,512]{1,0:T(8,128)S(1)} %bitcast.17), custom_call_target="tpu_custom_call" | custom-call | tf_op jit(solution)/shard_map/own_log/pallas_call | solution.py:378
  27.4 0.0 copy-start.3
  27.5 1.3 copy-done.3
  28.8 0.1 add_convert_fusion.where
  28.8 0.0 collective-permute-done.5
  28.8 3.5 %collective-permute-done.4 = f32[256,512]{1,0:T(8,128)} collective-permute-done((f32[256,512]{1,0:T(8,128)}, f32[256,512]{1,0:T(8,128)}, u32[]{:S(2)}, u32[]{:S(2)}) %collective-permute-start.4) | collective-permute-done | bytes 524320 | tf_op jit(solution)/shard_map/ppermute | solution.py:322
  32.4 1.7 %add_add_fusion = f32[256,512]{1,0:T(8,128)S(1)} fusion(f32[256,512]{1,0:T(8,128)} %collective-permute-done.5, f32[256,512]{1,0:T(8,128)} %collective-permute-done.4, f32[256,512]{1,0:T(8,128)} %collective-permute-done.3, f32[1024,512]{1,0:T(8,128)} %bitcast.19, s32[]{:T(128)S(6)} %select_n.42), kind=kLoop, calls=%fused_computation | loop fusion | flops 393216 | bytes 2621444 | tf_op jit(solution)/shard_map/add | solution.py:379
  34.1 7.3 %collective-permute-start.8 = (f32[256,512]{1,0:T(8,128)S(1)}, f32[256,512]{1,0:T(8,128)S(1)}, u32[]{:S(2)}, u32[]{:S(2)}) collective-permute-start(f32[256,512]{1,0:T(8,128)S(1)} %add_add_fusion), channel_id=1, source_target_pairs={{0,32},{32,0},{64,96},{96,64},{128,160},{160,128},{192,224},{224,1... | collective-permute-start | bytes 1572872 | tf_op jit(solution)/shard_map/ppermute | solution.py:322
  41.4 0.0 collective-permute-done.2.more
  41.4 0.0 collective-permute-done.1.far
  41.4 0.0 copy-start.2
  41.4 1.6 %copy-done.2 = f32[1,16,64,512]{3,2,1,0:T(8,128)S(1)} copy-done((f32[1,16,64,512]{3,2,1,0:T(8,128)S(1)}, f32[1,16,64,512]{3,2,1,0:T(8,128)}, u32[]{:S(2)}) %copy-start.2) | copy-done | bytes 2097176
  43.0 7.8 %potential.1 = (f32[1024,512]{1,0:T(8,128)S(1)}, f32[512,512]{1,0:T(8,128)}, f32[512,512]{1,0:T(8,128)}) custom-call(s32[3]{0:T(128)S(1)} %add_convert_fusion.where, f32[9]{0:T(128)S(1)} %compare_select_fusion.1.kz, f32[512,512]{1,0:T(8,128)} %collective-permute-done.near, f32[256,512]{1,0:T(8,128)} %collective-permute-done.1.far, ...), custom_call_target="tpu_custom_call" | custom-call | tf_op jit(solution)/shard_map/potential/pallas_call | solution.py:382
  50.9 0.1 collective-permute-start.6
  51.0 3.8 %collective-permute-start.7 = (f32[512,512]{1,0:T(8,128)}, f32[512,512]{1,0:T(8,128)}, u32[]{:S(2)}, u32[]{:S(2)}) collective-permute-start(f32[512,512]{1,0:T(8,128)} %get-tuple-element.38), channel_id=1, source_target_pairs={{1,2},{3,4},{5,6},{7,8},{9,10},{11,12},{13,14},{15,16},{17,18},{19... | collective-permute-start | bytes 3145736 | tf_op jit(solution)/shard_map/ppermute | solution.py:322
  54.8 3.3 %collective-permute-done.8 = f32[256,512]{1,0:T(8,128)S(1)} collective-permute-done((f32[256,512]{1,0:T(8,128)S(1)}, f32[256,512]{1,0:T(8,128)S(1)}, u32[]{:S(2)}, u32[]{:S(2)}) %collective-permute-start.8) | collective-permute-done | bytes 524320 | tf_op jit(solution)/shard_map/ppermute | solution.py:322
  58.1 0.9 add.91.sum0
  59.0 3.1 %collective-permute-start.11 = (f32[256,512]{1,0:T(8,128)}, f32[256,512]{1,0:T(8,128)}, u32[]{:S(2)}, u32[]{:S(2)}) collective-permute-start(f32[256,512]{1,0:T(8,128)} %add.91.sum0), channel_id=1, source_target_pairs={{0,64},{32,96},{64,128},{96,160},{128,192},{160,224},{192,0},{224,... | collective-permute-start | bytes 1572872 | tf_op jit(solution)/shard_map/ppermute | solution.py:322
  62.1 0.3 collective-permute-start.10
  62.4 1.7 %collective-permute-start.9 = (f32[256,512]{1,0:T(8,128)}, f32[256,512]{1,0:T(8,128)}, u32[]{:S(2)}, u32[]{:S(2)}) collective-permute-start(f32[256,512]{1,0:T(8,128)} %add.91.sum0), channel_id=1, source_target_pairs={{0,192},{32,224},{64,0},{96,32},{128,64},{160,96},{192,128},{224,1... | collective-permute-start | bytes 1572872 | tf_op jit(solution)/shard_map/ppermute | solution.py:322
  64.2 0.7 dynamic_slice.21
  64.8 0.8 pad_add_fusion.at
  65.6 1.3 fusion
  66.9 3.0 %own_log.3 = (f32[1024,512]{1,0:T(8,128)S(1)}, f32[8,128]{1,0:T(8,128)S(1)}) custom-call(f32[9]{0:T(128)S(1)} %compare_select_fusion.1.kz, f32[1024,512]{1,0:T(8,128)S(1)} %get-tuple-element.41.field.potential), custom_call_target="tpu_custom_call" | custom-call | tf_op jit(solution)/shard_map/own_log/pallas_call | solution.py:397
  69.9 0.0 collective-permute-done.6.near
  69.9 18.8 %collective-permute-done.7.far = f32[512,512]{1,0:T(8,128)} collective-permute-done((f32[512,512]{1,0:T(8,128)}, f32[512,512]{1,0:T(8,128)}, u32[]{:S(2)}, u32[]{:S(2)}) %collective-permute-start.7) | collective-permute-done | bytes 1048608 | tf_op jit(solution)/shard_map/ppermute | solution.py:322
  88.7 6.8 %second.1 = (f32[1024,512]{1,0:T(8,128)S(1)}, f32[8,128]{1,0:T(8,128)S(1)}) custom-call(s32[3]{0:T(128)S(1)} %add_convert_fusion.where, f32[9]{0:T(128)S(1)} %compare_select_fusion.1.kz, f32[512,512]{1,0:T(8,128)} %collective-permute-done.6.near, f32[512,512]{1,0:T(8,128)} %collective-permute-done.7.far, f32[1024,512]{1,0:T(8,128)S(1)} %get-tuple-element.42.y, ...), custom_call_target="tpu_custom_call" | custom-call | tf_op jit(solution)/shard_map/second/pallas_call | solution.py:398
  95.5 0.0 collective-permute-done.9.sum1
  95.6 3.7 %ratio.1 = (f32[1024,512]{1,0:T(8,128)S(1)}, f32[512,512]{1,0:T(8,128)S(1)}, f32[512,512]{1,0:T(8,128)S(1)}, f32[8,128]{1,0:T(8,128)S(1)}) custom-call(s32[3]{0:T(128)S(1)} %pad_add_fusion.at, f32[1]{0:T(128)} %bitcast.7.weight, f32[1024,512]{1,0:T(8,128)S(1)} %get-tuple-element.44.second, f32[8,128]{1,0:T(8,128)S(1)} %get-tuple-element.45.scale.stats, ...), custom_call_target="tpu_custom_call" | custom-call | tf_op jit(solution)/shard_map/ratio/pallas_call | solution.py:407
  99.3 0.1 collective-permute-start.21
  99.4 3.7 %collective-permute-start.22 = (f32[512,512]{1,0:T(8,128)S(1)}, f32[512,512]{1,0:T(8,128)S(1)}, u32[]{:S(2)}, u32[]{:S(2)}) collective-permute-start(f32[512,512]{1,0:T(8,128)S(1)} %get-tuple-element.52), channel_id=1, source_target_pairs={{1,2},{3,4},{5,6},{7,8},{9,10},{11,12},{13,14},{15,16},{17,18},{19... | collective-permute-start | bytes 3145736 | tf_op jit(solution)/shard_map/ppermute | solution.py:322
  103.1 0.1 collective-permute-start.12
  103.2 1.2 collective-permute-done.12
  104.3 0.0 collective-permute-start.15
  104.3 1.5 %collective-permute-start.14 = (f32[8,128]{1,0:T(8,128)S(1)}, f32[8,128]{1,0:T(8,128)S(1)}, u32[]{:S(2)}, u32[]{:S(2)}) collective-permute-start(f32[8,128]{1,0:T(8,128)S(1)} %add.92), channel_id=1, source_target_pairs={{0,128},{32,160},{64,192},{96,224},{128,0},{160,32},{192,64},{224,... | collective-permute-start | bytes 12296 | tf_op jit(solution)/shard_map/ppermute | solution.py:322
  105.8 2.6 %collective-permute-start.13 = (f32[8,128]{1,0:T(8,128)S(1)}, f32[8,128]{1,0:T(8,128)S(1)}, u32[]{:S(2)}, u32[]{:S(2)}) collective-permute-start(f32[8,128]{1,0:T(8,128)S(1)} %add.92), channel_id=1, source_target_pairs={{0,64},{32,96},{64,128},{96,160},{128,192},{160,224},{192,0},{224,... | collective-permute-start | bytes 12296 | tf_op jit(solution)/shard_map/ppermute | solution.py:322
  108.4 3.0 %own_linear.1 = (f32[1024,512]{1,0:T(8,128)S(1)}, f32[1024,512]{1,0:T(8,128)S(1)}) custom-call(f32[9]{0:T(128)S(1)} %compare_select_fusion.1.kz, f32[1024,512]{1,0:T(8,128)S(1)} %get-tuple-element.48.field, f32[1024,512]{1,0:T(8,128)S(1)} %get-tuple-element.41.field.potential, f32[8,128]{1,0:T(8,128)S(1)} %get-tuple-element.45.scale.stats), custom_call_target="tpu_custom_call" | custom-call | tf_op jit(solution)/shard_map/own_linear/pallas_call | solution.py:430
  111.4 0.0 collective-permute-done.13
  111.4 0.1 collective-permute-start.18
  111.5 3.0 %collective-permute-start.17 = (f32[8,128]{1,0:T(8,128)S(1)}, f32[8,128]{1,0:T(8,128)S(1)}, u32[]{:S(2)}, u32[]{:S(2)}) collective-permute-start(f32[8,128]{1,0:T(8,128)S(1)} %add_add_fusion.2), channel_id=1, source_target_pairs={{0,16},{1,17},{2,18},{3,19},{4,20},{5,21},{6,22},{7,23},{8,24},{9,... | collective-permute-start | bytes 12296 | tf_op jit(solution)/shard_map/ppermute | solution.py:322
  114.5 2.0 %collective-permute-start.16 = (f32[8,128]{1,0:T(8,128)S(1)}, f32[8,128]{1,0:T(8,128)S(1)}, u32[]{:S(2)}, u32[]{:S(2)}) collective-permute-start(f32[8,128]{1,0:T(8,128)S(1)} %add_add_fusion.2), channel_id=1, source_target_pairs={{0,8},{1,9},{2,10},{3,11},{4,12},{5,13},{6,14},{7,15},{8,16},{9,17... | collective-permute-start | bytes 12296 | tf_op jit(solution)/shard_map/ppermute | solution.py:322
  116.5 0.0 collective-permute-done.18
  116.5 0.2 collective-permute-done.17
  116.7 1.5 %collective-permute-done.16 = f32[8,128]{1,0:T(8,128)S(1)} collective-permute-done((f32[8,128]{1,0:T(8,128)S(1)}, f32[8,128]{1,0:T(8,128)S(1)}, u32[]{:S(2)}, u32[]{:S(2)}) %collective-permute-start.16) | collective-permute-done | bytes 4128 | tf_op jit(solution)/shard_map/ppermute | solution.py:322
  118.2 0.6 collective-permute-start.19
  118.8 6.6 %collective-permute-done.19 = f32[8,128]{1,0:T(8,128)S(1)} collective-permute-done((f32[8,128]{1,0:T(8,128)S(1)}, f32[8,128]{1,0:T(8,128)S(1)}, u32[]{:S(2)}, u32[]{:S(2)}) %collective-permute-start.19) | collective-permute-done | bytes 4128 | tf_op jit(solution)/shard_map/ppermute | solution.py:322
  125.3 0.8 collective-permute-start.20
  126.1 3.7 %collective-permute-done.20 = f32[8,128]{1,0:T(8,128)S(1)} collective-permute-done((f32[8,128]{1,0:T(8,128)S(1)}, f32[8,128]{1,0:T(8,128)S(1)}, u32[]{:S(2)}, u32[]{:S(2)}) %collective-permute-start.20) | collective-permute-done | bytes 4128 | tf_op jit(solution)/shard_map/ppermute | solution.py:322
  129.8 0.0 collective-permute-done.21.near
  129.8 6.1 %collective-permute-start.23 = (f32[8,128]{1,0:T(8,128)S(1)}, f32[8,128]{1,0:T(8,128)S(1)}, u32[]{:S(2)}, u32[]{:S(2)}) collective-permute-start(f32[8,128]{1,0:T(8,128)S(1)} %add.100), channel_id=1, source_target_pairs={{0,32},{32,0},{64,96},{96,64},{128,160},{160,128},{192,224},{224,1... | collective-permute-start | bytes 12296 | tf_op jit(solution)/shard_map/ppermute | solution.py:322
  135.9 5.9 %gradient.1 = f32[1024,512]{1,0:T(8,128)} custom-call(s32[3]{0:T(128)S(1)} %add_convert_fusion.where, f32[9]{0:T(128)S(1)} %compare_select_fusion.1.kz, f32[512,512]{1,0:T(8,128)S(1)} %collective-permute-done.21.near, f32[512,512]{1,0:T(8,128)S(1)} %collective-permute-done.22.far, f32[1024,512]{1,0:T(8,128)S(1)} %get-tuple-element.55.y, ...), custom_call_target="tpu_custom_call" | custom-call | tf_op jit(solution)/shard_map/gradient/pallas_call | solution.py:455
  141.8 0.5 multiply_bitcast_fusion
  (28 shorter events, 0.1 us)
Async XLA Ops:
  0.6 4.2 %copy-start = (f32[1,16,64,512]{3,2,1,0:T(8,128)S(1)}, f32[1,16,64,512]{3,2,1,0:T(8,128)}, u32[]{:S(2)}) copy-start(f32[1,16,64,512]{3,2,1,0:T(8,128)} %param.8) | copy-start | bytes 6291460
  3.3 14.9 %collective-permute-start.3 = (f32[256,512]{1,0:T(8,128)S(1)}, f32[256,512]{1,0:T(8,128)}, u32[]{:S(2)}, u32[]{:S(2)}) collective-permute-start(f32[256,512]{1,0:T(8,128)S(1)} %get-tuple-element.58), channel_id=1, source_target_pairs={{0,64},{32,96},{64,128},{96,160},{128,192},{160,224},{192,0},{224,... | collective-permute-start | bytes 1572872 | tf_op jit(solution)/shard_map/ppermute | solution.py:322
  4.8 17.3 %copy-start.6 = (s32[3]{0:T(128)S(1)}, s32[3]{0:T(128)}, u32[]{:S(2)}) copy-start(s32[3]{0:T(128)} %band.1) | copy-start | bytes 40
  5.8 35.5 %collective-permute-start = (f32[512,512]{1,0:T(8,128)}, f32[512,512]{1,0:T(8,128)}, u32[]{:S(2)}, u32[]{:S(2)}) collective-permute-start(f32[512,512]{1,0:T(8,128)} %constant_dynamic-slice_fusion.5), channel_id=1, source_target_pairs={{0,1},{1,0},{2,3},{3,2},{4,5},{5,4},{6,7},{7,6},{8,9},{9,8},{10,11... | collective-permute-start | bytes 3145736 | tf_op jit(solution)/shard_map/ppermute | solution.py:322
  5.9 23.0 %collective-permute-start.5 = (f32[256,512]{1,0:T(8,128)}, f32[256,512]{1,0:T(8,128)}, u32[]{:S(2)}, u32[]{:S(2)}) collective-permute-start(f32[256,512]{1,0:T(8,128)} %get-tuple-element.59), channel_id=1, source_target_pairs={{0,192},{32,224},{64,0},{96,32},{128,64},{160,96},{192,128},{224,1... | collective-permute-start | bytes 1572872 | tf_op jit(solution)/shard_map/ppermute | solution.py:322
  6.4 26.0 %collective-permute-start.4 = (f32[256,512]{1,0:T(8,128)}, f32[256,512]{1,0:T(8,128)}, u32[]{:S(2)}, u32[]{:S(2)}) collective-permute-start(f32[256,512]{1,0:T(8,128)} %get-tuple-element.60), channel_id=1, source_target_pairs={{0,128},{32,160},{64,192},{96,224},{128,0},{160,32},{192,64},{224,... | collective-permute-start | bytes 1572872 | tf_op jit(solution)/shard_map/ppermute | solution.py:322
  9.6 31.8 %collective-permute-start.2 = (f32[256,512]{1,0:T(8,128)}, f32[256,512]{1,0:T(8,128)}, u32[]{:S(2)}, u32[]{:S(2)}) collective-permute-start(f32[256,512]{1,0:T(8,128)} %get-tuple-element.61), channel_id=1, source_target_pairs={{1,2},{3,4},{5,6},{7,8},{9,10},{11,12},{13,14},{15,16},{17,18},{19... | collective-permute-start | bytes 1572872 | tf_op jit(solution)/shard_map/ppermute | solution.py:322
  18.2 23.2 %collective-permute-start.1 = (f32[256,512]{1,0:T(8,128)}, f32[256,512]{1,0:T(8,128)}, u32[]{:S(2)}, u32[]{:S(2)}) collective-permute-start(f32[256,512]{1,0:T(8,128)} %get-tuple-element.62), channel_id=1, source_target_pairs={{1,2},{3,4},{5,6},{7,8},{9,10},{11,12},{13,14},{15,16},{17,18},{19... | collective-permute-start | bytes 1572872 | tf_op jit(solution)/shard_map/ppermute | solution.py:322
  27.4 1.3 copy-start.3
  28.8 12.6 %copy-start.4 = (f32[1024,512]{1,0:T(8,128)S(1)}, f32[1024,512]{1,0:T(8,128)}, u32[]{:S(2)}) copy-start(f32[1024,512]{1,0:T(8,128)} %copy-done.3) | copy-start | bytes 6291460
  34.1 24.0 %collective-permute-start.8 = (f32[256,512]{1,0:T(8,128)S(1)}, f32[256,512]{1,0:T(8,128)S(1)}, u32[]{:S(2)}, u32[]{:S(2)}) collective-permute-start(f32[256,512]{1,0:T(8,128)S(1)} %add_add_fusion), channel_id=1, source_target_pairs={{0,32},{32,0},{64,96},{96,64},{128,160},{160,128},{192,224},{224,1... | collective-permute-start | bytes 1572872 | tf_op jit(solution)/shard_map/ppermute | solution.py:322
  41.4 1.6 %copy-start.2 = (f32[1,16,64,512]{3,2,1,0:T(8,128)S(1)}, f32[1,16,64,512]{3,2,1,0:T(8,128)}, u32[]{:S(2)}) copy-start(f32[1,16,64,512]{3,2,1,0:T(8,128)} %param.7) | copy-start | bytes 6291460
  43.0 21.2 %copy-start.7 = (s32[8]{0:T(128)S(1)}, s32[8]{0:T(128)}, u32[]{:S(2)}) copy-start(s32[8]{0:T(128)} %param.13) | copy-start | bytes 100
  43.0 22.6 %copy-start.8 = (f32[8]{0:T(128)S(1)}, f32[8]{0:T(128)}, u32[]{:S(2)}) copy-start(f32[8]{0:T(128)} %param.11) | copy-start | bytes 100
  50.9 19.0 %collective-permute-start.6 = (f32[512,512]{1,0:T(8,128)}, f32[512,512]{1,0:T(8,128)}, u32[]{:S(2)}, u32[]{:S(2)}) collective-permute-start(f32[512,512]{1,0:T(8,128)} %get-tuple-element.37), channel_id=1, source_target_pairs={{0,1},{1,0},{2,3},{3,2},{4,5},{5,4},{6,7},{7,6},{8,9},{9,8},{10,11... | collective-permute-start | bytes 3145736 | tf_op jit(solution)/shard_map/ppermute | solution.py:322
  51.0 37.8 %collective-permute-start.7 = (f32[512,512]{1,0:T(8,128)}, f32[512,512]{1,0:T(8,128)}, u32[]{:S(2)}, u32[]{:S(2)}) collective-permute-start(f32[512,512]{1,0:T(8,128)} %get-tuple-element.38), channel_id=1, source_target_pairs={{1,2},{3,4},{5,6},{7,8},{9,10},{11,12},{13,14},{15,16},{17,18},{19... | collective-permute-start | bytes 3145736 | tf_op jit(solution)/shard_map/ppermute | solution.py:322
  59.0 36.5 %collective-permute-start.11 = (f32[256,512]{1,0:T(8,128)}, f32[256,512]{1,0:T(8,128)}, u32[]{:S(2)}, u32[]{:S(2)}) collective-permute-start(f32[256,512]{1,0:T(8,128)} %add.91.sum0), channel_id=1, source_target_pairs={{0,64},{32,96},{64,128},{96,160},{128,192},{160,224},{192,0},{224,... | collective-permute-start | bytes 1572872 | tf_op jit(solution)/shard_map/ppermute | solution.py:322
  62.1 33.4 %collective-permute-start.10 = (f32[256,512]{1,0:T(8,128)}, f32[256,512]{1,0:T(8,128)}, u32[]{:S(2)}, u32[]{:S(2)}) collective-permute-start(f32[256,512]{1,0:T(8,128)} %add.91.sum0), channel_id=1, source_target_pairs={{0,128},{32,160},{64,192},{96,224},{128,0},{160,32},{192,64},{224,... | collective-permute-start | bytes 1572872 | tf_op jit(solution)/shard_map/ppermute | solution.py:322
  62.4 33.1 %collective-permute-start.9 = (f32[256,512]{1,0:T(8,128)}, f32[256,512]{1,0:T(8,128)}, u32[]{:S(2)}, u32[]{:S(2)}) collective-permute-start(f32[256,512]{1,0:T(8,128)} %add.91.sum0), channel_id=1, source_target_pairs={{0,192},{32,224},{64,0},{96,32},{128,64},{160,96},{192,128},{224,1... | collective-permute-start | bytes 1572872 | tf_op jit(solution)/shard_map/ppermute | solution.py:322
  88.7 6.8 %copy-start.1 = (f32[1,16,64,512]{3,2,1,0:T(8,128)S(1)}, f32[1,16,64,512]{3,2,1,0:T(8,128)}, u32[]{:S(2)}) copy-start(f32[1,16,64,512]{3,2,1,0:T(8,128)} %param.9) | copy-start | bytes 6291460
  88.7 6.8 %copy-start.5 = (f32[16,64,512]{2,1,0:T(8,128)S(1)}, f32[16,64,512]{2,1,0:T(8,128)}, u32[]{:S(2)}) copy-start(f32[16,64,512]{2,1,0:T(8,128)} %param.10) | copy-start | bytes 6291460
  99.3 30.6 %collective-permute-start.21 = (f32[512,512]{1,0:T(8,128)S(1)}, f32[512,512]{1,0:T(8,128)S(1)}, u32[]{:S(2)}, u32[]{:S(2)}) collective-permute-start(f32[512,512]{1,0:T(8,128)S(1)} %get-tuple-element.51), channel_id=1, source_target_pairs={{0,1},{1,0},{2,3},{3,2},{4,5},{5,4},{6,7},{7,6},{8,9},{9,8},{10,11... | collective-permute-start | bytes 3145736 | tf_op jit(solution)/shard_map/ppermute | solution.py:322
  99.4 30.5 %collective-permute-start.22 = (f32[512,512]{1,0:T(8,128)S(1)}, f32[512,512]{1,0:T(8,128)S(1)}, u32[]{:S(2)}, u32[]{:S(2)}) collective-permute-start(f32[512,512]{1,0:T(8,128)S(1)} %get-tuple-element.52), channel_id=1, source_target_pairs={{1,2},{3,4},{5,6},{7,8},{9,10},{11,12},{13,14},{15,16},{17,18},{19... | collective-permute-start | bytes 3145736 | tf_op jit(solution)/shard_map/ppermute | solution.py:322
  103.1 1.3 collective-permute-start.12
  104.3 7.1 %collective-permute-start.15 = (f32[8,128]{1,0:T(8,128)S(1)}, f32[8,128]{1,0:T(8,128)S(1)}, u32[]{:S(2)}, u32[]{:S(2)}) collective-permute-start(f32[8,128]{1,0:T(8,128)S(1)} %add.92), channel_id=1, source_target_pairs={{0,192},{32,224},{64,0},{96,32},{128,64},{160,96},{192,128},{224,1... | collective-permute-start | bytes 12296 | tf_op jit(solution)/shard_map/ppermute | solution.py:322
  104.3 7.1 %collective-permute-start.14 = (f32[8,128]{1,0:T(8,128)S(1)}, f32[8,128]{1,0:T(8,128)S(1)}, u32[]{:S(2)}, u32[]{:S(2)}) collective-permute-start(f32[8,128]{1,0:T(8,128)S(1)} %add.92), channel_id=1, source_target_pairs={{0,128},{32,160},{64,192},{96,224},{128,0},{160,32},{192,64},{224,... | collective-permute-start | bytes 12296 | tf_op jit(solution)/shard_map/ppermute | solution.py:322
  105.8 5.6 %collective-permute-start.13 = (f32[8,128]{1,0:T(8,128)S(1)}, f32[8,128]{1,0:T(8,128)S(1)}, u32[]{:S(2)}, u32[]{:S(2)}) collective-permute-start(f32[8,128]{1,0:T(8,128)S(1)} %add.92), channel_id=1, source_target_pairs={{0,64},{32,96},{64,128},{96,160},{128,192},{160,224},{192,0},{224,... | collective-permute-start | bytes 12296 | tf_op jit(solution)/shard_map/ppermute | solution.py:322
  111.4 5.1 %collective-permute-start.18 = (f32[8,128]{1,0:T(8,128)S(1)}, f32[8,128]{1,0:T(8,128)S(1)}, u32[]{:S(2)}, u32[]{:S(2)}) collective-permute-start(f32[8,128]{1,0:T(8,128)S(1)} %add_add_fusion.2), channel_id=1, source_target_pairs={{0,24},{1,25},{2,26},{3,27},{4,28},{5,29},{6,30},{7,31},{8,0},{9,1... | collective-permute-start | bytes 12296 | tf_op jit(solution)/shard_map/ppermute | solution.py:322
  111.5 5.2 %collective-permute-start.17 = (f32[8,128]{1,0:T(8,128)S(1)}, f32[8,128]{1,0:T(8,128)S(1)}, u32[]{:S(2)}, u32[]{:S(2)}) collective-permute-start(f32[8,128]{1,0:T(8,128)S(1)} %add_add_fusion.2), channel_id=1, source_target_pairs={{0,16},{1,17},{2,18},{3,19},{4,20},{5,21},{6,22},{7,23},{8,24},{9,... | collective-permute-start | bytes 12296 | tf_op jit(solution)/shard_map/ppermute | solution.py:322
  114.5 3.6 %collective-permute-start.16 = (f32[8,128]{1,0:T(8,128)S(1)}, f32[8,128]{1,0:T(8,128)S(1)}, u32[]{:S(2)}, u32[]{:S(2)}) collective-permute-start(f32[8,128]{1,0:T(8,128)S(1)} %add_add_fusion.2), channel_id=1, source_target_pairs={{0,8},{1,9},{2,10},{3,11},{4,12},{5,13},{6,14},{7,15},{8,16},{9,17... | collective-permute-start | bytes 12296 | tf_op jit(solution)/shard_map/ppermute | solution.py:322
  118.2 7.1 %collective-permute-start.19 = (f32[8,128]{1,0:T(8,128)S(1)}, f32[8,128]{1,0:T(8,128)S(1)}, u32[]{:S(2)}, u32[]{:S(2)}) collective-permute-start(f32[8,128]{1,0:T(8,128)S(1)} %add_add_fusion.1), channel_id=1, source_target_pairs={{0,2},{1,3},{2,0},{3,1},{4,6},{5,7},{6,4},{7,5},{8,10},{9,11},{10,... | collective-permute-start | bytes 12296 | tf_op jit(solution)/shard_map/ppermute | solution.py:322
  125.3 4.5 %collective-permute-start.20 = (f32[8,128]{1,0:T(8,128)S(1)}, f32[8,128]{1,0:T(8,128)S(1)}, u32[]{:S(2)}, u32[]{:S(2)}) collective-permute-start(f32[8,128]{1,0:T(8,128)S(1)} %add.99), channel_id=1, source_target_pairs={{0,4},{1,5},{2,6},{3,7},{4,0},{5,1},{6,2},{7,3},{8,12},{9,13},{10,... | collective-permute-start | bytes 12296 | tf_op jit(solution)/shard_map/ppermute | solution.py:322
  129.8 12.0 %collective-permute-start.23 = (f32[8,128]{1,0:T(8,128)S(1)}, f32[8,128]{1,0:T(8,128)S(1)}, u32[]{:S(2)}, u32[]{:S(2)}) collective-permute-start(f32[8,128]{1,0:T(8,128)S(1)} %add.100), channel_id=1, source_target_pairs={{0,32},{32,0},{64,96},{96,64},{128,160},{160,128},{192,224},{224,1... | collective-permute-start | bytes 12296 | tf_op jit(solution)/shard_map/ppermute | solution.py:322

commit v11 on v10

--- a/solution.py
+++ b/solution.py
@@ -257,9 +257,7 @@
         copy.wait()
 
 
-def gradient_kernel(
-    where, kz, near, far, y, shifted, stats, kyh, kyl, kxh, kxl, out, halo, z, mid, result, sems, *, ny
-):
+def gather_kernel(where, kz, near, far, y, stats, z, halo, sems, *, ny):
     arriving = halo_copies(near, far, halo, sems, where[2])
     for copy in arriving:
         copy.start()
@@ -279,6 +277,9 @@
         lambda v: jnp.where(has_left, v * f_left * f_left, 0.0),
         lambda v: jnp.where(has_right, v * f_right * f_right, 0.0),
     )
+
+
+def gradient_kernel(z, shifted, kyh, kyl, kxh, kxl, out, mid, result, sems):
     half = mid.shape[0]
     leaving = []
     for g in range(2):
@@ -446,21 +447,31 @@
     value = add(value, "atom", [ahead[k] for k in range(1, across)])
     value, y = in_order((value, y))
     value = add(value, "slab", [[(i, (i + k) % slabs) for i in range(slabs)] for k in (8, 16, 24)])
-    for hop in (2, 4):
-        value = add(value, "slab", [flips(hop)])
+    value = add(value, "slab", [flips(2)])
     value, near, far = in_order((value, near, far))
+    z = pl.pallas_call(
+        functools.partial(gather_kernel, ny=ny),
+        in_specs=[smem, smem, anywhere, anywhere, vmem, vmem],
+        out_specs=vmem,
+        out_shape=shape(rows, nx),
+        scratch_shapes=[halo, pltpu.SemaphoreType.DMA((2,))],
+        compiler_params=params,
+        name="gather",
+    )(where, kz, near, far, y, stats)
+    value = add(value, "slab", [flips(4)])
+    value, z = in_order((value, z))
     value = add(value, "atom", [swap])
     weight_grad = value[0, : weights.shape[0]] / (rows * nx * slabs)
 
     gradient = pl.pallas_call(
-        functools.partial(gradient_kernel, ny=ny),
-        in_specs=[smem, smem, anywhere, anywhere] + [vmem] * 7,
+        gradient_kernel,
+        in_specs=[vmem] * 6,
         out_specs=anywhere,
         out_shape=shape(rows, nx),
-        scratch_shapes=[halo, *scratch, whole, pltpu.SemaphoreType.DMA((2,))],
+        scratch_shapes=[scratch[1], whole, pltpu.SemaphoreType.DMA((2,))],
         compiler_params=params,
         name="gradient",
-    )(where, kz, near, far, y, shifted, stats, *tables)
+    )(z, shifted, *tables)
     return gradient.reshape(atom_log_density.shape), weight_grad
 
 

time: 143 us -> 141 us (0.986)
  starting transfers between devices: 50.8 us -> 47.9 us
    ppermute x24, starting transfers between devices: 50.8 us -> 47.9 us  [send(): return lax.ppermute(value, axis, pairs)]
    pallas_call x1 -> x2, Pallas kernels: 5.88 us -> 5.87 us  [the longest x1 3.62 us: body(): pl.pallas_call(gradient_kernel, in_specs=[vmem] * 6, out_specs=anywhere,...]
  transfers between devices with their start and end apart: 24 -> 24, of which waited for: 9 -> 10; matrix products, arithmetic and copies ran while one was open for 6% -> 6% of each run, Pallas kernels for 21% -> 22%
where the time goes in v11:
time: 141 us; the launch traced here: 140 us
  starting transfers between devices  47.9 us (34%)
  waiting for transfers between devices  42.1 us (30%)
  Pallas kernels  34.2 us (24%)
  local copies, waits for them, and re-layouts  8.92 us (6%)
  other arithmetic  5.91 us (4%)
    ppermute x24, starting transfers between devices, send(): return lax.ppermute(value, axis, pairs)  47.9 us
    ppermute x24, waiting for transfers between devices, send(): return lax.ppermute(value, axis, pairs)  42.1 us
    pallas_call x1, Pallas kernels, body(): pl.pallas_call(functools.partial(potential_kernel, ny=ny), in_specs=[smem...  7.84 us
    pallas_call x1, Pallas kernels, body(): pl.pallas_call(functools.partial(second_kernel, ny=ny), in_specs=[smem, s...  6.76 us
    pallas_call x1, Pallas kernels, body(): pl.pallas_call(ratio_kernel, in_specs=[smem, smem] + [vmem] * 4 + [anywhe...  3.7 us
    pallas_call x1, Pallas kernels, body(): pl.pallas_call(gradient_kernel, in_specs=[vmem] * 6, out_specs=anywhere,...  3.62 us
    pallas_call x1, Pallas kernels, body(): y, stats = own_log(kz, prior)  3.01 us
    pallas_call x1, Pallas kernels, body(): y, stats = own_log(kz, own_at)  3.01 us
  transfers between devices with their start and end apart: 24, of which 10 were waited for; matrix products, arithmetic and copies ran while one was open for 6% of the time, Pallas kernels for 22%

profile of v11, /device:TPU:10, one launch (start us, length us, event | category | flops | bytes accessed | tf_op | source)
XLA Modules:
  0.0 140.1 jit_solution(8070052844841241522)
XLA Ops:
  0.7 2.6 %constant_dynamic-slice_fusion.3 = (f32[256,512]{1,0:T(8,128)S(1)}, f32[256,512]{1,0:T(8,128)}, f32[256,512]{1,0:T(8,128)}) fusion(f32[1024,512]{1,0:T(8,128)} %bitcast.18, s32[]{:T(128)S(6)} %select_n.43, s32[]{:T(128)S(6)} %select_n.45, s32[]{:T(128)S(6)} %select_n.44), kind=kLoop, calls=%fused_computation.9 | loop fusion | bytes 3145740 | tf_op jit(solution)/shard_map/dynamic_slice | solution.py:338
  3.3 1.5 %collective-permute-start.3 = (f32[256,512]{1,0:T(8,128)S(1)}, f32[256,512]{1,0:T(8,128)}, u32[]{:S(2)}, u32[]{:S(2)}) collective-permute-start(f32[256,512]{1,0:T(8,128)S(1)} %get-tuple-element.62), channel_id=1, source_target_pairs={{0,64},{32,96},{64,128},{96,160},{128,192},{160,224},{192,0},{224,... | collective-permute-start | bytes 1572872 | tf_op jit(solution)/shard_map/ppermute | solution.py:323
  4.8 1.0 constant_dynamic-slice_fusion.5
  5.9 0.5 collective-permute-start.5
  6.4 2.1 %collective-permute-start.4 = (f32[256,512]{1,0:T(8,128)}, f32[256,512]{1,0:T(8,128)}, u32[]{:S(2)}, u32[]{:S(2)}) collective-permute-start(f32[256,512]{1,0:T(8,128)} %get-tuple-element.64), channel_id=1, source_target_pairs={{0,128},{32,160},{64,192},{96,224},{128,0},{160,32},{192,64},{224,... | collective-permute-start | bytes 1572872 | tf_op jit(solution)/shard_map/ppermute | solution.py:323
  8.5 1.1 constant_dynamic-slice_fusion.4
  9.6 6.0 %collective-permute-start.2 = (f32[256,512]{1,0:T(8,128)}, f32[256,512]{1,0:T(8,128)}, u32[]{:S(2)}, u32[]{:S(2)}) collective-permute-start(f32[256,512]{1,0:T(8,128)} %get-tuple-element.65), channel_id=1, source_target_pairs={{1,2},{3,4},{5,6},{7,8},{9,10},{11,12},{13,14},{15,16},{17,18},{19... | collective-permute-start | bytes 1572872 | tf_op jit(solution)/shard_map/ppermute | solution.py:323
  15.6 2.6 %collective-permute-done.3 = f32[256,512]{1,0:T(8,128)} collective-permute-done((f32[256,512]{1,0:T(8,128)S(1)}, f32[256,512]{1,0:T(8,128)}, u32[]{:S(2)}, u32[]{:S(2)}) %collective-permute-start.3) | collective-permute-done | bytes 524320 | tf_op jit(solution)/shard_map/ppermute | solution.py:323
  18.2 3.8 %collective-permute-start.1 = (f32[256,512]{1,0:T(8,128)}, f32[256,512]{1,0:T(8,128)}, u32[]{:S(2)}, u32[]{:S(2)}) collective-permute-start(f32[256,512]{1,0:T(8,128)} %get-tuple-element.66), channel_id=1, source_target_pairs={{1,2},{3,4},{5,6},{7,8},{9,10},{11,12},{13,14},{15,16},{17,18},{19... | collective-permute-start | bytes 1572872 | tf_op jit(solution)/shard_map/ppermute | solution.py:323
  22.1 0.6 slice.12
  22.7 1.1 tables.1
  23.8 0.7 compare_select_fusion.kz
  24.4 3.0 %own_log.2 = (f32[1024,512]{1,0:T(8,128)S(1)}, f32[8,128]{1,0:T(8,128)S(1)}) custom-call(f32[9]{0:T(128)S(1)} %compare_select_fusion.kz, f32[1024,512]{1,0:T(8,128)S(1)} %bitcast.17), custom_call_target="tpu_custom_call" | custom-call | tf_op jit(solution)/shard_map/own_log/pallas_call | solution.py:379
  27.4 0.0 copy-start.3
  27.5 1.3 copy-done.3
  28.8 0.1 add_convert_fusion.where
  28.8 0.0 collective-permute-done.5
  28.8 3.5 %collective-permute-done.4 = f32[256,512]{1,0:T(8,128)} collective-permute-done((f32[256,512]{1,0:T(8,128)}, f32[256,512]{1,0:T(8,128)}, u32[]{:S(2)}, u32[]{:S(2)}) %collective-permute-start.4) | collective-permute-done | bytes 524320 | tf_op jit(solution)/shard_map/ppermute | solution.py:323
  32.4 1.7 %add_add_fusion = f32[256,512]{1,0:T(8,128)S(1)} fusion(f32[256,512]{1,0:T(8,128)} %collective-permute-done.5, f32[256,512]{1,0:T(8,128)} %collective-permute-done.4, f32[256,512]{1,0:T(8,128)} %collective-permute-done.3, f32[1024,512]{1,0:T(8,128)} %bitcast.19, s32[]{:T(128)S(6)} %select_n.42), kind=kLoop, calls=%fused_computation | loop fusion | flops 393216 | bytes 2621444 | tf_op jit(solution)/shard_map/add | solution.py:380
  34.1 7.3 %collective-permute-start.8 = (f32[256,512]{1,0:T(8,128)S(1)}, f32[256,512]{1,0:T(8,128)S(1)}, u32[]{:S(2)}, u32[]{:S(2)}) collective-permute-start(f32[256,512]{1,0:T(8,128)S(1)} %add_add_fusion), channel_id=1, source_target_pairs={{0,32},{32,0},{64,96},{96,64},{128,160},{160,128},{192,224},{224,1... | collective-permute-start | bytes 1572872 | tf_op jit(solution)/shard_map/ppermute | solution.py:323
  41.4 0.0 collective-permute-done.2.more
  41.4 0.0 collective-permute-done.1.far
  41.4 0.0 copy-start.2
  41.4 1.6 %copy-done.2 = f32[1,16,64,512]{3,2,1,0:T(8,128)S(1)} copy-done((f32[1,16,64,512]{3,2,1,0:T(8,128)S(1)}, f32[1,16,64,512]{3,2,1,0:T(8,128)}, u32[]{:S(2)}) %copy-start.2) | copy-done | bytes 2097176
  43.0 7.8 %potential.1 = (f32[1024,512]{1,0:T(8,128)S(1)}, f32[512,512]{1,0:T(8,128)}, f32[512,512]{1,0:T(8,128)}) custom-call(s32[3]{0:T(128)S(1)} %add_convert_fusion.where, f32[9]{0:T(128)S(1)} %compare_select_fusion.kz, f32[512,512]{1,0:T(8,128)} %collective-permute-done.near, f32[256,512]{1,0:T(8,128)} %collective-permute-done.1.far, ...), custom_call_target="tpu_custom_call" | custom-call | tf_op jit(solution)/shard_map/potential/pallas_call | solution.py:383
  50.9 0.1 collective-permute-start.6
  51.0 3.8 %collective-permute-start.7 = (f32[512,512]{1,0:T(8,128)}, f32[512,512]{1,0:T(8,128)}, u32[]{:S(2)}, u32[]{:S(2)}) collective-permute-start(f32[512,512]{1,0:T(8,128)} %get-tuple-element.40), channel_id=1, source_target_pairs={{1,2},{3,4},{5,6},{7,8},{9,10},{11,12},{13,14},{15,16},{17,18},{19... | collective-permute-start | bytes 3145736 | tf_op jit(solution)/shard_map/ppermute | solution.py:323
  54.8 3.4 %collective-permute-done.8 = f32[256,512]{1,0:T(8,128)S(1)} collective-permute-done((f32[256,512]{1,0:T(8,128)S(1)}, f32[256,512]{1,0:T(8,128)S(1)}, u32[]{:S(2)}, u32[]{:S(2)}) %collective-permute-start.8) | collective-permute-done | bytes 524320 | tf_op jit(solution)/shard_map/ppermute | solution.py:323
  58.1 0.9 add.91.sum0
  59.0 3.1 %collective-permute-start.11 = (f32[256,512]{1,0:T(8,128)}, f32[256,512]{1,0:T(8,128)}, u32[]{:S(2)}, u32[]{:S(2)}) collective-permute-start(f32[256,512]{1,0:T(8,128)} %add.91.sum0), channel_id=1, source_target_pairs={{0,64},{32,96},{64,128},{96,160},{128,192},{160,224},{192,0},{224,... | collective-permute-start | bytes 1572872 | tf_op jit(solution)/shard_map/ppermute | solution.py:323
  62.1 0.3 collective-permute-start.10
  62.4 1.8 %collective-permute-start.9 = (f32[256,512]{1,0:T(8,128)}, f32[256,512]{1,0:T(8,128)}, u32[]{:S(2)}, u32[]{:S(2)}) collective-permute-start(f32[256,512]{1,0:T(8,128)} %add.91.sum0), channel_id=1, source_target_pairs={{0,192},{32,224},{64,0},{96,32},{128,64},{160,96},{192,128},{224,1... | collective-permute-start | bytes 1572872 | tf_op jit(solution)/shard_map/ppermute | solution.py:323
  64.2 0.7 dynamic_slice.21
  64.8 0.8 pad_add_fusion.at
  65.6 1.3 fusion
  66.9 3.0 %own_log.3 = (f32[1024,512]{1,0:T(8,128)S(1)}, f32[8,128]{1,0:T(8,128)S(1)}) custom-call(f32[9]{0:T(128)S(1)} %compare_select_fusion.kz, f32[1024,512]{1,0:T(8,128)S(1)} %get-tuple-element.43.field.potential), custom_call_target="tpu_custom_call" | custom-call | tf_op jit(solution)/shard_map/own_log/pallas_call | solution.py:398
  69.9 0.0 collective-permute-done.6.near
  69.9 18.8 %collective-permute-done.7.far = f32[512,512]{1,0:T(8,128)} collective-permute-done((f32[512,512]{1,0:T(8,128)}, f32[512,512]{1,0:T(8,128)}, u32[]{:S(2)}, u32[]{:S(2)}) %collective-permute-start.7) | collective-permute-done | bytes 1048608 | tf_op jit(solution)/shard_map/ppermute | solution.py:323
  88.7 6.8 %second.1 = (f32[1024,512]{1,0:T(8,128)S(1)}, f32[8,128]{1,0:T(8,128)S(1)}) custom-call(s32[3]{0:T(128)S(1)} %add_convert_fusion.where, f32[9]{0:T(128)S(1)} %compare_select_fusion.kz, f32[512,512]{1,0:T(8,128)} %collective-permute-done.6.near, f32[512,512]{1,0:T(8,128)} %collective-permute-done.7.far, f32[1024,512]{1,0:T(8,128)S(1)} %get-tuple-element.44.y, ...), custom_call_target="tpu_custom_call" | custom-call | tf_op jit(solution)/shard_map/second/pallas_call | solution.py:399
  95.5 0.0 collective-permute-done.10.sum2
  95.5 3.7 %ratio.1 = (f32[1024,512]{1,0:T(8,128)S(1)}, f32[512,512]{1,0:T(8,128)S(1)}, f32[512,512]{1,0:T(8,128)S(1)}, f32[8,128]{1,0:T(8,128)S(1)}) custom-call(s32[3]{0:T(128)S(1)} %pad_add_fusion.at, f32[1]{0:T(128)} %bitcast.3.weight, f32[1024,512]{1,0:T(8,128)S(1)} %get-tuple-element.46.second, f32[8,128]{1,0:T(8,128)S(1)} %get-tuple-element.47.scale.stats, ...), custom_call_target="tpu_custom_call" | custom-call | tf_op jit(solution)/shard_map/ratio/pallas_call | solution.py:408
  99.3 0.1 collective-permute-start.20
  99.4 3.7 %collective-permute-start.21 = (f32[512,512]{1,0:T(8,128)S(1)}, f32[512,512]{1,0:T(8,128)S(1)}, u32[]{:S(2)}, u32[]{:S(2)}) collective-permute-start(f32[512,512]{1,0:T(8,128)S(1)} %get-tuple-element.54), channel_id=1, source_target_pairs={{1,2},{3,4},{5,6},{7,8},{9,10},{11,12},{13,14},{15,16},{17,18},{19... | collective-permute-start | bytes 3145736 | tf_op jit(solution)/shard_map/ppermute | solution.py:323
  103.1 0.1 collective-permute-start.12
  103.2 1.2 collective-permute-done.12
  104.3 0.0 collective-permute-start.15
  104.3 1.5 %collective-permute-start.14 = (f32[8,128]{1,0:T(8,128)S(1)}, f32[8,128]{1,0:T(8,128)S(1)}, u32[]{:S(2)}, u32[]{:S(2)}) collective-permute-start(f32[8,128]{1,0:T(8,128)S(1)} %add.92), channel_id=1, source_target_pairs={{0,128},{32,160},{64,192},{96,224},{128,0},{160,32},{192,64},{224,... | collective-permute-start | bytes 12296 | tf_op jit(solution)/shard_map/ppermute | solution.py:323
  105.8 2.6 %collective-permute-start.13 = (f32[8,128]{1,0:T(8,128)S(1)}, f32[8,128]{1,0:T(8,128)S(1)}, u32[]{:S(2)}, u32[]{:S(2)}) collective-permute-start(f32[8,128]{1,0:T(8,128)S(1)} %add.92), channel_id=1, source_target_pairs={{0,64},{32,96},{64,128},{96,160},{128,192},{160,224},{192,0},{224,... | collective-permute-start | bytes 12296 | tf_op jit(solution)/shard_map/ppermute | solution.py:323
  108.4 3.0 %own_linear.1 = (f32[1024,512]{1,0:T(8,128)S(1)}, f32[1024,512]{1,0:T(8,128)S(1)}) custom-call(f32[9]{0:T(128)S(1)} %compare_select_fusion.kz, f32[1024,512]{1,0:T(8,128)S(1)} %get-tuple-element.50.field, f32[1024,512]{1,0:T(8,128)S(1)} %get-tuple-element.43.field.potential, f32[8,128]{1,0:T(8,128)S(1)} %get-tuple-element.47.scale.stats), custom_call_target="tpu_custom_call" | custom-call | tf_op jit(solution)/shard_map/own_linear/pallas_call | solution.py:431
  111.4 0.0 collective-permute-done.15
  111.4 0.0 collective-permute-done.13
  111.4 0.1 collective-permute-start.18
  111.5 3.0 %collective-permute-start.17 = (f32[8,128]{1,0:T(8,128)S(1)}, f32[8,128]{1,0:T(8,128)S(1)}, u32[]{:S(2)}, u32[]{:S(2)}) collective-permute-start(f32[8,128]{1,0:T(8,128)S(1)} %add_add_fusion.2), channel_id=1, source_target_pairs={{0,16},{1,17},{2,18},{3,19},{4,20},{5,21},{6,22},{7,23},{8,24},{9,... | collective-permute-start | bytes 12296 | tf_op jit(solution)/shard_map/ppermute | solution.py:323
  114.5 2.0 %collective-permute-start.16 = (f32[8,128]{1,0:T(8,128)S(1)}, f32[8,128]{1,0:T(8,128)S(1)}, u32[]{:S(2)}, u32[]{:S(2)}) collective-permute-start(f32[8,128]{1,0:T(8,128)S(1)} %add_add_fusion.2), channel_id=1, source_target_pairs={{0,8},{1,9},{2,10},{3,11},{4,12},{5,13},{6,14},{7,15},{8,16},{9,17... | collective-permute-start | bytes 12296 | tf_op jit(solution)/shard_map/ppermute | solution.py:323
  116.5 0.2 collective-permute-done.17
  116.7 1.5 %collective-permute-done.16 = f32[8,128]{1,0:T(8,128)S(1)} collective-permute-done((f32[8,128]{1,0:T(8,128)S(1)}, f32[8,128]{1,0:T(8,128)S(1)}, u32[]{:S(2)}, u32[]{:S(2)}) %collective-permute-start.16) | collective-permute-done | bytes 4128 | tf_op jit(solution)/shard_map/ppermute | solution.py:323
  118.2 0.6 collective-permute-start.19
  118.8 6.6 %collective-permute-done.19 = f32[8,128]{1,0:T(8,128)S(1)} collective-permute-done((f32[8,128]{1,0:T(8,128)S(1)}, f32[8,128]{1,0:T(8,128)S(1)}, u32[]{:S(2)}, u32[]{:S(2)}) %collective-permute-start.19) | collective-permute-done | bytes 4128 | tf_op jit(solution)/shard_map/ppermute | solution.py:323
  125.3 2.2 %collective-permute-done.21.far = f32[512,512]{1,0:T(8,128)S(1)} collective-permute-done((f32[512,512]{1,0:T(8,128)S(1)}, f32[512,512]{1,0:T(8,128)S(1)}, u32[]{:S(2)}, u32[]{:S(2)}) %collective-permute-start.21) | collective-permute-done | bytes 1048608 | tf_op jit(solution)/shard_map/ppermute | solution.py:323
  127.5 2.3 %gather.1.z = f32[1024,512]{1,0:T(8,128)S(1)} custom-call(s32[3]{0:T(128)S(1)} %add_convert_fusion.where, f32[9]{0:T(128)S(1)} %compare_select_fusion.kz, f32[512,512]{1,0:T(8,128)S(1)} %collective-permute-done.20.near, f32[512,512]{1,0:T(8,128)S(1)} %collective-permute-done.21.far, f32[1024,512]{1,0:T(8,128)S(1)} %get-tuple-element.58.y, ...), custom_call_target="tpu_custom_call" | custom-call | tf_op jit(solution)/shard_map/gather/pallas_call | solution.py:452
  129.7 2.2 %collective-permute-done.22 = f32[8,128]{1,0:T(8,128)S(1)} collective-permute-done((f32[8,128]{1,0:T(8,128)S(1)}, f32[8,128]{1,0:T(8,128)S(1)}, u32[]{:S(2)}, u32[]{:S(2)}) %collective-permute-start.22) | collective-permute-done | bytes 4128 | tf_op jit(solution)/shard_map/ppermute | solution.py:323
  132.0 4.0 %collective-permute-start.23 = (f32[8,128]{1,0:T(8,128)S(1)}, f32[8,128]{1,0:T(8,128)S(1)}, u32[]{:S(2)}, u32[]{:S(2)}) collective-permute-start(f32[8,128]{1,0:T(8,128)S(1)} %add.100), channel_id=1, source_target_pairs={{0,32},{32,0},{64,96},{96,64},{128,160},{160,128},{192,224},{224,1... | collective-permute-start | bytes 12296 | tf_op jit(solution)/shard_map/ppermute | solution.py:323
  136.0 3.6 %gradient.1 = f32[1024,512]{1,0:T(8,128)} custom-call(f32[1024,512]{1,0:T(8,128)S(1)} %gather.1.z, f32[1024,512]{1,0:T(8,128)S(1)} %get-tuple-element.60.shifted, bf16[256,256]{1,0:T(8,128)(2,1)S(1)} %get-tuple-element.35.kyh, bf16[256,256]{1,0:T(8,128)(2,1)S(1)} %get-tuple-element.36.kyl, bf16[512,512]{1,0:T(8,128)(2,1)S(1)} %get-tuple-element.37.kxh, ...), custom_call_target="tpu_custom_call" | custom-call | tf_op jit(solution)/shard_map/gradient/pallas_call | solution.py:466
  139.6 0.5 multiply_bitcast_fusion
  (29 shorter events, 0.1 us)
Async XLA Ops:
  0.6 4.2 %copy-start = (f32[1,16,64,512]{3,2,1,0:T(8,128)S(1)}, f32[1,16,64,512]{3,2,1,0:T(8,128)}, u32[]{:S(2)}) copy-start(f32[1,16,64,512]{3,2,1,0:T(8,128)} %param.8) | copy-start | bytes 6291460
  3.3 14.9 %collective-permute-start.3 = (f32[256,512]{1,0:T(8,128)S(1)}, f32[256,512]{1,0:T(8,128)}, u32[]{:S(2)}, u32[]{:S(2)}) collective-permute-start(f32[256,512]{1,0:T(8,128)S(1)} %get-tuple-element.62), channel_id=1, source_target_pairs={{0,64},{32,96},{64,128},{96,160},{128,192},{160,224},{192,0},{224,... | collective-permute-start | bytes 1572872 | tf_op jit(solution)/shard_map/ppermute | solution.py:323
  4.8 17.3 %copy-start.6 = (s32[3]{0:T(128)S(1)}, s32[3]{0:T(128)}, u32[]{:S(2)}) copy-start(s32[3]{0:T(128)} %band.1) | copy-start | bytes 40
  5.8 35.5 %collective-permute-start = (f32[512,512]{1,0:T(8,128)}, f32[512,512]{1,0:T(8,128)}, u32[]{:S(2)}, u32[]{:S(2)}) collective-permute-start(f32[512,512]{1,0:T(8,128)} %constant_dynamic-slice_fusion.5), channel_id=1, source_target_pairs={{0,1},{1,0},{2,3},{3,2},{4,5},{5,4},{6,7},{7,6},{8,9},{9,8},{10,11... | collective-permute-start | bytes 3145736 | tf_op jit(solution)/shard_map/ppermute | solution.py:323
  5.9 23.0 %collective-permute-start.5 = (f32[256,512]{1,0:T(8,128)}, f32[256,512]{1,0:T(8,128)}, u32[]{:S(2)}, u32[]{:S(2)}) collective-permute-start(f32[256,512]{1,0:T(8,128)} %get-tuple-element.63), channel_id=1, source_target_pairs={{0,192},{32,224},{64,0},{96,32},{128,64},{160,96},{192,128},{224,1... | collective-permute-start | bytes 1572872 | tf_op jit(solution)/shard_map/ppermute | solution.py:323
  6.4 26.0 %collective-permute-start.4 = (f32[256,512]{1,0:T(8,128)}, f32[256,512]{1,0:T(8,128)}, u32[]{:S(2)}, u32[]{:S(2)}) collective-permute-start(f32[256,512]{1,0:T(8,128)} %get-tuple-element.64), channel_id=1, source_target_pairs={{0,128},{32,160},{64,192},{96,224},{128,0},{160,32},{192,64},{224,... | collective-permute-start | bytes 1572872 | tf_op jit(solution)/shard_map/ppermute | solution.py:323
  9.6 31.8 %collective-permute-start.2 = (f32[256,512]{1,0:T(8,128)}, f32[256,512]{1,0:T(8,128)}, u32[]{:S(2)}, u32[]{:S(2)}) collective-permute-start(f32[256,512]{1,0:T(8,128)} %get-tuple-element.65), channel_id=1, source_target_pairs={{1,2},{3,4},{5,6},{7,8},{9,10},{11,12},{13,14},{15,16},{17,18},{19... | collective-permute-start | bytes 1572872 | tf_op jit(solution)/shard_map/ppermute | solution.py:323
  18.2 23.2 %collective-permute-start.1 = (f32[256,512]{1,0:T(8,128)}, f32[256,512]{1,0:T(8,128)}, u32[]{:S(2)}, u32[]{:S(2)}) collective-permute-start(f32[256,512]{1,0:T(8,128)} %get-tuple-element.66), channel_id=1, source_target_pairs={{1,2},{3,4},{5,6},{7,8},{9,10},{11,12},{13,14},{15,16},{17,18},{19... | collective-permute-start | bytes 1572872 | tf_op jit(solution)/shard_map/ppermute | solution.py:323
  27.4 1.3 copy-start.3
  28.8 12.6 %copy-start.4 = (f32[1024,512]{1,0:T(8,128)S(1)}, f32[1024,512]{1,0:T(8,128)}, u32[]{:S(2)}) copy-start(f32[1024,512]{1,0:T(8,128)} %copy-done.3) | copy-start | bytes 6291460
  34.1 24.0 %collective-permute-start.8 = (f32[256,512]{1,0:T(8,128)S(1)}, f32[256,512]{1,0:T(8,128)S(1)}, u32[]{:S(2)}, u32[]{:S(2)}) collective-permute-start(f32[256,512]{1,0:T(8,128)S(1)} %add_add_fusion), channel_id=1, source_target_pairs={{0,32},{32,0},{64,96},{96,64},{128,160},{160,128},{192,224},{224,1... | collective-permute-start | bytes 1572872 | tf_op jit(solution)/shard_map/ppermute | solution.py:323
  41.4 1.6 %copy-start.2 = (f32[1,16,64,512]{3,2,1,0:T(8,128)S(1)}, f32[1,16,64,512]{3,2,1,0:T(8,128)}, u32[]{:S(2)}) copy-start(f32[1,16,64,512]{3,2,1,0:T(8,128)} %param.7) | copy-start | bytes 6291460
  43.0 21.2 %copy-start.7 = (s32[8]{0:T(128)S(1)}, s32[8]{0:T(128)}, u32[]{:S(2)}) copy-start(s32[8]{0:T(128)} %param.13) | copy-start | bytes 100
  43.0 22.6 %copy-start.8 = (f32[8]{0:T(128)S(1)}, f32[8]{0:T(128)}, u32[]{:S(2)}) copy-start(f32[8]{0:T(128)} %param.11) | copy-start | bytes 100
  50.9 19.0 %collective-permute-start.6 = (f32[512,512]{1,0:T(8,128)}, f32[512,512]{1,0:T(8,128)}, u32[]{:S(2)}, u32[]{:S(2)}) collective-permute-start(f32[512,512]{1,0:T(8,128)} %get-tuple-element.39), channel_id=1, source_target_pairs={{0,1},{1,0},{2,3},{3,2},{4,5},{5,4},{6,7},{7,6},{8,9},{9,8},{10,11... | collective-permute-start | bytes 3145736 | tf_op jit(solution)/shard_map/ppermute | solution.py:323
  51.0 37.8 %collective-permute-start.7 = (f32[512,512]{1,0:T(8,128)}, f32[512,512]{1,0:T(8,128)}, u32[]{:S(2)}, u32[]{:S(2)}) collective-permute-start(f32[512,512]{1,0:T(8,128)} %get-tuple-element.40), channel_id=1, source_target_pairs={{1,2},{3,4},{5,6},{7,8},{9,10},{11,12},{13,14},{15,16},{17,18},{19... | collective-permute-start | bytes 3145736 | tf_op jit(solution)/shard_map/ppermute | solution.py:323
  59.0 36.5 %collective-permute-start.11 = (f32[256,512]{1,0:T(8,128)}, f32[256,512]{1,0:T(8,128)}, u32[]{:S(2)}, u32[]{:S(2)}) collective-permute-start(f32[256,512]{1,0:T(8,128)} %add.91.sum0), channel_id=1, source_target_pairs={{0,64},{32,96},{64,128},{96,160},{128,192},{160,224},{192,0},{224,... | collective-permute-start | bytes 1572872 | tf_op jit(solution)/shard_map/ppermute | solution.py:323
  62.1 33.4 %collective-permute-start.10 = (f32[256,512]{1,0:T(8,128)}, f32[256,512]{1,0:T(8,128)}, u32[]{:S(2)}, u32[]{:S(2)}) collective-permute-start(f32[256,512]{1,0:T(8,128)} %add.91.sum0), channel_id=1, source_target_pairs={{0,128},{32,160},{64,192},{96,224},{128,0},{160,32},{192,64},{224,... | collective-permute-start | bytes 1572872 | tf_op jit(solution)/shard_map/ppermute | solution.py:323
  62.4 33.1 %collective-permute-start.9 = (f32[256,512]{1,0:T(8,128)}, f32[256,512]{1,0:T(8,128)}, u32[]{:S(2)}, u32[]{:S(2)}) collective-permute-start(f32[256,512]{1,0:T(8,128)} %add.91.sum0), channel_id=1, source_target_pairs={{0,192},{32,224},{64,0},{96,32},{128,64},{160,96},{192,128},{224,1... | collective-permute-start | bytes 1572872 | tf_op jit(solution)/shard_map/ppermute | solution.py:323
  88.7 6.8 %copy-start.1 = (f32[1,16,64,512]{3,2,1,0:T(8,128)S(1)}, f32[1,16,64,512]{3,2,1,0:T(8,128)}, u32[]{:S(2)}) copy-start(f32[1,16,64,512]{3,2,1,0:T(8,128)} %param.9) | copy-start | bytes 6291460
  88.7 6.8 %copy-start.5 = (f32[16,64,512]{2,1,0:T(8,128)S(1)}, f32[16,64,512]{2,1,0:T(8,128)}, u32[]{:S(2)}) copy-start(f32[16,64,512]{2,1,0:T(8,128)} %param.10) | copy-start | bytes 6291460
  99.3 26.1 %collective-permute-start.20 = (f32[512,512]{1,0:T(8,128)S(1)}, f32[512,512]{1,0:T(8,128)S(1)}, u32[]{:S(2)}, u32[]{:S(2)}) collective-permute-start(f32[512,512]{1,0:T(8,128)S(1)} %get-tuple-element.53), channel_id=1, source_target_pairs={{0,1},{1,0},{2,3},{3,2},{4,5},{5,4},{6,7},{7,6},{8,9},{9,8},{10,11... | collective-permute-start | bytes 3145736 | tf_op jit(solution)/shard_map/ppermute | solution.py:323
  99.4 28.1 %collective-permute-start.21 = (f32[512,512]{1,0:T(8,128)S(1)}, f32[512,512]{1,0:T(8,128)S(1)}, u32[]{:S(2)}, u32[]{:S(2)}) collective-permute-start(f32[512,512]{1,0:T(8,128)S(1)} %get-tuple-element.54), channel_id=1, source_target_pairs={{1,2},{3,4},{5,6},{7,8},{9,10},{11,12},{13,14},{15,16},{17,18},{19... | collective-permute-start | bytes 3145736 | tf_op jit(solution)/shard_map/ppermute | solution.py:323
  103.1 1.3 collective-permute-start.12
  104.3 7.1 %collective-permute-start.15 = (f32[8,128]{1,0:T(8,128)S(1)}, f32[8,128]{1,0:T(8,128)S(1)}, u32[]{:S(2)}, u32[]{:S(2)}) collective-permute-start(f32[8,128]{1,0:T(8,128)S(1)} %add.92), channel_id=1, source_target_pairs={{0,192},{32,224},{64,0},{96,32},{128,64},{160,96},{192,128},{224,1... | collective-permute-start | bytes 12296 | tf_op jit(solution)/shard_map/ppermute | solution.py:323
  104.3 7.1 %collective-permute-start.14 = (f32[8,128]{1,0:T(8,128)S(1)}, f32[8,128]{1,0:T(8,128)S(1)}, u32[]{:S(2)}, u32[]{:S(2)}) collective-permute-start(f32[8,128]{1,0:T(8,128)S(1)} %add.92), channel_id=1, source_target_pairs={{0,128},{32,160},{64,192},{96,224},{128,0},{160,32},{192,64},{224,... | collective-permute-start | bytes 12296 | tf_op jit(solution)/shard_map/ppermute | solution.py:323
  105.8 5.6 %collective-permute-start.13 = (f32[8,128]{1,0:T(8,128)S(1)}, f32[8,128]{1,0:T(8,128)S(1)}, u32[]{:S(2)}, u32[]{:S(2)}) collective-permute-start(f32[8,128]{1,0:T(8,128)S(1)} %add.92), channel_id=1, source_target_pairs={{0,64},{32,96},{64,128},{96,160},{128,192},{160,224},{192,0},{224,... | collective-permute-start | bytes 12296 | tf_op jit(solution)/shard_map/ppermute | solution.py:323
  111.4 5.1 %collective-permute-start.18 = (f32[8,128]{1,0:T(8,128)S(1)}, f32[8,128]{1,0:T(8,128)S(1)}, u32[]{:S(2)}, u32[]{:S(2)}) collective-permute-start(f32[8,128]{1,0:T(8,128)S(1)} %add_add_fusion.2), channel_id=1, source_target_pairs={{0,24},{1,25},{2,26},{3,27},{4,28},{5,29},{6,30},{7,31},{8,0},{9,1... | collective-permute-start | bytes 12296 | tf_op jit(solution)/shard_map/ppermute | solution.py:323
  111.5 5.2 %collective-permute-start.17 = (f32[8,128]{1,0:T(8,128)S(1)}, f32[8,128]{1,0:T(8,128)S(1)}, u32[]{:S(2)}, u32[]{:S(2)}) collective-permute-start(f32[8,128]{1,0:T(8,128)S(1)} %add_add_fusion.2), channel_id=1, source_target_pairs={{0,16},{1,17},{2,18},{3,19},{4,20},{5,21},{6,22},{7,23},{8,24},{9,... | collective-permute-start | bytes 12296 | tf_op jit(solution)/shard_map/ppermute | solution.py:323
  114.5 3.6 %collective-permute-start.16 = (f32[8,128]{1,0:T(8,128)S(1)}, f32[8,128]{1,0:T(8,128)S(1)}, u32[]{:S(2)}, u32[]{:S(2)}) collective-permute-start(f32[8,128]{1,0:T(8,128)S(1)} %add_add_fusion.2), channel_id=1, source_target_pairs={{0,8},{1,9},{2,10},{3,11},{4,12},{5,13},{6,14},{7,15},{8,16},{9,17... | collective-permute-start | bytes 12296 | tf_op jit(solution)/shard_map/ppermute | solution.py:323
  118.2 7.1 %collective-permute-start.19 = (f32[8,128]{1,0:T(8,128)S(1)}, f32[8,128]{1,0:T(8,128)S(1)}, u32[]{:S(2)}, u32[]{:S(2)}) collective-permute-start(f32[8,128]{1,0:T(8,128)S(1)} %add_add_fusion.1), channel_id=1, source_target_pairs={{0,2},{1,3},{2,0},{3,1},{4,6},{5,7},{6,4},{7,5},{8,10},{9,11},{10,... | collective-permute-start | bytes 12296 | tf_op jit(solution)/shard_map/ppermute | solution.py:323
  127.5 4.5 %collective-permute-start.22 = (f32[8,128]{1,0:T(8,128)S(1)}, f32[8,128]{1,0:T(8,128)S(1)}, u32[]{:S(2)}, u32[]{:S(2)}) collective-permute-start(f32[8,128]{1,0:T(8,128)S(1)} %add.99), channel_id=1, source_target_pairs={{0,4},{1,5},{2,6},{3,7},{4,0},{5,1},{6,2},{7,3},{8,12},{9,13},{10,... | collective-permute-start | bytes 12296 | tf_op jit(solution)/shard_map/ppermute | solution.py:323
  132.0 7.6 %collective-permute-start.23 = (f32[8,128]{1,0:T(8,128)S(1)}, f32[8,128]{1,0:T(8,128)S(1)}, u32[]{:S(2)}, u32[]{:S(2)}) collective-permute-start(f32[8,128]{1,0:T(8,128)S(1)} %add.100), channel_id=1, source_target_pairs={{0,32},{32,0},{64,96},{96,64},{128,160},{160,128},{192,224},{224,1... | collective-permute-start | bytes 12296 | tf_op jit(solution)/shard_map/ppermute | solution.py:323

commit v12 on v11

--- a/solution.py
+++ b/solution.py
@@ -448,7 +448,7 @@
     value, y = in_order((value, y))
     value = add(value, "slab", [[(i, (i + k) % slabs) for i in range(slabs)] for k in (8, 16, 24)])
     value = add(value, "slab", [flips(2)])
-    value, near, far = in_order((value, near, far))
+    value, near, y = in_order((value, near, y))
     z = pl.pallas_call(
         functools.partial(gather_kernel, ny=ny),
         in_specs=[smem, smem, anywhere, anywhere, vmem, vmem],

time: 141 us -> 140 us (level)
  starting transfers between devices: 47.9 us -> 50.8 us
  waiting for transfers between devices: 42.1 us -> 39.2 us
    ppermute x24, waiting for transfers between devices: 42.1 us -> 39.2 us  [send(): return lax.ppermute(value, axis, pairs)]
    ppermute x24, starting transfers between devices: 47.9 us -> 50.8 us  [send(): return lax.ppermute(value, axis, pairs)]
where the time goes in v12:
time: 140 us
  starting transfers between devices  50.8 us (36%)
  waiting for transfers between devices  39.2 us (28%)
  Pallas kernels  34.2 us (24%)
  local copies, waits for them, and re-layouts  8.92 us (6%)
  other arithmetic  5.91 us (4%)
    ppermute x24, starting transfers between devices, send(): return lax.ppermute(value, axis, pairs)  50.8 us
    ppermute x24, waiting for transfers between devices, send(): return lax.ppermute(value, axis, pairs)  39.2 us
    pallas_call x1, Pallas kernels, body(): pl.pallas_call(functools.partial(potential_kernel, ny=ny), in_specs=[smem...  7.84 us
    pallas_call x1, Pallas kernels, body(): pl.pallas_call(functools.partial(second_kernel, ny=ny), in_specs=[smem, s...  6.76 us
    pallas_call x1, Pallas kernels, body(): pl.pallas_call(ratio_kernel, in_specs=[smem, smem] + [vmem] * 4 + [anywhe...  3.7 us
    pallas_call x1, Pallas kernels, body(): pl.pallas_call(gradient_kernel, in_specs=[vmem] * 6, out_specs=anywhere,...  3.62 us
    pallas_call x1, Pallas kernels, body(): y, stats = own_log(kz, prior)  3.01 us
    pallas_call x1, Pallas kernels, body(): y, stats = own_log(kz, own_at)  3.01 us
  transfers between devices with their start and end apart: 24, of which 10 were waited for; matrix products, arithmetic and copies ran while one was open for 6% of the time, Pallas kernels for 22%

profile of v12, /device:TPU:10, one launch (start us, length us, event | category | flops | bytes accessed | tf_op | source)
XLA Modules:
  0.0 140.0 jit_solution(8405351826120687705)
XLA Ops:
  0.7 2.6 %constant_dynamic-slice_fusion.3 = (f32[256,512]{1,0:T(8,128)S(1)}, f32[256,512]{1,0:T(8,128)}, f32[256,512]{1,0:T(8,128)}) fusion(f32[1024,512]{1,0:T(8,128)} %bitcast.18, s32[]{:T(128)S(6)} %select_n.43, s32[]{:T(128)S(6)} %select_n.45, s32[]{:T(128)S(6)} %select_n.44), kind=kLoop, calls=%fused_computation.9 | loop fusion | bytes 3145740 | tf_op jit(solution)/shard_map/dynamic_slice | solution.py:338
  3.3 1.5 %collective-permute-start.3 = (f32[256,512]{1,0:T(8,128)S(1)}, f32[256,512]{1,0:T(8,128)}, u32[]{:S(2)}, u32[]{:S(2)}) collective-permute-start(f32[256,512]{1,0:T(8,128)S(1)} %get-tuple-element.62), channel_id=1, source_target_pairs={{0,64},{32,96},{64,128},{96,160},{128,192},{160,224},{192,0},{224,... | collective-permute-start | bytes 1572872 | tf_op jit(solution)/shard_map/ppermute | solution.py:323
  4.8 1.0 constant_dynamic-slice_fusion.5
  5.8 0.0 collective-permute-start
  5.9 0.5 collective-permute-start.5
  6.4 2.1 %collective-permute-start.4 = (f32[256,512]{1,0:T(8,128)}, f32[256,512]{1,0:T(8,128)}, u32[]{:S(2)}, u32[]{:S(2)}) collective-permute-start(f32[256,512]{1,0:T(8,128)} %get-tuple-element.64), channel_id=1, source_target_pairs={{0,128},{32,160},{64,192},{96,224},{128,0},{160,32},{192,64},{224,... | collective-permute-start | bytes 1572872 | tf_op jit(solution)/shard_map/ppermute | solution.py:323
  8.5 1.1 constant_dynamic-slice_fusion.4
  9.6 6.0 %collective-permute-start.2 = (f32[256,512]{1,0:T(8,128)}, f32[256,512]{1,0:T(8,128)}, u32[]{:S(2)}, u32[]{:S(2)}) collective-permute-start(f32[256,512]{1,0:T(8,128)} %get-tuple-element.65), channel_id=1, source_target_pairs={{1,2},{3,4},{5,6},{7,8},{9,10},{11,12},{13,14},{15,16},{17,18},{19... | collective-permute-start | bytes 1572872 | tf_op jit(solution)/shard_map/ppermute | solution.py:323
  15.6 2.6 %collective-permute-done.3 = f32[256,512]{1,0:T(8,128)} collective-permute-done((f32[256,512]{1,0:T(8,128)S(1)}, f32[256,512]{1,0:T(8,128)}, u32[]{:S(2)}, u32[]{:S(2)}) %collective-permute-start.3) | collective-permute-done | bytes 524320 | tf_op jit(solution)/shard_map/ppermute | solution.py:323
  18.2 3.8 %collective-permute-start.1 = (f32[256,512]{1,0:T(8,128)}, f32[256,512]{1,0:T(8,128)}, u32[]{:S(2)}, u32[]{:S(2)}) collective-permute-start(f32[256,512]{1,0:T(8,128)} %get-tuple-element.66), channel_id=1, source_target_pairs={{1,2},{3,4},{5,6},{7,8},{9,10},{11,12},{13,14},{15,16},{17,18},{19... | collective-permute-start | bytes 1572872 | tf_op jit(solution)/shard_map/ppermute | solution.py:323
  22.1 0.6 slice.12
  22.7 1.1 tables.1
  23.8 0.7 compare_select_fusion.kz
  24.4 3.0 %own_log.2 = (f32[1024,512]{1,0:T(8,128)S(1)}, f32[8,128]{1,0:T(8,128)S(1)}) custom-call(f32[9]{0:T(128)S(1)} %compare_select_fusion.kz, f32[1024,512]{1,0:T(8,128)S(1)} %bitcast.17), custom_call_target="tpu_custom_call" | custom-call | tf_op jit(solution)/shard_map/own_log/pallas_call | solution.py:379
  27.4 0.0 copy-start.3
  27.5 1.3 copy-done.3
  28.8 0.1 add_convert_fusion.where
  28.8 3.5 %collective-permute-done.4 = f32[256,512]{1,0:T(8,128)} collective-permute-done((f32[256,512]{1,0:T(8,128)}, f32[256,512]{1,0:T(8,128)}, u32[]{:S(2)}, u32[]{:S(2)}) %collective-permute-start.4) | collective-permute-done | bytes 524320 | tf_op jit(solution)/shard_map/ppermute | solution.py:323
  32.4 1.7 %add_add_fusion = f32[256,512]{1,0:T(8,128)S(1)} fusion(f32[256,512]{1,0:T(8,128)} %collective-permute-done.5, f32[256,512]{1,0:T(8,128)} %collective-permute-done.4, f32[256,512]{1,0:T(8,128)} %collective-permute-done.3, f32[1024,512]{1,0:T(8,128)} %bitcast.19, s32[]{:T(128)S(6)} %select_n.42), kind=kLoop, calls=%fused_computation | loop fusion | flops 393216 | bytes 2621444 | tf_op jit(solution)/shard_map/add | solution.py:380
  34.1 7.3 %collective-permute-start.8 = (f32[256,512]{1,0:T(8,128)S(1)}, f32[256,512]{1,0:T(8,128)S(1)}, u32[]{:S(2)}, u32[]{:S(2)}) collective-permute-start(f32[256,512]{1,0:T(8,128)S(1)} %add_add_fusion), channel_id=1, source_target_pairs={{0,32},{32,0},{64,96},{96,64},{128,160},{160,128},{192,224},{224,1... | collective-permute-start | bytes 1572872 | tf_op jit(solution)/shard_map/ppermute | solution.py:323
  41.4 0.0 collective-permute-done.1.far
  41.4 0.0 collective-permute-done.near
  41.4 0.0 copy-start.2
  41.4 1.6 %copy-done.2 = f32[1,16,64,512]{3,2,1,0:T(8,128)S(1)} copy-done((f32[1,16,64,512]{3,2,1,0:T(8,128)S(1)}, f32[1,16,64,512]{3,2,1,0:T(8,128)}, u32[]{:S(2)}) %copy-start.2) | copy-done | bytes 2097176
  43.0 7.8 %potential.1 = (f32[1024,512]{1,0:T(8,128)S(1)}, f32[512,512]{1,0:T(8,128)}, f32[512,512]{1,0:T(8,128)}) custom-call(s32[3]{0:T(128)S(1)} %add_convert_fusion.where, f32[9]{0:T(128)S(1)} %compare_select_fusion.kz, f32[512,512]{1,0:T(8,128)} %collective-permute-done.near, f32[256,512]{1,0:T(8,128)} %collective-permute-done.1.far, ...), custom_call_target="tpu_custom_call" | custom-call | tf_op jit(solution)/shard_map/potential/pallas_call | solution.py:383
  50.9 0.1 collective-permute-start.6
  51.0 3.8 %collective-permute-start.7 = (f32[512,512]{1,0:T(8,128)}, f32[512,512]{1,0:T(8,128)}, u32[]{:S(2)}, u32[]{:S(2)}) collective-permute-start(f32[512,512]{1,0:T(8,128)} %get-tuple-element.40), channel_id=1, source_target_pairs={{1,2},{3,4},{5,6},{7,8},{9,10},{11,12},{13,14},{15,16},{17,18},{19... | collective-permute-start | bytes 3145736 | tf_op jit(solution)/shard_map/ppermute | solution.py:323
  54.8 3.4 %collective-permute-done.8 = f32[256,512]{1,0:T(8,128)S(1)} collective-permute-done((f32[256,512]{1,0:T(8,128)S(1)}, f32[256,512]{1,0:T(8,128)S(1)}, u32[]{:S(2)}, u32[]{:S(2)}) %collective-permute-start.8) | collective-permute-done | bytes 524320 | tf_op jit(solution)/shard_map/ppermute | solution.py:323
  58.1 0.9 add.91.sum0
  59.0 3.1 %collective-permute-start.11 = (f32[256,512]{1,0:T(8,128)}, f32[256,512]{1,0:T(8,128)}, u32[]{:S(2)}, u32[]{:S(2)}) collective-permute-start(f32[256,512]{1,0:T(8,128)} %add.91.sum0), channel_id=1, source_target_pairs={{0,64},{32,96},{64,128},{96,160},{128,192},{160,224},{192,0},{224,... | collective-permute-start | bytes 1572872 | tf_op jit(solution)/shard_map/ppermute | solution.py:323
  62.1 0.3 collective-permute-start.10
  62.4 1.8 %collective-permute-start.9 = (f32[256,512]{1,0:T(8,128)}, f32[256,512]{1,0:T(8,128)}, u32[]{:S(2)}, u32[]{:S(2)}) collective-permute-start(f32[256,512]{1,0:T(8,128)} %add.91.sum0), channel_id=1, source_target_pairs={{0,192},{32,224},{64,0},{96,32},{128,64},{160,96},{192,128},{224,1... | collective-permute-start | bytes 1572872 | tf_op jit(solution)/shard_map/ppermute | solution.py:323
  64.2 0.7 dynamic_slice.21
  64.8 0.8 pad_add_fusion.at
  65.6 1.3 fusion
  66.9 3.0 %own_log.3 = (f32[1024,512]{1,0:T(8,128)S(1)}, f32[8,128]{1,0:T(8,128)S(1)}) custom-call(f32[9]{0:T(128)S(1)} %compare_select_fusion.kz, f32[1024,512]{1,0:T(8,128)S(1)} %get-tuple-element.43.field.potential), custom_call_target="tpu_custom_call" | custom-call | tf_op jit(solution)/shard_map/own_log/pallas_call | solution.py:398
  69.9 18.8 %collective-permute-done.7.far = f32[512,512]{1,0:T(8,128)} collective-permute-done((f32[512,512]{1,0:T(8,128)}, f32[512,512]{1,0:T(8,128)}, u32[]{:S(2)}, u32[]{:S(2)}) %collective-permute-start.7) | collective-permute-done | bytes 1048608 | tf_op jit(solution)/shard_map/ppermute | solution.py:323
  88.7 6.8 %second.1 = (f32[1024,512]{1,0:T(8,128)S(1)}, f32[8,128]{1,0:T(8,128)S(1)}) custom-call(s32[3]{0:T(128)S(1)} %add_convert_fusion.where, f32[9]{0:T(128)S(1)} %compare_select_fusion.kz, f32[512,512]{1,0:T(8,128)} %collective-permute-done.6.near, f32[512,512]{1,0:T(8,128)} %collective-permute-done.7.far, f32[1024,512]{1,0:T(8,128)S(1)} %get-tuple-element.44.y, ...), custom_call_target="tpu_custom_call" | custom-call | tf_op jit(solution)/shard_map/second/pallas_call | solution.py:399
  95.5 0.0 collective-permute-done.11.sum3
  95.5 0.0 collective-permute-done.9.sum1
  95.5 3.7 %ratio.1 = (f32[1024,512]{1,0:T(8,128)S(1)}, f32[512,512]{1,0:T(8,128)S(1)}, f32[512,512]{1,0:T(8,128)S(1)}, f32[8,128]{1,0:T(8,128)S(1)}) custom-call(s32[3]{0:T(128)S(1)} %pad_add_fusion.at, f32[1]{0:T(128)} %bitcast.3.weight, f32[1024,512]{1,0:T(8,128)S(1)} %get-tuple-element.46.second, f32[8,128]{1,0:T(8,128)S(1)} %get-tuple-element.47.scale.stats, ...), custom_call_target="tpu_custom_call" | custom-call | tf_op jit(solution)/shard_map/ratio/pallas_call | solution.py:408
  99.3 0.1 collective-permute-start.20
  99.4 3.7 %collective-permute-start.22 = (f32[512,512]{1,0:T(8,128)S(1)}, f32[512,512]{1,0:T(8,128)S(1)}, u32[]{:S(2)}, u32[]{:S(2)}) collective-permute-start(f32[512,512]{1,0:T(8,128)S(1)} %get-tuple-element.57), channel_id=1, source_target_pairs={{1,2},{3,4},{5,6},{7,8},{9,10},{11,12},{13,14},{15,16},{17,18},{19... | collective-permute-start | bytes 3145736 | tf_op jit(solution)/shard_map/ppermute | solution.py:323
  103.1 0.1 collective-permute-start.12
  103.2 1.2 collective-permute-done.12
  104.3 0.0 collective-permute-start.15
  104.3 1.5 %collective-permute-start.14 = (f32[8,128]{1,0:T(8,128)S(1)}, f32[8,128]{1,0:T(8,128)S(1)}, u32[]{:S(2)}, u32[]{:S(2)}) collective-permute-start(f32[8,128]{1,0:T(8,128)S(1)} %add.92), channel_id=1, source_target_pairs={{0,128},{32,160},{64,192},{96,224},{128,0},{160,32},{192,64},{224,... | collective-permute-start | bytes 12296 | tf_op jit(solution)/shard_map/ppermute | solution.py:323
  105.8 2.6 %collective-permute-start.13 = (f32[8,128]{1,0:T(8,128)S(1)}, f32[8,128]{1,0:T(8,128)S(1)}, u32[]{:S(2)}, u32[]{:S(2)}) collective-permute-start(f32[8,128]{1,0:T(8,128)S(1)} %add.92), channel_id=1, source_target_pairs={{0,64},{32,96},{64,128},{96,160},{128,192},{160,224},{192,0},{224,... | collective-permute-start | bytes 12296 | tf_op jit(solution)/shard_map/ppermute | solution.py:323
  108.4 3.0 %own_linear.1 = (f32[1024,512]{1,0:T(8,128)S(1)}, f32[1024,512]{1,0:T(8,128)S(1)}) custom-call(f32[9]{0:T(128)S(1)} %compare_select_fusion.kz, f32[1024,512]{1,0:T(8,128)S(1)} %get-tuple-element.50.field, f32[1024,512]{1,0:T(8,128)S(1)} %get-tuple-element.43.field.potential, f32[8,128]{1,0:T(8,128)S(1)} %get-tuple-element.47.scale.stats), custom_call_target="tpu_custom_call" | custom-call | tf_op jit(solution)/shard_map/own_linear/pallas_call | solution.py:431
  111.4 0.0 collective-permute-done.15
  111.4 0.1 collective-permute-start.18
  111.5 3.0 %collective-permute-start.17 = (f32[8,128]{1,0:T(8,128)S(1)}, f32[8,128]{1,0:T(8,128)S(1)}, u32[]{:S(2)}, u32[]{:S(2)}) collective-permute-start(f32[8,128]{1,0:T(8,128)S(1)} %add_add_fusion.2), channel_id=1, source_target_pairs={{0,16},{1,17},{2,18},{3,19},{4,20},{5,21},{6,22},{7,23},{8,24},{9,... | collective-permute-start | bytes 12296 | tf_op jit(solution)/shard_map/ppermute | solution.py:323
  114.5 2.0 %collective-permute-start.16 = (f32[8,128]{1,0:T(8,128)S(1)}, f32[8,128]{1,0:T(8,128)S(1)}, u32[]{:S(2)}, u32[]{:S(2)}) collective-permute-start(f32[8,128]{1,0:T(8,128)S(1)} %add_add_fusion.2), channel_id=1, source_target_pairs={{0,8},{1,9},{2,10},{3,11},{4,12},{5,13},{6,14},{7,15},{8,16},{9,17... | collective-permute-start | bytes 12296 | tf_op jit(solution)/shard_map/ppermute | solution.py:323
  116.5 0.2 collective-permute-done.17
  116.7 1.5 %collective-permute-done.16 = f32[8,128]{1,0:T(8,128)S(1)} collective-permute-done((f32[8,128]{1,0:T(8,128)S(1)}, f32[8,128]{1,0:T(8,128)S(1)}, u32[]{:S(2)}, u32[]{:S(2)}) %collective-permute-start.16) | collective-permute-done | bytes 4128 | tf_op jit(solution)/shard_map/ppermute | solution.py:323
  118.2 0.6 collective-permute-start.19
  118.8 6.6 %collective-permute-done.19 = f32[8,128]{1,0:T(8,128)S(1)} collective-permute-done((f32[8,128]{1,0:T(8,128)S(1)}, f32[8,128]{1,0:T(8,128)S(1)}, u32[]{:S(2)}, u32[]{:S(2)}) %collective-permute-start.19) | collective-permute-done | bytes 4128 | tf_op jit(solution)/shard_map/ppermute | solution.py:323
  125.3 0.8 collective-permute-start.21
  126.1 1.3 collective-permute-done.22.far
  127.5 2.3 %gather.1.z = f32[1024,512]{1,0:T(8,128)S(1)} custom-call(s32[3]{0:T(128)S(1)} %add_convert_fusion.where, f32[9]{0:T(128)S(1)} %compare_select_fusion.kz, f32[512,512]{1,0:T(8,128)S(1)} %collective-permute-done.20.near, f32[512,512]{1,0:T(8,128)S(1)} %collective-permute-done.22.far, f32[1024,512]{1,0:T(8,128)S(1)} %get-tuple-element.58.y, ...), custom_call_target="tpu_custom_call" | custom-call | tf_op jit(solution)/shard_map/gather/pallas_call | solution.py:452
  129.7 0.1 collective-permute-done.21
  129.8 6.0 %collective-permute-start.23 = (f32[8,128]{1,0:T(8,128)S(1)}, f32[8,128]{1,0:T(8,128)S(1)}, u32[]{:S(2)}, u32[]{:S(2)}) collective-permute-start(f32[8,128]{1,0:T(8,128)S(1)} %add.100), channel_id=1, source_target_pairs={{0,32},{32,0},{64,96},{96,64},{128,160},{160,128},{192,224},{224,1... | collective-permute-start | bytes 12296 | tf_op jit(solution)/shard_map/ppermute | solution.py:323
  135.9 3.6 %gradient.1 = f32[1024,512]{1,0:T(8,128)} custom-call(f32[1024,512]{1,0:T(8,128)S(1)} %gather.1.z, f32[1024,512]{1,0:T(8,128)S(1)} %get-tuple-element.60.shifted, bf16[256,256]{1,0:T(8,128)(2,1)S(1)} %get-tuple-element.35.kyh, bf16[256,256]{1,0:T(8,128)(2,1)S(1)} %get-tuple-element.36.kyl, bf16[512,512]{1,0:T(8,128)(2,1)S(1)} %get-tuple-element.37.kxh, ...), custom_call_target="tpu_custom_call" | custom-call | tf_op jit(solution)/shard_map/gradient/pallas_call | solution.py:466
  139.5 0.5 multiply_bitcast_fusion
  (29 shorter events, 0.1 us)
Async XLA Ops:
  0.6 4.2 %copy-start = (f32[1,16,64,512]{3,2,1,0:T(8,128)S(1)}, f32[1,16,64,512]{3,2,1,0:T(8,128)}, u32[]{:S(2)}) copy-start(f32[1,16,64,512]{3,2,1,0:T(8,128)} %param.8) | copy-start | bytes 6291460
  3.3 14.9 %collective-permute-start.3 = (f32[256,512]{1,0:T(8,128)S(1)}, f32[256,512]{1,0:T(8,128)}, u32[]{:S(2)}, u32[]{:S(2)}) collective-permute-start(f32[256,512]{1,0:T(8,128)S(1)} %get-tuple-element.62), channel_id=1, source_target_pairs={{0,64},{32,96},{64,128},{96,160},{128,192},{160,224},{192,0},{224,... | collective-permute-start | bytes 1572872 | tf_op jit(solution)/shard_map/ppermute | solution.py:323
  4.8 17.3 %copy-start.6 = (s32[3]{0:T(128)S(1)}, s32[3]{0:T(128)}, u32[]{:S(2)}) copy-start(s32[3]{0:T(128)} %band.1) | copy-start | bytes 40
  5.8 35.5 %collective-permute-start = (f32[512,512]{1,0:T(8,128)}, f32[512,512]{1,0:T(8,128)}, u32[]{:S(2)}, u32[]{:S(2)}) collective-permute-start(f32[512,512]{1,0:T(8,128)} %constant_dynamic-slice_fusion.5), channel_id=1, source_target_pairs={{0,1},{1,0},{2,3},{3,2},{4,5},{5,4},{6,7},{7,6},{8,9},{9,8},{10,11... | collective-permute-start | bytes 3145736 | tf_op jit(solution)/shard_map/ppermute | solution.py:323
  5.9 23.0 %collective-permute-start.5 = (f32[256,512]{1,0:T(8,128)}, f32[256,512]{1,0:T(8,128)}, u32[]{:S(2)}, u32[]{:S(2)}) collective-permute-start(f32[256,512]{1,0:T(8,128)} %get-tuple-element.63), channel_id=1, source_target_pairs={{0,192},{32,224},{64,0},{96,32},{128,64},{160,96},{192,128},{224,1... | collective-permute-start | bytes 1572872 | tf_op jit(solution)/shard_map/ppermute | solution.py:323
  6.4 26.0 %collective-permute-start.4 = (f32[256,512]{1,0:T(8,128)}, f32[256,512]{1,0:T(8,128)}, u32[]{:S(2)}, u32[]{:S(2)}) collective-permute-start(f32[256,512]{1,0:T(8,128)} %get-tuple-element.64), channel_id=1, source_target_pairs={{0,128},{32,160},{64,192},{96,224},{128,0},{160,32},{192,64},{224,... | collective-permute-start | bytes 1572872 | tf_op jit(solution)/shard_map/ppermute | solution.py:323
  9.6 31.8 %collective-permute-start.2 = (f32[256,512]{1,0:T(8,128)}, f32[256,512]{1,0:T(8,128)}, u32[]{:S(2)}, u32[]{:S(2)}) collective-permute-start(f32[256,512]{1,0:T(8,128)} %get-tuple-element.65), channel_id=1, source_target_pairs={{1,2},{3,4},{5,6},{7,8},{9,10},{11,12},{13,14},{15,16},{17,18},{19... | collective-permute-start | bytes 1572872 | tf_op jit(solution)/shard_map/ppermute | solution.py:323
  18.2 23.2 %collective-permute-start.1 = (f32[256,512]{1,0:T(8,128)}, f32[256,512]{1,0:T(8,128)}, u32[]{:S(2)}, u32[]{:S(2)}) collective-permute-start(f32[256,512]{1,0:T(8,128)} %get-tuple-element.66), channel_id=1, source_target_pairs={{1,2},{3,4},{5,6},{7,8},{9,10},{11,12},{13,14},{15,16},{17,18},{19... | collective-permute-start | bytes 1572872 | tf_op jit(solution)/shard_map/ppermute | solution.py:323
  27.4 1.3 copy-start.3
  28.8 12.6 %copy-start.4 = (f32[1024,512]{1,0:T(8,128)S(1)}, f32[1024,512]{1,0:T(8,128)}, u32[]{:S(2)}) copy-start(f32[1024,512]{1,0:T(8,128)} %copy-done.3) | copy-start | bytes 6291460
  34.1 24.0 %collective-permute-start.8 = (f32[256,512]{1,0:T(8,128)S(1)}, f32[256,512]{1,0:T(8,128)S(1)}, u32[]{:S(2)}, u32[]{:S(2)}) collective-permute-start(f32[256,512]{1,0:T(8,128)S(1)} %add_add_fusion), channel_id=1, source_target_pairs={{0,32},{32,0},{64,96},{96,64},{128,160},{160,128},{192,224},{224,1... | collective-permute-start | bytes 1572872 | tf_op jit(solution)/shard_map/ppermute | solution.py:323
  41.4 1.6 %copy-start.2 = (f32[1,16,64,512]{3,2,1,0:T(8,128)S(1)}, f32[1,16,64,512]{3,2,1,0:T(8,128)}, u32[]{:S(2)}) copy-start(f32[1,16,64,512]{3,2,1,0:T(8,128)} %param.7) | copy-start | bytes 6291460
  43.0 21.2 %copy-start.7 = (s32[8]{0:T(128)S(1)}, s32[8]{0:T(128)}, u32[]{:S(2)}) copy-start(s32[8]{0:T(128)} %param.13) | copy-start | bytes 100
  43.0 22.6 %copy-start.8 = (f32[8]{0:T(128)S(1)}, f32[8]{0:T(128)}, u32[]{:S(2)}) copy-start(f32[8]{0:T(128)} %param.11) | copy-start | bytes 100
  50.9 19.0 %collective-permute-start.6 = (f32[512,512]{1,0:T(8,128)}, f32[512,512]{1,0:T(8,128)}, u32[]{:S(2)}, u32[]{:S(2)}) collective-permute-start(f32[512,512]{1,0:T(8,128)} %get-tuple-element.39), channel_id=1, source_target_pairs={{0,1},{1,0},{2,3},{3,2},{4,5},{5,4},{6,7},{7,6},{8,9},{9,8},{10,11... | collective-permute-start | bytes 3145736 | tf_op jit(solution)/shard_map/ppermute | solution.py:323
  51.0 37.8 %collective-permute-start.7 = (f32[512,512]{1,0:T(8,128)}, f32[512,512]{1,0:T(8,128)}, u32[]{:S(2)}, u32[]{:S(2)}) collective-permute-start(f32[512,512]{1,0:T(8,128)} %get-tuple-element.40), channel_id=1, source_target_pairs={{1,2},{3,4},{5,6},{7,8},{9,10},{11,12},{13,14},{15,16},{17,18},{19... | collective-permute-start | bytes 3145736 | tf_op jit(solution)/shard_map/ppermute | solution.py:323
  59.0 36.5 %collective-permute-start.11 = (f32[256,512]{1,0:T(8,128)}, f32[256,512]{1,0:T(8,128)}, u32[]{:S(2)}, u32[]{:S(2)}) collective-permute-start(f32[256,512]{1,0:T(8,128)} %add.91.sum0), channel_id=1, source_target_pairs={{0,64},{32,96},{64,128},{96,160},{128,192},{160,224},{192,0},{224,... | collective-permute-start | bytes 1572872 | tf_op jit(solution)/shard_map/ppermute | solution.py:323
  62.1 33.4 %collective-permute-start.10 = (f32[256,512]{1,0:T(8,128)}, f32[256,512]{1,0:T(8,128)}, u32[]{:S(2)}, u32[]{:S(2)}) collective-permute-start(f32[256,512]{1,0:T(8,128)} %add.91.sum0), channel_id=1, source_target_pairs={{0,128},{32,160},{64,192},{96,224},{128,0},{160,32},{192,64},{224,... | collective-permute-start | bytes 1572872 | tf_op jit(solution)/shard_map/ppermute | solution.py:323
  62.4 33.1 %collective-permute-start.9 = (f32[256,512]{1,0:T(8,128)}, f32[256,512]{1,0:T(8,128)}, u32[]{:S(2)}, u32[]{:S(2)}) collective-permute-start(f32[256,512]{1,0:T(8,128)} %add.91.sum0), channel_id=1, source_target_pairs={{0,192},{32,224},{64,0},{96,32},{128,64},{160,96},{192,128},{224,1... | collective-permute-start | bytes 1572872 | tf_op jit(solution)/shard_map/ppermute | solution.py:323
  88.7 6.8 %copy-start.1 = (f32[1,16,64,512]{3,2,1,0:T(8,128)S(1)}, f32[1,16,64,512]{3,2,1,0:T(8,128)}, u32[]{:S(2)}) copy-start(f32[1,16,64,512]{3,2,1,0:T(8,128)} %param.9) | copy-start | bytes 6291460
  88.7 6.8 %copy-start.5 = (f32[16,64,512]{2,1,0:T(8,128)S(1)}, f32[16,64,512]{2,1,0:T(8,128)}, u32[]{:S(2)}) copy-start(f32[16,64,512]{2,1,0:T(8,128)} %param.10) | copy-start | bytes 6291460
  99.3 26.1 %collective-permute-start.20 = (f32[512,512]{1,0:T(8,128)S(1)}, f32[512,512]{1,0:T(8,128)S(1)}, u32[]{:S(2)}, u32[]{:S(2)}) collective-permute-start(f32[512,512]{1,0:T(8,128)S(1)} %get-tuple-element.53), channel_id=1, source_target_pairs={{0,1},{1,0},{2,3},{3,2},{4,5},{5,4},{6,7},{7,6},{8,9},{9,8},{10,11... | collective-permute-start | bytes 3145736 | tf_op jit(solution)/shard_map/ppermute | solution.py:323
  99.4 28.1 %collective-permute-start.22 = (f32[512,512]{1,0:T(8,128)S(1)}, f32[512,512]{1,0:T(8,128)S(1)}, u32[]{:S(2)}, u32[]{:S(2)}) collective-permute-start(f32[512,512]{1,0:T(8,128)S(1)} %get-tuple-element.57), channel_id=1, source_target_pairs={{1,2},{3,4},{5,6},{7,8},{9,10},{11,12},{13,14},{15,16},{17,18},{19... | collective-permute-start | bytes 3145736 | tf_op jit(solution)/shard_map/ppermute | solution.py:323
  103.1 1.3 collective-permute-start.12
  104.3 7.1 %collective-permute-start.15 = (f32[8,128]{1,0:T(8,128)S(1)}, f32[8,128]{1,0:T(8,128)S(1)}, u32[]{:S(2)}, u32[]{:S(2)}) collective-permute-start(f32[8,128]{1,0:T(8,128)S(1)} %add.92), channel_id=1, source_target_pairs={{0,192},{32,224},{64,0},{96,32},{128,64},{160,96},{192,128},{224,1... | collective-permute-start | bytes 12296 | tf_op jit(solution)/shard_map/ppermute | solution.py:323
  104.3 7.1 %collective-permute-start.14 = (f32[8,128]{1,0:T(8,128)S(1)}, f32[8,128]{1,0:T(8,128)S(1)}, u32[]{:S(2)}, u32[]{:S(2)}) collective-permute-start(f32[8,128]{1,0:T(8,128)S(1)} %add.92), channel_id=1, source_target_pairs={{0,128},{32,160},{64,192},{96,224},{128,0},{160,32},{192,64},{224,... | collective-permute-start | bytes 12296 | tf_op jit(solution)/shard_map/ppermute | solution.py:323
  105.8 5.6 %collective-permute-start.13 = (f32[8,128]{1,0:T(8,128)S(1)}, f32[8,128]{1,0:T(8,128)S(1)}, u32[]{:S(2)}, u32[]{:S(2)}) collective-permute-start(f32[8,128]{1,0:T(8,128)S(1)} %add.92), channel_id=1, source_target_pairs={{0,64},{32,96},{64,128},{96,160},{128,192},{160,224},{192,0},{224,... | collective-permute-start | bytes 12296 | tf_op jit(solution)/shard_map/ppermute | solution.py:323
  111.4 5.1 %collective-permute-start.18 = (f32[8,128]{1,0:T(8,128)S(1)}, f32[8,128]{1,0:T(8,128)S(1)}, u32[]{:S(2)}, u32[]{:S(2)}) collective-permute-start(f32[8,128]{1,0:T(8,128)S(1)} %add_add_fusion.2), channel_id=1, source_target_pairs={{0,24},{1,25},{2,26},{3,27},{4,28},{5,29},{6,30},{7,31},{8,0},{9,1... | collective-permute-start | bytes 12296 | tf_op jit(solution)/shard_map/ppermute | solution.py:323
  111.5 5.2 %collective-permute-start.17 = (f32[8,128]{1,0:T(8,128)S(1)}, f32[8,128]{1,0:T(8,128)S(1)}, u32[]{:S(2)}, u32[]{:S(2)}) collective-permute-start(f32[8,128]{1,0:T(8,128)S(1)} %add_add_fusion.2), channel_id=1, source_target_pairs={{0,16},{1,17},{2,18},{3,19},{4,20},{5,21},{6,22},{7,23},{8,24},{9,... | collective-permute-start | bytes 12296 | tf_op jit(solution)/shard_map/ppermute | solution.py:323
  114.5 3.6 %collective-permute-start.16 = (f32[8,128]{1,0:T(8,128)S(1)}, f32[8,128]{1,0:T(8,128)S(1)}, u32[]{:S(2)}, u32[]{:S(2)}) collective-permute-start(f32[8,128]{1,0:T(8,128)S(1)} %add_add_fusion.2), channel_id=1, source_target_pairs={{0,8},{1,9},{2,10},{3,11},{4,12},{5,13},{6,14},{7,15},{8,16},{9,17... | collective-permute-start | bytes 12296 | tf_op jit(solution)/shard_map/ppermute | solution.py:323
  118.2 7.1 %collective-permute-start.19 = (f32[8,128]{1,0:T(8,128)S(1)}, f32[8,128]{1,0:T(8,128)S(1)}, u32[]{:S(2)}, u32[]{:S(2)}) collective-permute-start(f32[8,128]{1,0:T(8,128)S(1)} %add_add_fusion.1), channel_id=1, source_target_pairs={{0,2},{1,3},{2,0},{3,1},{4,6},{5,7},{6,4},{7,5},{8,10},{9,11},{10,... | collective-permute-start | bytes 12296 | tf_op jit(solution)/shard_map/ppermute | solution.py:323
  125.3 4.5 %collective-permute-start.21 = (f32[8,128]{1,0:T(8,128)S(1)}, f32[8,128]{1,0:T(8,128)S(1)}, u32[]{:S(2)}, u32[]{:S(2)}) collective-permute-start(f32[8,128]{1,0:T(8,128)S(1)} %add.99), channel_id=1, source_target_pairs={{0,4},{1,5},{2,6},{3,7},{4,0},{5,1},{6,2},{7,3},{8,12},{9,13},{10,... | collective-permute-start | bytes 12296 | tf_op jit(solution)/shard_map/ppermute | solution.py:323
  129.8 9.7 %collective-permute-start.23 = (f32[8,128]{1,0:T(8,128)S(1)}, f32[8,128]{1,0:T(8,128)S(1)}, u32[]{:S(2)}, u32[]{:S(2)}) collective-permute-start(f32[8,128]{1,0:T(8,128)S(1)} %add.100), channel_id=1, source_target_pairs={{0,32},{32,0},{64,96},{96,64},{128,160},{160,128},{192,224},{224,1... | collective-permute-start | bytes 12296 | tf_op jit(solution)/shard_map/ppermute | solution.py:323

commit v13 on v12

--- a/solution.py
+++ b/solution.py
@@ -282,7 +282,7 @@
 def gradient_kernel(z, shifted, kyh, kyl, kxh, kxl, out, mid, result, sems):
     half = mid.shape[0]
     leaving = []
-    for g in range(2):
+    for g in range(out.shape[0] // half):
         rows = slice(g * half, (g + 1) * half)
         result[rows, :] = shifted[rows, :] * rows_and_columns(z, g, kyh, kyl, kxh, kxl, mid)
         leaving.append(pltpu.make_async_copy(result.at[rows], out.at[rows], sems.at[g]))
@@ -468,7 +468,7 @@
         in_specs=[vmem] * 6,
         out_specs=anywhere,
         out_shape=shape(rows, nx),
-        scratch_shapes=[scratch[1], whole, pltpu.SemaphoreType.DMA((2,))],
+        scratch_shapes=[pltpu.VMEM((block, nx), F32), whole, pltpu.SemaphoreType.DMA((count,))],
         compiler_params=params,
         name="gradient",
     )(z, shifted, *tables)

time: 140 us -> 141 us (level)
  no operation moved by 1% of the time
where the time goes in v13:
time: 141 us; the launch traced here: 140 us
  starting transfers between devices  50.8 us (36%)
  waiting for transfers between devices  39.2 us (28%)
  Pallas kernels  34.4 us (24%)
  local copies, waits for them, and re-layouts  8.92 us (6%)
  other arithmetic  5.91 us (4%)
    ppermute x24, starting transfers between devices, send(): return lax.ppermute(value, axis, pairs)  50.8 us
    ppermute x24, waiting for transfers between devices, send(): return lax.ppermute(value, axis, pairs)  39.2 us
    pallas_call x1, Pallas kernels, body(): pl.pallas_call(functools.partial(potential_kernel, ny=ny), in_specs=[smem...  7.84 us
    pallas_call x1, Pallas kernels, body(): pl.pallas_call(functools.partial(second_kernel, ny=ny), in_specs=[smem, s...  6.76 us
    pallas_call x1, Pallas kernels, body(): pl.pallas_call(gradient_kernel, in_specs=[vmem] * 6, out_specs=anywhere,...  3.77 us
    pallas_call x1, Pallas kernels, body(): pl.pallas_call(ratio_kernel, in_specs=[smem, smem] + [vmem] * 4 + [anywhe...  3.7 us
    pallas_call x1, Pallas kernels, body(): y, stats = own_log(kz, prior)  3.01 us
    pallas_call x1, Pallas kernels, body(): y, stats = own_log(kz, own_at)  3.01 us
  transfers between devices with their start and end apart: 24, of which 10 were waited for; matrix products, arithmetic and copies ran while one was open for 6% of the time, Pallas kernels for 22%

profile of v13, /device:TPU:10, one launch (start us, length us, event | category | flops | bytes accessed | tf_op | source)
XLA Modules:
  0.0 140.2 jit_solution(16048448176142754152)
XLA Ops:
  0.7 2.6 %constant_dynamic-slice_fusion.3 = (f32[256,512]{1,0:T(8,128)S(1)}, f32[256,512]{1,0:T(8,128)}, f32[256,512]{1,0:T(8,128)}) fusion(f32[1024,512]{1,0:T(8,128)} %bitcast.18, s32[]{:T(128)S(6)} %select_n.43, s32[]{:T(128)S(6)} %select_n.45, s32[]{:T(128)S(6)} %select_n.44), kind=kLoop, calls=%fused_computation.9 | loop fusion | bytes 3145740 | tf_op jit(solution)/shard_map/dynamic_slice | solution.py:338
  3.3 1.5 %collective-permute-start.3 = (f32[256,512]{1,0:T(8,128)S(1)}, f32[256,512]{1,0:T(8,128)}, u32[]{:S(2)}, u32[]{:S(2)}) collective-permute-start(f32[256,512]{1,0:T(8,128)S(1)} %get-tuple-element.62), channel_id=1, source_target_pairs={{0,64},{32,96},{64,128},{96,160},{128,192},{160,224},{192,0},{224,... | collective-permute-start | bytes 1572872 | tf_op jit(solution)/shard_map/ppermute | solution.py:323
  4.8 1.0 constant_dynamic-slice_fusion.5
  5.9 0.5 collective-permute-start.5
  6.4 2.1 %collective-permute-start.4 = (f32[256,512]{1,0:T(8,128)}, f32[256,512]{1,0:T(8,128)}, u32[]{:S(2)}, u32[]{:S(2)}) collective-permute-start(f32[256,512]{1,0:T(8,128)} %get-tuple-element.64), channel_id=1, source_target_pairs={{0,128},{32,160},{64,192},{96,224},{128,0},{160,32},{192,64},{224,... | collective-permute-start | bytes 1572872 | tf_op jit(solution)/shard_map/ppermute | solution.py:323
  8.5 1.1 constant_dynamic-slice_fusion.4
  9.6 6.0 %collective-permute-start.2 = (f32[256,512]{1,0:T(8,128)}, f32[256,512]{1,0:T(8,128)}, u32[]{:S(2)}, u32[]{:S(2)}) collective-permute-start(f32[256,512]{1,0:T(8,128)} %get-tuple-element.65), channel_id=1, source_target_pairs={{1,2},{3,4},{5,6},{7,8},{9,10},{11,12},{13,14},{15,16},{17,18},{19... | collective-permute-start | bytes 1572872 | tf_op jit(solution)/shard_map/ppermute | solution.py:323
  15.6 2.6 %collective-permute-done.3 = f32[256,512]{1,0:T(8,128)} collective-permute-done((f32[256,512]{1,0:T(8,128)S(1)}, f32[256,512]{1,0:T(8,128)}, u32[]{:S(2)}, u32[]{:S(2)}) %collective-permute-start.3) | collective-permute-done | bytes 524320 | tf_op jit(solution)/shard_map/ppermute | solution.py:323
  18.2 3.8 %collective-permute-start.1 = (f32[256,512]{1,0:T(8,128)}, f32[256,512]{1,0:T(8,128)}, u32[]{:S(2)}, u32[]{:S(2)}) collective-permute-start(f32[256,512]{1,0:T(8,128)} %get-tuple-element.66), channel_id=1, source_target_pairs={{1,2},{3,4},{5,6},{7,8},{9,10},{11,12},{13,14},{15,16},{17,18},{19... | collective-permute-start | bytes 1572872 | tf_op jit(solution)/shard_map/ppermute | solution.py:323
  22.1 0.6 slice.12
  22.7 1.1 tables.1
  23.8 0.7 compare_select_fusion.kz
  24.4 3.0 %own_log.2 = (f32[1024,512]{1,0:T(8,128)S(1)}, f32[8,128]{1,0:T(8,128)S(1)}) custom-call(f32[9]{0:T(128)S(1)} %compare_select_fusion.kz, f32[1024,512]{1,0:T(8,128)S(1)} %bitcast.17), custom_call_target="tpu_custom_call" | custom-call | tf_op jit(solution)/shard_map/own_log/pallas_call | solution.py:379
  27.4 0.0 copy-start.3
  27.5 1.3 copy-done.3
  28.8 0.1 add_convert_fusion.where
  28.8 3.5 %collective-permute-done.4 = f32[256,512]{1,0:T(8,128)} collective-permute-done((f32[256,512]{1,0:T(8,128)}, f32[256,512]{1,0:T(8,128)}, u32[]{:S(2)}, u32[]{:S(2)}) %collective-permute-start.4) | collective-permute-done | bytes 524320 | tf_op jit(solution)/shard_map/ppermute | solution.py:323
  32.4 1.7 %add_add_fusion = f32[256,512]{1,0:T(8,128)S(1)} fusion(f32[256,512]{1,0:T(8,128)} %collective-permute-done.5, f32[256,512]{1,0:T(8,128)} %collective-permute-done.4, f32[256,512]{1,0:T(8,128)} %collective-permute-done.3, f32[1024,512]{1,0:T(8,128)} %bitcast.19, s32[]{:T(128)S(6)} %select_n.42), kind=kLoop, calls=%fused_computation | loop fusion | flops 393216 | bytes 2621444 | tf_op jit(solution)/shard_map/add | solution.py:380
  34.1 7.3 %collective-permute-start.8 = (f32[256,512]{1,0:T(8,128)S(1)}, f32[256,512]{1,0:T(8,128)S(1)}, u32[]{:S(2)}, u32[]{:S(2)}) collective-permute-start(f32[256,512]{1,0:T(8,128)S(1)} %add_add_fusion), channel_id=1, source_target_pairs={{0,32},{32,0},{64,96},{96,64},{128,160},{160,128},{192,224},{224,1... | collective-permute-start | bytes 1572872 | tf_op jit(solution)/shard_map/ppermute | solution.py:323
  41.4 0.0 collective-permute-done.2.more
  41.4 0.0 copy-start.2
  41.4 1.6 %copy-done.2 = f32[1,16,64,512]{3,2,1,0:T(8,128)S(1)} copy-done((f32[1,16,64,512]{3,2,1,0:T(8,128)S(1)}, f32[1,16,64,512]{3,2,1,0:T(8,128)}, u32[]{:S(2)}) %copy-start.2) | copy-done | bytes 2097176
  43.0 7.8 %potential.1 = (f32[1024,512]{1,0:T(8,128)S(1)}, f32[512,512]{1,0:T(8,128)}, f32[512,512]{1,0:T(8,128)}) custom-call(s32[3]{0:T(128)S(1)} %add_convert_fusion.where, f32[9]{0:T(128)S(1)} %compare_select_fusion.kz, f32[512,512]{1,0:T(8,128)} %collective-permute-done.near, f32[256,512]{1,0:T(8,128)} %collective-permute-done.1.far, ...), custom_call_target="tpu_custom_call" | custom-call | tf_op jit(solution)/shard_map/potential/pallas_call | solution.py:383
  50.9 0.1 collective-permute-start.6
  51.0 3.8 %collective-permute-start.7 = (f32[512,512]{1,0:T(8,128)}, f32[512,512]{1,0:T(8,128)}, u32[]{:S(2)}, u32[]{:S(2)}) collective-permute-start(f32[512,512]{1,0:T(8,128)} %get-tuple-element.40), channel_id=1, source_target_pairs={{1,2},{3,4},{5,6},{7,8},{9,10},{11,12},{13,14},{15,16},{17,18},{19... | collective-permute-start | bytes 3145736 | tf_op jit(solution)/shard_map/ppermute | solution.py:323
  54.8 3.4 %collective-permute-done.8 = f32[256,512]{1,0:T(8,128)S(1)} collective-permute-done((f32[256,512]{1,0:T(8,128)S(1)}, f32[256,512]{1,0:T(8,128)S(1)}, u32[]{:S(2)}, u32[]{:S(2)}) %collective-permute-start.8) | collective-permute-done | bytes 524320 | tf_op jit(solution)/shard_map/ppermute | solution.py:323
  58.1 0.9 add.91.sum0
  59.0 3.1 %collective-permute-start.11 = (f32[256,512]{1,0:T(8,128)}, f32[256,512]{1,0:T(8,128)}, u32[]{:S(2)}, u32[]{:S(2)}) collective-permute-start(f32[256,512]{1,0:T(8,128)} %add.91.sum0), channel_id=1, source_target_pairs={{0,64},{32,96},{64,128},{96,160},{128,192},{160,224},{192,0},{224,... | collective-permute-start | bytes 1572872 | tf_op jit(solution)/shard_map/ppermute | solution.py:323
  62.1 0.3 collective-permute-start.10
  62.4 1.8 %collective-permute-start.9 = (f32[256,512]{1,0:T(8,128)}, f32[256,512]{1,0:T(8,128)}, u32[]{:S(2)}, u32[]{:S(2)}) collective-permute-start(f32[256,512]{1,0:T(8,128)} %add.91.sum0), channel_id=1, source_target_pairs={{0,192},{32,224},{64,0},{96,32},{128,64},{160,96},{192,128},{224,1... | collective-permute-start | bytes 1572872 | tf_op jit(solution)/shard_map/ppermute | solution.py:323
  64.2 0.7 dynamic_slice.21
  64.8 0.8 pad_add_fusion.at
  65.6 1.3 fusion
  66.9 3.0 %own_log.3 = (f32[1024,512]{1,0:T(8,128)S(1)}, f32[8,128]{1,0:T(8,128)S(1)}) custom-call(f32[9]{0:T(128)S(1)} %compare_select_fusion.kz, f32[1024,512]{1,0:T(8,128)S(1)} %get-tuple-element.43.field.potential), custom_call_target="tpu_custom_call" | custom-call | tf_op jit(solution)/shard_map/own_log/pallas_call | solution.py:398
  69.9 0.0 collective-permute-done.6.near
  69.9 18.8 %collective-permute-done.7.far = f32[512,512]{1,0:T(8,128)} collective-permute-done((f32[512,512]{1,0:T(8,128)}, f32[512,512]{1,0:T(8,128)}, u32[]{:S(2)}, u32[]{:S(2)}) %collective-permute-start.7) | collective-permute-done | bytes 1048608 | tf_op jit(solution)/shard_map/ppermute | solution.py:323
  88.7 6.8 %second.1 = (f32[1024,512]{1,0:T(8,128)S(1)}, f32[8,128]{1,0:T(8,128)S(1)}) custom-call(s32[3]{0:T(128)S(1)} %add_convert_fusion.where, f32[9]{0:T(128)S(1)} %compare_select_fusion.kz, f32[512,512]{1,0:T(8,128)} %collective-permute-done.6.near, f32[512,512]{1,0:T(8,128)} %collective-permute-done.7.far, f32[1024,512]{1,0:T(8,128)S(1)} %get-tuple-element.44.y, ...), custom_call_target="tpu_custom_call" | custom-call | tf_op jit(solution)/shard_map/second/pallas_call | solution.py:399
  95.5 0.0 collective-permute-done.10.sum2
  95.5 0.0 collective-permute-done.9.sum1
  95.5 3.7 %ratio.1 = (f32[1024,512]{1,0:T(8,128)S(1)}, f32[512,512]{1,0:T(8,128)S(1)}, f32[512,512]{1,0:T(8,128)S(1)}, f32[8,128]{1,0:T(8,128)S(1)}) custom-call(s32[3]{0:T(128)S(1)} %pad_add_fusion.at, f32[1]{0:T(128)} %bitcast.3.weight, f32[1024,512]{1,0:T(8,128)S(1)} %get-tuple-element.46.second, f32[8,128]{1,0:T(8,128)S(1)} %get-tuple-element.47.scale.stats, ...), custom_call_target="tpu_custom_call" | custom-call | tf_op jit(solution)/shard_map/ratio/pallas_call | solution.py:408
  99.3 0.1 collective-permute-start.20
  99.4 3.7 %collective-permute-start.22 = (f32[512,512]{1,0:T(8,128)S(1)}, f32[512,512]{1,0:T(8,128)S(1)}, u32[]{:S(2)}, u32[]{:S(2)}) collective-permute-start(f32[512,512]{1,0:T(8,128)S(1)} %get-tuple-element.57), channel_id=1, source_target_pairs={{1,2},{3,4},{5,6},{7,8},{9,10},{11,12},{13,14},{15,16},{17,18},{19... | collective-permute-start | bytes 3145736 | tf_op jit(solution)/shard_map/ppermute | solution.py:323
  103.1 0.1 collective-permute-start.12
  103.2 1.2 collective-permute-done.12
  104.3 0.0 collective-permute-start.15
  104.3 1.5 %collective-permute-start.14 = (f32[8,128]{1,0:T(8,128)S(1)}, f32[8,128]{1,0:T(8,128)S(1)}, u32[]{:S(2)}, u32[]{:S(2)}) collective-permute-start(f32[8,128]{1,0:T(8,128)S(1)} %add.92), channel_id=1, source_target_pairs={{0,128},{32,160},{64,192},{96,224},{128,0},{160,32},{192,64},{224,... | collective-permute-start | bytes 12296 | tf_op jit(solution)/shard_map/ppermute | solution.py:323
  105.8 2.6 %collective-permute-start.13 = (f32[8,128]{1,0:T(8,128)S(1)}, f32[8,128]{1,0:T(8,128)S(1)}, u32[]{:S(2)}, u32[]{:S(2)}) collective-permute-start(f32[8,128]{1,0:T(8,128)S(1)} %add.92), channel_id=1, source_target_pairs={{0,64},{32,96},{64,128},{96,160},{128,192},{160,224},{192,0},{224,... | collective-permute-start | bytes 12296 | tf_op jit(solution)/shard_map/ppermute | solution.py:323
  108.4 3.0 %own_linear.1 = (f32[1024,512]{1,0:T(8,128)S(1)}, f32[1024,512]{1,0:T(8,128)S(1)}) custom-call(f32[9]{0:T(128)S(1)} %compare_select_fusion.kz, f32[1024,512]{1,0:T(8,128)S(1)} %get-tuple-element.50.field, f32[1024,512]{1,0:T(8,128)S(1)} %get-tuple-element.43.field.potential, f32[8,128]{1,0:T(8,128)S(1)} %get-tuple-element.47.scale.stats), custom_call_target="tpu_custom_call" | custom-call | tf_op jit(solution)/shard_map/own_linear/pallas_call | solution.py:431
  111.4 0.0 collective-permute-done.15
  111.4 0.0 collective-permute-done.13
  111.4 0.1 collective-permute-start.18
  111.5 3.0 %collective-permute-start.17 = (f32[8,128]{1,0:T(8,128)S(1)}, f32[8,128]{1,0:T(8,128)S(1)}, u32[]{:S(2)}, u32[]{:S(2)}) collective-permute-start(f32[8,128]{1,0:T(8,128)S(1)} %add_add_fusion.2), channel_id=1, source_target_pairs={{0,16},{1,17},{2,18},{3,19},{4,20},{5,21},{6,22},{7,23},{8,24},{9,... | collective-permute-start | bytes 12296 | tf_op jit(solution)/shard_map/ppermute | solution.py:323
  114.5 2.0 %collective-permute-start.16 = (f32[8,128]{1,0:T(8,128)S(1)}, f32[8,128]{1,0:T(8,128)S(1)}, u32[]{:S(2)}, u32[]{:S(2)}) collective-permute-start(f32[8,128]{1,0:T(8,128)S(1)} %add_add_fusion.2), channel_id=1, source_target_pairs={{0,8},{1,9},{2,10},{3,11},{4,12},{5,13},{6,14},{7,15},{8,16},{9,17... | collective-permute-start | bytes 12296 | tf_op jit(solution)/shard_map/ppermute | solution.py:323
  116.5 0.2 collective-permute-done.17
  116.7 1.5 %collective-permute-done.16 = f32[8,128]{1,0:T(8,128)S(1)} collective-permute-done((f32[8,128]{1,0:T(8,128)S(1)}, f32[8,128]{1,0:T(8,128)S(1)}, u32[]{:S(2)}, u32[]{:S(2)}) %collective-permute-start.16) | collective-permute-done | bytes 4128 | tf_op jit(solution)/shard_map/ppermute | solution.py:323
  118.2 0.6 collective-permute-start.19
  118.8 6.6 %collective-permute-done.19 = f32[8,128]{1,0:T(8,128)S(1)} collective-permute-done((f32[8,128]{1,0:T(8,128)S(1)}, f32[8,128]{1,0:T(8,128)S(1)}, u32[]{:S(2)}, u32[]{:S(2)}) %collective-permute-start.19) | collective-permute-done | bytes 4128 | tf_op jit(solution)/shard_map/ppermute | solution.py:323
  125.3 0.8 collective-permute-start.21
  126.1 1.3 collective-permute-done.22.far
  127.5 2.3 %gather.1.z = f32[1024,512]{1,0:T(8,128)S(1)} custom-call(s32[3]{0:T(128)S(1)} %add_convert_fusion.where, f32[9]{0:T(128)S(1)} %compare_select_fusion.kz, f32[512,512]{1,0:T(8,128)S(1)} %collective-permute-done.20.near, f32[512,512]{1,0:T(8,128)S(1)} %collective-permute-done.22.far, f32[1024,512]{1,0:T(8,128)S(1)} %get-tuple-element.58.y, ...), custom_call_target="tpu_custom_call" | custom-call | tf_op jit(solution)/shard_map/gather/pallas_call | solution.py:452
  129.7 0.1 collective-permute-done.21
  129.8 6.0 %collective-permute-start.23 = (f32[8,128]{1,0:T(8,128)S(1)}, f32[8,128]{1,0:T(8,128)S(1)}, u32[]{:S(2)}, u32[]{:S(2)}) collective-permute-start(f32[8,128]{1,0:T(8,128)S(1)} %add.100), channel_id=1, source_target_pairs={{0,32},{32,0},{64,96},{96,64},{128,160},{160,128},{192,224},{224,1... | collective-permute-start | bytes 12296 | tf_op jit(solution)/shard_map/ppermute | solution.py:323
  135.9 3.8 %gradient.1 = f32[1024,512]{1,0:T(8,128)} custom-call(f32[1024,512]{1,0:T(8,128)S(1)} %gather.1.z, f32[1024,512]{1,0:T(8,128)S(1)} %get-tuple-element.60.shifted, bf16[256,256]{1,0:T(8,128)(2,1)S(1)} %get-tuple-element.35.kyh, bf16[256,256]{1,0:T(8,128)(2,1)S(1)} %get-tuple-element.36.kyl, bf16[512,512]{1,0:T(8,128)(2,1)S(1)} %get-tuple-element.37.kxh, ...), custom_call_target="tpu_custom_call" | custom-call | tf_op jit(solution)/shard_map/gradient/pallas_call | solution.py:466
  139.7 0.5 multiply_bitcast_fusion
  (29 shorter events, 0.1 us)
Async XLA Ops:
  0.6 4.2 %copy-start = (f32[1,16,64,512]{3,2,1,0:T(8,128)S(1)}, f32[1,16,64,512]{3,2,1,0:T(8,128)}, u32[]{:S(2)}) copy-start(f32[1,16,64,512]{3,2,1,0:T(8,128)} %param.8) | copy-start | bytes 6291460
  3.3 14.9 %collective-permute-start.3 = (f32[256,512]{1,0:T(8,128)S(1)}, f32[256,512]{1,0:T(8,128)}, u32[]{:S(2)}, u32[]{:S(2)}) collective-permute-start(f32[256,512]{1,0:T(8,128)S(1)} %get-tuple-element.62), channel_id=1, source_target_pairs={{0,64},{32,96},{64,128},{96,160},{128,192},{160,224},{192,0},{224,... | collective-permute-start | bytes 1572872 | tf_op jit(solution)/shard_map/ppermute | solution.py:323
  4.8 17.3 %copy-start.6 = (s32[3]{0:T(128)S(1)}, s32[3]{0:T(128)}, u32[]{:S(2)}) copy-start(s32[3]{0:T(128)} %band.1) | copy-start | bytes 40
  5.8 35.5 %collective-permute-start = (f32[512,512]{1,0:T(8,128)}, f32[512,512]{1,0:T(8,128)}, u32[]{:S(2)}, u32[]{:S(2)}) collective-permute-start(f32[512,512]{1,0:T(8,128)} %constant_dynamic-slice_fusion.5), channel_id=1, source_target_pairs={{0,1},{1,0},{2,3},{3,2},{4,5},{5,4},{6,7},{7,6},{8,9},{9,8},{10,11... | collective-permute-start | bytes 3145736 | tf_op jit(solution)/shard_map/ppermute | solution.py:323
  5.9 23.0 %collective-permute-start.5 = (f32[256,512]{1,0:T(8,128)}, f32[256,512]{1,0:T(8,128)}, u32[]{:S(2)}, u32[]{:S(2)}) collective-permute-start(f32[256,512]{1,0:T(8,128)} %get-tuple-element.63), channel_id=1, source_target_pairs={{0,192},{32,224},{64,0},{96,32},{128,64},{160,96},{192,128},{224,1... | collective-permute-start | bytes 1572872 | tf_op jit(solution)/shard_map/ppermute | solution.py:323
  6.4 26.0 %collective-permute-start.4 = (f32[256,512]{1,0:T(8,128)}, f32[256,512]{1,0:T(8,128)}, u32[]{:S(2)}, u32[]{:S(2)}) collective-permute-start(f32[256,512]{1,0:T(8,128)} %get-tuple-element.64), channel_id=1, source_target_pairs={{0,128},{32,160},{64,192},{96,224},{128,0},{160,32},{192,64},{224,... | collective-permute-start | bytes 1572872 | tf_op jit(solution)/shard_map/ppermute | solution.py:323
  9.6 31.8 %collective-permute-start.2 = (f32[256,512]{1,0:T(8,128)}, f32[256,512]{1,0:T(8,128)}, u32[]{:S(2)}, u32[]{:S(2)}) collective-permute-start(f32[256,512]{1,0:T(8,128)} %get-tuple-element.65), channel_id=1, source_target_pairs={{1,2},{3,4},{5,6},{7,8},{9,10},{11,12},{13,14},{15,16},{17,18},{19... | collective-permute-start | bytes 1572872 | tf_op jit(solution)/shard_map/ppermute | solution.py:323
  18.2 23.2 %collective-permute-start.1 = (f32[256,512]{1,0:T(8,128)}, f32[256,512]{1,0:T(8,128)}, u32[]{:S(2)}, u32[]{:S(2)}) collective-permute-start(f32[256,512]{1,0:T(8,128)} %get-tuple-element.66), channel_id=1, source_target_pairs={{1,2},{3,4},{5,6},{7,8},{9,10},{11,12},{13,14},{15,16},{17,18},{19... | collective-permute-start | bytes 1572872 | tf_op jit(solution)/shard_map/ppermute | solution.py:323
  27.4 1.3 copy-start.3
  28.8 12.6 %copy-start.4 = (f32[1024,512]{1,0:T(8,128)S(1)}, f32[1024,512]{1,0:T(8,128)}, u32[]{:S(2)}) copy-start(f32[1024,512]{1,0:T(8,128)} %copy-done.3) | copy-start | bytes 6291460
  34.1 24.0 %collective-permute-start.8 = (f32[256,512]{1,0:T(8,128)S(1)}, f32[256,512]{1,0:T(8,128)S(1)}, u32[]{:S(2)}, u32[]{:S(2)}) collective-permute-start(f32[256,512]{1,0:T(8,128)S(1)} %add_add_fusion), channel_id=1, source_target_pairs={{0,32},{32,0},{64,96},{96,64},{128,160},{160,128},{192,224},{224,1... | collective-permute-start | bytes 1572872 | tf_op jit(solution)/shard_map/ppermute | solution.py:323
  41.4 1.6 %copy-start.2 = (f32[1,16,64,512]{3,2,1,0:T(8,128)S(1)}, f32[1,16,64,512]{3,2,1,0:T(8,128)}, u32[]{:S(2)}) copy-start(f32[1,16,64,512]{3,2,1,0:T(8,128)} %param.7) | copy-start | bytes 6291460
  43.0 21.2 %copy-start.7 = (s32[8]{0:T(128)S(1)}, s32[8]{0:T(128)}, u32[]{:S(2)}) copy-start(s32[8]{0:T(128)} %param.13) | copy-start | bytes 100
  43.0 22.6 %copy-start.8 = (f32[8]{0:T(128)S(1)}, f32[8]{0:T(128)}, u32[]{:S(2)}) copy-start(f32[8]{0:T(128)} %param.11) | copy-start | bytes 100
  50.9 19.0 %collective-permute-start.6 = (f32[512,512]{1,0:T(8,128)}, f32[512,512]{1,0:T(8,128)}, u32[]{:S(2)}, u32[]{:S(2)}) collective-permute-start(f32[512,512]{1,0:T(8,128)} %get-tuple-element.39), channel_id=1, source_target_pairs={{0,1},{1,0},{2,3},{3,2},{4,5},{5,4},{6,7},{7,6},{8,9},{9,8},{10,11... | collective-permute-start | bytes 3145736 | tf_op jit(solution)/shard_map/ppermute | solution.py:323
  51.0 37.8 %collective-permute-start.7 = (f32[512,512]{1,0:T(8,128)}, f32[512,512]{1,0:T(8,128)}, u32[]{:S(2)}, u32[]{:S(2)}) collective-permute-start(f32[512,512]{1,0:T(8,128)} %get-tuple-element.40), channel_id=1, source_target_pairs={{1,2},{3,4},{5,6},{7,8},{9,10},{11,12},{13,14},{15,16},{17,18},{19... | collective-permute-start | bytes 3145736 | tf_op jit(solution)/shard_map/ppermute | solution.py:323
  59.0 36.5 %collective-permute-start.11 = (f32[256,512]{1,0:T(8,128)}, f32[256,512]{1,0:T(8,128)}, u32[]{:S(2)}, u32[]{:S(2)}) collective-permute-start(f32[256,512]{1,0:T(8,128)} %add.91.sum0), channel_id=1, source_target_pairs={{0,64},{32,96},{64,128},{96,160},{128,192},{160,224},{192,0},{224,... | collective-permute-start | bytes 1572872 | tf_op jit(solution)/shard_map/ppermute | solution.py:323
  62.1 33.4 %collective-permute-start.10 = (f32[256,512]{1,0:T(8,128)}, f32[256,512]{1,0:T(8,128)}, u32[]{:S(2)}, u32[]{:S(2)}) collective-permute-start(f32[256,512]{1,0:T(8,128)} %add.91.sum0), channel_id=1, source_target_pairs={{0,128},{32,160},{64,192},{96,224},{128,0},{160,32},{192,64},{224,... | collective-permute-start | bytes 1572872 | tf_op jit(solution)/shard_map/ppermute | solution.py:323
  62.4 33.1 %collective-permute-start.9 = (f32[256,512]{1,0:T(8,128)}, f32[256,512]{1,0:T(8,128)}, u32[]{:S(2)}, u32[]{:S(2)}) collective-permute-start(f32[256,512]{1,0:T(8,128)} %add.91.sum0), channel_id=1, source_target_pairs={{0,192},{32,224},{64,0},{96,32},{128,64},{160,96},{192,128},{224,1... | collective-permute-start | bytes 1572872 | tf_op jit(solution)/shard_map/ppermute | solution.py:323
  88.7 6.8 %copy-start.1 = (f32[1,16,64,512]{3,2,1,0:T(8,128)S(1)}, f32[1,16,64,512]{3,2,1,0:T(8,128)}, u32[]{:S(2)}) copy-start(f32[1,16,64,512]{3,2,1,0:T(8,128)} %param.9) | copy-start | bytes 6291460
  88.7 6.8 %copy-start.5 = (f32[16,64,512]{2,1,0:T(8,128)S(1)}, f32[16,64,512]{2,1,0:T(8,128)}, u32[]{:S(2)}) copy-start(f32[16,64,512]{2,1,0:T(8,128)} %param.10) | copy-start | bytes 6291460
  99.3 26.1 %collective-permute-start.20 = (f32[512,512]{1,0:T(8,128)S(1)}, f32[512,512]{1,0:T(8,128)S(1)}, u32[]{:S(2)}, u32[]{:S(2)}) collective-permute-start(f32[512,512]{1,0:T(8,128)S(1)} %get-tuple-element.53), channel_id=1, source_target_pairs={{0,1},{1,0},{2,3},{3,2},{4,5},{5,4},{6,7},{7,6},{8,9},{9,8},{10,11... | collective-permute-start | bytes 3145736 | tf_op jit(solution)/shard_map/ppermute | solution.py:323
  99.4 28.1 %collective-permute-start.22 = (f32[512,512]{1,0:T(8,128)S(1)}, f32[512,512]{1,0:T(8,128)S(1)}, u32[]{:S(2)}, u32[]{:S(2)}) collective-permute-start(f32[512,512]{1,0:T(8,128)S(1)} %get-tuple-element.57), channel_id=1, source_target_pairs={{1,2},{3,4},{5,6},{7,8},{9,10},{11,12},{13,14},{15,16},{17,18},{19... | collective-permute-start | bytes 3145736 | tf_op jit(solution)/shard_map/ppermute | solution.py:323
  103.1 1.3 collective-permute-start.12
  104.3 7.1 %collective-permute-start.15 = (f32[8,128]{1,0:T(8,128)S(1)}, f32[8,128]{1,0:T(8,128)S(1)}, u32[]{:S(2)}, u32[]{:S(2)}) collective-permute-start(f32[8,128]{1,0:T(8,128)S(1)} %add.92), channel_id=1, source_target_pairs={{0,192},{32,224},{64,0},{96,32},{128,64},{160,96},{192,128},{224,1... | collective-permute-start | bytes 12296 | tf_op jit(solution)/shard_map/ppermute | solution.py:323
  104.3 7.1 %collective-permute-start.14 = (f32[8,128]{1,0:T(8,128)S(1)}, f32[8,128]{1,0:T(8,128)S(1)}, u32[]{:S(2)}, u32[]{:S(2)}) collective-permute-start(f32[8,128]{1,0:T(8,128)S(1)} %add.92), channel_id=1, source_target_pairs={{0,128},{32,160},{64,192},{96,224},{128,0},{160,32},{192,64},{224,... | collective-permute-start | bytes 12296 | tf_op jit(solution)/shard_map/ppermute | solution.py:323
  105.8 5.6 %collective-permute-start.13 = (f32[8,128]{1,0:T(8,128)S(1)}, f32[8,128]{1,0:T(8,128)S(1)}, u32[]{:S(2)}, u32[]{:S(2)}) collective-permute-start(f32[8,128]{1,0:T(8,128)S(1)} %add.92), channel_id=1, source_target_pairs={{0,64},{32,96},{64,128},{96,160},{128,192},{160,224},{192,0},{224,... | collective-permute-start | bytes 12296 | tf_op jit(solution)/shard_map/ppermute | solution.py:323
  111.4 5.1 %collective-permute-start.18 = (f32[8,128]{1,0:T(8,128)S(1)}, f32[8,128]{1,0:T(8,128)S(1)}, u32[]{:S(2)}, u32[]{:S(2)}) collective-permute-start(f32[8,128]{1,0:T(8,128)S(1)} %add_add_fusion.2), channel_id=1, source_target_pairs={{0,24},{1,25},{2,26},{3,27},{4,28},{5,29},{6,30},{7,31},{8,0},{9,1... | collective-permute-start | bytes 12296 | tf_op jit(solution)/shard_map/ppermute | solution.py:323
  111.5 5.2 %collective-permute-start.17 = (f32[8,128]{1,0:T(8,128)S(1)}, f32[8,128]{1,0:T(8,128)S(1)}, u32[]{:S(2)}, u32[]{:S(2)}) collective-permute-start(f32[8,128]{1,0:T(8,128)S(1)} %add_add_fusion.2), channel_id=1, source_target_pairs={{0,16},{1,17},{2,18},{3,19},{4,20},{5,21},{6,22},{7,23},{8,24},{9,... | collective-permute-start | bytes 12296 | tf_op jit(solution)/shard_map/ppermute | solution.py:323
  114.5 3.6 %collective-permute-start.16 = (f32[8,128]{1,0:T(8,128)S(1)}, f32[8,128]{1,0:T(8,128)S(1)}, u32[]{:S(2)}, u32[]{:S(2)}) collective-permute-start(f32[8,128]{1,0:T(8,128)S(1)} %add_add_fusion.2), channel_id=1, source_target_pairs={{0,8},{1,9},{2,10},{3,11},{4,12},{5,13},{6,14},{7,15},{8,16},{9,17... | collective-permute-start | bytes 12296 | tf_op jit(solution)/shard_map/ppermute | solution.py:323
  118.2 7.1 %collective-permute-start.19 = (f32[8,128]{1,0:T(8,128)S(1)}, f32[8,128]{1,0:T(8,128)S(1)}, u32[]{:S(2)}, u32[]{:S(2)}) collective-permute-start(f32[8,128]{1,0:T(8,128)S(1)} %add_add_fusion.1), channel_id=1, source_target_pairs={{0,2},{1,3},{2,0},{3,1},{4,6},{5,7},{6,4},{7,5},{8,10},{9,11},{10,... | collective-permute-start | bytes 12296 | tf_op jit(solution)/shard_map/ppermute | solution.py:323
  125.3 4.5 %collective-permute-start.21 = (f32[8,128]{1,0:T(8,128)S(1)}, f32[8,128]{1,0:T(8,128)S(1)}, u32[]{:S(2)}, u32[]{:S(2)}) collective-permute-start(f32[8,128]{1,0:T(8,128)S(1)} %add.99), channel_id=1, source_target_pairs={{0,4},{1,5},{2,6},{3,7},{4,0},{5,1},{6,2},{7,3},{8,12},{9,13},{10,... | collective-permute-start | bytes 12296 | tf_op jit(solution)/shard_map/ppermute | solution.py:323
  129.8 9.8 %collective-permute-start.23 = (f32[8,128]{1,0:T(8,128)S(1)}, f32[8,128]{1,0:T(8,128)S(1)}, u32[]{:S(2)}, u32[]{:S(2)}) collective-permute-start(f32[8,128]{1,0:T(8,128)S(1)} %add.100), channel_id=1, source_target_pairs={{0,32},{32,0},{64,96},{96,64},{128,160},{160,128},{192,224},{224,1... | collective-permute-start | bytes 12296 | tf_op jit(solution)/shard_map/ppermute | solution.py:323
